TPU v7x, 32 devices: a whole 2x2x4 slice. The times are simulated.
32 devices in a mesh: rows: 4 (over y, x), seq: 8 (over z, core).
Axes of the slice: x: 2, y: 2, z: 4, core: 2. Of those that a mesh axis runs over, the one named last changes fastest.
Arguments:
- inputs: bfloat16 [4, 1024, 768], P('rows', 'seq'), may hold values from -6 to 6
- doc_lengths: int32 [4, 12], P('rows'), may hold values from 1 to 640, 960 in all within a row
- ln1_gain: float32 [768], replicated, may hold values from 0.1 to 1.9
- ln1_bias: float32 [768], replicated, may hold values from -3 to 3
- w_query: bfloat16 [768, 768], replicated, may hold values from -0.21875 to 0.21875
- w_key: bfloat16 [768, 768], replicated, may hold values from -0.21875 to 0.21875
- w_value: bfloat16 [768, 768], replicated, may hold values from -0.21875 to 0.21875
- ln2_gain: float32 [768], replicated, may hold values from 0.1 to 1.9
- ln2_bias: float32 [768], replicated, may hold values from -3 to 3
- w_out: bfloat16 [768, 768], replicated, may hold values from -0.21875 to 0.21875
- ln3_gain: float32 [768], replicated, may hold values from 0.1 to 1.9
- ln3_bias: float32 [768], replicated, may hold values from -3 to 3
- w_up: bfloat16 [768, 3072], replicated, may hold values from -0.21875 to 0.21875
- w_down: bfloat16 [3072, 768], replicated, may hold values from -0.109375 to 0.109375
- out_grad: bfloat16 [4, 1024, 768], P('rows', 'seq'), may hold values from -6 to 6
Outputs:
- output: bfloat16 [4, 1024, 768], P('rows', 'seq')
- grad_inputs: bfloat16 [4, 1024, 768], P('rows', 'seq')
- grad_ln1_gain: float32 [768], P(('rows', 'seq'))
- grad_ln1_bias: float32 [768], P(('rows', 'seq'))
- grad_w_query: float32 [768, 768], P(('rows', 'seq'))
- grad_w_key: float32 [768, 768], P(('rows', 'seq'))
- grad_w_value: float32 [768, 768], P(('rows', 'seq'))
- grad_ln2_gain: float32 [768], P(('rows', 'seq'))
- grad_ln2_bias: float32 [768], P(('rows', 'seq'))
- grad_w_out: float32 [768, 768], P(('rows', 'seq'))
- grad_ln3_gain: float32 [768], P(('rows', 'seq'))
- grad_ln3_bias: float32 [768], P(('rows', 'seq'))
- grad_w_up: float32 [768, 3072], P(('rows', 'seq'))
- grad_w_down: float32 [3072, 768], P(('rows', 'seq'))
Inputs may be any that keep to these rules, and one draw needn't show every extreme that they name: `doc_lengths`: each row's 12 document lengths sum to 960; the last 64 positions of a row are padding; in every row one document has exactly 640 tokens.
All inputs are finite; a program needn't handle non-finite values.
Results may differ from a plain program's by a relative error of at most 0.019.
Values may be sent and summed in bfloat16 or wider, within the bound.
No kernel may reach another device: no remote copies, remote signals or barrier semaphores. Data moves between devices by JAX's collectives and lax.ppermute only.
A program may use at most 192 MiB of HBM per device.

v0:
```python
import math

import jax
import jax.numpy as jnp
from jax import lax
from jax.sharding import PartitionSpec as P

HEADS = 12
HEAD_DIM = 64


segment_pairs = ((2048, 1), (4096, 2), (8192, 4), (16384, 6))
masked_value = -1e30


def layer_norm(vector, gain_vec, bias_vec):
    row_mean = jnp.mean(vector, axis=-1, keepdims=True)
    centered = vector - row_mean
    row_var = jnp.mean(centered * centered, axis=-1, keepdims=True)
    return centered * lax.rsqrt(row_var + 1e-05) * gain_vec + bias_vec


def doc_of(positions, doc_ends):
    return jnp.sum((positions[:, None] >= doc_ends[None, :]).astype(jnp.int32), axis=1)


def pair_terms(query_pos, key_pos, query_doc, key_doc, head_count):
    head_ids = jnp.arange(head_count, dtype=jnp.int32)
    multiplicity = jnp.zeros((head_count, query_pos.shape[0], key_pos.shape[0]), jnp.float32)
    for seg_width, dilation in segment_pairs:
        same_seg = query_pos[:, None] // seg_width == key_pos[None, :] // seg_width
        query_pick = (query_pos % seg_width % dilation)[None, :] == (head_ids % dilation)[:, None]
        key_pick = (key_pos % seg_width % dilation)[None, :] == (head_ids % dilation)[:, None]
        joined = same_seg[None] & query_pick[:, :, None] & key_pick[:, None, :]
        multiplicity = multiplicity + joined.astype(jnp.float32)
    allowed = (key_pos[None, :] <= query_pos[:, None]) & (query_doc[:, None] == key_doc[None, :])
    allowed = allowed[None] & (multiplicity > 0.0)
    return (jnp.log(jnp.maximum(multiplicity, 1.0)), allowed)


def rows_inner(left, right):
    return lax.dot_general(
        left, right, (((0,), (0,)), ((), ())), preferred_element_type=jnp.float32
    )


def cols_inner(left, right):
    return lax.dot_general(
        left, right, (((1,), (1,)), ((), ())), preferred_element_type=jnp.float32
    )


def over_blocks(state, piece, step_fn):
    total_rows = piece[0].shape[0]
    block_rows = math.gcd(total_rows, 512)
    block_total = total_rows // block_rows
    split = tuple((part.reshape((block_total, block_rows) + part.shape[1:]) for part in piece))

    def inner(carried, block_item):
        return (step_fn(carried, block_item[1], block_item[0] * block_rows), None)

    result, unused = lax.scan(inner, state, (jnp.arange(block_total, dtype=jnp.int32), split))
    return result


def add_rows(buffer, start_pos, addend):
    current = lax.dynamic_slice_in_dim(buffer, start_pos, addend.shape[0], 0)
    return lax.dynamic_update_slice_in_dim(buffer, current + addend, start_pos, 0)


def shards(
    inputs,
    doc_lengths,
    ln1_gain,
    ln1_bias,
    w_query,
    w_key,
    w_value,
    ln2_gain,
    ln2_bias,
    w_out,
    ln3_gain,
    ln3_bias,
    w_up,
    w_down,
    out_grad,
):
    tok_rows = inputs.shape[1]
    head_count = HEADS
    head_size = HEAD_DIM
    model_width = inputs.shape[2]
    row_total = tok_rows * lax.axis_size("seq")
    layer_in = inputs[0].astype(jnp.float32)
    doc_ends = jnp.cumsum(doc_lengths[0])
    first_pos = lax.axis_index("seq") * tok_rows
    query_pos = first_pos + jnp.arange(tok_rows, dtype=jnp.int32)
    query_doc = doc_of(query_pos, doc_ends)
    valid = (query_doc < doc_lengths.shape[1]).astype(jnp.float32)
    first_norm, first_back = jax.vjp(layer_norm, layer_in, ln1_gain, ln1_bias)
    normed_one = first_norm.astype(jnp.bfloat16)
    queries = jnp.dot(normed_one, w_query, preferred_element_type=jnp.float32).astype(jnp.bfloat16)
    keys_local = jnp.dot(normed_one, w_key, preferred_element_type=jnp.float32).astype(jnp.bfloat16)
    values_local = jnp.dot(normed_one, w_value, preferred_element_type=jnp.float32).astype(
        jnp.bfloat16
    )
    query_heads = queries.reshape(tok_rows, head_count, head_size)

    def key_block_terms(key_start, key_count):
        key_pos = key_start + jnp.arange(key_count, dtype=jnp.int32)
        key_doc = doc_of(key_pos, doc_ends)
        return pair_terms(query_pos, key_pos, query_doc, key_doc, head_count)

    def with_pruning(step_fn):

        def wrapped(state, parts, start_pos):
            return step_fn(state, parts, start_pos)

        return wrapped

    def forward_step(state, parts, key_start):
        run_max, run_total, run_acc = state
        key_blk = parts[0].reshape(-1, head_count, head_size)
        value_blk = parts[1].reshape(-1, head_count, head_size)
        log_mult, allowed = key_block_terms(key_start, key_blk.shape[0])
        scores = 0.125 * jnp.einsum(
            "qhd,khd->hqk", query_heads, key_blk, preferred_element_type=jnp.float32
        )
        logits = jnp.where(allowed, scores + log_mult, masked_value)
        new_max = jnp.maximum(run_max, jnp.max(logits, axis=-1))
        weights = jnp.where(allowed, jnp.exp(logits - new_max[..., None]), 0.0)
        factor = jnp.exp(run_max - new_max)
        run_total = run_total * factor + jnp.sum(weights, axis=-1)
        run_acc = run_acc * factor[..., None] + jnp.einsum(
            "hqk,khd->hqd",
            weights.astype(jnp.bfloat16),
            value_blk,
            preferred_element_type=jnp.float32,
        )
        return (new_max, run_total, run_acc)

    forward_pruned = with_pruning(forward_step)
    start_state = (
        jnp.full((head_count, tok_rows), masked_value, jnp.float32),
        jnp.zeros((head_count, tok_rows), jnp.float32),
        jnp.zeros((head_count, tok_rows, head_size), jnp.float32),
    )
    final_state = over_blocks(
        start_state,
        (
            lax.all_gather(keys_local, "seq", axis=0, tiled=True),
            lax.all_gather(values_local, "seq", axis=0, tiled=True),
        ),
        forward_pruned,
    )
    run_max, run_total, run_acc = final_state
    row_lse = run_max + jnp.log(run_total)
    attn = (run_acc / run_total[..., None]).transpose(1, 0, 2).reshape(tok_rows, model_width)
    second_norm, second_back = jax.vjp(layer_norm, attn, ln2_gain, ln2_bias)
    normed_two = second_norm.astype(jnp.bfloat16)
    middle = layer_in + jnp.dot(normed_two, w_out, preferred_element_type=jnp.float32)
    third_norm, third_back = jax.vjp(layer_norm, middle, ln3_gain, ln3_bias)
    normed_three = third_norm.astype(jnp.bfloat16)
    upper = jnp.dot(normed_three, w_up, preferred_element_type=jnp.float32)
    activated_f, gelu_back = jax.vjp(
        lambda upper_in: jax.nn.gelu(upper_in, approximate=False), upper
    )
    activated = activated_f.astype(jnp.bfloat16)
    layer_out = middle + jnp.dot(activated, w_down, preferred_element_type=jnp.float32)
    grad_out = out_grad[0].astype(jnp.float32) * valid[:, None]
    grad_branch = grad_out.astype(jnp.bfloat16)
    grad_w_down = rows_inner(activated, grad_branch)
    grad_act = cols_inner(grad_branch, w_down)
    grad_upper = gelu_back(grad_act)[0].astype(jnp.bfloat16)
    grad_w_up = rows_inner(normed_three, grad_upper)
    grad_n3 = cols_inner(grad_upper, w_up)
    grad_mid_norm, grad_ln3_gain, grad_ln3_bias = third_back(grad_n3)
    grad_middle = grad_out + grad_mid_norm
    grad_proj = grad_middle.astype(jnp.bfloat16)
    grad_w_out = rows_inner(normed_two, grad_proj)
    grad_n2 = cols_inner(grad_proj, w_out)
    grad_attn_f, grad_ln2_gain, grad_ln2_bias = second_back(grad_n2)
    grad_attn = grad_attn_f.astype(jnp.bfloat16)
    grad_heads = grad_attn.reshape(tok_rows, head_count, head_size)
    row_delta = jnp.sum(
        (grad_attn.astype(jnp.float32) * attn).reshape(tok_rows, head_count, head_size), axis=-1
    )

    def backward_step(state, parts, key_start):
        grad_q_acc, grad_k_rows, grad_v_rows = state
        key_blk = parts[0].reshape(-1, head_count, head_size)
        value_blk = parts[1].reshape(-1, head_count, head_size)
        key_count = key_blk.shape[0]
        log_mult, allowed = key_block_terms(key_start, key_count)
        scores = 0.125 * jnp.einsum(
            "qhd,khd->hqk", query_heads, key_blk, preferred_element_type=jnp.float32
        )
        logits = jnp.where(allowed, scores + log_mult, masked_value)
        weights = jnp.where(allowed, jnp.exp(logits - row_lse[..., None]), 0.0)
        grad_weights = jnp.einsum(
            "qhd,khd->hqk", grad_heads, value_blk, preferred_element_type=jnp.float32
        )
        grad_scores = (weights * (grad_weights - row_delta.T[..., None])).astype(jnp.bfloat16)
        grad_q_acc = grad_q_acc + 0.125 * jnp.einsum(
            "hqk,khd->qhd", grad_scores, key_blk, preferred_element_type=jnp.float32
        )
        value_part = jnp.einsum(
            "hqk,qhd->khd",
            weights.astype(jnp.bfloat16),
            grad_heads,
            preferred_element_type=jnp.float32,
        ).reshape(key_count, model_width)
        key_part = 0.125 * jnp.einsum(
            "hqk,qhd->khd", grad_scores, query_heads, preferred_element_type=jnp.float32
        ).reshape(key_count, model_width)
        grad_k_rows = add_rows(grad_k_rows, key_start, key_part)
        grad_v_rows = add_rows(grad_v_rows, key_start, value_part)
        return (grad_q_acc, grad_k_rows, grad_v_rows)

    backward_pruned = with_pruning(backward_step)
    zero_state = (
        jnp.zeros((tok_rows, head_count, head_size), jnp.float32),
        jnp.zeros((row_total, model_width), jnp.float32),
        jnp.zeros((row_total, model_width), jnp.float32),
    )
    back_state = over_blocks(
        zero_state,
        (
            lax.all_gather(keys_local, "seq", axis=0, tiled=True),
            lax.all_gather(values_local, "seq", axis=0, tiled=True),
        ),
        backward_pruned,
    )
    grad_q_acc, grad_k_rows, grad_v_rows = back_state
    grad_k_acc, grad_v_acc = (
        lax.psum_scatter(
            grad_k_rows.astype(jnp.bfloat16), "seq", scatter_dimension=0, tiled=True
        ).astype(jnp.float32),
        lax.psum_scatter(
            grad_v_rows.astype(jnp.bfloat16), "seq", scatter_dimension=0, tiled=True
        ).astype(jnp.float32),
    )
    grad_queries = grad_q_acc.reshape(tok_rows, model_width).astype(jnp.bfloat16)
    grad_keys = grad_k_acc.astype(jnp.bfloat16)
    grad_values = grad_v_acc.astype(jnp.bfloat16)
    grad_w_query = rows_inner(normed_one, grad_queries)
    grad_w_key = rows_inner(normed_one, grad_keys)
    grad_w_value = rows_inner(normed_one, grad_values)
    grad_n1 = (
        cols_inner(grad_queries, w_query)
        + cols_inner(grad_keys, w_key)
        + cols_inner(grad_values, w_value)
    )
    grad_in_norm, grad_ln1_gain, grad_ln1_bias = first_back(grad_n1)
    grad_inputs = (grad_middle + grad_in_norm).astype(jnp.bfloat16)
    summed = (
        lax.psum_scatter(grad_ln1_gain, ("rows", "seq"), scatter_dimension=0, tiled=True),
        lax.psum_scatter(grad_ln1_bias, ("rows", "seq"), scatter_dimension=0, tiled=True),
        lax.psum_scatter(grad_w_query, ("rows", "seq"), scatter_dimension=0, tiled=True),
        lax.psum_scatter(grad_w_key, ("rows", "seq"), scatter_dimension=0, tiled=True),
        lax.psum_scatter(grad_w_value, ("rows", "seq"), scatter_dimension=0, tiled=True),
        lax.psum_scatter(grad_ln2_gain, ("rows", "seq"), scatter_dimension=0, tiled=True),
        lax.psum_scatter(grad_ln2_bias, ("rows", "seq"), scatter_dimension=0, tiled=True),
        lax.psum_scatter(grad_w_out, ("rows", "seq"), scatter_dimension=0, tiled=True),
        lax.psum_scatter(grad_ln3_gain, ("rows", "seq"), scatter_dimension=0, tiled=True),
        lax.psum_scatter(grad_ln3_bias, ("rows", "seq"), scatter_dimension=0, tiled=True),
        lax.psum_scatter(grad_w_up, ("rows", "seq"), scatter_dimension=0, tiled=True),
        lax.psum_scatter(grad_w_down, ("rows", "seq"), scatter_dimension=0, tiled=True),
    )
    return (
        layer_out.astype(jnp.bfloat16)[None],
        grad_inputs[None],
        summed[0],
        summed[1],
        summed[2],
        summed[3],
        summed[4],
        summed[5],
        summed[6],
        summed[7],
        summed[8],
        summed[9],
        summed[10],
        summed[11],
    )


def solution(mesh):
    return jax.shard_map(
        shards,
        mesh=mesh,
        in_specs=(
            P("rows", "seq", None),
            P("rows", None),
            P(),
            P(),
            P(),
            P(),
            P(),
            P(),
            P(),
            P(),
            P(),
            P(),
            P(),
            P(),
            P("rows", "seq", None),
        ),
        out_specs=(
            P("rows", "seq", None),
            P("rows", "seq", None),
            P(("rows", "seq")),
            P(("rows", "seq")),
            P(("rows", "seq"), None),
            P(("rows", "seq"), None),
            P(("rows", "seq"), None),
            P(("rows", "seq")),
            P(("rows", "seq")),
            P(("rows", "seq"), None),
            P(("rows", "seq")),
            P(("rows", "seq")),
            P(("rows", "seq"), None),
            P(("rows", "seq"), None),
        ),
        check_vma=False,
    )
```

profile of v0, /device:TPU:0, one launch (start us, length us, event | category | flops | bytes accessed | tf_op | source)
XLA Modules:
  0.0 937.9 jit_solution(5224450766365633413)
XLA Ops:
  9.6 2.5 convolution_convert_fusion
  12.3 2.3 convolution_convert_fusion.2
  16.2 24.2 %all-gather.5.cloned.1.call-done = bf16[1024,768]{1,0:T(8,128)(2,1)} async-done(((bf16[128,768]{1,0:T(8,128)(2,1)}), bf16[1024,768]{1,0:T(8,128)(2,1)}) %all-gather.5.cloned.1.call-update) | async-done | bytes 1572880 | tf_op jit(solution)/shard_map/all_gather | solution.py:151
  40.3 1.7 copy.73
  42.1 24.9 %all-gather.3.cloned.1.call-done = bf16[1024,768]{1,0:T(8,128)(2,1)} async-done(((bf16[128,768]{1,0:T(8,128)(2,1)}), bf16[1024,768]{1,0:T(8,128)(2,1)}) %all-gather.3.cloned.1.call-update) | async-done | bytes 1572880 | tf_op jit(solution)/shard_map/all_gather | solution.py:150
  67.0 2.6 copy.72
  69.6 30.2 %while.44 = (s32[]{:T(128)}, f32[12,128]{1,0:T(8,128)S(1)}, f32[12,128]{1,0:T(8,128)S(1)}, f32[12,128,64]{1,2,0:T(8,128)}, s32[2]{0:T(128)S(1)}, /*index=5*/s32[...) while((s32[]{:T(128)}, f32[12,128]{1,0:T(8,128)S(1)}, ...), condition=%wide.region_8.9_spmd.clone.clone.clone, body=%wide.region_4.8_spmd.clone.clone.clone.sunk | while | flops 243943392 | bytes 20620524 | solution.py:62
  72.3 1.2 constant_dynamic-slice_fusion.6
  73.6 3.1 fusion.197
  76.7 3.9 fusion.198
  80.6 3.2 fusion.200
  87.3 1.2 constant_dynamic-slice_fusion.6
  88.6 3.1 fusion.197
  91.7 3.9 fusion.198
  95.6 3.2 fusion.200
  103.8 1.6 fusion.127
  105.7 8.2 multiply_convert_fusion
  113.9 1.9 add_convert_fusion
  116.7 2.4 multiply_reduce_fusion
  122.9 2.0 broadcast.3694
  125.0 32.3 %while.45 = (s32[]{:T(128)}, f32[128,12,64]{0,2,1:T(8,128)}, f32[1024,768]{0,1:T(8,128)}, f32[1024,768]{0,1:T(8,128)S(1)}, bf16[2,512,768]{1,2,0:T(8,128)(2,1)},...) while((s32[]{:T(128)}, f32[128,12,64]{0,2,1:T(8,128)}, ...), condition=%wide.region_20.21_spmd.clone.clone.clone, body=%wide.region_18.20_spmd.clone.clone.clone.sunk | while | flops 524298720 | bytes 64094628 | solution.py:62
  129.9 1.5 constant_dynamic-slice_fusion.7
  131.5 3.3 fusion.213
  137.8 1.4 copy-done.2
  146.0 1.5 constant_dynamic-slice_fusion.7
  147.5 3.3 fusion.213
  153.8 1.4 copy-done.2
  157.3 1.4 convert_element_type.228
  158.7 2.7 copy.86
  161.6 1.4 convert_element_type.227
  163.0 2.6 copy.84
  166.6 2.0 fusion.111
  169.7 2.0 fusion.95
  171.8 23.3 %reduce-scatter.27.cloned.1.call-done = bf16[128,768]{1,0:T(8,128)(2,1)} async-done(((bf16[1024,768]{1,0:T(8,128)(2,1)}), bf16[128,768]{1,0:T(8,128)(2,1)}) %reduce-scatter.27.cloned.1.call-update) | async-done | bytes 196624
  195.1 3.0 fusion.114
  198.2 31.7 %reduce-scatter.25.cloned.1.call-done = bf16[128,768]{1,0:T(8,128)(2,1)} async-done(((bf16[1024,768]{1,0:T(8,128)(2,1)}), bf16[128,768]{1,0:T(8,128)(2,1)}) %reduce-scatter.25.cloned.1.call-update) | async-done | bytes 196624
  229.9 2.9 fusion.116
  234.1 5.1 fusion.112
  240.4 5.1 fusion.101
  245.5 1.3 copy-done.26
  247.3 4.0 fusion.71
  253.7 38.5 %all-reduce.6 = (f32[768]{0:T(1024)S(1)}, f32[768]{0:T(1024)S(1)}, f32[768]{0:T(1024)S(1)}, f32[768]{0:T(1024)S(1)}, f32[768]{0:T(1024)S(1)}, /*index=5*/f32[768]{0:T(1024)S(1)}) all-reduce(f32[768]{0:T(1024)S(1)} %get-tuple-element.1105, f32[768]{0:T(1024)S(1)} %get-tuple-element.1109, ...), channel_id=4, replica_groups=mesh['rows'=4,'seq'=8] {'rows','seq'}, use_global_device_ids=true, to_apply=%region_26.27.clone | all-reduce | flops 4608 | bytes 36864
  296.6 37.5 %reduce-scatter.19.cloned.1.call-done = f32[24,768]{1,0:T(8,128)} async-done(((f32[768,768]{1,0:T(8,128)}), f32[24,768]{1,0:T(8,128)}) %reduce-scatter.19.cloned.1.call-update) | async-done | bytes 73744 | tf_op jit(solution)/shard_map/reduce_scatter | solution.py:263
  334.1 104.4 %reduce-scatter.13.cloned.1.call-done = f32[24,768]{1,0:T(8,128)} async-done(((f32[768,768]{1,0:T(8,128)}), f32[24,768]{1,0:T(8,128)}) %reduce-scatter.13.cloned.1.call-update) | async-done | bytes 73744 | tf_op jit(solution)/shard_map/reduce_scatter | solution.py:258
  438.5 104.5 %reduce-scatter.17.cloned.1.call-done = f32[24,768]{1,0:T(8,128)} async-done(((f32[768,768]{1,0:T(8,128)}), f32[24,768]{1,0:T(8,128)}) %reduce-scatter.17.cloned.1.call-update) | async-done | bytes 73744 | tf_op jit(solution)/shard_map/reduce_scatter | solution.py:260
  543.0 104.5 %reduce-scatter.15.cloned.1.call-done = f32[24,768]{1,0:T(8,128)} async-done(((f32[768,768]{1,0:T(8,128)}), f32[24,768]{1,0:T(8,128)}) %reduce-scatter.15.cloned.1.call-update) | async-done | bytes 73744 | tf_op jit(solution)/shard_map/reduce_scatter | solution.py:259
  647.6 141.6 %reduce-scatter.21.cloned.1.call-done = f32[24,3072]{1,0:T(8,128)} async-done(((f32[768,3072]{1,0:T(8,128)}), f32[24,3072]{1,0:T(8,128)}) %reduce-scatter.21.cloned.1.call-update) | async-done | bytes 294928 | tf_op jit(solution)/shard_map/reduce_scatter | solution.py:266
  789.2 141.5 %reduce-scatter.23.cloned.1.call-done = f32[96,768]{1,0:T(8,128)} async-done(((f32[3072,768]{1,0:T(8,128)}), f32[96,768]{1,0:T(8,128)}) %reduce-scatter.23.cloned.1.call-update) | async-done | bytes 294928 | tf_op jit(solution)/shard_map/reduce_scatter | solution.py:267
  (353 shorter events, 48.0 us)
Async XLA Ops:
  7.2 96.6 %copy-start = (bf16[768,768]{1,0:T(8,128)(2,1)S(1)}, bf16[768,768]{1,0:T(8,128)(2,1)}, u32[]{:S(2)}) copy-start(bf16[768,768]{1,0:T(8,128)(2,1)} %param.28) | copy-start | bytes 3538948
  7.2 5.0 copy-start.6
  7.2 5.0 copy-start.34
  7.2 5.0 copy-start.41
  7.2 33.1 %all-gather.5.cloned.1.call-start = ((), (), s32[]{:S(2)}) async-start(), calls=%async_computation.9 | async-start | bytes 1769472 | tf_op jit(solution)/shard_map/all_gather | solution.py:151
  8.4 6.5 copy-start.43
  9.6 5.0 copy-start.69
  9.6 5.3 copy-start.50
  9.6 5.1 copy-start.73
  9.6 5.3 copy-start.25
  12.2 54.8 %all-gather.3.cloned.1.call-start = ((), (), s32[]{:S(2)}) async-start(), calls=%async_computation.8 | async-start | bytes 1769472 | tf_op jit(solution)/shard_map/all_gather | solution.py:150
  14.6 180.5 %reduce-scatter.27.cloned.1.call-start = ((), (), s32[]{:S(2)}) async-start(), calls=%async_computation.17 | async-start | bytes 1769472
  76.6 3.9 copy-start.31
  91.7 3.9 copy-start.31
  99.8 3.0 copy-start.14
  99.8 14.1 %copy-start.5 = (bf16[2,512,768]{1,2,0:T(8,128)(2,1)}, bf16[2,512,768]{1,2,0:T(8,128)(2,1)S(1)}, u32[]{:S(2)}) copy-start(bf16[2,512,768]{1,2,0:T(8,128)(2,1)S(1)} %get-tuple-element.1573) | copy-start | bytes 4718596
  102.2 3.3 copy-start.55
  102.8 2.8 copy-start.61
  102.8 2.9 copy-start.33
  102.8 2.9 copy-start.37
  103.8 10.2 %slice-start.2 = ((s8[4718592]{0:T(1024)(128)(4,1)}), s8[4194304]{0:T(1024)(128)(4,1)S(1)}, s32[]{:S(2)}) async-start(s8[4718592]{0:T(1024)(128)(4,1)} %bitcast.261), calls=%async_computation.20 | async-start | bytes 8388608
  103.8 13.0 %slice-start = ((s8[4718592]{0:T(1024)(128)(4,1)}), s8[4194304]{0:T(1024)(128)(4,1)S(1)}, s32[]{:S(2)}) async-start(s8[4718592]{0:T(1024)(128)(4,1)} %bitcast.259), calls=%async_computation.18 | async-start | bytes 8388608
  105.4 13.7 %copy-start.7 = (f32[128,768]{1,0:T(8,128)}, f32[128,768]{1,0:T(8,128)S(1)}, u32[]{:S(2)}) copy-start(f32[128,768]{1,0:T(8,128)S(1)} %get-tuple-element.1222) | copy-start | bytes 1179652
  105.4 13.7 %copy-start.53 = (f32[128]{0:T(128)}, f32[128]{0:T(128)S(1)}, u32[]{:S(2)}) copy-start(f32[128]{0:T(128)S(1)} %broadcast_multiply_fusion) | copy-start | bytes 1540
  105.7 13.4 %copy-start.58 = (f32[128]{0:T(128)}, f32[128]{0:T(128)S(1)}, u32[]{:S(2)}) copy-start(f32[128]{0:T(128)S(1)} %fusion.109) | copy-start | bytes 1540
  105.7 8.2 slice-start.3
  105.7 8.2 copy-start.21
  105.7 8.2 copy-start.64
  105.7 11.0 %slice-start.1 = ((s8[4718592]{0:T(1024)(128)(4,1)}), s8[524288]{0:T(1024)(128)(4,1)S(1)}, s32[]{:S(2)}) async-start(s8[4718592]{0:T(1024)(128)(4,1)} %bitcast.259), calls=%async_computation.19 | async-start | bytes 1048576
  119.4 2.1 copy-start.17
  119.4 2.1 copy-start.67
  137.1 2.9 copy-start.10
  137.1 2.0 copy-start.2
  153.1 2.9 copy-start.10
  158.7 2.8 copy-start.4
  161.5 68.4 %reduce-scatter.25.cloned.1.call-start = ((), (), s32[]{:S(2)}) async-start(), calls=%async_computation.16 | async-start | bytes 1769472
  165.6 168.5 %reduce-scatter.19.cloned.1.call-start = ((), (), s32[]{:S(2)}) async-start(), calls=%async_computation.13 | async-start | bytes 2433024 | tf_op jit(solution)/shard_map/reduce_scatter | solution.py:263
  168.7 269.8 %reduce-scatter.13.cloned.1.call-start = ((), (), s32[]{:S(2)}) async-start(), calls=%async_computation.10 | async-start | bytes 2433024 | tf_op jit(solution)/shard_map/reduce_scatter | solution.py:258
  171.8 371.3 %reduce-scatter.17.cloned.1.call-start = ((), (), s32[]{:S(2)}) async-start(), calls=%async_computation.12 | async-start | bytes 2433024 | tf_op jit(solution)/shard_map/reduce_scatter | solution.py:260
  198.1 449.4 %reduce-scatter.15.cloned.1.call-start = ((), (), s32[]{:S(2)}) async-start(), calls=%async_computation.11 | async-start | bytes 2433024 | tf_op jit(solution)/shard_map/reduce_scatter | solution.py:259
  232.9 556.3 %reduce-scatter.21.cloned.1.call-start = ((), (), s32[]{:S(2)}) async-start(), calls=%async_computation.14 | async-start | bytes 9732096 | tf_op jit(solution)/shard_map/reduce_scatter | solution.py:266
  239.3 691.4 %reduce-scatter.23.cloned.1.call-start = ((), (), s32[]{:S(2)}) async-start(), calls=%async_computation.15 | async-start | bytes 9732096 | tf_op jit(solution)/shard_map/reduce_scatter | solution.py:267
  247.3 4.0 copy-start.27
  247.3 4.0 copy-start.30
  252.7 43.0 %copy-start.18 = (f32[128,768]{1,0:T(8,128)S(1)}, f32[128,768]{1,0:T(8,128)}, u32[]{:S(2)}) copy-start(f32[128,768]{1,0:T(8,128)} %copy-done.17) | copy-start | bytes 1179652
  252.7 43.0 %copy-start.66 = (f32[128]{0:T(128)S(1)}, f32[128]{0:T(128)}, u32[]{:S(2)}) copy-start(f32[128]{0:T(128)} %compare_convert_fusion.2) | copy-start | bytes 1540
  252.7 43.0 %copy-start.68 = (f32[128]{0:T(128)S(1)}, f32[128]{0:T(128)}, u32[]{:S(2)}) copy-start(f32[128]{0:T(128)} %copy-done.67) | copy-start | bytes 1540
  252.7 678.0 %copy-start.1 = (bf16[768,768]{1,0:T(8,128)(2,1)S(1)}, bf16[768,768]{1,0:T(8,128)(2,1)}, u32[]{:S(2)}) copy-start(bf16[768,768]{1,0:T(8,128)(2,1)} %param.28) | copy-start | bytes 3538948
  (48 other events, 54.1 us)
Sparse Core Ops, SparseCore 0:
  12.3 27.9 all-gather.4
  42.6 24.3 all-gather.2
  161.6 33.4 reduce-scatter.26
  197.3 32.6 reduce-scatter.24
  235.6 98.4 reduce-scatter.18
  339.8 98.6 reduce-scatter.12
  444.4 98.6 reduce-scatter.16
  548.9 98.6 reduce-scatter.14
  654.0 135.1 reduce-scatter.20
  795.5 135.0 reduce-scatter.22
where the time goes:
time: 946 us; the launch traced here: 938 us
  waiting for transfers between devices  738 us (78%)
  matrix products  70.9 us (7%)
  local copies, waits for them, and re-layouts  42.5 us (4%)
  blocking collectives  38.5 us (4%)
  other arithmetic  28 us (3%)
  between operations  15.4 us (2%)
    reduce_scatter x1, waiting for transfers between devices, shards(): lax.psum_scatter(grad_w_up, ('rows', 'seq'), scatter_dimension=0, tiled=T...  142 us
    reduce_scatter x1, waiting for transfers between devices, shards(): lax.psum_scatter(grad_w_down, ('rows', 'seq'), scatter_dimension=0, tiled...  141 us
    reduce_scatter x1, waiting for transfers between devices, shards(): lax.psum_scatter(grad_w_value, ('rows', 'seq'), scatter_dimension=0, tile...  105 us
    reduce_scatter x1, waiting for transfers between devices, shards(): lax.psum_scatter(grad_w_key, ('rows', 'seq'), scatter_dimension=0, tiled=...  105 us
    reduce_scatter x1, waiting for transfers between devices, shards(): lax.psum_scatter(grad_w_query, ('rows', 'seq'), scatter_dimension=0, tile...  104 us
    unnamed x12, waiting for transfers between devices  55.2 us
    unnamed x1, blocking collectives  38.5 us
    reduce_scatter x1, waiting for transfers between devices, shards(): lax.psum_scatter(grad_w_out, ('rows', 'seq'), scatter_dimension=0, tiled=...  37.5 us
  transfers between devices with their start and end apart: 10, of which 10 were waited for; matrix products, arithmetic and copies ran while one was open for 4% of the time, Pallas kernels for 0%

commit v1 on v0

--- a/solution.py
+++ b/solution.py
@@ -3,6 +3,8 @@
 import jax
 import jax.numpy as jnp
 from jax import lax
+from jax.experimental import pallas as pl
+from jax.experimental.pallas import tpu as pltpu
 from jax.sharding import PartitionSpec as P
 
 HEADS = 12
@@ -284,42 +286,681 @@
     )
 
 
+def mapped(step, mesh, seq):
+    spread = P(("rows",) + (seq if isinstance(seq, tuple) else (seq,)))
+    tokens, plain = P("rows", seq, None), P()
+    weights = P(spread[0], None)
+    return jax.shard_map(
+        step,
+        mesh=mesh,
+        in_specs=(tokens, P("rows", None)) + (plain,) * 12 + (tokens,),
+        out_specs=(tokens, tokens, spread, spread, weights, weights, weights, spread, spread, weights)
+        + (spread, spread, weights, weights),
+        check_vma=False,
+    )
+
+
+F32 = jnp.float32
+BF16 = jnp.bfloat16
+NT = (((1,), (1,)), ((), ()))
+TN = (((0,), (0,)), ((), ()))
+NN = (((1,), (0,)), ((), ()))
+
+
+def mm(left, right, dims):
+    return lax.dot_general(left, right, dims, preferred_element_type=F32)
+
+
+def unit_norm(vector):
+    centered = vector - jnp.mean(vector, axis=-1, keepdims=True)
+    scale = lax.rsqrt(jnp.mean(centered * centered, axis=-1, keepdims=True) + 1e-05)
+    return centered * scale, scale
+
+
+def norm_back(grad, gain, unit, scale):
+    weighted = grad * gain
+    mean_w = jnp.mean(weighted, axis=-1, keepdims=True)
+    mean_wu = jnp.mean(weighted * unit, axis=-1, keepdims=True)
+    return scale * (weighted - mean_w - unit * mean_wu)
+
+
+def cost(flops, nbytes, trans=0):
+    return pl.CostEstimate(flops=int(flops), bytes_accessed=int(nbytes), transcendentals=int(trans))
+
+
+def vmem_specs(count):
+    return [pl.BlockSpec(memory_space=pltpu.VMEM)] * count
+
+
+def smem_spec():
+    return pl.BlockSpec(memory_space=pltpu.SMEM)
+
+
+def qkv_call(blocks, place, gain, bias, weight, width):
+    count = len(blocks)
+    rows, model = blocks[0].shape
+
+    def body(place_ref, *refs):
+        xs, (gain_ref, bias_ref, weight_ref, q_ref, kv_ref, unit_ref) = refs[:count], refs[count:]
+        z_index = place_ref[0]
+        for k in range(count):
+            unit, _ = unit_norm(xs[k][...].astype(F32))
+            normed = (unit * gain_ref[...] + bias_ref[...]).astype(BF16)
+            made = mm(normed, weight_ref[...], NN)
+            at = z_index ^ k
+            q_ref[at] = (made[:, :width].astype(BF16).astype(F32) * 0.125).astype(BF16)
+            kv_ref[at] = made[:, width:].astype(BF16)
+            unit_ref[at] = unit.astype(BF16)
+
+    return pl.pallas_call(
+        body,
+        out_shape=(
+            jax.ShapeDtypeStruct((count, rows, width), BF16),
+            jax.ShapeDtypeStruct((count, rows, 2 * width), BF16),
+            jax.ShapeDtypeStruct((count, rows, model), BF16),
+        ),
+        in_specs=[smem_spec()] + vmem_specs(count + 3),
+        out_specs=tuple(vmem_specs(3)),
+        cost_estimate=cost(2 * count * rows * model * 3 * width, 4 * count * rows * model + 6 * model * width),
+        name="qkv_heads",
+    )(place, *blocks, gain, bias, weight)
+
+
+def lane_head(lanes, heads_here):
+    return lax.broadcasted_iota(jnp.int32, (1, lanes), 1) // HEAD_DIM
+
+
+def residue(pos_f, modulus):
+    return pos_f - modulus * jnp.floor((pos_f + 0.5) * (1.0 / modulus))
+
+
+def stack_heads(block, heads_here):
+    head_of = lane_head(block.shape[1], heads_here)
+    return jnp.concatenate(
+        [jnp.where(head_of == h, block, jnp.zeros_like(block)) for h in range(heads_here)], axis=0
+    )
+
+
+def fold_heads(stacked, rows, heads_here):
+    head_of = lane_head(stacked.shape[1], heads_here)
+    total = jnp.zeros((rows, stacked.shape[1]), stacked.dtype)
+    for h in range(heads_here):
+        total = jnp.where(head_of == h, stacked[h * rows : (h + 1) * rows], total)
+    return total
+
+
+def attend_call(place, lengths, queries, kv_own, kv_other, heads_here):
+    count, rows, width = queries.shape
+    tall, wide = heads_here * rows, count * rows
+    docs = lengths.shape[1]
+    step = 16
+
+    def body(place_ref, len_ref, q_ref, own_ref, oth_ref, send_ref, out_ref, prob_ref, s_scr, m_scr, hot_scr):
+        z_index, core = place_ref[0], place_ref[1]
+        sides = (own_ref, oth_ref)
+        cores = (core, 1 - core)
+        lane = lax.broadcasted_iota(jnp.int32, (rows, 128), 1).astype(F32)
+        for side in range(2):
+            for b in range(count):
+                pos = lax.broadcasted_iota(jnp.int32, (rows, 1), 0) + (2 * b + cores[side]) * rows
+                hot = (residue(pos.astype(F32), 12.0) == lane).astype(F32)
+                hot_scr[side, b * rows : (b + 1) * rows, :] = hot.astype(BF16)
+        for i in range(count):
+            keys = (i + 1) * rows
+            pos = lax.broadcasted_iota(jnp.int32, (rows, 1), 0) + (2 * i + core) * rows
+            pos_f = pos.astype(F32)
+            begin = jnp.zeros_like(pos)
+            run = jnp.int32(0)
+            for d in range(docs):
+                run = run + len_ref[0, d]
+                begin = jnp.where(pos >= run, run, begin)
+            tables = []
+            for h in range(heads_here):
+                head = (z_index * heads_here + h).astype(F32)
+                table = jnp.ones((rows, 128), F32)
+                for r in (2.0, 4.0, 6.0):
+                    mine = residue(head, r)
+                    pick_q = (residue(pos_f, r) == mine).astype(F32)
+                    pick_k = (residue(lane, r) == mine).astype(F32)
+                    table = table + pick_q * pick_k
+                tables.append(jnp.where(lane < 12.0, table, 0.0))
+            table = jnp.concatenate(tables, axis=0).astype(BF16)
+            stacked = stack_heads(q_ref[i], heads_here)
+            for side in range(2):
+                key = sides[side][:, :, :width].reshape(wide, width)[:keys]
+                s_scr[side, :, :keys] = mm(stacked, key, NT)
+                m_scr[side, :, :keys] = mm(table, hot_scr[side, :keys], NT)
+            key_pos = [
+                jnp.concatenate(
+                    [
+                        lax.broadcasted_iota(jnp.int32, (1, rows), 1) + (2 * b + cores[side]) * rows
+                        for b in range(i + 1)
+                    ],
+                    axis=1,
+                )
+                for side in range(2)
+            ]
+            for h in range(heads_here):
+                for at in range(0, rows, step):
+                    lo = h * rows + at
+                    pos_c, begin_c = pos[at : at + step], begin[at : at + step]
+                    masked = []
+                    for side in range(2):
+                        ok = (key_pos[side] <= pos_c) & (key_pos[side] >= begin_c)
+                        masked.append(jnp.where(ok, s_scr[side, lo : lo + step, :keys], masked_value))
+                    top = jnp.maximum(
+                        jnp.max(masked[0], axis=1, keepdims=True), jnp.max(masked[1], axis=1, keepdims=True)
+                    )
+                    parts = [
+                        jnp.exp(masked[side] - top) * m_scr[side, lo : lo + step, :keys] for side in range(2)
+                    ]
+                    total = jnp.sum(parts[0], axis=1, keepdims=True) + jnp.sum(parts[1], axis=1, keepdims=True)
+                    inverse = 1.0 / total
+                    for side in range(2):
+                        prob_ref[i, side, lo : lo + step, :keys] = (parts[side] * inverse).astype(BF16)
+            mixed = jnp.zeros((tall, width), F32)
+            for side in range(2):
+                value = sides[side][:, :, width:].reshape(wide, width)[:keys]
+                mixed = mixed + mm(prob_ref[i, side, :, :keys], value, NN)
+            result = fold_heads(mixed, rows, heads_here)
+            out_ref[i] = result
+            send_ref[i] = result.astype(BF16)
+
+    return pl.pallas_call(
+        body,
+        out_shape=(
+            jax.ShapeDtypeStruct((count, rows, width), BF16),
+            jax.ShapeDtypeStruct((count, rows, width), F32),
+            jax.ShapeDtypeStruct((count, 2, tall, wide), BF16),
+        ),
+        in_specs=[smem_spec(), smem_spec()] + vmem_specs(3),
+        out_specs=tuple(vmem_specs(3)),
+        scratch_shapes=[
+            pltpu.VMEM((2, tall, wide), F32),
+            pltpu.VMEM((2, tall, wide), F32),
+            pltpu.VMEM((2, wide, 128), BF16),
+        ],
+        cost_estimate=cost(4 * tall * wide * count * width, 8 * count * tall * wide, count * tall * wide),
+        name="attend",
+    )(place, lengths, queries, kv_own, kv_other)
+
+
+def attend_back_call(queries, kv_own, kv_other, prob, attn, grad_attn, heads_here):
+    count, rows, width = queries.shape
+    tall, wide = heads_here * rows, count * rows
+    step = 16
+
+    def body(q_ref, own_ref, oth_ref, prob_ref, attn_ref, grad_ref, dq_ref, down_ref, doth_ref, p_scr, d_scr, acc):
+        sides = (own_ref, oth_ref)
+        acc[...] = jnp.zeros_like(acc)
+        for i in range(count):
+            keys = (i + 1) * rows
+            grad = grad_ref[i]
+            stacked_q = stack_heads(q_ref[i], heads_here)
+            stacked_g = stack_heads(grad, heads_here)
+            product = grad.astype(F32) * attn_ref[i]
+            head_of = lane_head(width, heads_here)
+            delta = [
+                jnp.sum(jnp.where(head_of == h, product, 0.0), axis=1, keepdims=True) for h in range(heads_here)
+            ]
+            for side in range(2):
+                value = sides[side][:, :, width:].reshape(wide, width)[:keys]
+                p_scr[side, :, :keys] = mm(stacked_g, value, NT)
+            for h in range(heads_here):
+                for at in range(0, rows, step):
+                    lo = h * rows + at
+                    for side in range(2):
+                        weights = prob_ref[i, side, lo : lo + step, :keys].astype(F32)
+                        shifted = p_scr[side, lo : lo + step, :keys] - delta[h][at : at + step]
+                        d_scr[side, lo : lo + step, :keys] = (weights * shifted).astype(BF16)
+            grad_q = jnp.zeros((tall, width), F32)
+            for side in range(2):
+                key = sides[side][:, :, :width].reshape(wide, width)[:keys]
+                moved = d_scr[side, :, :keys]
+                grad_q = grad_q + mm(moved, key, NN)
+                acc[side, :keys, :width] += mm(moved, stacked_q, TN)
+                acc[side, :keys, width:] += mm(prob_ref[i, side, :, :keys], stacked_g, TN)
+            dq_ref[i] = (0.125 * fold_heads(grad_q, rows, heads_here)).astype(BF16)
+        down_ref[...] = acc[0].reshape(count, rows, 2 * width)
+        doth_ref[...] = acc[1].reshape(count, rows, 2 * width).astype(BF16)
+
+    return pl.pallas_call(
+        body,
+        out_shape=(
+            jax.ShapeDtypeStruct((count, rows, width), BF16),
+            jax.ShapeDtypeStruct((count, rows, 2 * width), F32),
+            jax.ShapeDtypeStruct((count, rows, 2 * width), BF16),
+        ),
+        in_specs=vmem_specs(6),
+        out_specs=tuple(vmem_specs(3)),
+        scratch_shapes=[
+            pltpu.VMEM((2, tall, wide), F32),
+            pltpu.VMEM((2, tall, wide), BF16),
+            pltpu.VMEM((2, wide, 2 * width), F32),
+        ],
+        cost_estimate=cost(8 * tall * wide * count * width, 8 * count * tall * wide),
+        name="attend_back",
+    )(queries, kv_own, kv_other, prob, attn, grad_attn)
+
+
+def gather_heads(pieces, live):
+    return jnp.concatenate([pieces[k][:, :live] for k in range(pieces.shape[0])], axis=1)
+
+
+def forward_call(pieces, layer_in, vectors, w_out, w_up, parts, live):
+    count, rows, width = pieces.shape
+    model, hidden = w_up.shape
+    part = hidden // parts
+    quarter = model // parts
+    pad_q = -(-quarter // 128) * 128
+
+    def body(piece_ref, in_ref, g2, b2, g3, b3, wo_ref, wu_ref, msg_ref, mid_ref, act_ref, slope_ref, n3_scr, n2_scr):
+        @pl.when(pl.program_id(0) == 0)
+        def _():
+            unit2, _ = unit_norm(gather_heads(piece_ref, live).astype(F32))
+            normed2 = (unit2 * g2[...] + b2[...]).astype(BF16)
+            middle = in_ref[...].astype(F32) + mm(normed2, wo_ref[...], NN)
+            mid_ref[...] = middle
+            unit3, _ = unit_norm(middle)
+            n3_scr[...] = (unit3 * g3[...] + b3[...]).astype(BF16)
+            for r in range(parts):
+                n2_scr[r, :, :quarter] = normed2[:, r * quarter : (r + 1) * quarter]
+                if pad_q > quarter:
+                    n2_scr[r, :, quarter:] = jnp.zeros((rows, pad_q - quarter), BF16)
+
+        normed3 = n3_scr[...]
+        upper = mm(normed3, wu_ref[...], NN)
+        cumulative = 0.5 * (1.0 + lax.erf(upper * 0.7071067811865476))
+        density = jnp.exp(-0.5 * upper * upper) * 0.3989422804014327
+        act = (upper * cumulative).astype(BF16)
+        act_ref[...] = act
+        slope_ref[...] = (cumulative + upper * density).astype(BF16)
+        msg_ref[0, :, :part] = act
+        msg_ref[0, :, part : part + model] = normed3
+        msg_ref[0, :, part + model :] = n2_scr[pl.program_id(0)]
+
+    fixed = lambda *shape: pl.BlockSpec(shape, lambda r: (0,) * len(shape))
+    return pl.pallas_call(
+        body,
+        grid=(parts,),
+        out_shape=(
+            jax.ShapeDtypeStruct((parts, rows, part + model + pad_q), BF16),
+            jax.ShapeDtypeStruct((rows, model), F32),
+            jax.ShapeDtypeStruct((rows, hidden), BF16),
+            jax.ShapeDtypeStruct((rows, hidden), BF16),
+        ),
+        in_specs=[fixed(count, rows, width), fixed(rows, model)]
+        + [fixed(1, model)] * 4
+        + [fixed(model, model), pl.BlockSpec((model, part), lambda r: (0, r))],
+        out_specs=(
+            pl.BlockSpec((1, rows, part + model + pad_q), lambda r: (r, 0, 0)),
+            fixed(rows, model),
+            pl.BlockSpec((rows, part), lambda r: (0, r)),
+            pl.BlockSpec((rows, part), lambda r: (0, r)),
+        ),
+        scratch_shapes=[pltpu.VMEM((rows, model), BF16), pltpu.VMEM((parts, rows, pad_q), BF16)],
+        cost_estimate=cost(2 * rows * model * (model + hidden), 2 * model * (model + hidden) + 8 * rows * hidden, 2 * rows * hidden),
+        name="token_forward",
+    )(pieces, layer_in, *vectors, w_out, w_up)
+
+
+def backward_call(pieces, middle, act, slope, grad_out, vectors, w_out, w_up, w_down, parts, live):
+    count, rows, width = pieces.shape
+    model, hidden = w_up.shape
+    part = hidden // parts
+    quarter = model // parts
+
+    def body(
+        piece_ref, mid_ref, act_ref, slope_ref, go_ref, g2, b2, g3, b3, wo_ref, wu_ref, wd_ref,
+        out_ref, msg_ref, gmid_ref, gattn_ref, down_scr, n3_scr,
+    ):
+        r = pl.program_id(0)
+
+        @pl.when(r == 0)
+        def _():
+            down_scr[...] = mid_ref[...]
+            n3_scr[...] = jnp.zeros_like(n3_scr)
+
+        go = go_ref[...]
+        down_scr[...] += mm(act_ref[...], wd_ref[...], NN)
+        grad_up = (mm(go, wd_ref[...], NT) * slope_ref[...].astype(F32)).astype(BF16)
+        msg_ref[r, :rows, :part] = grad_up
+        n3_scr[...] += mm(grad_up, wu_ref[...], NT)
+
+        @pl.when(r == parts - 1)
+        def _():
+            out_ref[...] = down_scr[...].astype(BF16)
+            grad3 = n3_scr[...]
+            unit3, scale3 = unit_norm(mid_ref[...])
+            grad_mid = go.astype(F32) + norm_back(grad3, g3[...], unit3, scale3)
+            gmid_ref[...] = grad_mid
+            proj = grad_mid.astype(BF16)
+            grad2 = mm(proj, wo_ref[...], NT)
+            unit2, scale2 = unit_norm(gather_heads(piece_ref, live).astype(F32))
+            grad_attn = norm_back(grad2, g2[...], unit2, scale2).astype(BF16)
+            for k in range(count):
+                gattn_ref[k, :, :live] = grad_attn[:, k * live : (k + 1) * live]
+                if width > live:
+                    gattn_ref[k, :, live:] = jnp.zeros((rows, width - live), BF16)
+            sums = [
+                jnp.sum(grad2 * unit2, axis=0, keepdims=True),
+                jnp.sum(grad2, axis=0, keepdims=True),
+                jnp.sum(grad3 * unit3, axis=0, keepdims=True),
+                jnp.sum(grad3, axis=0, keepdims=True),
+            ]
+            table = jnp.concatenate(sums + [jnp.zeros((12, model), F32)], axis=0).astype(BF16)
+            for k in range(parts):
+                msg_ref[k, :rows, part:] = proj
+                msg_ref[k, rows:, part : part + quarter] = table[:, k * quarter : (k + 1) * quarter]
+
+    fixed = lambda *shape: pl.BlockSpec(shape, lambda r: (0,) * len(shape))
+    return pl.pallas_call(
+        body,
+        grid=(parts,),
+        out_shape=(
+            jax.ShapeDtypeStruct((rows, model), BF16),
+            jax.ShapeDtypeStruct((parts, rows + 16, part + model), BF16),
+            jax.ShapeDtypeStruct((rows, model), F32),
+            jax.ShapeDtypeStruct((count, rows, width), BF16),
+        ),
+        in_specs=[
+            fixed(count, rows, width),
+            fixed(rows, model),
+            pl.BlockSpec((rows, part), lambda r: (0, r)),
+            pl.BlockSpec((rows, part), lambda r: (0, r)),
+            fixed(rows, model),
+        ]
+        + [fixed(1, model)] * 4
+        + [
+            fixed(model, model),
+            pl.BlockSpec((model, part), lambda r: (0, r)),
+            pl.BlockSpec((part, model), lambda r: (r, 0)),
+        ],
+        out_specs=(
+            fixed(rows, model),
+            fixed(parts, rows + 16, part + model),
+            fixed(rows, model),
+            fixed(count, rows, width),
+        ),
+        scratch_shapes=[pltpu.VMEM((rows, model), F32), pltpu.VMEM((rows, model), F32)],
+        cost_estimate=cost(2 * rows * model * (model + 3 * hidden), 2 * model * (model + 2 * hidden) + 8 * rows * hidden),
+        name="token_backward",
+    )(pieces, middle, act, slope, grad_out, *vectors, w_out, w_up, w_down)
+
+
+def down_grad_call(place, sent, grads, parts, chips, part, model):
+    rows = sent.shape[1]
+    own = part // (2 * chips)
+
+    def body(place_ref, sent_ref, grad_ref, keep_ref, send_ref, scr):
+        core = place_ref[1]
+        act = sent_ref[:, :, :part].reshape(parts * rows, part)
+        scr[...] = mm(act, grad_ref[...].reshape(parts * rows, model), TN).reshape(chips, 2, own, model)
+        for k in range(chips):
+            keep_ref[k] = scr[k, core]
+            send_ref[k] = scr[k, 1 - core].astype(BF16)
+
+    return pl.pallas_call(
+        body,
+        out_shape=(
+            jax.ShapeDtypeStruct((chips, own, model), F32),
+            jax.ShapeDtypeStruct((chips, own, model), BF16),
+        ),
+        in_specs=[smem_spec()] + vmem_specs(2),
+        out_specs=tuple(vmem_specs(2)),
+        scratch_shapes=[pltpu.VMEM((chips, 2, own, model), F32)],
+        cost_estimate=cost(2 * parts * rows * part * model, 2 * parts * rows * (part + model) + 4 * part * model),
+        name="grad_down",
+    )(place, sent, grads)
+
+
+def up_grad_call(place, sent, back, parts, chips, part, model):
+    rows = sent.shape[1]
+    quarter = model // parts
+    own = model // (parts * chips * 2)
+    tall = (parts + 1) * own + 8
+
+    def body(place_ref, sent_ref, back_ref, keep_ref, send_ref, up_scr, out_scr):
+        core = place_ref[1]
+        normed3 = sent_ref[:, :, part : part + model].reshape(parts * rows, model)
+        normed2 = sent_ref[:, :, part + model :].reshape(parts * rows, sent.shape[2] - part - model)
+        grad_up = back_ref[:, :rows, :part].reshape(parts * rows, part)
+        proj = back_ref[:, :rows, part:].reshape(parts * rows, model)
+        up_scr[...] = mm(normed3, grad_up, TN).reshape(parts, chips, 2, own, part)
+        out_scr[...] = mm(normed2, proj, TN)[:quarter].reshape(chips, 2, own, model)
+        table = jnp.zeros((8, quarter), F32)
+        for r in range(parts):
+            table = table + back_ref[r, rows : rows + 8, part : part + quarter].astype(F32)
+        for k in range(chips):
+            for side in range(2):
+                at = (2 * k + side) * own
+                piece = jnp.concatenate([table[:, at : at + own], jnp.zeros((8, model - own), F32)], axis=1)
+
+                @pl.when(core == side)
+                def _(piece=piece):
+                    keep_ref[k, tall - 8 :, :] = piece
+
+                @pl.when(core != side)
+                def _(piece=piece):
+                    send_ref[k, tall - 8 :, :] = piece.astype(BF16)
+
+            kept = [up_scr[r, k, core] for r in range(parts)] + [out_scr[k, core]]
+            keep_ref[k, : tall - 8, :] = jnp.concatenate(kept, axis=0)
+            passed = [up_scr[r, k, 1 - core] for r in range(parts)] + [out_scr[k, 1 - core]]
+            send_ref[k, : tall - 8, :] = jnp.concatenate(passed, axis=0).astype(BF16)
+
+    return pl.pallas_call(
+        body,
+        out_shape=(
+            jax.ShapeDtypeStruct((chips, tall, model), F32),
+            jax.ShapeDtypeStruct((chips, tall, model), BF16),
+        ),
+        in_specs=[smem_spec()] + vmem_specs(2),
+        out_specs=tuple(vmem_specs(2)),
+        scratch_shapes=[
+            pltpu.VMEM((parts, chips, 2, own, part), F32),
+            pltpu.VMEM((chips, 2, own, model), F32),
+        ],
+        cost_estimate=cost(2 * parts * rows * (part + quarter) * model, 2 * parts * rows * (part + 2 * model) + 6 * part * model),
+        name="grad_up_out",
+    )(place, sent, back)
+
+
+def qkv_grad_call(place, unit, grads, gain_col, bias_col, weight, parts, chips, live, width):
+    count, rows, model = unit.shape
+    own = model // (parts * chips * 2)
+
+    def body(place_ref, unit_ref, grad_ref, gain_ref, bias_ref, weight_ref, keep_ref, send_ref, scr):
+        core = place_ref[1]
+        grad = grad_ref[...].reshape(count * rows, 3 * width)
+        cross = mm(unit_ref[...].reshape(count * rows, model), grad, TN)
+        total = jnp.sum(grad.astype(F32), axis=0, keepdims=True)
+        weight_f = weight_ref[...].astype(F32)
+        grad_gain = jnp.sum(weight_f * cross, axis=1, keepdims=True)
+        grad_bias = jnp.sum(weight_f * total, axis=1, keepdims=True)
+        lane = lax.broadcasted_iota(jnp.int32, (1, 3 * width), 1)
+        made = gain_ref[...] * cross + bias_ref[...] * total
+        made = jnp.where(lane == live, grad_gain, jnp.where(lane == live + 1, grad_bias, made))
+        scr[...] = made.reshape(parts, chips, 2, own, 3 * width)
+        for r in range(parts):
+            keep_ref[r] = jnp.concatenate([scr[r, k, core] for k in range(chips)], axis=0)
+            send_ref[r] = jnp.concatenate([scr[r, k, 1 - core] for k in range(chips)], axis=0).astype(BF16)
+
+    return pl.pallas_call(
+        body,
+        out_shape=(
+            jax.ShapeDtypeStruct((parts, chips * own, 3 * width), F32),
+            jax.ShapeDtypeStruct((parts, chips * own, 3 * width), BF16),
+        ),
+        in_specs=[smem_spec()] + vmem_specs(5),
+        out_specs=tuple(vmem_specs(2)),
+        scratch_shapes=[pltpu.VMEM((parts, chips, 2, own, 3 * width), F32)],
+        cost_estimate=cost(2 * count * rows * model * 3 * width, 20 * model * width),
+        name="grad_qkv",
+    )(place, unit, grads, gain_col, bias_col, weight)
+
+
+def input_grad_call(pieces, layer_in, grad_mid, gain, w_query, w_key, w_value, live, width):
+    count, rows, _ = pieces.shape
+    model = layer_in.shape[1]
+
+    def body(piece_ref, in_ref, gmid_ref, gain_ref, wq_ref, wk_ref, wv_ref, out_ref):
+        grad = jnp.zeros((rows, model), F32)
+        for at, w_ref in enumerate((wq_ref, wk_ref, wv_ref)):
+            part = jnp.concatenate(
+                [piece_ref[k, :, at * width : at * width + live] for k in range(count)], axis=1
+            )
+            grad = grad + mm(part, w_ref[...], NT)
+        unit, scale = unit_norm(in_ref[...].astype(F32))
+        out_ref[...] = (gmid_ref[...] + norm_back(grad, gain_ref[...], unit, scale)).astype(BF16)
+
+    return pl.pallas_call(
+        body,
+        out_shape=jax.ShapeDtypeStruct((rows, model), BF16),
+        in_specs=vmem_specs(7),
+        out_specs=pl.BlockSpec(memory_space=pltpu.VMEM),
+        cost_estimate=cost(6 * rows * model * model, 6 * model * model),
+        name="grad_inputs",
+    )(pieces, layer_in, grad_mid, gain, w_query, w_key, w_value)
+
+
+def swap_core(value):
+    return lax.ppermute(value, "core", [(0, 1), (1, 0)])
+
+
+def swap_chip(value, bit, chips):
+    return lax.ppermute(value, "chip", [(k, k ^ bit) for k in range(chips)])
+
+
+def exchange(value, axis):
+    return lax.all_to_all(value, axis, 0, 0, tiled=True)
+
+
+def gather_chips(block, chips):
+    found = {0: block}
+    bit = chips // 2
+    while bit >= 1:
+        for k in sorted(found):
+            found[k | bit] = swap_chip(found[k], bit, chips)
+        bit //= 2
+    return [found[k] for k in range(chips)]
+
+
+def scatter_chips(value, z_index, chips):
+    bit = 1
+    while bit < chips:
+        pairs = value.reshape((value.shape[0] // 2, 2) + value.shape[1:])
+        mine = (z_index // bit) % 2
+        away = lax.dynamic_index_in_dim(pairs, 1 - mine, 1, keepdims=False).astype(BF16)
+        stay = lax.dynamic_index_in_dim(pairs, mine, 1, keepdims=False)
+        value = stay + swap_chip(away, bit, chips).astype(F32)
+        bit *= 2
+    return value[0]
+
+
+def fast_shards(
+    inputs, doc_lengths, ln1_gain, ln1_bias, w_query, w_key, w_value, ln2_gain, ln2_bias, w_out,
+    ln3_gain, ln3_bias, w_up, w_down, out_grad,
+):
+    rows, model = inputs.shape[1:]
+    chips, parts = lax.axis_size("chip"), lax.axis_size("rows")
+    z_index, core = lax.axis_index("chip"), lax.axis_index("core")
+    heads_here = HEADS // chips
+    live = heads_here * HEAD_DIM
+    width = -(-live // 128) * 128
+    hidden = w_up.shape[1]
+    part = hidden // parts
+    own = model // (parts * chips * 2)
+    place = jnp.stack([z_index, core]).astype(jnp.int32)
+    layer_in = inputs[0]
+    as_row = lambda v: v.reshape(1, model)
+
+    blocks = gather_chips(layer_in, chips)
+    pos = (2 * z_index + core) * rows + jnp.arange(rows, dtype=jnp.int32)
+    valid = pos < jnp.sum(doc_lengths[0])
+    grad_out = jnp.where(valid[:, None], out_grad[0], jnp.zeros_like(out_grad[0]))
+    grads_plane = exchange(jnp.broadcast_to(grad_out[None], (parts, rows, model)), "rows")
+
+    def columns(weight):
+        mine = lax.dynamic_slice_in_dim(weight, z_index * live, live, 1)
+        return jnp.pad(mine, ((0, 0), (0, width - live)))
+
+    w_heads = jnp.concatenate([columns(w_query), columns(w_key), columns(w_value)], axis=1)
+
+    queries, kv_own, unit_one = qkv_call(blocks, place, as_row(ln1_gain), as_row(ln1_bias), w_heads, width)
+    kv_other = swap_core(kv_own)
+    attn_send, attn_heads, prob = attend_call(place, doc_lengths, queries, kv_own, kv_other, heads_here)
+    pieces = exchange(attn_send, "chip")
+
+    vectors = tuple(as_row(v) for v in (ln2_gain, ln2_bias, ln3_gain, ln3_bias))
+    sent, middle, act, slope = forward_call(pieces, layer_in, vectors, w_out, w_up, parts, live)
+    sent = exchange(sent, "rows")
+    output, back, grad_mid, grad_attn = backward_call(
+        pieces, middle, act, slope, grad_out, vectors, w_out, w_up, w_down, parts, live
+    )
+    grad_heads = exchange(grad_attn, "chip")
+    back = exchange(back, "rows")
+    down_keep, down_send = down_grad_call(place, sent, grads_plane, parts, chips, part, model)
+    grad_w_down = scatter_chips(down_keep + swap_core(down_send).astype(F32), z_index, chips)
+
+    grad_q, grad_kv, grad_kv_other = attend_back_call(
+        queries, kv_own, kv_other, prob, attn_heads, grad_heads, heads_here
+    )
+    grad_kv = (grad_kv + swap_core(grad_kv_other).astype(F32)).astype(BF16)
+    grad_qkv = jnp.concatenate([grad_q, grad_kv], axis=2)
+    grad_pieces = exchange(grad_qkv, "chip")
+
+    qkv_keep, qkv_send = qkv_grad_call(
+        place, unit_one, grad_qkv, ln1_gain.reshape(model, 1), ln1_bias.reshape(model, 1), w_heads,
+        parts, chips, live, width,
+    )
+    qkv_sum = (qkv_keep + swap_core(qkv_send).astype(F32)).astype(BF16)
+    qkv_sum = jnp.sum(exchange(qkv_sum, "rows").astype(F32), axis=0).astype(BF16)
+    qkv_all = exchange(qkv_sum.reshape(chips, own, 3 * width), "chip")
+
+    up_keep, up_send = up_grad_call(place, sent, back, parts, chips, part, model)
+    up_sum = scatter_chips(up_keep + swap_core(up_send).astype(F32), z_index, chips)
+    up_all = exchange(up_sum[: parts * own].astype(BF16).reshape(parts, own, part), "rows")
+    grad_w_up = up_all.astype(F32).transpose(1, 0, 2).reshape(own, hidden)
+    grad_w_out = up_sum[parts * own : (parts + 1) * own]
+    norm_sums = up_sum[(parts + 1) * own :, :own]
+
+    grad_inputs = input_grad_call(
+        grad_pieces, layer_in, grad_mid, as_row(ln1_gain), w_query, w_key, w_value, live, width
+    )
+    qkv_f = qkv_all.astype(F32)
+
+    def final_columns(at):
+        return qkv_f[:, :, at * width : at * width + live].transpose(1, 0, 2).reshape(own, model)
+
+    norm_one = jnp.sum(qkv_f[:, :, live : live + 2], axis=0)
+    return (
+        output[None],
+        grad_inputs[None],
+        norm_one[:, 0],
+        norm_one[:, 1],
+        final_columns(0),
+        final_columns(1),
+        final_columns(2),
+        norm_sums[0],
+        norm_sums[1],
+        grad_w_out,
+        norm_sums[2],
+        norm_sums[3],
+        grad_w_up,
+        grad_w_down,
+    )
+
+
+def takes_fast(mesh):
+    seq = mesh.shape["seq"]
+    chips = seq // 2
+    return seq % 2 == 0 and chips & (chips - 1) == 0 and HEADS % max(chips, 1) == 0
+
+
 def solution(mesh):
-    return jax.shard_map(
-        shards,
-        mesh=mesh,
-        in_specs=(
-            P("rows", "seq", None),
-            P("rows", None),
-            P(),
-            P(),
-            P(),
-            P(),
-            P(),
-            P(),
-            P(),
-            P(),
-            P(),
-            P(),
-            P(),
-            P(),
-            P("rows", "seq", None),
-        ),
-        out_specs=(
-            P("rows", "seq", None),
-            P("rows", "seq", None),
-            P(("rows", "seq")),
-            P(("rows", "seq")),
-            P(("rows", "seq"), None),
-            P(("rows", "seq"), None),
-            P(("rows", "seq"), None),
-            P(("rows", "seq")),
-            P(("rows", "seq")),
-            P(("rows", "seq"), None),
-            P(("rows", "seq")),
-            P(("rows", "seq")),
-            P(("rows", "seq"), None),
-            P(("rows", "seq"), None),
-        ),
-        check_vma=False,
-    )
+    if takes_fast(mesh):
+        parts, seq = mesh.shape["rows"], mesh.shape["seq"]
+        split = jax.sharding.Mesh(mesh.devices.reshape(parts, seq // 2, 2), ("rows", "chip", "core"))
+        return mapped(fast_shards, split, ("chip", "core"))
+    return mapped(shards, mesh, "seq")

time: 946 us -> 214 us (0.23)
  waiting for transfers between devices: 738 us -> 58.8 us
  matrix products: 70.9 us -> 0 us
  Pallas kernels: 0 us -> 52 us
  starting transfers between devices: 0.67 us -> 42.1 us
  local copies, waits for them, and re-layouts: 42.5 us -> 21.4 us
  blocking collectives: 38.5 us -> 22.5 us
  between operations: 15.4 us -> 0.9 us
  other arithmetic: 28 us -> 14.3 us
    reduce_scatter x6 -> x0, waiting for transfers between devices: 634 us -> none  [the longest x1 142 us: shards(): lax.psum_scatter(grad_w_up, ('rows', 'seq'), scatter_dimension=0, tiled=T...]
    dot_general x32 -> x0, matrix products: 70.9 us -> none  [the longest x6 20.2 us: rows_inner(): lax.dot_general(left, right, (((0,), (0,)), ((), ())), preferred_element_...]
    unnamed x12 -> x0, waiting for transfers between devices: 55.2 us -> none
    pallas_call x0 -> x9, Pallas kernels: none -> 52 us  [the longest x1 10.4 us: backward_call(): pl.pallas_call(body, grid=(parts,), out_shape=(jax.ShapeDtypeStruct((rows...]
    all_gather x2 -> x0, waiting for transfers between devices: 49.1 us -> none  [the longest x1 24.9 us: shards(): lax.all_gather(keys_local, 'seq', axis=0, tiled=True)]
    unnamed x1 -> x0, blocking collectives: 38.5 us -> none
    all_to_all x0 -> x7, waiting for transfers between devices: none -> 36.8 us  [exchange(): return lax.all_to_all(value, axis, 0, 0, tiled=True)]
    all_to_all x0 -> x7, starting transfers between devices: none -> 26.1 us  [exchange(): return lax.all_to_all(value, axis, 0, 0, tiled=True)]
  transfers between devices with their start and end apart: 10 -> 19, of which waited for: 10 -> 12; matrix products, arithmetic and copies ran while one was open for 4% -> 14% of each run, Pallas kernels for 0% -> 20%
where the time goes in v1:
time: 214 us; the launch traced here: 212 us
  waiting for transfers between devices  58.8 us (27%)
  Pallas kernels  52 us (24%)
  starting transfers between devices  42.1 us (20%)
  blocking collectives  22.5 us (11%)
  local copies, waits for them, and re-layouts  21.4 us (10%)
  other arithmetic  14.3 us (7%)
    all_to_all x7, waiting for transfers between devices, exchange(): return lax.all_to_all(value, axis, 0, 0, tiled=True)  36.8 us
    all_to_all x7, starting transfers between devices, exchange(): return lax.all_to_all(value, axis, 0, 0, tiled=True)  26.1 us
    all_to_all x2, blocking collectives, exchange(): return lax.all_to_all(value, axis, 0, 0, tiled=True)  22.5 us
    ppermute x7, waiting for transfers between devices, swap_chip(): return lax.ppermute(value, 'chip', [(k, k ^ bit) for k in range(chips)])  17.7 us
    ppermute x7, starting transfers between devices, swap_chip(): return lax.ppermute(value, 'chip', [(k, k ^ bit) for k in range(chips)])  15.6 us
    pallas_call x1, Pallas kernels, backward_call(): pl.pallas_call(body, grid=(parts,), out_shape=(jax.ShapeDtypeStruct((rows...  10.4 us
    pallas_call x1, Pallas kernels, attend_call(): pl.pallas_call(body, out_shape=(jax.ShapeDtypeStruct((count, rows, width)...  6.72 us
    pallas_call x1, Pallas kernels, forward_call(): pl.pallas_call(body, grid=(parts,), out_shape=(jax.ShapeDtypeStruct((part...  6.72 us
  transfers between devices with their start and end apart: 19, of which 12 were waited for; matrix products, arithmetic and copies ran while one was open for 14% of the time, Pallas kernels for 20%

profile of v1, /device:TPU:0, one launch (start us, length us, event | category | flops | bytes accessed | tf_op | source)
XLA Modules:
  0.0 212.2 jit_solution(11060868809405269114)
XLA Ops:
  0.6 3.1 %collective-permute-start = (bf16[128,768]{1,0:T(8,128)(2,1)}, bf16[128,768]{1,0:T(8,128)(2,1)S(1)}, u32[]{:S(2)}, u32[]{:S(2)}) collective-permute-start(bf16[128,768]{1,0:T(8,128)(2,1)} %bitcast.57), channel_id=1, source_target_pairs={{0,2},{2,0},{4,6},{6,4},{1,3},{3,1},{5,7},{7,5},{8,10},{10,8},{12,... | collective-permute-start | bytes 589832 | tf_op jit(solution)/shard_map/ppermute | solution.py:832
  3.8 2.6 %collective-permute-start.1 = (bf16[128,768]{1,0:T(8,128)(2,1)}, bf16[128,768]{1,0:T(8,128)(2,1)S(1)}, u32[]{:S(2)}, u32[]{:S(2)}) collective-permute-start(bf16[128,768]{1,0:T(8,128)(2,1)} %bitcast.58), channel_id=1, source_target_pairs={{0,4},{2,6},{4,0},{6,2},{1,5},{3,7},{5,1},{7,3},{8,12},{10,14},{12... | collective-permute-start | bytes 589832 | tf_op jit(solution)/shard_map/ppermute | solution.py:832
  6.4 1.3 reshape.110.refs_4_.gain_ref
  7.6 1.3 reshape.111.refs_5_
  8.9 1.2 constant_dynamic-slice_fusion.2
  10.7 1.6 constant_dynamic-slice_fusion
  12.3 3.2 %collective-permute-done.1.refs_2_ = bf16[128,768]{1,0:T(8,128)(2,1)S(1)} collective-permute-done((bf16[128,768]{1,0:T(8,128)(2,1)}, bf16[128,768]{1,0:T(8,128)(2,1)S(1)}, u32[]{:S(2)}, u32[]{:S(2)}) %collective-permute-start.1) | collective-permute-done | bytes 196640 | tf_op jit(solution)/shard_map/ppermute | solution.py:832
  15.9 1.2 fusion.5.refs_6_.weight_ref
  17.2 4.0 %collective-permute-done.2.refs_3_ = bf16[128,768]{1,0:T(8,128)(2,1)S(1)} collective-permute-done((bf16[128,768]{1,0:T(8,128)(2,1)S(1)}, bf16[128,768]{1,0:T(8,128)(2,1)S(1)}, u32[]{:S(2)}, u32[]{:S(2)}) %collective-permute-start.2) | collective-permute-done | bytes 196640 | tf_op jit(solution)/shard_map/ppermute | solution.py:832
  21.9 3.8 %qkv_heads.1 = (bf16[4,128,256]{2,1,0:T(8,128)(2,1)}, bf16[4,128,512]{2,1,0:T(8,128)(2,1)}, bf16[4,128,768]{2,1,0:T(8,128)(2,1)}) custom-call(s32[2]{0:T(128)} %pad_add_fusion.place_ref, bf16[128,768]{1,0:T(8,128)(2,1)} %bitcast.59, bf16[128,768]{1,0:T(8,128)(2,1)} %copy-done.16, bf16[128,768]{1,0:T(8,128)(2,1)} %copy-done.17, bf16[128,768]{1,0:T(8,128)(2,1)} %copy-done.18, ...), custom_call_target="tpu_custom_call" | custom-call | flops 603979776 | bytes 2752512 | tf_op jit(solution)/shard_map/qkv_heads/pallas_call | solution.py:355
  25.7 2.1 collective-permute-done.3.oth_ref
  28.7 6.7 %attend.1 = (bf16[4,128,256]{2,1,0:T(8,128)(2,1)}, f32[4,128,256]{2,1,0:T(8,128)}, bf16[4,2,384,512]{3,2,1,0:T(8,128)(2,1)}) custom-call(s32[2]{0:T(128)} %pad_add_fusion.place_ref, s32[1,12]{1,0:T(1,128)} %len_ref.1, bf16[4,128,256]{2,1,0:T(8,128)(2,1)} %get-tuple-element.37.q_ref, bf16[4,128,512]{2,1,0:T(8,128)(2,1)} %get-tuple-element.38.own_ref, ...), custom_call_target="tpu_custom_call" | custom-call | flops 805306368 | bytes 6291456 | tf_op jit(solution)/shard_map/attend/pallas_call | solution.py:469
  35.4 3.8 %all-to-all-start = ((bf16[4,128,256]{2,1,0:T(8,128)(2,1)}), bf16[4,128,256]{2,1,0:T(8,128)(2,1)S(1)}, u32[]{:S(2)}, u32[]{:S(2)}) async-start(bf16[4,128,256]{2,1,0:T(8,128)(2,1)} %get-tuple-element.39), calls=%async_computation | async-start | bytes 524288 | tf_op jit(solution)/shard_map/all_to_all | solution.py:836
  40.6 7.8 %all-to-all-done.piece_ref = bf16[4,128,256]{2,1,0:T(8,128)(2,1)S(1)} async-done(((bf16[4,128,256]{2,1,0:T(8,128)(2,1)}), bf16[4,128,256]{2,1,0:T(8,128)(2,1)S(1)}, u32[]{:S(2)}, u32[]{:S(2)}) %all-to-all-start) | async-done | bytes 262176 | tf_op jit(solution)/shard_map/all_to_all | solution.py:836
  48.4 1.1 broadcast_in_dim.37
  49.5 3.7 %all-to-all-start.8 = ((bf16[4,128,768]{2,1,0:T(8,128)(2,1)}), bf16[4,128,768]{2,1,0:T(8,128)(2,1)S(1)}, u32[]{:S(2)}, u32[]{:S(2)}) async-start(bf16[4,128,768]{2,1,0:T(8,128)(2,1)} %broadcast_in_dim.37), calls=%async_computation.8 | async-start | bytes 1572864 | tf_op jit(solution)/shard_map/all_to_all | solution.py:836
  56.3 6.7 %token_forward.1 = (bf16[4,128,1792]{2,1,0:T(8,128)(2,1)}, f32[128,768]{1,0:T(8,128)}, bf16[128,3072]{1,0:T(8,128)(2,1)}, bf16[128,3072]{1,0:T(8,128)(2,1)}) custom-call(bf16[4,128,256]{2,1,0:T(8,128)(2,1)} %copy-done.4, bf16[128,768]{1,0:T(8,128)(2,1)} %bitcast.60, f32[1,768]{1,0:T(1,128)} %reshape.112.g2, f32[1,768]{1,0:T(1,128)} %reshape.113.b2, ...), custom_call_target="tpu_custom_call" | custom-call | flops 754974720 | bytes 9043968 | tf_op jit(solution)/shard_map/token_forward/pallas_call | solution.py:583
  63.0 10.4 %token_backward.1 = (bf16[128,768]{1,0:T(8,128)(2,1)}, bf16[4,144,1536]{2,1,0:T(8,128)(2,1)}, f32[128,768]{1,0:T(8,128)}, bf16[4,128,256]{2,1,0:T(8,128)(2,1)}) custom-call(bf16[4,128,256]{2,1,0:T(8,128)(2,1)} %copy-done.4, f32[128,768]{1,0:T(8,128)} %get-tuple-element.40.mid_ref, bf16[128,3072]{1,0:T(8,128)(2,1)} %get-tuple-element.41.act_ref, ...), custom_call_target="tpu_custom_call" | custom-call | flops 1962934272 | bytes 13762560 | tf_op jit(solution)/shard_map/token_backward/pallas_call | solution.py:657
  73.4 11.2 %all_to_all.45.grad_ref = bf16[4,128,256]{2,1,0:T(8,128)(2,1)} all-to-all(bf16[4,128,256]{2,1,0:T(8,128)(2,1)} %get-tuple-element.46), channel_id=1, replica_groups=mesh['rows'=4,'chip'=4,'core'=2] {'chip'}, dimensions={0} | all-to-all | bytes 524288 | tf_op jit(solution)/shard_map/all_to_all | solution.py:836
  84.6 4.2 %all-to-all-start.6 = ((bf16[4,144,1536]{2,1,0:T(8,128)(2,1)}), bf16[4,144,1536]{2,1,0:T(8,128)(2,1)S(1)}, u32[]{:S(2)}, u32[]{:S(2)}) async-start(bf16[4,144,1536]{2,1,0:T(8,128)(2,1)} %get-tuple-element.55), calls=%async_computation.6 | async-start | bytes 3538944 | tf_op jit(solution)/shard_map/all_to_all | solution.py:836
  88.8 6.4 %attend_back.1 = (bf16[4,128,256]{2,1,0:T(8,128)(2,1)}, f32[4,128,512]{2,1,0:T(8,128)}, bf16[4,128,512]{2,1,0:T(8,128)(2,1)}) custom-call(bf16[4,128,256]{2,1,0:T(8,128)(2,1)} %get-tuple-element.37.q_ref, bf16[4,128,512]{2,1,0:T(8,128)(2,1)} %get-tuple-element.38.own_ref, bf16[4,128,512]{2,1,0:T(8,128)(2,1)} %copy-done.15, ...), custom_call_target="tpu_custom_call" | custom-call | flops 1610612736 | bytes 6291456 | tf_op jit(solution)/shard_map/attend_back/pallas_call | solution.py:527
  95.2 11.6 %all-to-all-done.6.back_ref = bf16[4,144,1536]{2,1,0:T(8,128)(2,1)S(1)} async-done(((bf16[4,144,1536]{2,1,0:T(8,128)(2,1)}), bf16[4,144,1536]{2,1,0:T(8,128)(2,1)S(1)}, u32[]{:S(2)}, u32[]{:S(2)}) %all-to-all-start.6) | async-done | bytes 1769504 | tf_op jit(solution)/shard_map/all_to_all | solution.py:836
  106.9 1.2 copy-done.1
  108.1 3.6 %all-to-all-start.5 = ((bf16[4,128,1792]{2,1,0:T(8,128)(2,1)}), bf16[4,128,1792]{2,1,0:T(8,128)(2,1)S(1)}, u32[]{:S(2)}, u32[]{:S(2)}) async-start(bf16[4,128,1792]{2,1,0:T(8,128)(2,1)} %get-tuple-element.54), calls=%async_computation.5 | async-start | bytes 3670016 | tf_op jit(solution)/shard_map/all_to_all | solution.py:836
  113.5 1.4 add_convert_fusion.1
  114.9 1.0 pad_maximum_fusion.grad_ref
  116.0 4.5 %grad_qkv.1 = (f32[4,96,768]{2,1,0:T(8,128)}, bf16[4,96,768]{2,1,0:T(8,128)(2,1)}) custom-call(s32[2]{0:T(128)} %pad_add_fusion.place_ref, bf16[4,128,768]{2,1,0:T(8,128)(2,1)} %get-tuple-element.51.unit_ref, bf16[4,128,768]{2,1,0:T(8,128)(2,1)} %pad_maximum_fusion.grad_ref, f32[768,1]{1,0:T(8,128)} %reshape.129.gain_ref, f32[768,1]{1,0:T(8,128)} %reshape.130.bias_ref, ...), custom_call_target="tpu_custom_call" | custom-call | flops 603979776 | bytes 3932160 | tf_op jit(solution)/shard_map/grad_qkv/pallas_call | solution.py:789
  120.5 2.2 %collective-permute-done.5 = bf16[4,96,768]{2,1,0:T(8,128)(2,1)S(1)} collective-permute-done((bf16[4,96,768]{2,1,0:T(8,128)(2,1)}, bf16[4,96,768]{2,1,0:T(8,128)(2,1)S(1)}, u32[]{:S(2)}, u32[]{:S(2)}) %collective-permute-start.5) | collective-permute-done | bytes 589856 | tf_op jit(solution)/shard_map/ppermute | solution.py:828
  122.7 1.4 add_convert_fusion
  124.1 9.2 %all-to-all-done.5.sent_ref = bf16[4,128,1792]{2,1,0:T(8,128)(2,1)S(1)} async-done(((bf16[4,128,1792]{2,1,0:T(8,128)(2,1)}), bf16[4,128,1792]{2,1,0:T(8,128)(2,1)S(1)}, u32[]{:S(2)}, u32[]{:S(2)}) %all-to-all-start.5) | async-done | bytes 1835040 | tf_op jit(solution)/shard_map/all_to_all | solution.py:836
  133.2 11.3 %all_to_all.46 = bf16[4,96,768]{2,1,0:T(8,128)(2,1)S(1)} all-to-all(bf16[4,96,768]{2,1,0:T(8,128)(2,1)S(1)} %add_convert_fusion), channel_id=1, replica_groups=mesh['rows'=4,'chip'=4,'core'=2] {'rows'}, dimensions={0} | all-to-all | bytes 1179648 | tf_op jit(solution)/shard_map/all_to_all | solution.py:836
  144.5 3.5 %all-to-all-start.2 = ((bf16[4,128,768]{2,1,0:T(8,128)(2,1)}), bf16[4,128,768]{2,1,0:T(8,128)(2,1)S(1)}, u32[]{:S(2)}, u32[]{:S(2)}) async-start(bf16[4,128,768]{2,1,0:T(8,128)(2,1)} %pad_maximum_fusion.grad_ref), calls=%async_computation.2 | async-start | bytes 1572864 | tf_op jit(solution)/shard_map/all_to_all | solution.py:836
  148.0 3.8 %grad_down.1 = (f32[4,96,768]{2,1,0:T(8,128)}, bf16[4,96,768]{2,1,0:T(8,128)(2,1)}) custom-call(s32[2]{0:T(128)} %pad_add_fusion.place_ref, bf16[4,128,1792]{2,1,0:T(8,128)(2,1)} %copy-done, bf16[4,128,768]{2,1,0:T(8,128)(2,1)} %copy-done.2), custom_call_target="tpu_custom_call" | custom-call | flops 603979776 | bytes 3932160 | tf_op jit(solution)/shard_map/grad_down/pallas_call | solution.py:703
  151.8 5.0 %grad_up_out.1 = (f32[4,128,768]{2,1,0:T(8,128)}, bf16[4,128,768]{2,1,0:T(8,128)(2,1)}) custom-call(s32[2]{0:T(128)} %pad_add_fusion.place_ref, bf16[4,128,1792]{2,1,0:T(8,128)(2,1)} %copy-done, bf16[4,144,1536]{2,1,0:T(8,128)(2,1)} %copy-done.1), custom_call_target="tpu_custom_call" | custom-call | flops 754974720 | bytes 5898240 | tf_op jit(solution)/shard_map/grad_up_out/pallas_call | solution.py:752
  158.9 1.2 convert_add_fusion.1
  160.8 2.0 collective-permute-start.10
  162.8 3.7 %all-to-all-done.2.piece_ref = bf16[4,128,768]{2,1,0:T(8,128)(2,1)S(1)} async-done(((bf16[4,128,768]{2,1,0:T(8,128)(2,1)}), bf16[4,128,768]{2,1,0:T(8,128)(2,1)S(1)}, u32[]{:S(2)}, u32[]{:S(2)}) %all-to-all-start.2) | async-done | bytes 786464 | tf_op jit(solution)/shard_map/all_to_all | solution.py:836
  166.5 4.0 %all-to-all-start.4 = ((bf16[4,24,768]{2,1,0:T(8,128)(2,1)}), bf16[4,24,768]{2,1,0:T(8,128)(2,1)}, u32[]{:S(2)}, u32[]{:S(2)}) async-start(bf16[4,24,768]{2,1,0:T(8,128)(2,1)} %bitcast.6), calls=%async_computation.4 | async-start | bytes 294912 | tf_op jit(solution)/shard_map/all_to_all | solution.py:836
  170.5 4.6 %grad_inputs.1 = bf16[128,768]{1,0:T(8,128)(2,1)} custom-call(bf16[4,128,768]{2,1,0:T(8,128)(2,1)} %copy-done.3, bf16[128,768]{1,0:T(8,128)(2,1)} %bitcast.61, f32[128,768]{1,0:T(8,128)} %get-tuple-element.50.gmid_ref, f32[1,768]{1,0:T(1,128)} %reshape.110.refs_4_.gain_ref, bf16[768,768]{1,0:T(8,128)(2,1)} %wq_ref.1, bf16[768,768]{1,0:T(8,128)(2,1)} %wk_ref.1, ...), custom_call_target="tpu_custom_call" | custom-call | flops 452984832 | bytes 3538944 | tf_op jit(solution)/shard_map/grad_inputs/pallas_call | solution.py:817
  175.1 1.8 convert_add_fusion
  177.7 2.0 collective-permute-start.7
  184.8 2.4 %collective-permute-start.11 = (bf16[1,96,768]{2,1,0:T(8,128)(2,1)S(1)}, bf16[1,96,768]{2,1,0:T(8,128)(2,1)S(1)}, u32[]{:S(2)}, u32[]{:S(2)}) collective-permute-start(bf16[1,96,768]{2,1,0:T(8,128)(2,1)S(1)} %dynamic-slice_convert_fusion.1), channel_id=1, source_target_pairs={{0,4},{2,6},{4,0},{6,2},{1,5},{3,7},{5,1},{7,3},{8,12},{10,14},{12... | collective-permute-start | bytes 442376 | tf_op jit(solution)/shard_map/ppermute | solution.py:832
  187.2 2.5 %collective-permute-done.7 = bf16[2,128,768]{2,1,0:T(8,128)(2,1)S(1)} collective-permute-done((bf16[2,128,768]{2,1,0:T(8,128)(2,1)}, bf16[2,128,768]{2,1,0:T(8,128)(2,1)S(1)}, u32[]{:S(2)}, u32[]{:S(2)}) %collective-permute-start.7) | collective-permute-done | bytes 393248 | tf_op jit(solution)/shard_map/ppermute | solution.py:832
  189.8 3.1 %collective-permute-start.8 = (bf16[1,128,768]{2,1,0:T(8,128)(2,1)S(1)}, bf16[1,128,768]{2,1,0:T(8,128)(2,1)S(1)}, u32[]{:S(2)}, u32[]{:S(2)}) collective-permute-start(bf16[1,128,768]{2,1,0:T(8,128)(2,1)S(1)} %dynamic-slice_convert_fusion), channel_id=1, source_target_pairs={{0,4},{2,6},{4,0},{6,2},{1,5},{3,7},{5,1},{7,3},{8,12},{10,14},{12... | collective-permute-start | bytes 589832 | tf_op jit(solution)/shard_map/ppermute | solution.py:832
  192.9 5.9 %collective-permute-done.11 = bf16[1,96,768]{2,1,0:T(8,128)(2,1)S(1)} collective-permute-done((bf16[1,96,768]{2,1,0:T(8,128)(2,1)S(1)}, bf16[1,96,768]{2,1,0:T(8,128)(2,1)S(1)}, u32[]{:S(2)}, u32[]{:S(2)}) %collective-permute-start.11) | collective-permute-done | bytes 147488 | tf_op jit(solution)/shard_map/ppermute | solution.py:832
  199.6 2.1 collective-permute-done.8
  203.0 3.3 %all-to-all-start.7 = ((bf16[4,24,768]{2,1,0:T(8,128)(2,1)}), bf16[4,24,768]{2,1,0:T(8,128)(2,1)S(1)}, u32[]{:S(2)}, u32[]{:S(2)}) async-start(bf16[4,24,768]{2,1,0:T(8,128)(2,1)} %bitcast.19), calls=%async_computation.7 | async-start | bytes 294912 | tf_op jit(solution)/shard_map/all_to_all | solution.py:836
  206.9 4.5 %all-to-all-done.7 = bf16[4,24,768]{2,1,0:T(8,128)(2,1)S(1)} async-done(((bf16[4,24,768]{2,1,0:T(8,128)(2,1)}), bf16[4,24,768]{2,1,0:T(8,128)(2,1)S(1)}, u32[]{:S(2)}, u32[]{:S(2)}) %all-to-all-start.7) | async-done | bytes 147488 | tf_op jit(solution)/shard_map/all_to_all | solution.py:836
  (87 shorter events, 21.0 us)
Async XLA Ops:
  0.6 16.5 %collective-permute-start = (bf16[128,768]{1,0:T(8,128)(2,1)}, bf16[128,768]{1,0:T(8,128)(2,1)S(1)}, u32[]{:S(2)}, u32[]{:S(2)}) collective-permute-start(bf16[128,768]{1,0:T(8,128)(2,1)} %bitcast.57), channel_id=1, source_target_pairs={{0,2},{2,0},{4,6},{6,4},{1,3},{3,1},{5,7},{7,5},{8,10},{10,8},{12,... | collective-permute-start | bytes 589832 | tf_op jit(solution)/shard_map/ppermute | solution.py:832
  3.8 11.7 %collective-permute-start.1 = (bf16[128,768]{1,0:T(8,128)(2,1)}, bf16[128,768]{1,0:T(8,128)(2,1)S(1)}, u32[]{:S(2)}, u32[]{:S(2)}) collective-permute-start(bf16[128,768]{1,0:T(8,128)(2,1)} %bitcast.58), channel_id=1, source_target_pairs={{0,4},{2,6},{4,0},{6,2},{1,5},{3,7},{5,1},{7,3},{8,12},{10,14},{12... | collective-permute-start | bytes 589832 | tf_op jit(solution)/shard_map/ppermute | solution.py:832
  15.5 5.7 %copy-start.17 = (bf16[128,768]{1,0:T(8,128)(2,1)}, bf16[128,768]{1,0:T(8,128)(2,1)S(1)}, u32[]{:S(2)}) copy-start(bf16[128,768]{1,0:T(8,128)(2,1)S(1)} %collective-permute-done.1.refs_2_) | copy-start | bytes 589828
  15.5 5.7 %collective-permute-start.2 = (bf16[128,768]{1,0:T(8,128)(2,1)S(1)}, bf16[128,768]{1,0:T(8,128)(2,1)S(1)}, u32[]{:S(2)}, u32[]{:S(2)}) collective-permute-start(bf16[128,768]{1,0:T(8,128)(2,1)S(1)} %collective-permute-done.1.refs_2_), channel_id=1, source_target_pairs={{0,2},{2,0},{4,6},{6,4},{1,3},{3,1},{5,7},{7,5},{8,10},{10,8},{12,... | collective-permute-start | bytes 589832 | tf_op jit(solution)/shard_map/ppermute | solution.py:832
  17.2 4.0 %copy-start.16 = (bf16[128,768]{1,0:T(8,128)(2,1)}, bf16[128,768]{1,0:T(8,128)(2,1)S(1)}, u32[]{:S(2)}) copy-start(bf16[128,768]{1,0:T(8,128)(2,1)S(1)} %collective-permute-done.refs_1_) | copy-start | bytes 589828
  21.2 0.7 copy-start.18
  25.7 2.1 collective-permute-start.3
  27.8 0.8 copy-start.15
  28.7 10.6 %copy-start.19 = (s32[1,12]{1,0:T(1,128)S(1)}, s32[1,12]{1,0:T(1,128)}, u32[]{:S(2)}) copy-start(s32[1,12]{1,0:T(1,128)} %len_ref.1) | copy-start | bytes 148
  28.7 11.9 %copy-start.6 = (bf16[1,128,768]{2,1,0:T(8,128)(2,1)S(1)}, bf16[1,128,768]{2,1,0:T(8,128)(2,1)}, u32[]{:S(2)}) copy-start(bf16[1,128,768]{2,1,0:T(8,128)(2,1)} %param.29) | copy-start | bytes 589828
  35.4 13.0 %all-to-all-start = ((bf16[4,128,256]{2,1,0:T(8,128)(2,1)}), bf16[4,128,256]{2,1,0:T(8,128)(2,1)S(1)}, u32[]{:S(2)}, u32[]{:S(2)}) async-start(bf16[4,128,256]{2,1,0:T(8,128)(2,1)} %get-tuple-element.39), calls=%async_computation | async-start | bytes 524288 | tf_op jit(solution)/shard_map/all_to_all | solution.py:836
  39.2 14.0 %copy-start.11 = (f32[768]{0:T(1024)S(1)}, f32[768]{0:T(1024)}, u32[]{:S(2)}) copy-start(f32[768]{0:T(1024)} %param.22) | copy-start | bytes 9220
  39.2 14.6 %copy-start.12 = (f32[768]{0:T(1024)S(1)}, f32[768]{0:T(1024)}, u32[]{:S(2)}) copy-start(f32[768]{0:T(1024)} %param.23) | copy-start | bytes 9220
  39.2 15.1 %copy-start.13 = (f32[768]{0:T(1024)S(1)}, f32[768]{0:T(1024)}, u32[]{:S(2)}) copy-start(f32[768]{0:T(1024)} %param.25) | copy-start | bytes 9220
  39.2 15.7 %copy-start.14 = (f32[768]{0:T(1024)S(1)}, f32[768]{0:T(1024)}, u32[]{:S(2)}) copy-start(f32[768]{0:T(1024)} %param.26) | copy-start | bytes 9220
  48.4 7.9 %copy-start.4 = (bf16[4,128,256]{2,1,0:T(8,128)(2,1)}, bf16[4,128,256]{2,1,0:T(8,128)(2,1)S(1)}, u32[]{:S(2)}) copy-start(bf16[4,128,256]{2,1,0:T(8,128)(2,1)S(1)} %all-to-all-done.piece_ref) | copy-start | bytes 786436
  49.5 23.9 %all-to-all-start.8 = ((bf16[4,128,768]{2,1,0:T(8,128)(2,1)}), bf16[4,128,768]{2,1,0:T(8,128)(2,1)S(1)}, u32[]{:S(2)}, u32[]{:S(2)}) async-start(bf16[4,128,768]{2,1,0:T(8,128)(2,1)} %broadcast_in_dim.37), calls=%async_computation.8 | async-start | bytes 1572864 | tf_op jit(solution)/shard_map/all_to_all | solution.py:836
  73.4 11.2 %copy-start.2 = (bf16[4,128,768]{2,1,0:T(8,128)(2,1)}, bf16[4,128,768]{2,1,0:T(8,128)(2,1)S(1)}, u32[]{:S(2)}) copy-start(bf16[4,128,768]{2,1,0:T(8,128)(2,1)S(1)} %all-to-all-done.8.grad_ref) | copy-start | bytes 2359300
  84.6 22.2 %all-to-all-start.6 = ((bf16[4,144,1536]{2,1,0:T(8,128)(2,1)}), bf16[4,144,1536]{2,1,0:T(8,128)(2,1)S(1)}, u32[]{:S(2)}, u32[]{:S(2)}) async-start(bf16[4,144,1536]{2,1,0:T(8,128)(2,1)} %get-tuple-element.55), calls=%async_computation.6 | async-start | bytes 3538944 | tf_op jit(solution)/shard_map/all_to_all | solution.py:836
  95.2 18.3 %collective-permute-start.4 = (bf16[4,128,512]{2,1,0:T(8,128)(2,1)}, bf16[4,128,512]{2,1,0:T(8,128)(2,1)S(1)}, u32[]{:S(2)}, u32[]{:S(2)}) collective-permute-start(bf16[4,128,512]{2,1,0:T(8,128)(2,1)} %get-tuple-element.49), channel_id=1, source_target_pairs={{0,1},{1,0},{2,3},{3,2},{4,5},{5,4},{6,7},{7,6},{8,9},{9,8},{10,11... | collective-permute-start | bytes 1572872 | tf_op jit(solution)/shard_map/ppermute | solution.py:828
  106.8 1.2 copy-start.1
  106.8 4.8 %copy-start.9 = (f32[768]{0:T(1024)S(1)}, f32[768]{0:T(1024)}, u32[]{:S(2)}) copy-start(f32[768]{0:T(1024)} %param.17) | copy-start | bytes 9220
  106.8 5.8 %copy-start.10 = (f32[768]{0:T(1024)S(1)}, f32[768]{0:T(1024)}, u32[]{:S(2)}) copy-start(f32[768]{0:T(1024)} %param.18) | copy-start | bytes 9220
  108.1 25.2 %all-to-all-start.5 = ((bf16[4,128,1792]{2,1,0:T(8,128)(2,1)}), bf16[4,128,1792]{2,1,0:T(8,128)(2,1)S(1)}, u32[]{:S(2)}, u32[]{:S(2)}) async-start(bf16[4,128,1792]{2,1,0:T(8,128)(2,1)} %get-tuple-element.54), calls=%async_computation.5 | async-start | bytes 3670016 | tf_op jit(solution)/shard_map/all_to_all | solution.py:836
  111.7 3.2 %copy-start.8 = (bf16[4,128,256]{2,1,0:T(8,128)(2,1)S(1)}, bf16[4,128,256]{2,1,0:T(8,128)(2,1)}, u32[]{:S(2)}) copy-start(bf16[4,128,256]{2,1,0:T(8,128)(2,1)} %get-tuple-element.47) | copy-start | bytes 786436
  120.5 2.2 %collective-permute-start.5 = (bf16[4,96,768]{2,1,0:T(8,128)(2,1)}, bf16[4,96,768]{2,1,0:T(8,128)(2,1)S(1)}, u32[]{:S(2)}, u32[]{:S(2)}) collective-permute-start(bf16[4,96,768]{2,1,0:T(8,128)(2,1)} %get-tuple-element.53), channel_id=1, source_target_pairs={{0,1},{1,0},{2,3},{3,2},{4,5},{5,4},{6,7},{7,6},{8,9},{9,8},{10,11... | collective-permute-start | bytes 1769480 | tf_op jit(solution)/shard_map/ppermute | solution.py:828
  133.2 14.8 %copy-start = (bf16[4,128,1792]{2,1,0:T(8,128)(2,1)}, bf16[4,128,1792]{2,1,0:T(8,128)(2,1)S(1)}, u32[]{:S(2)}) copy-start(bf16[4,128,1792]{2,1,0:T(8,128)(2,1)S(1)} %all-to-all-done.5.sent_ref) | copy-start | bytes 5505028
  144.5 22.0 %all-to-all-start.2 = ((bf16[4,128,768]{2,1,0:T(8,128)(2,1)}), bf16[4,128,768]{2,1,0:T(8,128)(2,1)S(1)}, u32[]{:S(2)}, u32[]{:S(2)}) async-start(bf16[4,128,768]{2,1,0:T(8,128)(2,1)} %pad_maximum_fusion.grad_ref), calls=%async_computation.2 | async-start | bytes 1572864 | tf_op jit(solution)/shard_map/all_to_all | solution.py:836
  151.8 7.1 %copy-start.5 = (f32[4,96,768]{2,1,0:T(8,128)S(1)}, f32[4,96,768]{2,1,0:T(8,128)}, u32[]{:S(2)}) copy-start(f32[4,96,768]{2,1,0:T(8,128)} %get-tuple-element.58) | copy-start | bytes 3538948
  151.8 6.2 %collective-permute-start.9 = (bf16[4,96,768]{2,1,0:T(8,128)(2,1)}, bf16[4,96,768]{2,1,0:T(8,128)(2,1)S(1)}, u32[]{:S(2)}, u32[]{:S(2)}) collective-permute-start(bf16[4,96,768]{2,1,0:T(8,128)(2,1)} %get-tuple-element.59), channel_id=1, source_target_pairs={{0,1},{1,0},{2,3},{3,2},{4,5},{5,4},{6,7},{7,6},{8,9},{9,8},{10,11... | collective-permute-start | bytes 1769480 | tf_op jit(solution)/shard_map/ppermute | solution.py:828
  156.9 18.2 %collective-permute-start.6 = (bf16[4,128,768]{2,1,0:T(8,128)(2,1)}, bf16[4,128,768]{2,1,0:T(8,128)(2,1)}, u32[]{:S(2)}, u32[]{:S(2)}) collective-permute-start(bf16[4,128,768]{2,1,0:T(8,128)(2,1)} %get-tuple-element.57), channel_id=1, source_target_pairs={{0,1},{1,0},{2,3},{3,2},{4,5},{5,4},{6,7},{7,6},{8,9},{9,8},{10,11... | collective-permute-start | bytes 2359304 | tf_op jit(solution)/shard_map/ppermute | solution.py:828
  158.1 0.8 copy-start.7
  160.8 22.9 %collective-permute-start.10 = (bf16[2,96,768]{2,1,0:T(8,128)(2,1)}, bf16[2,96,768]{2,1,0:T(8,128)(2,1)}, u32[]{:S(2)}, u32[]{:S(2)}) collective-permute-start(bf16[2,96,768]{2,1,0:T(8,128)(2,1)} %fusion.7), channel_id=1, source_target_pairs={{0,2},{2,0},{4,6},{6,4},{1,3},{3,1},{5,7},{7,5},{8,10},{10,8},{12,... | collective-permute-start | bytes 884744 | tf_op jit(solution)/shard_map/ppermute | solution.py:832
  166.5 4.0 %copy-start.3 = (bf16[4,128,768]{2,1,0:T(8,128)(2,1)}, bf16[4,128,768]{2,1,0:T(8,128)(2,1)S(1)}, u32[]{:S(2)}) copy-start(bf16[4,128,768]{2,1,0:T(8,128)(2,1)S(1)} %all-to-all-done.2.piece_ref) | copy-start | bytes 2359300
  166.5 13.1 %all-to-all-start.4 = ((bf16[4,24,768]{2,1,0:T(8,128)(2,1)}), bf16[4,24,768]{2,1,0:T(8,128)(2,1)}, u32[]{:S(2)}, u32[]{:S(2)}) async-start(bf16[4,24,768]{2,1,0:T(8,128)(2,1)} %bitcast.6), calls=%async_computation.4 | async-start | bytes 294912 | tf_op jit(solution)/shard_map/all_to_all | solution.py:836
  177.7 12.0 %collective-permute-start.7 = (bf16[2,128,768]{2,1,0:T(8,128)(2,1)}, bf16[2,128,768]{2,1,0:T(8,128)(2,1)S(1)}, u32[]{:S(2)}, u32[]{:S(2)}) collective-permute-start(bf16[2,128,768]{2,1,0:T(8,128)(2,1)} %fusion.6), channel_id=1, source_target_pairs={{0,2},{2,0},{4,6},{6,4},{1,3},{3,1},{5,7},{7,5},{8,10},{10,8},{12,... | collective-permute-start | bytes 1179656 | tf_op jit(solution)/shard_map/ppermute | solution.py:832
  184.8 14.0 %collective-permute-start.11 = (bf16[1,96,768]{2,1,0:T(8,128)(2,1)S(1)}, bf16[1,96,768]{2,1,0:T(8,128)(2,1)S(1)}, u32[]{:S(2)}, u32[]{:S(2)}) collective-permute-start(bf16[1,96,768]{2,1,0:T(8,128)(2,1)S(1)} %dynamic-slice_convert_fusion.1), channel_id=1, source_target_pairs={{0,4},{2,6},{4,0},{6,2},{1,5},{3,7},{5,1},{7,3},{8,12},{10,14},{12... | collective-permute-start | bytes 442376 | tf_op jit(solution)/shard_map/ppermute | solution.py:832
  189.8 11.9 %collective-permute-start.8 = (bf16[1,128,768]{2,1,0:T(8,128)(2,1)S(1)}, bf16[1,128,768]{2,1,0:T(8,128)(2,1)S(1)}, u32[]{:S(2)}, u32[]{:S(2)}) collective-permute-start(bf16[1,128,768]{2,1,0:T(8,128)(2,1)S(1)} %dynamic-slice_convert_fusion), channel_id=1, source_target_pairs={{0,4},{2,6},{4,0},{6,2},{1,5},{3,7},{5,1},{7,3},{8,12},{10,14},{12... | collective-permute-start | bytes 589832 | tf_op jit(solution)/shard_map/ppermute | solution.py:832
  203.0 8.4 %all-to-all-start.7 = ((bf16[4,24,768]{2,1,0:T(8,128)(2,1)}), bf16[4,24,768]{2,1,0:T(8,128)(2,1)S(1)}, u32[]{:S(2)}, u32[]{:S(2)}) async-start(bf16[4,24,768]{2,1,0:T(8,128)(2,1)} %bitcast.19), calls=%async_computation.7 | async-start | bytes 294912 | tf_op jit(solution)/shard_map/all_to_all | solution.py:836

commit v2 on v0

--- a/solution.py
+++ b/solution.py
@@ -3,6 +3,8 @@
 import jax
 import jax.numpy as jnp
 from jax import lax
+from jax.experimental import pallas as pl
+from jax.experimental.pallas import tpu as pltpu
 from jax.sharding import PartitionSpec as P
 
 HEADS = 12
@@ -284,42 +286,831 @@
     )
 
 
+def mapped(step, mesh, seq):
+    spread = P(("rows",) + (seq if isinstance(seq, tuple) else (seq,)))
+    tokens, plain = P("rows", seq, None), P()
+    weights = P(spread[0], None)
+    return jax.shard_map(
+        step,
+        mesh=mesh,
+        in_specs=(tokens, P("rows", None)) + (plain,) * 12 + (tokens,),
+        out_specs=(tokens, tokens, spread, spread, weights, weights, weights, spread, spread, weights)
+        + (spread, spread, weights, weights),
+        check_vma=False,
+    )
+
+
+F32 = jnp.float32
+PACE = 1e6
+BF16 = jnp.bfloat16
+NT = (((1,), (1,)), ((), ()))
+TN = (((0,), (0,)), ((), ()))
+NN = (((1,), (0,)), ((), ()))
+
+
+def mm(left, right, dims):
+    return lax.dot_general(left, right, dims, preferred_element_type=F32)
+
+
+def unit_norm(vector):
+    centered = vector - jnp.mean(vector, axis=-1, keepdims=True)
+    scale = lax.rsqrt(jnp.mean(centered * centered, axis=-1, keepdims=True) + 1e-05)
+    return centered * scale, scale
+
+
+def norm_back(grad, gain, unit, scale):
+    weighted = grad * gain
+    mean_w = jnp.mean(weighted, axis=-1, keepdims=True)
+    mean_wu = jnp.mean(weighted * unit, axis=-1, keepdims=True)
+    return scale * (weighted - mean_w - unit * mean_wu)
+
+
+def shape(dtype, *dims):
+    return jax.ShapeDtypeStruct(dims, dtype)
+
+
+def row(ref):
+    return ref[...].reshape(1, ref.shape[0])
+
+
+def size_of(item):
+    total = jnp.dtype(item.dtype).itemsize
+    for dim in item.shape:
+        total *= dim
+    return total
+
+
+def kernel(body, outs, scalars, operands, scratch=(), micros=2.0, name=None):
+    single = not isinstance(outs, (tuple, list))
+    listed = (outs,) if single else tuple(outs)
+    vmem = pl.BlockSpec(memory_space=pltpu.VMEM)
+    smem = pl.BlockSpec(memory_space=pltpu.SMEM)
+    moved = sum(size_of(v) for v in (*operands, *listed))
+    held = sum(size_of(v) for v in scratch)
+    return pl.pallas_call(
+        body,
+        out_shape=outs if single else listed,
+        in_specs=[smem] * len(scalars) + [vmem] * len(operands),
+        out_specs=vmem if single else (vmem,) * len(listed),
+        scratch_shapes=[pltpu.VMEM(v.shape, v.dtype) for v in scratch],
+        compiler_params=pltpu.CompilerParams(vmem_limit_bytes=min(60 << 20, (moved + held) * 5 // 4 + (6 << 20))),
+        cost_estimate=pl.CostEstimate(flops=int(micros * PACE), bytes_accessed=int(micros * PACE / 1e3), transcendentals=0),
+        name=name,
+    )(*scalars, *operands)
+
+
+def packed_rows(rows, live):
+    return rows * live // 128
+
+
+def pack(block):
+    rows, live = block.shape
+    whole = live // 128
+    pieces = [block[:, 128 * j : 128 * (j + 1)] for j in range(whole)]
+    if live % 128:
+        rest = block[:, 128 * whole :]
+        pieces.append(jnp.concatenate([rest[: rows // 2], rest[rows // 2 :]], axis=1))
+    return jnp.concatenate(pieces, axis=0)
+
+
+def unpack(block, rows, live):
+    whole = live // 128
+    pieces = [block[rows * j : rows * (j + 1)] for j in range(whole)]
+    if live % 128:
+        rest = block[rows * whole :]
+        pieces.append(jnp.concatenate([rest[:, :64], rest[:, 64:]], axis=0))
+    return jnp.concatenate(pieces, axis=1)
+
+
+def mask_call(place, lengths, out_grad):
+    rows, model = out_grad.shape
+
+    def body(place_ref, len_ref, in_ref, out_ref):
+        last = jnp.int32(0)
+        for d in range(lengths.shape[1]):
+            last = last + len_ref[0, d]
+        pos = lax.broadcasted_iota(jnp.int32, (rows, 1), 0) + (2 * place_ref[0] + place_ref[1]) * rows
+        out_ref[...] = jnp.where(pos < last, in_ref[...].astype(F32), 0.0).astype(BF16)
+
+    return kernel(body, shape(BF16, rows, model), (place, lengths), (out_grad,), micros=0.7, name="mask_grad")
+
+
+def qkv_call(blocks, gain, bias, weight, width):
+    count = len(blocks)
+    rows, model = blocks[0].shape
+
+    def body(*refs):
+        xs, (gain_ref, bias_ref, weight_ref, q_ref, kv_ref, unit_ref) = refs[:count], refs[count:]
+        for k in range(count):
+            unit, _ = unit_norm(xs[k][...].astype(F32))
+            normed = (unit * row(gain_ref) + row(bias_ref)).astype(BF16)
+            made = mm(normed, weight_ref[...], NN)
+            q_ref[k] = (made[:, :width].astype(BF16).astype(F32) * 0.125).astype(BF16)
+            kv_ref[k] = made[:, width:].astype(BF16)
+            unit_ref[k] = unit.astype(BF16)
+
+    outs = (
+        shape(BF16, count, rows, width),
+        shape(BF16, count, rows, 2 * width),
+        shape(BF16, count, rows, model),
+    )
+    return kernel(body, outs, (), (*blocks, gain, bias, weight), micros=1.2 * count, name="qkv_heads")
+
+
+def lane_head(lanes):
+    return lax.broadcasted_iota(jnp.int32, (1, lanes), 1) // HEAD_DIM
+
+
+def residue(pos_f, modulus):
+    return pos_f - modulus * jnp.floor((pos_f + 0.5) * (1.0 / modulus))
+
+
+def stack_heads(block, heads_here):
+    head_of = lane_head(block.shape[1])
+    return jnp.concatenate(
+        [jnp.where(head_of == h, block, jnp.zeros_like(block)) for h in range(heads_here)], axis=0
+    )
+
+
+def fold_heads(stacked, rows, heads_here):
+    head_of = lane_head(stacked.shape[1])
+    total = jnp.zeros((rows, stacked.shape[1]), stacked.dtype)
+    for h in range(heads_here):
+        total = jnp.where(head_of == h, stacked[h * rows : (h + 1) * rows], total)
+    return total
+
+
+def attend_call(place, lengths, groups, queries, kv_own, kv_other, heads_here):
+    count = sum(len(g) for g in groups)
+    rows, width = queries[0].shape[1:]
+    tall, wide = heads_here * rows, count * rows
+    docs = lengths.shape[1]
+    step = 16
+    n = len(groups)
+
+    def body(place_ref, len_ref, *refs):
+        q_in, own_in, oth_in = refs[:n], refs[n : 2 * n], refs[2 * n : 3 * n]
+        out_ref, prob_ref, q_ref, own_ref, oth_ref = refs[3 * n : 3 * n + 5]
+        msgs, (s_scr, m_scr, hot_scr, send_scr) = refs[3 * n + 5 : 3 * n + 5 + count], refs[3 * n + 5 + count :]
+        z_index, core = place_ref[0], place_ref[1]
+        for g, ks in enumerate(groups):
+            for j, k in enumerate(ks):
+                q_ref[z_index ^ k] = q_in[g][j]
+                own_ref[z_index ^ k] = own_in[g][j]
+                oth_ref[z_index ^ k] = oth_in[g][j]
+        sides = (own_ref, oth_ref)
+        cores = (core, 1 - core)
+        lane = lax.broadcasted_iota(jnp.int32, (rows, 128), 1).astype(F32)
+        for side in range(2):
+            for b in range(count):
+                pos = lax.broadcasted_iota(jnp.int32, (rows, 1), 0) + (2 * b + cores[side]) * rows
+                hot = (residue(pos.astype(F32), 12.0) == lane).astype(F32)
+                hot_scr[side, b * rows : (b + 1) * rows, :] = hot.astype(BF16)
+        for i in range(count):
+            keys = (i + 1) * rows
+            pos = lax.broadcasted_iota(jnp.int32, (rows, 1), 0) + (2 * i + core) * rows
+            pos_f = pos.astype(F32)
+            begin = jnp.zeros_like(pos)
+            run = jnp.int32(0)
+            for d in range(docs):
+                run = run + len_ref[0, d]
+                begin = jnp.where(pos >= run, run, begin)
+            tables = []
+            for h in range(heads_here):
+                head = (z_index * heads_here + h).astype(F32)
+                table = jnp.ones((rows, 128), F32)
+                for r in (2.0, 4.0, 6.0):
+                    mine = residue(head, r)
+                    pick_q = (residue(pos_f, r) == mine).astype(F32)
+                    pick_k = (residue(lane, r) == mine).astype(F32)
+                    table = table + pick_q * pick_k
+                tables.append(jnp.where(lane < 12.0, table, 0.0))
+            table = jnp.concatenate(tables, axis=0).astype(BF16)
+            stacked = stack_heads(q_ref[i], heads_here)
+            for side in range(2):
+                key = sides[side][:, :, :width].reshape(wide, width)[:keys]
+                s_scr[side, :, :keys] = mm(stacked, key, NT)
+                m_scr[side, :, :keys] = mm(table, hot_scr[side, :keys], NT)
+            key_pos = [
+                jnp.concatenate(
+                    [
+                        lax.broadcasted_iota(jnp.int32, (1, rows), 1) + (2 * b + cores[side]) * rows
+                        for b in range(i + 1)
+                    ],
+                    axis=1,
+                )
+                for side in range(2)
+            ]
+            for h in range(heads_here):
+                for at in range(0, rows, step):
+                    lo = h * rows + at
+                    pos_c, begin_c = pos[at : at + step], begin[at : at + step]
+                    masked = []
+                    for side in range(2):
+                        ok = (key_pos[side] <= pos_c) & (key_pos[side] >= begin_c)
+                        masked.append(jnp.where(ok, s_scr[side, lo : lo + step, :keys], masked_value))
+                    top = jnp.maximum(
+                        jnp.max(masked[0], axis=1, keepdims=True), jnp.max(masked[1], axis=1, keepdims=True)
+                    )
+                    parts = [
+                        jnp.exp(masked[side] - top) * m_scr[side, lo : lo + step, :keys] for side in range(2)
+                    ]
+                    total = jnp.sum(parts[0], axis=1, keepdims=True) + jnp.sum(parts[1], axis=1, keepdims=True)
+                    inverse = 1.0 / total
+                    for side in range(2):
+                        prob_ref[i, side, lo : lo + step, :keys] = (parts[side] * inverse).astype(BF16)
+            mixed = jnp.zeros((tall, width), F32)
+            for side in range(2):
+                value = sides[side][:, :, width:].reshape(wide, width)[:keys]
+                mixed = mixed + mm(prob_ref[i, side, :, :keys], value, NN)
+            result = fold_heads(mixed, rows, heads_here)
+            out_ref[i] = result
+            send_scr[i] = pack(result.astype(BF16)[:, :live])
+        for k in range(count):
+            msgs[k][...] = send_scr[z_index ^ k]
+
+    live = heads_here * HEAD_DIM
+    outs = (
+        shape(F32, count, rows, width),
+        shape(BF16, count, 2, tall, wide),
+        shape(BF16, count, rows, width),
+        shape(BF16, count, rows, 2 * width),
+        shape(BF16, count, rows, 2 * width),
+    ) + (shape(BF16, packed_rows(rows, live), 128),) * count
+    scratch = (
+        shape(F32, 2, tall, wide),
+        shape(F32, 2, tall, wide),
+        shape(BF16, 2, wide, 128),
+        shape(BF16, count, packed_rows(rows, live), 128),
+    )
+    operands = (*queries, *kv_own, *kv_other)
+    found = kernel(
+        body, outs, (place, lengths), operands, scratch, micros=6.0, name="attend"
+    )
+    return found[0], found[1:5], list(found[5:])
+
+
+def attend_back_call(place, queries, kv_own, kv_other, prob, attn, grads, heads_here):
+    count, rows, width = queries.shape
+    tall, wide = heads_here * rows, count * rows
+    step = 16
+
+    live = heads_here * HEAD_DIM
+
+    def body(place_ref, q_ref, own_ref, oth_ref, prob_ref, attn_ref, *refs):
+        grad_refs, (dq_ref, down_ref, doth_ref, p_scr, d_scr, acc, grad_ref) = refs[:count], refs[count:]
+        sides = (own_ref, oth_ref)
+        acc[...] = jnp.zeros_like(acc)
+        grad_ref[...] = jnp.zeros_like(grad_ref)
+        for k in range(count):
+            grad_ref[place_ref[0] ^ k, :, :live] = unpack(grad_refs[k][...], rows, live)
+        for i in range(count):
+            keys = (i + 1) * rows
+            grad = grad_ref[i]
+            stacked_q = stack_heads(q_ref[i], heads_here)
+            stacked_g = stack_heads(grad, heads_here)
+            product = grad.astype(F32) * attn_ref[i]
+            head_of = lane_head(width)
+            delta = [
+                jnp.sum(jnp.where(head_of == h, product, 0.0), axis=1, keepdims=True) for h in range(heads_here)
+            ]
+            for side in range(2):
+                value = sides[side][:, :, width:].reshape(wide, width)[:keys]
+                p_scr[side, :, :keys] = mm(stacked_g, value, NT)
+            for h in range(heads_here):
+                for at in range(0, rows, step):
+                    lo = h * rows + at
+                    for side in range(2):
+                        weights = prob_ref[i, side, lo : lo + step, :keys].astype(F32)
+                        shifted = p_scr[side, lo : lo + step, :keys] - delta[h][at : at + step]
+                        d_scr[side, lo : lo + step, :keys] = (weights * shifted).astype(BF16)
+            grad_q = jnp.zeros((tall, width), F32)
+            for side in range(2):
+                key = sides[side][:, :, :width].reshape(wide, width)[:keys]
+                moved = d_scr[side, :, :keys]
+                grad_q = grad_q + mm(moved, key, NN)
+                acc[side, :keys, :width] += mm(moved, stacked_q, TN)
+                acc[side, :keys, width:] += mm(prob_ref[i, side, :, :keys], stacked_g, TN)
+            dq_ref[i] = (0.125 * fold_heads(grad_q, rows, heads_here)).astype(BF16)
+        down_ref[...] = acc[0].reshape(count, rows, 2 * width)
+        doth_ref[...] = acc[1].reshape(count, rows, 2 * width).astype(BF16)
+
+    outs = (
+        shape(BF16, count, rows, width),
+        shape(F32, count, rows, 2 * width),
+        shape(BF16, count, rows, 2 * width),
+    )
+    scratch = (
+        shape(F32, 2, tall, wide),
+        shape(BF16, 2, tall, wide),
+        shape(F32, 2, wide, 2 * width),
+        shape(BF16, count, rows, width),
+    )
+    operands = (queries, kv_own, kv_other, prob, attn, *grads)
+    return kernel(body, outs, (place,), operands, scratch, micros=6.0, name="attend_back")
+
+
+def join_call(place, grad_q, grad_kv, arrived, live):
+    count, rows, width = grad_q.shape
+
+    def body(place_ref, q_ref, kv_ref, in_ref, out_ref, *rest):
+        msgs, scr = rest[:count], rest[count]
+        for b in range(count):
+            both = (kv_ref[b] + in_ref[b].astype(F32)).astype(BF16)
+            out_ref[b, :, :width] = q_ref[b]
+            out_ref[b, :, width:] = both
+            dense = [q_ref[b][:, :live], both[:, :live], both[:, width : width + live]]
+            scr[b] = pack(jnp.concatenate(dense, axis=1))
+        for k in range(count):
+            msgs[k][...] = scr[place_ref[0] ^ k]
+
+    message = shape(BF16, packed_rows(rows, 3 * live), 128)
+    outs = (shape(BF16, count, rows, 3 * width),) + (message,) * count
+    scratch = (shape(BF16, count, *message.shape),)
+    joined, *msgs = kernel(body, outs, (place,), (grad_q, grad_kv, arrived), scratch, micros=0.7, name="join_grads")
+    return joined, msgs
+
+
+def gather_heads(place_ref, pieces, scr, rows, live):
+    for k, ref in enumerate(pieces):
+        scr[place_ref[0] ^ k] = ref[...]
+    return jnp.concatenate([unpack(scr[k], rows, live) for k in range(len(pieces))], axis=1)
+
+
+def norms_call(place, pieces, layer_in, vectors, w_out, parts, live):
+    count, rows = len(pieces), layer_in.shape[0]
+    model = w_out.shape[0]
+    quarter = model // parts
+    pad_q = -(-quarter // 128) * 128
+
+    def body(place_ref, *refs):
+        in_ref, g2, b2, g3, b3, wo_ref, mid_ref, attn_ref = refs[count : count + 8]
+        msgs, (n2_scr, piece_scr) = refs[count + 8 : count + 8 + parts], refs[count + 8 + parts :]
+        attn = gather_heads(place_ref, refs[:count], piece_scr, rows, live)
+        attn_ref[...] = attn
+        unit2, _ = unit_norm(attn.astype(F32))
+        normed2 = (unit2 * row(g2) + row(b2)).astype(BF16)
+        for r in range(parts):
+            n2_scr[r, :, :quarter] = normed2[:, r * quarter : (r + 1) * quarter]
+            if pad_q > quarter:
+                n2_scr[r, :, quarter:] = jnp.zeros((rows, pad_q - quarter), BF16)
+        middle = in_ref[...].astype(F32) + mm(normed2, wo_ref[...], NN)
+        mid_ref[...] = middle
+        unit3, _ = unit_norm(middle)
+        normed3 = (unit3 * row(g3) + row(b3)).astype(BF16)
+        for k in range(parts):
+            msgs[k][:, :model] = normed3
+            msgs[k][:, model:] = n2_scr[place_ref[2] ^ k]
+
+    outs = (shape(F32, rows, model), shape(BF16, rows, model)) + (shape(BF16, rows, model + pad_q),) * parts
+    operands = (*pieces, layer_in, *vectors, w_out)
+    scratch = (shape(BF16, parts, rows, pad_q), shape(BF16, count, *pieces[0].shape))
+    mid, attn, *msgs = kernel(body, outs, (place,), operands, scratch, micros=1.5, name="norms")
+    return mid, attn, msgs
+
+
+def up_call(place, normed3, w_up, parts):
+    rows, (model, hidden) = normed3.shape[0], w_up.shape
+    part = hidden // parts
+
+    def body(place_ref, n3_ref, wu_ref, act_ref, slope_ref, *msgs):
+        normed = n3_ref[:, :model]
+        for r in range(parts):
+            upper = mm(normed, wu_ref[:, r * part : (r + 1) * part], NN)
+            cumulative = 0.5 * (1.0 + lax.erf(upper * 0.7071067811865476))
+            density = jnp.exp(-0.5 * upper * upper) * 0.3989422804014327
+            act_ref[r] = (upper * cumulative).astype(BF16)
+            slope_ref[r] = (cumulative + upper * density).astype(BF16)
+        for k in range(parts):
+            msgs[k][...] = act_ref[place_ref[2] ^ k]
+
+    outs = (shape(BF16, parts, rows, part),) * 2 + (shape(BF16, rows, part),) * parts
+    act, slope, *msgs = kernel(body, outs, (place,), (normed3, w_up), micros=2.0, name="up_gelu")
+    return act, slope, msgs
+
+
+def backward_call(place, attn, middle, act, slope, grad_out, vectors, w_out, w_up, w_down, parts, count, live):
+    rows = attn.shape[0]
+    model, hidden = w_up.shape
+    part, quarter = hidden // parts, model // parts
+    message = shape(BF16, packed_rows(rows, live), 128)
+
+    def body(
+        place_ref, attn_ref, mid_ref, act_ref, slope_ref, go_ref, g2, b2, g3, b3, wo_ref, wu_ref, wd_ref,
+        out_ref, gmid_ref, *rest,
+    ):
+        msgs, heads = rest[:parts], rest[parts : parts + count]
+        up_scr, table_scr, head_scr = rest[parts + count :]
+        here = place_ref[2]
+        go = go_ref[...]
+        middle = mid_ref[...]
+        out = middle
+        grad3 = jnp.zeros((rows, model), F32)
+        for r in range(parts):
+            w_d = wd_ref[r * part : (r + 1) * part, :]
+            out = out + mm(act_ref[r], w_d, NN)
+            grad_up = (mm(go, w_d, NT) * slope_ref[r].astype(F32)).astype(BF16)
+            up_scr[r] = grad_up
+            grad3 = grad3 + mm(grad_up, wu_ref[:, r * part : (r + 1) * part], NT)
+        out_ref[...] = out.astype(BF16)
+        unit3, scale3 = unit_norm(middle)
+        grad_mid = go.astype(F32) + norm_back(grad3, row(g3), unit3, scale3)
+        gmid_ref[...] = grad_mid
+        proj = grad_mid.astype(BF16)
+        grad2 = mm(proj, wo_ref[...], NT)
+        unit2, scale2 = unit_norm(attn_ref[...].astype(F32))
+        grad_attn = norm_back(grad2, row(g2), unit2, scale2).astype(BF16)
+        for k in range(count):
+            head_scr[k] = pack(grad_attn[:, k * live : (k + 1) * live])
+        for k in range(count):
+            heads[k][...] = head_scr[place_ref[0] ^ k]
+        sums = [
+            jnp.sum(grad2 * unit2, axis=0, keepdims=True),
+            jnp.sum(grad2, axis=0, keepdims=True),
+            jnp.sum(grad3 * unit3, axis=0, keepdims=True),
+            jnp.sum(grad3, axis=0, keepdims=True),
+        ]
+        table = jnp.concatenate(sums + [jnp.zeros((12, model), F32)], axis=0).astype(BF16)
+        for r in range(parts):
+            table_scr[r, :, :quarter] = table[:, r * quarter : (r + 1) * quarter]
+        for k in range(parts):
+            msgs[k][:rows, :part] = up_scr[here ^ k]
+            msgs[k][:rows, part:] = proj
+            msgs[k][rows:, :] = jnp.zeros((16, part + model), BF16)
+            msgs[k][rows:, part : part + quarter] = table_scr[here ^ k, :, :quarter]
+
+    outs = (
+        shape(BF16, rows, model),
+        shape(F32, rows, model),
+    )
+    outs += (shape(BF16, rows + 16, part + model),) * parts + (message,) * count
+    operands = (attn, middle, act, slope, grad_out, *vectors, w_out, w_up, w_down)
+    scratch = (
+        shape(BF16, parts, rows, part),
+        shape(BF16, parts, 16, -(-quarter // 128) * 128),
+        shape(BF16, count, *message.shape),
+    )
+    found = kernel(body, outs, (place,), operands, scratch, micros=9.0, name="token_backward")
+    found = list(found)
+    return found[0], found[1], found[2 : 2 + parts], found[2 + parts :]
+
+
+def down_grad_call(place, acts, grads, chips):
+    parts = len(acts)
+    part, model = acts[0].shape[1], grads[0].shape[1]
+    own = part // (2 * chips)
+
+    def body(place_ref, *refs):
+        act_refs, grad_refs, (keep_ref, send_ref, scr) = refs[:parts], refs[parts : 2 * parts], refs[2 * parts :]
+        core = place_ref[1]
+        act = jnp.concatenate([ref[...] for ref in act_refs], axis=0)
+        grad = jnp.concatenate([ref[...] for ref in grad_refs], axis=0)
+        scr[...] = mm(act, grad, TN).reshape(chips, 2, own, model)
+        for k in range(chips):
+            keep_ref[k] = scr[k, core]
+            send_ref[k] = scr[k, 1 - core].astype(BF16)
+
+    outs = (shape(F32, chips, own, model), shape(BF16, chips, own, model))
+    scratch = (shape(F32, chips, 2, own, model),)
+    return kernel(body, outs, (place,), (*acts, *grads), scratch, micros=3.0, name="grad_down")
+
+
+def up_grad_call(place, sent, back, chips, part, model):
+    parts = len(sent)
+    rows = sent[0].shape[0]
+    quarter = model // parts
+    own = model // (parts * chips * 2)
+    tall = (parts + 1) * own + 8
+
+    def body(place_ref, *refs):
+        sent_refs, back_refs = refs[:parts], refs[parts : 2 * parts]
+        keep_ref, send_ref, up_scr, out_scr, vec_scr = refs[2 * parts :]
+        core = place_ref[1]
+        normed3 = jnp.concatenate([ref[:, :model] for ref in sent_refs], axis=0)
+        normed2 = jnp.concatenate([ref[:, model:] for ref in sent_refs], axis=0)
+        grad_up = jnp.concatenate([ref[:rows, :part] for ref in back_refs], axis=0)
+        proj = jnp.concatenate([ref[:rows, part:] for ref in back_refs], axis=0)
+        up_scr[...] = mm(normed3, grad_up, TN).reshape(parts, chips, 2, own, part)
+        out_scr[...] = mm(normed2, proj, TN)[:quarter].reshape(chips, 2, own, model)
+        table = jnp.zeros((8, quarter), F32)
+        for ref in back_refs:
+            table = table + ref[rows:, part : part + quarter].astype(F32)[:8]
+        vec_scr[...] = jnp.zeros_like(vec_scr)
+        for k in range(chips):
+            for side in range(2):
+                at = (2 * k + side) * own
+                vec_scr[k, side, :, :own] = table[:, at : at + own]
+        for k in range(chips):
+            for side, ref in ((core, keep_ref), (1 - core, send_ref)):
+                pieces = [up_scr[r, k, side] for r in range(parts)] + [out_scr[k, side], vec_scr[k, side]]
+                ref[k] = jnp.concatenate(pieces, axis=0).astype(ref.dtype)
+
+    outs = (shape(F32, chips, tall, model), shape(BF16, chips, tall, model))
+    scratch = (
+        shape(F32, parts, chips, 2, own, part),
+        shape(F32, chips, 2, own, model),
+        shape(F32, chips, 2, 8, model),
+    )
+    return kernel(body, outs, (place,), (*sent, *back), scratch, micros=4.0, name="grad_up_out")
+
+
+def qkv_grad_call(place, groups, units, grads, gain, bias, weight, parts, live, width):
+    count, rows = grads.shape[:2]
+    model = weight.shape[0]
+    own = model // (parts * count * 2)
+    n = len(units)
+
+    def body(place_ref, *refs):
+        unit_refs = refs[:n]
+        grad_ref, gain_ref, bias_ref, weight_ref, keep_ref, send_ref, unit_scr, scr = refs[n:]
+        z_index, core = place_ref[0], place_ref[1]
+        for g, ks in enumerate(groups):
+            for j, k in enumerate(ks):
+                unit_scr[z_index ^ k] = unit_refs[g][j]
+        grad = grad_ref[...].reshape(count * rows, 3 * width)
+        cross = mm(unit_scr[...].reshape(count * rows, model), grad, TN)
+        total = jnp.sum(grad.astype(F32), axis=0, keepdims=True)
+        columns = jnp.concatenate([row(gain_ref), row(bias_ref), jnp.zeros((6, model), F32)], axis=0).T
+        weight_f = weight_ref[...].astype(F32)
+        grad_gain = jnp.sum(weight_f * cross, axis=1, keepdims=True)
+        grad_bias = jnp.sum(weight_f * total, axis=1, keepdims=True)
+        lane = lax.broadcasted_iota(jnp.int32, (1, 3 * width), 1)
+        made = columns[:, 0:1] * cross + columns[:, 1:2] * total
+        made = jnp.where(lane == live, grad_gain, jnp.where(lane == live + 1, grad_bias, made))
+        scr[...] = made.reshape(parts, count, 2, own, 3 * width)
+        for r in range(parts):
+            keep_ref[r] = jnp.concatenate([scr[r, k, core] for k in range(count)], axis=0)
+            send_ref[r] = jnp.concatenate([scr[r, k, 1 - core] for k in range(count)], axis=0).astype(BF16)
+
+    outs = (shape(F32, parts, count * own, 3 * width), shape(BF16, parts, count * own, 3 * width))
+    scratch = (shape(BF16, count, rows, model), shape(F32, parts, count, 2, own, 3 * width))
+    operands = (*units, grads, gain, bias, weight)
+    return kernel(body, outs, (place,), operands, scratch, micros=4.0, name="grad_qkv")
+
+
+def spread_call(place, keep, arrived):
+    parts = keep.shape[0]
+
+    def body(place_ref, keep_ref, in_ref, *outs):
+        for k in range(parts):
+            at = place_ref[2] ^ k
+            outs[k][...] = (keep_ref[at] + in_ref[at].astype(F32)).astype(BF16)
+
+    return kernel(body, (shape(BF16, *keep.shape[1:]),) * parts, (place,), (keep, arrived), micros=0.8, name="spread")
+
+
+def halve_call(place, keep, arrived, bit):
+    half = keep.shape[0] // 2
+
+    def body(place_ref, keep_ref, in_ref, stay_ref, away_ref):
+        mine = (place_ref[0] // bit) % 2
+        for j in range(half):
+            here, there = 2 * j + mine, 2 * j + 1 - mine
+            stay_ref[j] = keep_ref[here] + in_ref[here].astype(F32)
+            away_ref[j] = (keep_ref[there] + in_ref[there].astype(F32)).astype(BF16)
+
+    rest = keep.shape[1:]
+    return kernel(body, (shape(F32, half, *rest), shape(BF16, half, *rest)), (place,), (keep, arrived), micros=0.8, name="halve")
+
+
+def finish_down_call(keep, arrived):
+    def body(keep_ref, in_ref, out_ref):
+        out_ref[...] = keep_ref[0] + in_ref[0].astype(F32)
+
+    return kernel(body, shape(F32, *keep.shape[1:]), (), (keep, arrived), micros=0.6, name="finish_down")
+
+
+def finish_up_call(place, keep, arrived, parts, own, part):
+    model = keep.shape[2]
+
+    def body(place_ref, keep_ref, in_ref, out_ref, g2, b2, g3, b3, *rest):
+        msgs, scr = rest[:parts], rest[parts]
+        value = keep_ref[0] + in_ref[0].astype(F32)
+        out_ref[...] = value[parts * own : (parts + 1) * own]
+        for at, ref in enumerate((g2, b2, g3, b3)):
+            line = (parts + 1) * own + at
+            ref[...] = value[line : line + 1, :own].reshape(own)
+        scr[...] = value[: parts * own].reshape(parts, own, part)
+        for k in range(parts):
+            msgs[k][...] = scr[place_ref[2] ^ k].astype(BF16)
+
+    outs = (shape(F32, own, model),) + (shape(F32, own),) * 4 + (shape(BF16, own, part),) * parts
+    scratch = (shape(F32, parts, own, part),)
+    return kernel(body, outs, (place,), (keep, arrived), scratch, micros=0.8, name="finish_up")
+
+
+def place_up_call(place, pieces):
+    parts = len(pieces)
+    own, part = pieces[0].shape
+
+    def body(place_ref, *refs):
+        for k in range(parts):
+            at = pl.multiple_of((place_ref[2] ^ k) * part, 128)
+            refs[parts][:, pl.ds(at, part)] = refs[k][...].astype(F32)
+
+    return kernel(body, shape(F32, own, parts * part), (place,), tuple(pieces), micros=0.5, name="place_up")
+
+
+def share_call(place, pieces, chips):
+    own = pieces[0].shape[0] // chips
+
+    def body(place_ref, *refs):
+        ins, outs, scr = refs[: len(pieces)], refs[len(pieces) : -1], refs[-1]
+        total = ins[0][...].astype(F32)
+        for ref in ins[1:]:
+            total = total + ref[...].astype(F32)
+        scr[...] = total.reshape(chips, own, total.shape[1])
+        for k in range(chips):
+            outs[k][...] = scr[place_ref[0] ^ k].astype(BF16)
+
+    lanes = pieces[0].shape[1]
+    outs = (shape(BF16, own, lanes),) * chips
+    return kernel(body, outs, (place,), tuple(pieces), (shape(F32, chips, own, lanes),), micros=0.7, name="share")
+
+
+def finish_qkv_call(place, pieces, model, live, width):
+    count, own = len(pieces), pieces[0].shape[0]
+
+    def body(place_ref, *refs):
+        q_ref, k_ref, v_ref, gain_ref, bias_ref, in_ref = refs[count:]
+        for k in range(count):
+            in_ref[place_ref[0] ^ k] = refs[k][...].astype(F32)
+        for at, ref in enumerate((q_ref, k_ref, v_ref)):
+            ref[...] = jnp.concatenate(
+                [in_ref[k, :, at * width : at * width + live] for k in range(count)], axis=1
+            )
+        total = jnp.sum(in_ref[:, :, live : live + 2], axis=0).T
+        gain_ref[...] = total[0:1].reshape(own)
+        bias_ref[...] = total[1:2].reshape(own)
+
+    outs = (shape(F32, own, model),) * 3 + (shape(F32, own),) * 2
+    scratch = (shape(F32, count, *pieces[0].shape),)
+    return kernel(body, outs, (place,), tuple(pieces), scratch, micros=0.8, name="finish_qkv")
+
+
+def input_grad_call(place, pieces, layer_in, grad_mid, gain, w_query, w_key, w_value, live):
+    count = len(pieces)
+    rows, model = layer_in.shape
+
+    def body(place_ref, *refs):
+        in_ref, gmid_ref, gain_ref, wq_ref, wk_ref, wv_ref, out_ref, scr = refs[count:]
+        for k in range(count):
+            scr[place_ref[0] ^ k] = refs[k][...]
+        blocks = [unpack(scr[k], rows, 3 * live) for k in range(count)]
+        grad = jnp.zeros((rows, model), F32)
+        for at, w_ref in enumerate((wq_ref, wk_ref, wv_ref)):
+            part = jnp.concatenate([block[:, at * live : (at + 1) * live] for block in blocks], axis=1)
+            grad = grad + mm(part, w_ref[...], NT)
+        unit, scale = unit_norm(in_ref[...].astype(F32))
+        out_ref[...] = (gmid_ref[...] + norm_back(grad, row(gain_ref), unit, scale)).astype(BF16)
+
+    operands = (*pieces, layer_in, grad_mid, gain, w_query, w_key, w_value)
+    scratch = (shape(BF16, count, *pieces[0].shape),)
+    return kernel(body, shape(BF16, rows, model), (place,), operands, scratch, micros=3.0, name="grad_inputs")
+
+
+def swap_core(value):
+    return lax.ppermute(value, "core", [(0, 1), (1, 0)])
+
+
+def swap(value, axis, bit):
+    return lax.ppermute(value, axis, [(k, k ^ bit) for k in range(lax.axis_size(axis))])
+
+
+def trade(messages, axis):
+    return [messages[0]] + [swap(messages[k], axis, k) for k in range(1, len(messages))]
+
+
+def gather_chips(block, chips):
+    found = {0: block}
+    bit = chips // 2
+    while bit >= 1:
+        for k in sorted(found):
+            found[k | bit] = swap(found[k], "chip", bit)
+        bit //= 2
+    return [found[k] for k in range(chips)]
+
+
+def scatter_chips(place, keep, arrived, chips, bit):
+    while bit < chips:
+        keep, away = halve_call(place, keep, arrived, bit)
+        arrived = swap(away, "chip", bit)
+        bit *= 2
+    return keep, arrived
+
+
+def fast_shards(
+    inputs, doc_lengths, ln1_gain, ln1_bias, w_query, w_key, w_value, ln2_gain, ln2_bias, w_out,
+    ln3_gain, ln3_bias, w_up, w_down, out_grad,
+):
+    rows, model = inputs.shape[1:]
+    chips, parts = lax.axis_size("chip"), lax.axis_size("rows")
+    z_index = lax.axis_index("chip")
+    heads_here = HEADS // chips
+    live = heads_here * HEAD_DIM
+    width = -(-live // 128) * 128
+    hidden = w_up.shape[1]
+    part = hidden // parts
+    own = model // (parts * chips * 2)
+    place = jnp.stack([z_index, lax.axis_index("core"), lax.axis_index("rows")]).astype(jnp.int32)
+    scope = jax.named_scope
+
+    def columns(weight):
+        mine = lax.dynamic_slice_in_dim(weight, z_index * live, live, 1)
+        return jnp.pad(mine, ((0, 0), (0, width - live)))
+
+    place, layer_in, out_grad = lax.optimization_barrier((place, inputs[0], out_grad[0]))
+    with scope("gather_in"):
+        blocks = gather_chips(layer_in, chips)
+    grad_out = mask_call(place, doc_lengths, out_grad)
+    w_heads = jnp.concatenate([columns(w_query), columns(w_key), columns(w_value)], axis=1)
+    groups = [g for g in ([0], list(range(1, chips - 1)), [chips - 1]) if g] if chips > 1 else [[0]]
+    made = [qkv_call([blocks[k] for k in g], ln1_gain, ln1_bias, w_heads, width) for g in groups]
+    queries, kv_own, units = ([m[at] for m in made] for at in range(3))
+    with scope("core_kv"):
+        kv_other = [swap_core(v) for v in kv_own]
+    attn_heads, (prob, queries, kv_own, kv_other), messages = attend_call(
+        place, doc_lengths, groups, queries, kv_own, kv_other, heads_here
+    )
+    fence = lax.optimization_barrier
+    messages, grad_out = fence((messages, grad_out))
+    with scope("chip_attn"):
+        pieces = trade(messages, "chip")
+    with scope("plane_out"):
+        grads_plane = trade([grad_out] * parts, "rows")
+    pieces, grads_plane = fence((pieces, grads_plane))
+
+    vectors = (ln2_gain, ln2_bias, ln3_gain, ln3_bias)
+    middle, attn, sent = norms_call(place, pieces, layer_in, vectors, w_out, parts, live)
+    act, slope, acts = up_call(place, sent[0], w_up, parts)
+    with scope("plane_norms"):
+        sent = trade(sent, "rows")
+    with scope("plane_act"):
+        acts = trade(acts, "rows")
+    output, grad_mid, back, messages = backward_call(
+        place, attn, middle, act, slope, grad_out, vectors, w_out, w_up, w_down, parts, chips, live
+    )
+    with scope("chip_grad"):
+        grad_heads = trade(messages, "chip")
+    grad_heads, sent = fence((grad_heads, sent))
+    grad_q, grad_kv, grad_kv_other = attend_back_call(
+        place, queries, kv_own, kv_other, prob, attn_heads, grad_heads, heads_here
+    )
+    grad_kv_other, acts = fence((grad_kv_other, acts))
+    down_keep, down_send = down_grad_call(place, acts, grads_plane, chips)
+    with scope("core_grad"):
+        grad_kv_other = swap_core(grad_kv_other)
+    with scope("core_down"):
+        down_recv = swap_core(down_send)
+    grad_qkv, messages = join_call(place, grad_q, grad_kv, grad_kv_other, live)
+    down_keep, down_away = halve_call(place, down_keep, down_recv, 1)
+    messages, down_away, back, grad_qkv = fence((messages, down_away, back, grad_qkv))
+    with scope("chip_qkv"):
+        grad_pieces = trade(messages, "chip")
+    with scope("plane_back"):
+        back = trade(back, "rows")
+    with scope("down_one"):
+        down_recv = swap(down_away, "chip", 1)
+    qkv_keep, qkv_send = qkv_grad_call(
+        place, groups, units, grad_qkv, ln1_gain, ln1_bias, w_heads, parts, live, width
+    )
+    qkv_send, down_recv, grad_pieces, back = fence((qkv_send, down_recv, grad_pieces, back))
+    up_keep, up_send = up_grad_call(place, sent, back, chips, part, model)
+    with scope("core_w"):
+        qkv_send = swap_core(qkv_send)
+    with scope("core_up"):
+        up_recv = swap_core(up_send)
+    with scope("down_two"):
+        down_keep, down_last = scatter_chips(place, down_keep, down_recv, chips, 2)
+    with scope("plane_w"):
+        qkv_sums = trade(spread_call(place, qkv_keep, qkv_send), "rows")
+    with scope("up_sum"):
+        up_keep, up_last = scatter_chips(place, up_keep, up_recv, chips, 1)
+    with scope("chip_w"):
+        qkv_all = trade(share_call(place, qkv_sums, chips), "chip")
+    gwo, g2, b2, g3, b3, *up_rows = finish_up_call(place, up_keep, up_last, parts, own, part)
+    with scope("plane_rows"):
+        up_rows = trade(up_rows, "rows")
+    gwq, gwk, gwv, g1, b1 = finish_qkv_call(place, qkv_all, model, live, width)
+    gwu = place_up_call(place, up_rows)
+    gwd = finish_down_call(down_keep, down_last)
+    grad_inputs = input_grad_call(
+        place, grad_pieces, layer_in, grad_mid, ln1_gain, w_query, w_key, w_value, live
+    )
+    return (
+        output[None], grad_inputs[None], g1, b1, gwq, gwk, gwv, g2, b2, gwo, g3, b3, gwu, gwd,
+    )
+
+
+def takes_fast(mesh):
+    seq, parts = mesh.shape["seq"], mesh.shape["rows"]
+    chips = seq // 2
+    return seq % 2 == 0 and chips & (chips - 1) == 0 and parts & (parts - 1) == 0 and HEADS % max(chips, 1) == 0
+
+
 def solution(mesh):
-    return jax.shard_map(
-        shards,
-        mesh=mesh,
-        in_specs=(
-            P("rows", "seq", None),
-            P("rows", None),
-            P(),
-            P(),
-            P(),
-            P(),
-            P(),
-            P(),
-            P(),
-            P(),
-            P(),
-            P(),
-            P(),
-            P(),
-            P("rows", "seq", None),
-        ),
-        out_specs=(
-            P("rows", "seq", None),
-            P("rows", "seq", None),
-            P(("rows", "seq")),
-            P(("rows", "seq")),
-            P(("rows", "seq"), None),
-            P(("rows", "seq"), None),
-            P(("rows", "seq"), None),
-            P(("rows", "seq")),
-            P(("rows", "seq")),
-            P(("rows", "seq"), None),
-            P(("rows", "seq")),
-            P(("rows", "seq")),
-            P(("rows", "seq"), None),
-            P(("rows", "seq"), None),
-        ),
-        check_vma=False,
-    )
+    if takes_fast(mesh):
+        parts, seq = mesh.shape["rows"], mesh.shape["seq"]
+        split = jax.sharding.Mesh(mesh.devices.reshape(parts, seq // 2, 2), ("rows", "chip", "core"))
+        return mapped(fast_shards, split, ("chip", "core"))
+    return mapped(shards, mesh, "seq")

time: 946 us -> 148 us (0.16)
  waiting for transfers between devices: 738 us -> 43.3 us
  matrix products: 70.9 us -> 0 us
  starting transfers between devices: 0.67 us -> 62.1 us
  blocking collectives: 38.5 us -> 0 us
  local copies, waits for them, and re-layouts: 42.5 us -> 4.03 us
  Pallas kernels: 0 us -> 36.9 us
  other arithmetic: 28 us -> 0.24 us
  between operations: 15.4 us -> 1.07 us
    reduce_scatter x6 -> x0, waiting for transfers between devices: 634 us -> none  [the longest x1 142 us: shards(): lax.psum_scatter(grad_w_up, ('rows', 'seq'), scatter_dimension=0, tiled=T...]
    dot_general x32 -> x0, matrix products: 70.9 us -> none  [the longest x6 20.2 us: rows_inner(): lax.dot_general(left, right, (((0,), (0,)), ((), ())), preferred_element_...]
    ppermute x0 -> x44, starting transfers between devices: none -> 62.1 us  [the longest x37 60.3 us: swap(): lax.ppermute(value, axis, [(k, k ^ bit) for k in range(lax.axis_size(axis...]
    unnamed x12 -> x0, waiting for transfers between devices: 55.2 us -> none
    all_gather x2 -> x0, waiting for transfers between devices: 49.1 us -> none  [the longest x1 24.9 us: shards(): lax.all_gather(keys_local, 'seq', axis=0, tiled=True)]
    ppermute x0 -> x44, waiting for transfers between devices: none -> 43.3 us  [the longest x37 38.6 us: swap(): lax.ppermute(value, axis, [(k, k ^ bit) for k in range(lax.axis_size(axis...]
    unnamed x1 -> x0, blocking collectives: 38.5 us -> none
    pallas_call x0 -> x24, Pallas kernels: none -> 36.9 us  [kernel(): pl.pallas_call(body, out_shape=outs if single else listed, in_specs=[smem...]
  transfers between devices with their start and end apart: 10 -> 44, of which waited for: 10 -> 17; matrix products, arithmetic and copies ran while one was open for 4% -> 2% of each run, Pallas kernels for 0% -> 18%
where the time goes in v2:
time: 148 us
  starting transfers between devices  62.1 us (42%)
  waiting for transfers between devices  43.3 us (29%)
  Pallas kernels  36.9 us (25%)
  local copies, waits for them, and re-layouts  4.03 us (3%)
    ppermute x37, starting transfers between devices, swap(): lax.ppermute(value, axis, [(k, k ^ bit) for k in range(lax.axis_size(axis...  60.3 us
    ppermute x37, waiting for transfers between devices, swap(): lax.ppermute(value, axis, [(k, k ^ bit) for k in range(lax.axis_size(axis...  38.6 us
    pallas_call x24, Pallas kernels, kernel(): pl.pallas_call(body, out_shape=outs if single else listed, in_specs=[smem...  36.9 us
    ppermute x7, waiting for transfers between devices, swap_core(): return lax.ppermute(value, 'core', [(0, 1), (1, 0)])  4.73 us
    dynamic_slice x2, local copies, waits for them, and re-layouts, columns(): mine = lax.dynamic_slice_in_dim(weight, z_index * live, live, 1)  3 us
  transfers between devices with their start and end apart: 44, of which 17 were waited for; matrix products, arithmetic and copies ran while one was open for 2% of the time, Pallas kernels for 18%

profile of v2, /device:TPU:0, one launch (start us, length us, event | category | flops | bytes accessed | tf_op | source)
XLA Modules:
  0.0 147.6 jit_solution(12834958785696048554)
XLA Ops:
  0.7 4.1 %collective-permute-start.1 = (bf16[128,768]{1,0:T(8,128)(2,1)}, bf16[128,768]{1,0:T(8,128)(2,1)S(1)}, u32[]{:S(2)}, u32[]{:S(2)}) collective-permute-start(bf16[128,768]{1,0:T(8,128)(2,1)} %bitcast.9), channel_id=1, source_target_pairs={{0,4},{2,6},{4,0},{6,2},{1,5},{3,7},{5,1},{7,3},{8,12},{10,14},{12... | collective-permute-start | bytes 589832 | tf_op jit(solution)/shard_map/gather_in/ppermute | solution.py:977
  4.8 1.6 %collective-permute-start = (bf16[128,768]{1,0:T(8,128)(2,1)}, bf16[128,768]{1,0:T(8,128)(2,1)S(1)}, u32[]{:S(2)}, u32[]{:S(2)}) collective-permute-start(bf16[128,768]{1,0:T(8,128)(2,1)} %bitcast.10), channel_id=1, source_target_pairs={{0,2},{2,0},{4,6},{6,4},{1,3},{3,1},{5,7},{7,5},{8,10},{10,8},{12,... | collective-permute-start | bytes 589832 | tf_op jit(solution)/shard_map/gather_in/ppermute | solution.py:977
  6.4 1.4 constant_dynamic-slice_fusion.2
  7.8 1.6 %constant_dynamic-slice_fusion = (bf16[768,192]{1,0:T(8,128)(2,1)S(1)}, bf16[768,192]{1,0:T(8,128)(2,1)S(1)}) fusion(bf16[768,768]{1,0:T(8,128)(2,1)} %refs_9_.3, s32[]{:T(128)S(6)} %select_n.2, bf16[768,768]{1,0:T(8,128)(2,1)} %refs_8_.3), kind=kLoop, calls=%fused_computation.10 | loop fusion | bytes 1179652 | tf_op jit(solution)/shard_map/dynamic_slice | solution.py:1019
  9.4 4.8 %collective-permute-done.1.refs_1_ = bf16[128,768]{1,0:T(8,128)(2,1)S(1)} collective-permute-done((bf16[128,768]{1,0:T(8,128)(2,1)}, bf16[128,768]{1,0:T(8,128)(2,1)S(1)}, u32[]{:S(2)}, u32[]{:S(2)}) %collective-permute-start.1) | collective-permute-done | bytes 196640 | tf_op jit(solution)/shard_map/gather_in/ppermute | solution.py:977
  17.6 2.7 %collective-permute-done.2.refs_0_ = bf16[128,768]{1,0:T(8,128)(2,1)S(1)} collective-permute-done((bf16[128,768]{1,0:T(8,128)(2,1)S(1)}, bf16[128,768]{1,0:T(8,128)(2,1)S(1)}, u32[]{:S(2)}, u32[]{:S(2)}) %collective-permute-start.2) | collective-permute-done | bytes 196640 | tf_op jit(solution)/shard_map/gather_in/ppermute | solution.py:977
  22.2 4.3 %attend.1 = (f32[4,128,256]{2,1,0:T(8,128)S(1)}, bf16[4,2,384,512]{3,2,1,0:T(8,128)(2,1)S(1)}, bf16[4,128,256]{2,1,0:T(8,128)(2,1)S(1)}, bf16[4,128,512]{2,1,0:T...) custom-call(s32[3]{0:T(128)S(1)} %pad_add_fusion.place_ref, ...), custom_call_target="tpu_custom_call" | custom-call | flops 6000000 | bytes 6000 | tf_op jit(solution)/shard_map/attend/pallas_call | solution.py:350
  26.5 2.3 %collective-permute-start.11 = (bf16[128,768]{1,0:T(8,128)(2,1)S(1)}, bf16[128,768]{1,0:T(8,128)(2,1)S(1)}, u32[]{:S(2)}, u32[]{:S(2)}) collective-permute-start(bf16[128,768]{1,0:T(8,128)(2,1)S(1)} %mask_grad.1.go_ref.refs_4_), channel_id=1, source_target_pairs={{0,24},{8,16},{16,8},{24,0},{1,25},{9,17},{17,9},{25,1},{2,26},{10... | collective-permute-start | bytes 589832 | tf_op jit(solution)/shard_map/plane_out/ppermute | solution.py:977
  30.0 1.5 %collective-permute-start.6 = (bf16[192,128]{1,0:T(8,128)(2,1)S(1)}, bf16[192,128]{1,0:T(8,128)(2,1)S(1)}, u32[]{:S(2)}, u32[]{:S(2)}) collective-permute-start(bf16[192,128]{1,0:T(8,128)(2,1)S(1)} %get-tuple-element.161), channel_id=1, source_target_pairs={{0,2},{2,0},{4,6},{6,4},{1,3},{3,1},{5,7},{7,5},{8,10},{10,8},{12,... | collective-permute-start | bytes 147464 | tf_op jit(solution)/shard_map/chip_attn/ppermute | solution.py:977
  31.6 3.3 %collective-permute-start.7 = (bf16[192,128]{1,0:T(8,128)(2,1)S(1)}, bf16[192,128]{1,0:T(8,128)(2,1)S(1)}, u32[]{:S(2)}, u32[]{:S(2)}) collective-permute-start(bf16[192,128]{1,0:T(8,128)(2,1)S(1)} %get-tuple-element.162), channel_id=1, source_target_pairs={{0,4},{2,6},{4,0},{6,2},{1,5},{3,7},{5,1},{7,3},{8,12},{10,14},{12... | collective-permute-start | bytes 147464 | tf_op jit(solution)/shard_map/chip_attn/ppermute | solution.py:977
  34.9 3.5 %collective-permute-start.8 = (bf16[192,128]{1,0:T(8,128)(2,1)S(1)}, bf16[192,128]{1,0:T(8,128)(2,1)S(1)}, u32[]{:S(2)}, u32[]{:S(2)}) collective-permute-start(bf16[192,128]{1,0:T(8,128)(2,1)S(1)} %get-tuple-element.163), channel_id=1, source_target_pairs={{0,6},{2,4},{4,2},{6,0},{1,7},{3,5},{5,3},{7,1},{8,14},{10,12},{12... | collective-permute-start | bytes 147464 | tf_op jit(solution)/shard_map/chip_attn/ppermute | solution.py:977
  38.4 2.4 %collective-permute-done.8.refs_3_ = bf16[192,128]{1,0:T(8,128)(2,1)S(1)} collective-permute-done((bf16[192,128]{1,0:T(8,128)(2,1)S(1)}, bf16[192,128]{1,0:T(8,128)(2,1)S(1)}, u32[]{:S(2)}, u32[]{:S(2)}) %collective-permute-start.8) | collective-permute-done | bytes 49184 | tf_op jit(solution)/shard_map/chip_attn/ppermute | solution.py:977
  40.8 1.4 norms.1
  42.2 1.6 %collective-permute-start.15 = (bf16[128,1024]{1,0:T(8,128)(2,1)S(1)}, bf16[128,1024]{1,0:T(8,128)(2,1)S(1)}, u32[]{:S(2)}, u32[]{:S(2)}) collective-permute-start(bf16[128,1024]{1,0:T(8,128)(2,1)S(1)} %get-tuple-element.187), channel_id=1, source_target_pairs={{0,8},{8,0},{16,24},{24,16},{1,9},{9,1},{17,25},{25,17},{2,10},{10... | collective-permute-start | bytes 786440 | tf_op jit(solution)/shard_map/plane_norms/ppermute | solution.py:977
  43.8 1.9 %up_gelu.1 = (bf16[4,128,768]{2,1,0:T(8,128)(2,1)S(1)}, bf16[4,128,768]{2,1,0:T(8,128)(2,1)S(1)}, bf16[128,768]{1,0:T(8,128)(2,1)S(1)}, bf16[128,768]{1,0:T(8,12...) custom-call(s32[3]{0:T(128)S(1)} %pad_add_fusion.place_ref, ...), custom_call_target="tpu_custom_call" | custom-call | flops 2000000 | bytes 2000 | tf_op jit(solution)/shard_map/up_gelu/pallas_call | solution.py:350
  46.1 5.5 %token_backward.1 = (bf16[128,768]{1,0:T(8,128)(2,1)}, f32[128,768]{1,0:T(8,128)S(1)}, bf16[144,1536]{1,0:T(8,128)(2,1)S(1)}, bf16[144,1536]{1,0:T(8,128)(2,1)S(...) custom-call(s32[3]{0:T(128)S(1)} %pad_add_fusion.place_ref, ...), custom_call_target="tpu_custom_call" | custom-call | flops 9000000 | bytes 9000 | tf_op jit(solution)/shard_map/token_backward/pallas_call | solution.py:350
  51.6 1.6 %collective-permute-start.16 = (bf16[128,1024]{1,0:T(8,128)(2,1)S(1)}, bf16[128,1024]{1,0:T(8,128)(2,1)S(1)}, u32[]{:S(2)}, u32[]{:S(2)}) collective-permute-start(bf16[128,1024]{1,0:T(8,128)(2,1)S(1)} %get-tuple-element.188), channel_id=1, source_target_pairs={{0,16},{8,24},{16,0},{24,8},{1,17},{9,25},{17,1},{25,9},{2,18},{10... | collective-permute-start | bytes 786440 | tf_op jit(solution)/shard_map/plane_norms/ppermute | solution.py:977
  53.7 4.0 %collective-permute-start.13 = (bf16[192,128]{1,0:T(8,128)(2,1)S(1)}, bf16[192,128]{1,0:T(8,128)(2,1)S(1)}, u32[]{:S(2)}, u32[]{:S(2)}) collective-permute-start(bf16[192,128]{1,0:T(8,128)(2,1)S(1)} %get-tuple-element.185), channel_id=1, source_target_pairs={{0,4},{2,6},{4,0},{6,2},{1,5},{3,7},{5,1},{7,3},{8,12},{10,14},{12... | collective-permute-start | bytes 147464 | tf_op jit(solution)/shard_map/chip_grad/ppermute | solution.py:977
  57.7 1.8 %collective-permute-start.14 = (bf16[192,128]{1,0:T(8,128)(2,1)S(1)}, bf16[192,128]{1,0:T(8,128)(2,1)S(1)}, u32[]{:S(2)}, u32[]{:S(2)}) collective-permute-start(bf16[192,128]{1,0:T(8,128)(2,1)S(1)} %get-tuple-element.186), channel_id=1, source_target_pairs={{0,6},{2,4},{4,2},{6,0},{1,7},{3,5},{5,3},{7,1},{8,14},{10,12},{12... | collective-permute-start | bytes 147464 | tf_op jit(solution)/shard_map/chip_grad/ppermute | solution.py:977
  59.5 1.3 collective-permute-done.13.refs_2_
  60.8 1.5 %collective-permute-start.18 = (bf16[128,768]{1,0:T(8,128)(2,1)S(1)}, bf16[128,768]{1,0:T(8,128)(2,1)S(1)}, u32[]{:S(2)}, u32[]{:S(2)}) collective-permute-start(bf16[128,768]{1,0:T(8,128)(2,1)S(1)} %get-tuple-element.198), channel_id=1, source_target_pairs={{0,8},{8,0},{16,24},{24,16},{1,9},{9,1},{17,25},{25,17},{2,10},{10... | collective-permute-start | bytes 589832 | tf_op jit(solution)/shard_map/plane_act/ppermute | solution.py:977
  63.6 1.5 %collective-permute-start.19 = (bf16[128,768]{1,0:T(8,128)(2,1)S(1)}, bf16[128,768]{1,0:T(8,128)(2,1)S(1)}, u32[]{:S(2)}, u32[]{:S(2)}) collective-permute-start(bf16[128,768]{1,0:T(8,128)(2,1)S(1)} %get-tuple-element.199), channel_id=1, source_target_pairs={{0,16},{8,24},{16,0},{24,8},{1,17},{9,25},{17,1},{25,9},{2,18},{10... | collective-permute-start | bytes 589832 | tf_op jit(solution)/shard_map/plane_act/ppermute | solution.py:977
  65.1 1.4 collective-permute-start.20
  66.6 3.8 %attend_back.1 = (bf16[4,128,256]{2,1,0:T(8,128)(2,1)S(1)}, f32[4,128,512]{2,1,0:T(8,128)S(1)}, bf16[4,128,512]{2,1,0:T(8,128)(2,1)S(1)}) custom-call(s32[3]{0:T(128)S(1)} %pad_add_fusion.place_ref, bf16[4,128,256]{2,1,0:T(8,128)(2,1)S(1)} %get-tuple-element.178.q_ref, bf16[4,128,512]{2,1,0:T(8,128)(2,1)S(1)} %get-tuple-element.179.own_ref, ...), custom_call_target="tpu_custom_call" | custom-call | flops 6000000 | bytes 6000 | tf_op jit(solution)/shard_map/attend_back/pallas_call | solution.py:350
  70.4 2.3 %collective-permute-done.19.refs_2_ = bf16[128,768]{1,0:T(8,128)(2,1)S(1)} collective-permute-done((bf16[128,768]{1,0:T(8,128)(2,1)S(1)}, bf16[128,768]{1,0:T(8,128)(2,1)S(1)}, u32[]{:S(2)}, u32[]{:S(2)}) %collective-permute-start.19) | collective-permute-done | bytes 196640 | tf_op jit(solution)/shard_map/plane_act/ppermute | solution.py:977
  72.7 1.5 %grad_down.1 = (f32[4,96,768]{2,1,0:T(8,128)S(1)}, bf16[4,96,768]{2,1,0:T(8,128)(2,1)S(1)}) custom-call(s32[3]{0:T(128)S(1)} %pad_add_fusion.place_ref, bf16[128,768]{1,0:T(8,128)(2,1)S(1)} %get-tuple-element.206.refs_0_, bf16[128,768]{1,0:T(8,128)(2,1)S(1)} %collective-permute-done.18.refs_1_, bf16[128,768]{1,0:T(8,128)(2,1)S(1)} %collective-permute-done.19.refs_2_, ...), custom_call_target="tpu_custom_call" | custom-call | flops 3000000 | bytes 3000 | tf_op jit(solution)/shard_map/grad_down/pallas_call | solution.py:350
  74.8 2.2 %collective-permute-done.21.in_ref = bf16[4,128,512]{2,1,0:T(8,128)(2,1)S(1)} collective-permute-done((bf16[4,128,512]{2,1,0:T(8,128)(2,1)S(1)}, bf16[4,128,512]{2,1,0:T(8,128)(2,1)S(1)}, u32[]{:S(2)}, u32[]{:S(2)}) %collective-permute-start.21) | collective-permute-done | bytes 524320 | tf_op jit(solution)/shard_map/core_grad/ppermute | solution.py:973
  79.6 2.4 %collective-permute-start.28 = (bf16[144,1536]{1,0:T(8,128)(2,1)S(1)}, bf16[144,1536]{1,0:T(8,128)(2,1)S(1)}, u32[]{:S(2)}, u32[]{:S(2)}) collective-permute-start(bf16[144,1536]{1,0:T(8,128)(2,1)S(1)} %get-tuple-element.231), channel_id=1, source_target_pairs={{0,16},{8,24},{16,0},{24,8},{1,17},{9,25},{17,1},{25,9},{2,18},{10... | collective-permute-start | bytes 1327112 | tf_op jit(solution)/shard_map/plane_back/ppermute | solution.py:977
  82.8 3.2 %collective-permute-start.25 = (bf16[576,128]{1,0:T(8,128)(2,1)S(1)}, bf16[576,128]{1,0:T(8,128)(2,1)S(1)}, u32[]{:S(2)}, u32[]{:S(2)}) collective-permute-start(bf16[576,128]{1,0:T(8,128)(2,1)S(1)} %get-tuple-element.227), channel_id=1, source_target_pairs={{0,4},{2,6},{4,0},{6,2},{1,5},{3,7},{5,1},{7,3},{8,12},{10,14},{12... | collective-permute-start | bytes 442376 | tf_op jit(solution)/shard_map/chip_qkv/ppermute | solution.py:977
  85.9 1.7 %collective-permute-start.23 = (bf16[2,96,768]{2,1,0:T(8,128)(2,1)S(1)}, bf16[2,96,768]{2,1,0:T(8,128)(2,1)S(1)}, u32[]{:S(2)}, u32[]{:S(2)}) collective-permute-start(bf16[2,96,768]{2,1,0:T(8,128)(2,1)S(1)} %get-tuple-element.224), channel_id=1, source_target_pairs={{0,2},{2,0},{4,6},{6,4},{1,3},{3,1},{5,7},{7,5},{8,10},{10,8},{12,... | collective-permute-start | bytes 884744 | tf_op jit(solution)/shard_map/down_one/ppermute | solution.py:977
  87.6 5.0 %collective-permute-done.25.refs_2_ = bf16[576,128]{1,0:T(8,128)(2,1)S(1)} collective-permute-done((bf16[576,128]{1,0:T(8,128)(2,1)S(1)}, bf16[576,128]{1,0:T(8,128)(2,1)S(1)}, u32[]{:S(2)}, u32[]{:S(2)}) %collective-permute-start.25) | collective-permute-done | bytes 147488 | tf_op jit(solution)/shard_map/chip_qkv/ppermute | solution.py:977
  92.6 3.5 %collective-permute-start.26 = (bf16[576,128]{1,0:T(8,128)(2,1)S(1)}, bf16[576,128]{1,0:T(8,128)(2,1)S(1)}, u32[]{:S(2)}, u32[]{:S(2)}) collective-permute-start(bf16[576,128]{1,0:T(8,128)(2,1)S(1)} %get-tuple-element.228), channel_id=1, source_target_pairs={{0,6},{2,4},{4,2},{6,0},{1,7},{3,5},{5,3},{7,1},{8,14},{10,12},{12... | collective-permute-start | bytes 442376 | tf_op jit(solution)/shard_map/chip_qkv/ppermute | solution.py:977
  96.1 2.5 %grad_qkv.1 = (f32[4,96,768]{2,1,0:T(8,128)S(1)}, bf16[4,96,768]{2,1,0:T(8,128)(2,1)S(1)}) custom-call(s32[3]{0:T(128)S(1)} %pad_add_fusion.place_ref, bf16[1,128,768]{2,1,0:T(8,128)(2,1)S(1)} %get-tuple-element.175.refs_0_, bf16[2,128,768]{2,1,0:T(8,128)(2,1)S(1)} %get-tuple-element.176.refs_1_, bf16[1,128,768]{2,1,0:T(8,128)(2,1)S(1)} %get-tuple-element.177.refs_2_, ...), custom_call_target="tpu_custom_call" | custom-call | flops 4000000 | bytes 4000 | tf_op jit(solution)/shard_map/grad_qkv/pallas_call | solution.py:350
  98.6 1.6 %collective-permute-done.26.refs_3_ = bf16[576,128]{1,0:T(8,128)(2,1)S(1)} collective-permute-done((bf16[576,128]{1,0:T(8,128)(2,1)S(1)}, bf16[576,128]{1,0:T(8,128)(2,1)S(1)}, u32[]{:S(2)}, u32[]{:S(2)}) %collective-permute-start.26) | collective-permute-done | bytes 147488 | tf_op jit(solution)/shard_map/chip_qkv/ppermute | solution.py:977
  100.6 1.5 %collective-permute-done.29.refs_7_ = bf16[144,1536]{1,0:T(8,128)(2,1)S(1)} collective-permute-done((bf16[144,1536]{1,0:T(8,128)(2,1)S(1)}, bf16[144,1536]{1,0:T(8,128)(2,1)S(1)}, u32[]{:S(2)}, u32[]{:S(2)}) %collective-permute-start.29) | collective-permute-done | bytes 442400 | tf_op jit(solution)/shard_map/plane_back/ppermute | solution.py:977
  102.1 1.7 %grad_up_out.1 = (f32[4,128,768]{2,1,0:T(8,128)S(1)}, bf16[4,128,768]{2,1,0:T(8,128)(2,1)S(1)}) custom-call(s32[3]{0:T(128)S(1)} %pad_add_fusion.place_ref, bf16[128,1024]{1,0:T(8,128)(2,1)S(1)} %get-tuple-element.253.n3_ref.refs_0_, bf16[128,1024]{1,0:T(8,128)(2,1)S(1)} %collective-permute-done.15.refs_1_, ...), custom_call_target="tpu_custom_call" | custom-call | flops 4000000 | bytes 4000 | tf_op jit(solution)/shard_map/grad_up_out/pallas_call | solution.py:350
  104.4 1.8 %collective-permute-done.37.in_ref = bf16[4,128,768]{2,1,0:T(8,128)(2,1)S(1)} collective-permute-done((bf16[4,128,768]{2,1,0:T(8,128)(2,1)S(1)}, bf16[4,128,768]{2,1,0:T(8,128)(2,1)S(1)}, u32[]{:S(2)}, u32[]{:S(2)}) %collective-permute-start.37) | collective-permute-done | bytes 786464 | tf_op jit(solution)/shard_map/core_up/ppermute | solution.py:973
  107.3 10.8 %collective-permute-done.38.in_ref = bf16[2,128,768]{2,1,0:T(8,128)(2,1)S(1)} collective-permute-done((bf16[2,128,768]{2,1,0:T(8,128)(2,1)S(1)}, bf16[2,128,768]{2,1,0:T(8,128)(2,1)S(1)}, u32[]{:S(2)}, u32[]{:S(2)}) %collective-permute-start.38) | collective-permute-done | bytes 393248 | tf_op jit(solution)/shard_map/up_sum/ppermute | solution.py:977
  118.7 3.5 %collective-permute-start.39 = (bf16[1,128,768]{2,1,0:T(8,128)(2,1)S(1)}, bf16[1,128,768]{2,1,0:T(8,128)(2,1)S(1)}, u32[]{:S(2)}, u32[]{:S(2)}) collective-permute-start(bf16[1,128,768]{2,1,0:T(8,128)(2,1)S(1)} %get-tuple-element.266), channel_id=1, source_target_pairs={{0,4},{2,6},{4,0},{6,2},{1,5},{3,7},{5,1},{7,3},{8,12},{10,14},{12... | collective-permute-start | bytes 589832 | tf_op jit(solution)/shard_map/up_sum/ppermute | solution.py:977
  123.4 1.5 collective-permute-start.32
  124.9 1.7 %collective-permute-start.33 = (bf16[96,768]{1,0:T(8,128)(2,1)S(1)}, bf16[96,768]{1,0:T(8,128)(2,1)S(1)}, u32[]{:S(2)}, u32[]{:S(2)}) collective-permute-start(bf16[96,768]{1,0:T(8,128)(2,1)S(1)} %get-tuple-element.243), channel_id=1, source_target_pairs={{0,24},{8,16},{16,8},{24,0},{1,25},{9,17},{17,9},{25,1},{2,26},{10... | collective-permute-start | bytes 442376 | tf_op jit(solution)/shard_map/plane_w/ppermute | solution.py:977
  127.3 2.1 %collective-permute-done.31.refs_1_ = bf16[96,768]{1,0:T(8,128)(2,1)S(1)} collective-permute-done((bf16[96,768]{1,0:T(8,128)(2,1)S(1)}, bf16[96,768]{1,0:T(8,128)(2,1)S(1)}, u32[]{:S(2)}, u32[]{:S(2)}) %collective-permute-start.31) | collective-permute-done | bytes 147488 | tf_op jit(solution)/shard_map/plane_w/ppermute | solution.py:977
  129.4 2.2 %collective-permute-done.32.refs_2_ = bf16[96,768]{1,0:T(8,128)(2,1)S(1)} collective-permute-done((bf16[96,768]{1,0:T(8,128)(2,1)S(1)}, bf16[96,768]{1,0:T(8,128)(2,1)S(1)}, u32[]{:S(2)}, u32[]{:S(2)}) %collective-permute-start.32) | collective-permute-done | bytes 147488 | tf_op jit(solution)/shard_map/plane_w/ppermute | solution.py:977
  132.3 1.7 %collective-permute-start.34 = (bf16[24,768]{1,0:T(8,128)(2,1)S(1)}, bf16[24,768]{1,0:T(8,128)(2,1)S(1)}, u32[]{:S(2)}, u32[]{:S(2)}) collective-permute-start(bf16[24,768]{1,0:T(8,128)(2,1)S(1)} %get-tuple-element.245), channel_id=1, source_target_pairs={{0,2},{2,0},{4,6},{6,4},{1,3},{3,1},{5,7},{7,5},{8,10},{10,8},{12,... | collective-permute-start | bytes 110600 | tf_op jit(solution)/shard_map/chip_w/ppermute | solution.py:977
  134.1 2.6 %collective-permute-start.36 = (bf16[24,768]{1,0:T(8,128)(2,1)S(1)}, bf16[24,768]{1,0:T(8,128)(2,1)S(1)}, u32[]{:S(2)}, u32[]{:S(2)}) collective-permute-start(bf16[24,768]{1,0:T(8,128)(2,1)S(1)} %get-tuple-element.247), channel_id=1, source_target_pairs={{0,6},{2,4},{4,2},{6,0},{1,7},{3,5},{5,3},{7,1},{8,14},{10,12},{12... | collective-permute-start | bytes 110600 | tf_op jit(solution)/shard_map/chip_w/ppermute | solution.py:977
  141.5 2.7 %grad_inputs.1 = bf16[128,768]{1,0:T(8,128)(2,1)} custom-call(s32[3]{0:T(128)S(1)} %pad_add_fusion.place_ref, bf16[576,128]{1,0:T(8,128)(2,1)S(1)} %get-tuple-element.233.refs_0_, bf16[576,128]{1,0:T(8,128)(2,1)S(1)} %collective-permute-done.24.refs_1_, bf16[576,128]{1,0:T(8,128)(2,1)S(1)} %collective-permute-done.25.refs_2_, ...), custom_call_target="tpu_custom_call" | custom-call | flops 3000000 | bytes 3000 | tf_op jit(solution)/shard_map/grad_inputs/pallas_call | solution.py:350
  145.0 1.3 finish_qkv.1
  146.3 1.3 place_up.1
  (101 shorter events, 23.4 us)
Async XLA Ops:
  0.7 13.5 %collective-permute-start.1 = (bf16[128,768]{1,0:T(8,128)(2,1)}, bf16[128,768]{1,0:T(8,128)(2,1)S(1)}, u32[]{:S(2)}, u32[]{:S(2)}) collective-permute-start(bf16[128,768]{1,0:T(8,128)(2,1)} %bitcast.9), channel_id=1, source_target_pairs={{0,4},{2,6},{4,0},{6,2},{1,5},{3,7},{5,1},{7,3},{8,12},{10,14},{12... | collective-permute-start | bytes 589832 | tf_op jit(solution)/shard_map/gather_in/ppermute | solution.py:977
  4.8 10.4 %collective-permute-start = (bf16[128,768]{1,0:T(8,128)(2,1)}, bf16[128,768]{1,0:T(8,128)(2,1)S(1)}, u32[]{:S(2)}, u32[]{:S(2)}) collective-permute-start(bf16[128,768]{1,0:T(8,128)(2,1)} %bitcast.10), channel_id=1, source_target_pairs={{0,2},{2,0},{4,6},{6,4},{1,3},{3,1},{5,7},{7,5},{8,10},{10,8},{12,... | collective-permute-start | bytes 589832 | tf_op jit(solution)/shard_map/gather_in/ppermute | solution.py:977
  6.4 37.4 %slice-start = ((s8[4718592]{0:T(1024)(128)(4,1)}), s8[4194304]{0:T(1024)(128)(4,1)S(1)}, s32[]{:S(2)}) async-start(s8[4718592]{0:T(1024)(128)(4,1)} %bitcast.7), calls=%async_computation | async-start | bytes 8388608
  14.2 6.0 %collective-permute-start.2 = (bf16[128,768]{1,0:T(8,128)(2,1)S(1)}, bf16[128,768]{1,0:T(8,128)(2,1)S(1)}, u32[]{:S(2)}, u32[]{:S(2)}) collective-permute-start(bf16[128,768]{1,0:T(8,128)(2,1)S(1)} %collective-permute-done.1.refs_1_), channel_id=1, source_target_pairs={{0,2},{2,0},{4,6},{6,4},{1,3},{3,1},{5,7},{7,5},{8,10},{10,8},{12,... | collective-permute-start | bytes 589832 | tf_op jit(solution)/shard_map/gather_in/ppermute | solution.py:977
  15.1 28.7 %slice-start.1 = ((s8[4718592]{0:T(1024)(128)(4,1)}), s8[524288]{0:T(1024)(128)(4,1)S(1)}, s32[]{:S(2)}) async-start(s8[4718592]{0:T(1024)(128)(4,1)} %bitcast.7), calls=%async_computation.1 | async-start | bytes 1048576
  16.4 5.1 %collective-permute-start.4 = (bf16[2,128,512]{2,1,0:T(8,128)(2,1)S(1)}, bf16[2,128,512]{2,1,0:T(8,128)(2,1)S(1)}, u32[]{:S(2)}, u32[]{:S(2)}) collective-permute-start(bf16[2,128,512]{2,1,0:T(8,128)(2,1)S(1)} %get-tuple-element.153.refs_4_), channel_id=1, source_target_pairs={{0,1},{1,0},{2,3},{3,2},{4,5},{5,4},{6,7},{7,6},{8,9},{9,8},{10,11... | collective-permute-start | bytes 786440 | tf_op jit(solution)/shard_map/core_kv/ppermute | solution.py:973
  17.0 4.5 %collective-permute-start.3 = (bf16[1,128,512]{2,1,0:T(8,128)(2,1)S(1)}, bf16[1,128,512]{2,1,0:T(8,128)(2,1)S(1)}, u32[]{:S(2)}, u32[]{:S(2)}) collective-permute-start(bf16[1,128,512]{2,1,0:T(8,128)(2,1)S(1)} %get-tuple-element.152.refs_3_), channel_id=1, source_target_pairs={{0,1},{1,0},{2,3},{3,2},{4,5},{5,4},{6,7},{7,6},{8,9},{9,8},{10,11... | collective-permute-start | bytes 393224 | tf_op jit(solution)/shard_map/core_kv/ppermute | solution.py:973
  20.7 20.0 %copy-start = (bf16[768,768]{1,0:T(8,128)(2,1)S(1)}, bf16[768,768]{1,0:T(8,128)(2,1)}, u32[]{:S(2)}) copy-start(bf16[768,768]{1,0:T(8,128)(2,1)} %wo_ref.1) | copy-start | bytes 3538948
  20.7 20.0 %copy-start.9 = (f32[768]{0:T(1024)S(1)}, f32[768]{0:T(1024)}, u32[]{:S(2)}) copy-start(f32[768]{0:T(1024)} %g2.1) | copy-start | bytes 9220
  20.8 1.4 collective-permute-start.5
  26.5 14.3 %collective-permute-start.11 = (bf16[128,768]{1,0:T(8,128)(2,1)S(1)}, bf16[128,768]{1,0:T(8,128)(2,1)S(1)}, u32[]{:S(2)}, u32[]{:S(2)}) collective-permute-start(bf16[128,768]{1,0:T(8,128)(2,1)S(1)} %mask_grad.1.go_ref.refs_4_), channel_id=1, source_target_pairs={{0,24},{8,16},{16,8},{24,0},{1,25},{9,17},{17,9},{25,1},{2,26},{10... | collective-permute-start | bytes 589832 | tf_op jit(solution)/shard_map/plane_out/ppermute | solution.py:977
  28.8 12.0 %collective-permute-start.10 = (bf16[128,768]{1,0:T(8,128)(2,1)S(1)}, bf16[128,768]{1,0:T(8,128)(2,1)S(1)}, u32[]{:S(2)}, u32[]{:S(2)}) collective-permute-start(bf16[128,768]{1,0:T(8,128)(2,1)S(1)} %mask_grad.1.go_ref.refs_4_), channel_id=1, source_target_pairs={{0,16},{8,24},{16,0},{24,8},{1,17},{9,25},{17,1},{25,9},{2,18},{10... | collective-permute-start | bytes 589832 | tf_op jit(solution)/shard_map/plane_out/ppermute | solution.py:977
  29.3 11.5 %collective-permute-start.9 = (bf16[128,768]{1,0:T(8,128)(2,1)S(1)}, bf16[128,768]{1,0:T(8,128)(2,1)S(1)}, u32[]{:S(2)}, u32[]{:S(2)}) collective-permute-start(bf16[128,768]{1,0:T(8,128)(2,1)S(1)} %mask_grad.1.go_ref.refs_4_), channel_id=1, source_target_pairs={{0,8},{8,0},{16,24},{24,16},{1,9},{9,1},{17,25},{25,17},{2,10},{10... | collective-permute-start | bytes 589832 | tf_op jit(solution)/shard_map/plane_out/ppermute | solution.py:977
  30.0 4.8 %collective-permute-start.6 = (bf16[192,128]{1,0:T(8,128)(2,1)S(1)}, bf16[192,128]{1,0:T(8,128)(2,1)S(1)}, u32[]{:S(2)}, u32[]{:S(2)}) collective-permute-start(bf16[192,128]{1,0:T(8,128)(2,1)S(1)} %get-tuple-element.161), channel_id=1, source_target_pairs={{0,2},{2,0},{4,6},{6,4},{1,3},{3,1},{5,7},{7,5},{8,10},{10,8},{12,... | collective-permute-start | bytes 147464 | tf_op jit(solution)/shard_map/chip_attn/ppermute | solution.py:977
  31.6 6.8 %collective-permute-start.7 = (bf16[192,128]{1,0:T(8,128)(2,1)S(1)}, bf16[192,128]{1,0:T(8,128)(2,1)S(1)}, u32[]{:S(2)}, u32[]{:S(2)}) collective-permute-start(bf16[192,128]{1,0:T(8,128)(2,1)S(1)} %get-tuple-element.162), channel_id=1, source_target_pairs={{0,4},{2,6},{4,0},{6,2},{1,5},{3,7},{5,1},{7,3},{8,12},{10,14},{12... | collective-permute-start | bytes 147464 | tf_op jit(solution)/shard_map/chip_attn/ppermute | solution.py:977
  34.9 5.9 %collective-permute-start.8 = (bf16[192,128]{1,0:T(8,128)(2,1)S(1)}, bf16[192,128]{1,0:T(8,128)(2,1)S(1)}, u32[]{:S(2)}, u32[]{:S(2)}) collective-permute-start(bf16[192,128]{1,0:T(8,128)(2,1)S(1)} %get-tuple-element.163), channel_id=1, source_target_pairs={{0,6},{2,4},{4,2},{6,0},{1,7},{3,5},{5,3},{7,1},{8,14},{10,12},{12... | collective-permute-start | bytes 147464 | tf_op jit(solution)/shard_map/chip_attn/ppermute | solution.py:977
  42.2 22.9 %collective-permute-start.15 = (bf16[128,1024]{1,0:T(8,128)(2,1)S(1)}, bf16[128,1024]{1,0:T(8,128)(2,1)S(1)}, u32[]{:S(2)}, u32[]{:S(2)}) collective-permute-start(bf16[128,1024]{1,0:T(8,128)(2,1)S(1)} %get-tuple-element.187), channel_id=1, source_target_pairs={{0,8},{8,0},{16,24},{24,16},{1,9},{9,1},{17,25},{25,17},{2,10},{10... | collective-permute-start | bytes 786440 | tf_op jit(solution)/shard_map/plane_norms/ppermute | solution.py:977
  51.6 6.1 %collective-permute-start.12 = (bf16[192,128]{1,0:T(8,128)(2,1)S(1)}, bf16[192,128]{1,0:T(8,128)(2,1)S(1)}, u32[]{:S(2)}, u32[]{:S(2)}) collective-permute-start(bf16[192,128]{1,0:T(8,128)(2,1)S(1)} %get-tuple-element.184), channel_id=1, source_target_pairs={{0,2},{2,0},{4,6},{6,4},{1,3},{3,1},{5,7},{7,5},{8,10},{10,8},{12,... | collective-permute-start | bytes 147464 | tf_op jit(solution)/shard_map/chip_grad/ppermute | solution.py:977
  51.6 14.9 %collective-permute-start.16 = (bf16[128,1024]{1,0:T(8,128)(2,1)S(1)}, bf16[128,1024]{1,0:T(8,128)(2,1)S(1)}, u32[]{:S(2)}, u32[]{:S(2)}) collective-permute-start(bf16[128,1024]{1,0:T(8,128)(2,1)S(1)} %get-tuple-element.188), channel_id=1, source_target_pairs={{0,16},{8,24},{16,0},{24,8},{1,17},{9,25},{17,1},{25,9},{2,18},{10... | collective-permute-start | bytes 786440 | tf_op jit(solution)/shard_map/plane_norms/ppermute | solution.py:977
  53.2 13.4 %collective-permute-start.17 = (bf16[128,1024]{1,0:T(8,128)(2,1)S(1)}, bf16[128,1024]{1,0:T(8,128)(2,1)S(1)}, u32[]{:S(2)}, u32[]{:S(2)}) collective-permute-start(bf16[128,1024]{1,0:T(8,128)(2,1)S(1)} %get-tuple-element.189), channel_id=1, source_target_pairs={{0,24},{8,16},{16,8},{24,0},{1,25},{9,17},{17,9},{25,1},{2,26},{10... | collective-permute-start | bytes 786440 | tf_op jit(solution)/shard_map/plane_norms/ppermute | solution.py:977
  53.7 7.2 %collective-permute-start.13 = (bf16[192,128]{1,0:T(8,128)(2,1)S(1)}, bf16[192,128]{1,0:T(8,128)(2,1)S(1)}, u32[]{:S(2)}, u32[]{:S(2)}) collective-permute-start(bf16[192,128]{1,0:T(8,128)(2,1)S(1)} %get-tuple-element.185), channel_id=1, source_target_pairs={{0,4},{2,6},{4,0},{6,2},{1,5},{3,7},{5,1},{7,3},{8,12},{10,14},{12... | collective-permute-start | bytes 147464 | tf_op jit(solution)/shard_map/chip_grad/ppermute | solution.py:977
  57.7 5.9 %collective-permute-start.14 = (bf16[192,128]{1,0:T(8,128)(2,1)S(1)}, bf16[192,128]{1,0:T(8,128)(2,1)S(1)}, u32[]{:S(2)}, u32[]{:S(2)}) collective-permute-start(bf16[192,128]{1,0:T(8,128)(2,1)S(1)} %get-tuple-element.186), channel_id=1, source_target_pairs={{0,6},{2,4},{4,2},{6,0},{1,7},{3,5},{5,3},{7,1},{8,14},{10,12},{12... | collective-permute-start | bytes 147464 | tf_op jit(solution)/shard_map/chip_grad/ppermute | solution.py:977
  60.8 9.6 %collective-permute-start.18 = (bf16[128,768]{1,0:T(8,128)(2,1)S(1)}, bf16[128,768]{1,0:T(8,128)(2,1)S(1)}, u32[]{:S(2)}, u32[]{:S(2)}) collective-permute-start(bf16[128,768]{1,0:T(8,128)(2,1)S(1)} %get-tuple-element.198), channel_id=1, source_target_pairs={{0,8},{8,0},{16,24},{24,16},{1,9},{9,1},{17,25},{25,17},{2,10},{10... | collective-permute-start | bytes 589832 | tf_op jit(solution)/shard_map/plane_act/ppermute | solution.py:977
  63.6 9.1 %collective-permute-start.19 = (bf16[128,768]{1,0:T(8,128)(2,1)S(1)}, bf16[128,768]{1,0:T(8,128)(2,1)S(1)}, u32[]{:S(2)}, u32[]{:S(2)}) collective-permute-start(bf16[128,768]{1,0:T(8,128)(2,1)S(1)} %get-tuple-element.199), channel_id=1, source_target_pairs={{0,16},{8,24},{16,0},{24,8},{1,17},{9,25},{17,1},{25,9},{2,18},{10... | collective-permute-start | bytes 589832 | tf_op jit(solution)/shard_map/plane_act/ppermute | solution.py:977
  65.1 7.6 %collective-permute-start.20 = (bf16[128,768]{1,0:T(8,128)(2,1)S(1)}, bf16[128,768]{1,0:T(8,128)(2,1)S(1)}, u32[]{:S(2)}, u32[]{:S(2)}) collective-permute-start(bf16[128,768]{1,0:T(8,128)(2,1)S(1)} %get-tuple-element.200), channel_id=1, source_target_pairs={{0,24},{8,16},{16,8},{24,0},{1,25},{9,17},{17,9},{25,1},{2,26},{10... | collective-permute-start | bytes 589832 | tf_op jit(solution)/shard_map/plane_act/ppermute | solution.py:977
  74.2 3.6 %collective-permute-start.22 = (bf16[4,96,768]{2,1,0:T(8,128)(2,1)S(1)}, bf16[4,96,768]{2,1,0:T(8,128)(2,1)S(1)}, u32[]{:S(2)}, u32[]{:S(2)}) collective-permute-start(bf16[4,96,768]{2,1,0:T(8,128)(2,1)S(1)} %get-tuple-element.215), channel_id=1, source_target_pairs={{0,1},{1,0},{2,3},{3,2},{4,5},{5,4},{6,7},{7,6},{8,9},{9,8},{10,11... | collective-permute-start | bytes 1769480 | tf_op jit(solution)/shard_map/core_down/ppermute | solution.py:973
  74.3 2.7 %collective-permute-start.21 = (bf16[4,128,512]{2,1,0:T(8,128)(2,1)S(1)}, bf16[4,128,512]{2,1,0:T(8,128)(2,1)S(1)}, u32[]{:S(2)}, u32[]{:S(2)}) collective-permute-start(bf16[4,128,512]{2,1,0:T(8,128)(2,1)S(1)} %get-tuple-element.201), channel_id=1, source_target_pairs={{0,1},{1,0},{2,3},{3,2},{4,5},{5,4},{6,7},{7,6},{8,9},{9,8},{10,11... | collective-permute-start | bytes 1572872 | tf_op jit(solution)/shard_map/core_grad/ppermute | solution.py:973
  78.5 7.4 %collective-permute-start.24 = (bf16[576,128]{1,0:T(8,128)(2,1)S(1)}, bf16[576,128]{1,0:T(8,128)(2,1)S(1)}, u32[]{:S(2)}, u32[]{:S(2)}) collective-permute-start(bf16[576,128]{1,0:T(8,128)(2,1)S(1)} %get-tuple-element.226), channel_id=1, source_target_pairs={{0,2},{2,0},{4,6},{6,4},{1,3},{3,1},{5,7},{7,5},{8,10},{10,8},{12,... | collective-permute-start | bytes 442376 | tf_op jit(solution)/shard_map/chip_qkv/ppermute | solution.py:977
  78.9 21.3 %collective-permute-start.27 = (bf16[144,1536]{1,0:T(8,128)(2,1)S(1)}, bf16[144,1536]{1,0:T(8,128)(2,1)S(1)}, u32[]{:S(2)}, u32[]{:S(2)}) collective-permute-start(bf16[144,1536]{1,0:T(8,128)(2,1)S(1)} %get-tuple-element.230), channel_id=1, source_target_pairs={{0,8},{8,0},{16,24},{24,16},{1,9},{9,1},{17,25},{25,17},{2,10},{10... | collective-permute-start | bytes 1327112 | tf_op jit(solution)/shard_map/plane_back/ppermute | solution.py:977
  79.6 21.0 %collective-permute-start.28 = (bf16[144,1536]{1,0:T(8,128)(2,1)S(1)}, bf16[144,1536]{1,0:T(8,128)(2,1)S(1)}, u32[]{:S(2)}, u32[]{:S(2)}) collective-permute-start(bf16[144,1536]{1,0:T(8,128)(2,1)S(1)} %get-tuple-element.231), channel_id=1, source_target_pairs={{0,16},{8,24},{16,0},{24,8},{1,17},{9,25},{17,1},{25,9},{2,18},{10... | collective-permute-start | bytes 1327112 | tf_op jit(solution)/shard_map/plane_back/ppermute | solution.py:977
  82.0 20.2 %collective-permute-start.29 = (bf16[144,1536]{1,0:T(8,128)(2,1)S(1)}, bf16[144,1536]{1,0:T(8,128)(2,1)S(1)}, u32[]{:S(2)}, u32[]{:S(2)}) collective-permute-start(bf16[144,1536]{1,0:T(8,128)(2,1)S(1)} %get-tuple-element.232), channel_id=1, source_target_pairs={{0,24},{8,16},{16,8},{24,0},{1,25},{9,17},{17,9},{25,1},{2,26},{10... | collective-permute-start | bytes 1327112 | tf_op jit(solution)/shard_map/plane_back/ppermute | solution.py:977
  82.8 9.8 %collective-permute-start.25 = (bf16[576,128]{1,0:T(8,128)(2,1)S(1)}, bf16[576,128]{1,0:T(8,128)(2,1)S(1)}, u32[]{:S(2)}, u32[]{:S(2)}) collective-permute-start(bf16[576,128]{1,0:T(8,128)(2,1)S(1)} %get-tuple-element.227), channel_id=1, source_target_pairs={{0,4},{2,6},{4,0},{6,2},{1,5},{3,7},{5,1},{7,3},{8,12},{10,14},{12... | collective-permute-start | bytes 442376 | tf_op jit(solution)/shard_map/chip_qkv/ppermute | solution.py:977
  85.9 14.3 %collective-permute-start.23 = (bf16[2,96,768]{2,1,0:T(8,128)(2,1)S(1)}, bf16[2,96,768]{2,1,0:T(8,128)(2,1)S(1)}, u32[]{:S(2)}, u32[]{:S(2)}) collective-permute-start(bf16[2,96,768]{2,1,0:T(8,128)(2,1)S(1)} %get-tuple-element.224), channel_id=1, source_target_pairs={{0,2},{2,0},{4,6},{6,4},{1,3},{3,1},{5,7},{7,5},{8,10},{10,8},{12,... | collective-permute-start | bytes 884744 | tf_op jit(solution)/shard_map/down_one/ppermute | solution.py:977
  92.6 7.6 %collective-permute-start.26 = (bf16[576,128]{1,0:T(8,128)(2,1)S(1)}, bf16[576,128]{1,0:T(8,128)(2,1)S(1)}, u32[]{:S(2)}, u32[]{:S(2)}) collective-permute-start(bf16[576,128]{1,0:T(8,128)(2,1)S(1)} %get-tuple-element.228), channel_id=1, source_target_pairs={{0,6},{2,4},{4,2},{6,0},{1,7},{3,5},{5,3},{7,1},{8,14},{10,12},{12... | collective-permute-start | bytes 442376 | tf_op jit(solution)/shard_map/chip_qkv/ppermute | solution.py:977
  103.9 2.4 %collective-permute-start.37 = (bf16[4,128,768]{2,1,0:T(8,128)(2,1)S(1)}, bf16[4,128,768]{2,1,0:T(8,128)(2,1)S(1)}, u32[]{:S(2)}, u32[]{:S(2)}) collective-permute-start(bf16[4,128,768]{2,1,0:T(8,128)(2,1)S(1)} %get-tuple-element.262), channel_id=1, source_target_pairs={{0,1},{1,0},{2,3},{3,2},{4,5},{5,4},{6,7},{7,6},{8,9},{9,8},{10,11... | collective-permute-start | bytes 2359304 | tf_op jit(solution)/shard_map/core_up/ppermute | solution.py:973
  103.9 18.4 %collective-permute-start.30 = (bf16[4,96,768]{2,1,0:T(8,128)(2,1)S(1)}, bf16[4,96,768]{2,1,0:T(8,128)(2,1)S(1)}, u32[]{:S(2)}, u32[]{:S(2)}) collective-permute-start(bf16[4,96,768]{2,1,0:T(8,128)(2,1)S(1)} %get-tuple-element.239), channel_id=1, source_target_pairs={{0,1},{1,0},{2,3},{3,2},{4,5},{5,4},{6,7},{7,6},{8,9},{9,8},{10,11... | collective-permute-start | bytes 1769480 | tf_op jit(solution)/shard_map/core_w/ppermute | solution.py:973
  106.9 11.2 %collective-permute-start.38 = (bf16[2,128,768]{2,1,0:T(8,128)(2,1)S(1)}, bf16[2,128,768]{2,1,0:T(8,128)(2,1)S(1)}, u32[]{:S(2)}, u32[]{:S(2)}) collective-permute-start(bf16[2,128,768]{2,1,0:T(8,128)(2,1)S(1)} %get-tuple-element.264), channel_id=1, source_target_pairs={{0,2},{2,0},{4,6},{6,4},{1,3},{3,1},{5,7},{7,5},{8,10},{10,8},{12,... | collective-permute-start | bytes 1179656 | tf_op jit(solution)/shard_map/up_sum/ppermute | solution.py:977
  118.7 18.0 %collective-permute-start.39 = (bf16[1,128,768]{2,1,0:T(8,128)(2,1)S(1)}, bf16[1,128,768]{2,1,0:T(8,128)(2,1)S(1)}, u32[]{:S(2)}, u32[]{:S(2)}) collective-permute-start(bf16[1,128,768]{2,1,0:T(8,128)(2,1)S(1)} %get-tuple-element.266), channel_id=1, source_target_pairs={{0,4},{2,6},{4,0},{6,2},{1,5},{3,7},{5,1},{7,3},{8,12},{10,14},{12... | collective-permute-start | bytes 589832 | tf_op jit(solution)/shard_map/up_sum/ppermute | solution.py:977
  123.0 6.4 %collective-permute-start.31 = (bf16[96,768]{1,0:T(8,128)(2,1)S(1)}, bf16[96,768]{1,0:T(8,128)(2,1)S(1)}, u32[]{:S(2)}, u32[]{:S(2)}) collective-permute-start(bf16[96,768]{1,0:T(8,128)(2,1)S(1)} %get-tuple-element.241), channel_id=1, source_target_pairs={{0,8},{8,0},{16,24},{24,16},{1,9},{9,1},{17,25},{25,17},{2,10},{10... | collective-permute-start | bytes 442376 | tf_op jit(solution)/shard_map/plane_w/ppermute | solution.py:977
  123.4 8.2 %collective-permute-start.32 = (bf16[96,768]{1,0:T(8,128)(2,1)S(1)}, bf16[96,768]{1,0:T(8,128)(2,1)S(1)}, u32[]{:S(2)}, u32[]{:S(2)}) collective-permute-start(bf16[96,768]{1,0:T(8,128)(2,1)S(1)} %get-tuple-element.242), channel_id=1, source_target_pairs={{0,16},{8,24},{16,0},{24,8},{1,17},{9,25},{17,1},{25,9},{2,18},{10... | collective-permute-start | bytes 442376 | tf_op jit(solution)/shard_map/plane_w/ppermute | solution.py:977
  124.9 6.8 %collective-permute-start.33 = (bf16[96,768]{1,0:T(8,128)(2,1)S(1)}, bf16[96,768]{1,0:T(8,128)(2,1)S(1)}, u32[]{:S(2)}, u32[]{:S(2)}) collective-permute-start(bf16[96,768]{1,0:T(8,128)(2,1)S(1)} %get-tuple-element.243), channel_id=1, source_target_pairs={{0,24},{8,16},{16,8},{24,0},{1,25},{9,17},{17,9},{25,1},{2,26},{10... | collective-permute-start | bytes 442376 | tf_op jit(solution)/shard_map/plane_w/ppermute | solution.py:977
  127.2 12.0 %collective-permute-start.43 = (bf16[1,96,768]{2,1,0:T(8,128)(2,1)S(1)}, bf16[1,96,768]{2,1,0:T(8,128)(2,1)S(1)}, u32[]{:S(2)}, u32[]{:S(2)}) collective-permute-start(bf16[1,96,768]{2,1,0:T(8,128)(2,1)S(1)} %get-tuple-element.279), channel_id=1, source_target_pairs={{0,4},{2,6},{4,0},{6,2},{1,5},{3,7},{5,1},{7,3},{8,12},{10,14},{12... | collective-permute-start | bytes 442376 | tf_op jit(solution)/shard_map/down_two/ppermute | solution.py:977
  132.3 8.0 %collective-permute-start.34 = (bf16[24,768]{1,0:T(8,128)(2,1)S(1)}, bf16[24,768]{1,0:T(8,128)(2,1)S(1)}, u32[]{:S(2)}, u32[]{:S(2)}) collective-permute-start(bf16[24,768]{1,0:T(8,128)(2,1)S(1)} %get-tuple-element.245), channel_id=1, source_target_pairs={{0,2},{2,0},{4,6},{6,4},{1,3},{3,1},{5,7},{7,5},{8,10},{10,8},{12,... | collective-permute-start | bytes 110600 | tf_op jit(solution)/shard_map/chip_w/ppermute | solution.py:977
  134.0 10.9 %collective-permute-start.35 = (bf16[24,768]{1,0:T(8,128)(2,1)S(1)}, bf16[24,768]{1,0:T(8,128)(2,1)S(1)}, u32[]{:S(2)}, u32[]{:S(2)}) collective-permute-start(bf16[24,768]{1,0:T(8,128)(2,1)S(1)} %get-tuple-element.246), channel_id=1, source_target_pairs={{0,4},{2,6},{4,0},{6,2},{1,5},{3,7},{5,1},{7,3},{8,12},{10,14},{12... | collective-permute-start | bytes 110600 | tf_op jit(solution)/shard_map/chip_w/ppermute | solution.py:977
  134.1 10.8 %collective-permute-start.36 = (bf16[24,768]{1,0:T(8,128)(2,1)S(1)}, bf16[24,768]{1,0:T(8,128)(2,1)S(1)}, u32[]{:S(2)}, u32[]{:S(2)}) collective-permute-start(bf16[24,768]{1,0:T(8,128)(2,1)S(1)} %get-tuple-element.247), channel_id=1, source_target_pairs={{0,6},{2,4},{4,2},{6,0},{1,7},{3,5},{5,3},{7,1},{8,14},{10,12},{12... | collective-permute-start | bytes 110600 | tf_op jit(solution)/shard_map/chip_w/ppermute | solution.py:977
  138.0 8.3 %collective-permute-start.40 = (bf16[24,768]{1,0:T(8,128)(2,1)S(1)}, bf16[24,768]{1,0:T(8,128)(2,1)S(1)}, u32[]{:S(2)}, u32[]{:S(2)}) collective-permute-start(bf16[24,768]{1,0:T(8,128)(2,1)S(1)} %get-tuple-element.273), channel_id=1, source_target_pairs={{0,8},{8,0},{16,24},{24,16},{1,9},{9,1},{17,25},{25,17},{2,10},{10... | collective-permute-start | bytes 110600 | tf_op jit(solution)/shard_map/plane_rows/ppermute | solution.py:977
  139.2 7.1 %collective-permute-start.41 = (bf16[24,768]{1,0:T(8,128)(2,1)S(1)}, bf16[24,768]{1,0:T(8,128)(2,1)S(1)}, u32[]{:S(2)}, u32[]{:S(2)}) collective-permute-start(bf16[24,768]{1,0:T(8,128)(2,1)S(1)} %get-tuple-element.274), channel_id=1, source_target_pairs={{0,16},{8,24},{16,0},{24,8},{1,17},{9,25},{17,1},{25,9},{2,18},{10... | collective-permute-start | bytes 110600 | tf_op jit(solution)/shard_map/plane_rows/ppermute | solution.py:977
  140.2 6.1 %collective-permute-start.42 = (bf16[24,768]{1,0:T(8,128)(2,1)S(1)}, bf16[24,768]{1,0:T(8,128)(2,1)S(1)}, u32[]{:S(2)}, u32[]{:S(2)}) collective-permute-start(bf16[24,768]{1,0:T(8,128)(2,1)S(1)} %get-tuple-element.275), channel_id=1, source_target_pairs={{0,24},{8,16},{16,8},{24,0},{1,25},{9,17},{17,9},{25,1},{2,26},{10... | collective-permute-start | bytes 110600 | tf_op jit(solution)/shard_map/plane_rows/ppermute | solution.py:977
  (12 other events, 130.9 us)

commit v3 on v2

--- a/solution.py
+++ b/solution.py
@@ -382,17 +382,21 @@
     return jnp.concatenate(pieces, axis=1)
 
 
-def mask_call(place, lengths, out_grad):
+def mask_call(place, lengths, out_grad, parts):
     rows, model = out_grad.shape
 
-    def body(place_ref, len_ref, in_ref, out_ref):
+    def body(place_ref, len_ref, in_ref, out_ref, msg_ref):
         last = jnp.int32(0)
         for d in range(lengths.shape[1]):
             last = last + len_ref[0, d]
         pos = lax.broadcasted_iota(jnp.int32, (rows, 1), 0) + (2 * place_ref[0] + place_ref[1]) * rows
-        out_ref[...] = jnp.where(pos < last, in_ref[...].astype(F32), 0.0).astype(BF16)
-
-    return kernel(body, shape(BF16, rows, model), (place, lengths), (out_grad,), micros=0.7, name="mask_grad")
+        masked = jnp.where(pos < last, in_ref[...].astype(F32), 0.0).astype(BF16)
+        out_ref[...] = masked
+        for r in range(parts):
+            msg_ref[r] = masked
+
+    outs = (shape(BF16, rows, model), shape(BF16, parts, rows, model))
+    return kernel(body, outs, (place, lengths), (out_grad,), micros=0.7, name="mask_grad")
 
 
 def qkv_call(blocks, gain, bias, weight, width):
@@ -637,36 +641,25 @@
     return jnp.concatenate([unpack(scr[k], rows, live) for k in range(len(pieces))], axis=1)
 
 
-def norms_call(place, pieces, layer_in, vectors, w_out, parts, live):
+def norms_call(place, pieces, layer_in, vectors, w_out, live):
     count, rows = len(pieces), layer_in.shape[0]
     model = w_out.shape[0]
-    quarter = model // parts
-    pad_q = -(-quarter // 128) * 128
 
     def body(place_ref, *refs):
-        in_ref, g2, b2, g3, b3, wo_ref, mid_ref, attn_ref = refs[count : count + 8]
-        msgs, (n2_scr, piece_scr) = refs[count + 8 : count + 8 + parts], refs[count + 8 + parts :]
+        in_ref, g2, b2, g3, b3, wo_ref, mid_ref, attn_ref, n3_ref, piece_scr = refs[count:]
         attn = gather_heads(place_ref, refs[:count], piece_scr, rows, live)
         attn_ref[...] = attn
         unit2, _ = unit_norm(attn.astype(F32))
         normed2 = (unit2 * row(g2) + row(b2)).astype(BF16)
-        for r in range(parts):
-            n2_scr[r, :, :quarter] = normed2[:, r * quarter : (r + 1) * quarter]
-            if pad_q > quarter:
-                n2_scr[r, :, quarter:] = jnp.zeros((rows, pad_q - quarter), BF16)
         middle = in_ref[...].astype(F32) + mm(normed2, wo_ref[...], NN)
         mid_ref[...] = middle
         unit3, _ = unit_norm(middle)
-        normed3 = (unit3 * row(g3) + row(b3)).astype(BF16)
-        for k in range(parts):
-            msgs[k][:, :model] = normed3
-            msgs[k][:, model:] = n2_scr[place_ref[2] ^ k]
-
-    outs = (shape(F32, rows, model), shape(BF16, rows, model)) + (shape(BF16, rows, model + pad_q),) * parts
+        n3_ref[...] = (unit3 * row(g3) + row(b3)).astype(BF16)
+
+    outs = (shape(F32, rows, model), shape(BF16, rows, model), shape(BF16, rows, model))
     operands = (*pieces, layer_in, *vectors, w_out)
-    scratch = (shape(BF16, parts, rows, pad_q), shape(BF16, count, *pieces[0].shape))
-    mid, attn, *msgs = kernel(body, outs, (place,), operands, scratch, micros=1.5, name="norms")
-    return mid, attn, msgs
+    scratch = (shape(BF16, count, *pieces[0].shape),)
+    return kernel(body, outs, (place,), operands, scratch, micros=1.5, name="norms")
 
 
 def up_call(place, normed3, w_up, parts):
@@ -674,7 +667,7 @@
     part = hidden // parts
 
     def body(place_ref, n3_ref, wu_ref, act_ref, slope_ref, *msgs):
-        normed = n3_ref[:, :model]
+        normed = n3_ref[...]
         for r in range(parts):
             upper = mm(normed, wu_ref[:, r * part : (r + 1) * part], NN)
             cumulative = 0.5 * (1.0 + lax.erf(upper * 0.7071067811865476))
@@ -689,19 +682,22 @@
     return act, slope, msgs
 
 
+def padded_quarter(quarter):
+    return -(-(quarter + 64) // 128) * 128
+
+
 def backward_call(place, attn, middle, act, slope, grad_out, vectors, w_out, w_up, w_down, parts, count, live):
     rows = attn.shape[0]
     model, hidden = w_up.shape
     part, quarter = hidden // parts, model // parts
+    pad_q = padded_quarter(quarter)
     message = shape(BF16, packed_rows(rows, live), 128)
 
     def body(
         place_ref, attn_ref, mid_ref, act_ref, slope_ref, go_ref, g2, b2, g3, b3, wo_ref, wu_ref, wd_ref,
         out_ref, gmid_ref, *rest,
     ):
-        msgs, heads = rest[:parts], rest[parts : parts + count]
-        up_scr, table_scr, head_scr = rest[parts + count :]
-        here = place_ref[2]
+        msg_ref, heads, head_scr = rest[0], rest[1 : 1 + count], rest[1 + count]
         go = go_ref[...]
         middle = mid_ref[...]
         out = middle
@@ -710,7 +706,7 @@
             w_d = wd_ref[r * part : (r + 1) * part, :]
             out = out + mm(act_ref[r], w_d, NN)
             grad_up = (mm(go, w_d, NT) * slope_ref[r].astype(F32)).astype(BF16)
-            up_scr[r] = grad_up
+            msg_ref[r, :, :part] = grad_up
             grad3 = grad3 + mm(grad_up, wu_ref[:, r * part : (r + 1) * part], NT)
         out_ref[...] = out.astype(BF16)
         unit3, scale3 = unit_norm(middle)
@@ -730,41 +726,42 @@
             jnp.sum(grad3 * unit3, axis=0, keepdims=True),
             jnp.sum(grad3, axis=0, keepdims=True),
         ]
-        table = jnp.concatenate(sums + [jnp.zeros((12, model), F32)], axis=0).astype(BF16)
+        table = jnp.concatenate(sums + [jnp.zeros((4, model), F32)], axis=0)
+        normed2 = (unit2 * row(g2) + row(b2)).astype(BF16)
+        normed3 = (unit3 * row(g3) + row(b3)).astype(BF16)
+        spare, lines = pad_q - quarter, quarter // 64
         for r in range(parts):
-            table_scr[r, :, :quarter] = table[:, r * quarter : (r + 1) * quarter]
-        for k in range(parts):
-            msgs[k][:rows, :part] = up_scr[here ^ k]
-            msgs[k][:rows, part:] = proj
-            msgs[k][rows:, :] = jnp.zeros((16, part + model), BF16)
-            msgs[k][rows:, part : part + quarter] = table_scr[here ^ k, :, :quarter]
+            chunks = [table[:, r * quarter + 64 * j : r * quarter + 64 * (j + 1)] for j in range(lines)]
+            side = jnp.concatenate(chunks + [jnp.zeros((rows - 8 * lines, 64), F32)], axis=0).astype(BF16)
+            pieces = [normed2[:, r * quarter : (r + 1) * quarter], side]
+            if spare > 64:
+                pieces.append(jnp.zeros((rows, spare - 64), BF16))
+            msg_ref[r, :, part : part + model] = proj
+            msg_ref[r, :, part + model : part + 2 * model] = normed3
+            msg_ref[r, :, part + 2 * model :] = jnp.concatenate(pieces, axis=1)
 
     outs = (
         shape(BF16, rows, model),
         shape(F32, rows, model),
     )
-    outs += (shape(BF16, rows + 16, part + model),) * parts + (message,) * count
+    outs += (shape(BF16, parts, rows, part + 2 * model + pad_q),) + (message,) * count
     operands = (attn, middle, act, slope, grad_out, *vectors, w_out, w_up, w_down)
-    scratch = (
-        shape(BF16, parts, rows, part),
-        shape(BF16, parts, 16, -(-quarter // 128) * 128),
-        shape(BF16, count, *message.shape),
-    )
+    scratch = (shape(BF16, count, *message.shape),)
     found = kernel(body, outs, (place,), operands, scratch, micros=9.0, name="token_backward")
     found = list(found)
-    return found[0], found[1], found[2 : 2 + parts], found[2 + parts :]
+    return found[0], found[1], found[2], found[3:]
 
 
 def down_grad_call(place, acts, grads, chips):
     parts = len(acts)
-    part, model = acts[0].shape[1], grads[0].shape[1]
+    part, model = acts[0].shape[1], grads.shape[2]
     own = part // (2 * chips)
 
     def body(place_ref, *refs):
-        act_refs, grad_refs, (keep_ref, send_ref, scr) = refs[:parts], refs[parts : 2 * parts], refs[2 * parts :]
+        act_refs, (grads_ref, keep_ref, send_ref, scr) = refs[:parts], refs[parts:]
         core = place_ref[1]
         act = jnp.concatenate([ref[...] for ref in act_refs], axis=0)
-        grad = jnp.concatenate([ref[...] for ref in grad_refs], axis=0)
+        grad = jnp.concatenate([grads_ref[place_ref[2] ^ k] for k in range(parts)], axis=0)
         scr[...] = mm(act, grad, TN).reshape(chips, 2, own, model)
         for k in range(chips):
             keep_ref[k] = scr[k, core]
@@ -772,29 +769,29 @@
 
     outs = (shape(F32, chips, own, model), shape(BF16, chips, own, model))
     scratch = (shape(F32, chips, 2, own, model),)
-    return kernel(body, outs, (place,), (*acts, *grads), scratch, micros=3.0, name="grad_down")
-
-
-def up_grad_call(place, sent, back, chips, part, model):
-    parts = len(sent)
-    rows = sent[0].shape[0]
+    return kernel(body, outs, (place,), (*acts, grads), scratch, micros=3.0, name="grad_down")
+
+
+def up_grad_call(place, back, chips, part, model):
+    parts, rows = back.shape[:2]
     quarter = model // parts
     own = model // (parts * chips * 2)
     tall = (parts + 1) * own + 8
 
-    def body(place_ref, *refs):
-        sent_refs, back_refs = refs[:parts], refs[parts : 2 * parts]
-        keep_ref, send_ref, up_scr, out_scr, vec_scr = refs[2 * parts :]
+    def body(place_ref, back_ref, keep_ref, send_ref, up_scr, out_scr, vec_scr):
         core = place_ref[1]
-        normed3 = jnp.concatenate([ref[:, :model] for ref in sent_refs], axis=0)
-        normed2 = jnp.concatenate([ref[:, model:] for ref in sent_refs], axis=0)
-        grad_up = jnp.concatenate([ref[:rows, :part] for ref in back_refs], axis=0)
-        proj = jnp.concatenate([ref[:rows, part:] for ref in back_refs], axis=0)
+        ends = (0, part, part + model, part + 2 * model, back.shape[2])
+        grad_up, proj, normed3, normed2 = (
+            back_ref[:, :, lo:hi].reshape(parts * rows, hi - lo) for lo, hi in zip(ends, ends[1:])
+        )
         up_scr[...] = mm(normed3, grad_up, TN).reshape(parts, chips, 2, own, part)
         out_scr[...] = mm(normed2, proj, TN)[:quarter].reshape(chips, 2, own, model)
-        table = jnp.zeros((8, quarter), F32)
-        for ref in back_refs:
-            table = table + ref[rows:, part : part + quarter].astype(F32)[:8]
+        lines = quarter // 64
+        side = jnp.zeros((8 * lines, 64), F32)
+        for r in range(parts):
+            block = back_ref[r, :, ends[3] :].astype(F32)
+            side = side + block[: 8 * lines, quarter : quarter + 64]
+        table = jnp.concatenate([side[8 * j : 8 * (j + 1)] for j in range(lines)], axis=1)
         vec_scr[...] = jnp.zeros_like(vec_scr)
         for k in range(chips):
             for side in range(2):
@@ -811,7 +808,7 @@
         shape(F32, chips, 2, own, model),
         shape(F32, chips, 2, 8, model),
     )
-    return kernel(body, outs, (place,), (*sent, *back), scratch, micros=4.0, name="grad_up_out")
+    return kernel(body, outs, (place,), (back,), scratch, micros=4.0, name="grad_up_out")
 
 
 def qkv_grad_call(place, groups, units, grads, gain, bias, weight, parts, live, width):
@@ -848,15 +845,11 @@
     return kernel(body, outs, (place,), operands, scratch, micros=4.0, name="grad_qkv")
 
 
-def spread_call(place, keep, arrived):
-    parts = keep.shape[0]
-
-    def body(place_ref, keep_ref, in_ref, *outs):
-        for k in range(parts):
-            at = place_ref[2] ^ k
-            outs[k][...] = (keep_ref[at] + in_ref[at].astype(F32)).astype(BF16)
-
-    return kernel(body, (shape(BF16, *keep.shape[1:]),) * parts, (place,), (keep, arrived), micros=0.8, name="spread")
+def spread_call(keep, arrived):
+    def body(keep_ref, in_ref, out_ref):
+        out_ref[...] = (keep_ref[...] + in_ref[...].astype(F32)).astype(BF16)
+
+    return kernel(body, shape(BF16, *keep.shape), (), (keep, arrived), micros=0.8, name="spread")
 
 
 def halve_call(place, keep, arrived, bit):
@@ -880,52 +873,46 @@
     return kernel(body, shape(F32, *keep.shape[1:]), (), (keep, arrived), micros=0.6, name="finish_down")
 
 
-def finish_up_call(place, keep, arrived, parts, own, part):
+def finish_up_call(keep, arrived, parts, own, part):
     model = keep.shape[2]
 
-    def body(place_ref, keep_ref, in_ref, out_ref, g2, b2, g3, b3, *rest):
-        msgs, scr = rest[:parts], rest[parts]
+    def body(keep_ref, in_ref, out_ref, g2, b2, g3, b3, rows_ref):
         value = keep_ref[0] + in_ref[0].astype(F32)
         out_ref[...] = value[parts * own : (parts + 1) * own]
         for at, ref in enumerate((g2, b2, g3, b3)):
             line = (parts + 1) * own + at
             ref[...] = value[line : line + 1, :own].reshape(own)
-        scr[...] = value[: parts * own].reshape(parts, own, part)
-        for k in range(parts):
-            msgs[k][...] = scr[place_ref[2] ^ k].astype(BF16)
-
-    outs = (shape(F32, own, model),) + (shape(F32, own),) * 4 + (shape(BF16, own, part),) * parts
-    scratch = (shape(F32, parts, own, part),)
-    return kernel(body, outs, (place,), (keep, arrived), scratch, micros=0.8, name="finish_up")
-
-
-def place_up_call(place, pieces):
-    parts = len(pieces)
-    own, part = pieces[0].shape
-
-    def body(place_ref, *refs):
-        for k in range(parts):
-            at = pl.multiple_of((place_ref[2] ^ k) * part, 128)
-            refs[parts][:, pl.ds(at, part)] = refs[k][...].astype(F32)
-
-    return kernel(body, shape(F32, own, parts * part), (place,), tuple(pieces), micros=0.5, name="place_up")
+        rows_ref[...] = value[: parts * own].reshape(parts, own, part).astype(BF16)
+
+    outs = (shape(F32, own, model),) + (shape(F32, own),) * 4 + (shape(BF16, parts, own, part),)
+    return kernel(body, outs, (), (keep, arrived), micros=0.8, name="finish_up")
+
+
+def place_up_call(pieces):
+    parts, own, part = pieces.shape
+
+    def body(in_ref, out_ref):
+        for r in range(parts):
+            out_ref[:, r * part : (r + 1) * part] = in_ref[r].astype(F32)
+
+    return kernel(body, shape(F32, own, parts * part), (), (pieces,), micros=0.5, name="place_up")
 
 
 def share_call(place, pieces, chips):
-    own = pieces[0].shape[0] // chips
-
-    def body(place_ref, *refs):
-        ins, outs, scr = refs[: len(pieces)], refs[len(pieces) : -1], refs[-1]
-        total = ins[0][...].astype(F32)
-        for ref in ins[1:]:
-            total = total + ref[...].astype(F32)
-        scr[...] = total.reshape(chips, own, total.shape[1])
+    parts, tall, lanes = pieces.shape
+    own = tall // chips
+
+    def body(place_ref, in_ref, *refs):
+        outs, scr = refs[:-1], refs[-1]
+        total = in_ref[0].astype(F32)
+        for r in range(1, parts):
+            total = total + in_ref[r].astype(F32)
+        scr[...] = total.reshape(chips, own, lanes)
         for k in range(chips):
             outs[k][...] = scr[place_ref[0] ^ k].astype(BF16)
 
-    lanes = pieces[0].shape[1]
     outs = (shape(BF16, own, lanes),) * chips
-    return kernel(body, outs, (place,), tuple(pieces), (shape(F32, chips, own, lanes),), micros=0.7, name="share")
+    return kernel(body, outs, (place,), (pieces,), (shape(F32, chips, own, lanes),), micros=0.7, name="share")
 
 
 def finish_qkv_call(place, pieces, model, live, width):
@@ -981,6 +968,10 @@
     return [messages[0]] + [swap(messages[k], axis, k) for k in range(1, len(messages))]
 
 
+def plane_trade(messages):
+    return lax.all_to_all(messages, "rows", 0, 0)
+
+
 def gather_chips(block, chips):
     found = {0: block}
     bit = chips // 2
@@ -997,6 +988,10 @@
         arrived = swap(away, "chip", bit)
         bit *= 2
     return keep, arrived
+
+
+def after(values, *others):
+    return lax.optimization_barrier((values, others))[0]
 
 
 def fast_shards(
@@ -1022,7 +1017,7 @@
     place, layer_in, out_grad = lax.optimization_barrier((place, inputs[0], out_grad[0]))
     with scope("gather_in"):
         blocks = gather_chips(layer_in, chips)
-    grad_out = mask_call(place, doc_lengths, out_grad)
+    grad_out, grads_plane = mask_call(place, doc_lengths, out_grad, parts)
     w_heads = jnp.concatenate([columns(w_query), columns(w_key), columns(w_value)], axis=1)
     groups = [g for g in ([0], list(range(1, chips - 1)), [chips - 1]) if g] if chips > 1 else [[0]]
     made = [qkv_call([blocks[k] for k in g], ln1_gain, ln1_bias, w_heads, width) for g in groups]
@@ -1033,70 +1028,77 @@
         place, doc_lengths, groups, queries, kv_own, kv_other, heads_here
     )
     fence = lax.optimization_barrier
-    messages, grad_out = fence((messages, grad_out))
     with scope("chip_attn"):
         pieces = trade(messages, "chip")
     with scope("plane_out"):
-        grads_plane = trade([grad_out] * parts, "rows")
-    pieces, grads_plane = fence((pieces, grads_plane))
+        grads_plane = plane_trade(grads_plane)
+    pieces = after(pieces, grads_plane)
 
     vectors = (ln2_gain, ln2_bias, ln3_gain, ln3_bias)
-    middle, attn, sent = norms_call(place, pieces, layer_in, vectors, w_out, parts, live)
-    act, slope, acts = up_call(place, sent[0], w_up, parts)
-    with scope("plane_norms"):
-        sent = trade(sent, "rows")
+    middle, attn, normed3 = norms_call(place, pieces, layer_in, vectors, w_out, live)
+    act, slope, acts = up_call(place, normed3, w_up, parts)
     with scope("plane_act"):
         acts = trade(acts, "rows")
     output, grad_mid, back, messages = backward_call(
         place, attn, middle, act, slope, grad_out, vectors, w_out, w_up, w_down, parts, chips, live
     )
+    acts[:3], messages, back = fence((acts[:3], messages, back))
     with scope("chip_grad"):
         grad_heads = trade(messages, "chip")
-    grad_heads, sent = fence((grad_heads, sent))
+    with scope("plane_back"):
+        back = plane_trade(after(back, grad_heads[1:2]))
+    acts = after(acts, grad_heads[1:])
+    down_keep, down_send = down_grad_call(place, acts, grads_plane, chips)
+    with scope("core_down"):
+        down_recv = swap_core(down_send)
     grad_q, grad_kv, grad_kv_other = attend_back_call(
         place, queries, kv_own, kv_other, prob, attn_heads, grad_heads, heads_here
     )
-    grad_kv_other, acts = fence((grad_kv_other, acts))
-    down_keep, down_send = down_grad_call(place, acts, grads_plane, chips)
     with scope("core_grad"):
         grad_kv_other = swap_core(grad_kv_other)
-    with scope("core_down"):
-        down_recv = swap_core(down_send)
+    down_recv = after(down_recv, grad_q)
+    with scope("down_sum"):
+        down_keep, down_away = halve_call(place, down_keep, down_recv, 1)
+        grad_kv_other, down_away = fence((grad_kv_other, down_away))
+        down_recv = swap(down_away, "chip", 1)
     grad_qkv, messages = join_call(place, grad_q, grad_kv, grad_kv_other, live)
-    down_keep, down_away = halve_call(place, down_keep, down_recv, 1)
-    messages, down_away, back, grad_qkv = fence((messages, down_away, back, grad_qkv))
     with scope("chip_qkv"):
         grad_pieces = trade(messages, "chip")
-    with scope("plane_back"):
-        back = trade(back, "rows")
-    with scope("down_one"):
-        down_recv = swap(down_away, "chip", 1)
     qkv_keep, qkv_send = qkv_grad_call(
         place, groups, units, grad_qkv, ln1_gain, ln1_bias, w_heads, parts, live, width
     )
-    qkv_send, down_recv, grad_pieces, back = fence((qkv_send, down_recv, grad_pieces, back))
-    up_keep, up_send = up_grad_call(place, sent, back, chips, part, model)
     with scope("core_w"):
         qkv_send = swap_core(qkv_send)
+    qkv_send = after(qkv_send, (grad_pieces, down_recv))
+    qkv_sums = spread_call(qkv_keep, qkv_send)
+    with scope("down_sum"):
+        down_keep, down_last = scatter_chips(place, down_keep, down_recv, chips, 2)
+    back = after(back, (down_keep, qkv_sums))
+    up_keep, up_send = up_grad_call(place, back, chips, part, model)
+    with scope("plane_w"):
+        traded = plane_trade(qkv_sums)
     with scope("core_up"):
         up_recv = swap_core(up_send)
-    with scope("down_two"):
-        down_keep, down_last = scatter_chips(place, down_keep, down_recv, chips, 2)
-    with scope("plane_w"):
-        qkv_sums = trade(spread_call(place, qkv_keep, qkv_send), "rows")
+    up_keep, up_away = halve_call(place, up_keep, up_recv, 1)
     with scope("up_sum"):
-        up_keep, up_last = scatter_chips(place, up_keep, up_recv, chips, 1)
+        up_recv = swap(up_away, "chip", 1)
+    traded = after(traded, up_away)
     with scope("chip_w"):
-        qkv_all = trade(share_call(place, qkv_sums, chips), "chip")
-    gwo, g2, b2, g3, b3, *up_rows = finish_up_call(place, up_keep, up_last, parts, own, part)
-    with scope("plane_rows"):
-        up_rows = trade(up_rows, "rows")
-    gwq, gwk, gwv, g1, b1 = finish_qkv_call(place, qkv_all, model, live, width)
-    gwu = place_up_call(place, up_rows)
-    gwd = finish_down_call(down_keep, down_last)
+        shared = share_call(place, traded, chips)
+        qkv_all = trade(shared, "chip")
     grad_inputs = input_grad_call(
         place, grad_pieces, layer_in, grad_mid, ln1_gain, w_query, w_key, w_value, live
     )
+    gwd = finish_down_call(down_keep, down_last)
+    up_recv = after(up_recv, down_last)
+    with scope("up_sum"):
+        up_keep, up_last = scatter_chips(place, up_keep, up_recv, chips, 2)
+    up_last = after(up_last, (qkv_all, gwd, grad_inputs))
+    gwo, g2, b2, g3, b3, up_rows = finish_up_call(up_keep, up_last, parts, own, part)
+    with scope("plane_rows"):
+        up_rows = plane_trade(up_rows)
+    gwq, gwk, gwv, g1, b1 = finish_qkv_call(place, qkv_all, model, live, width)
+    gwu = place_up_call(up_rows)
     return (
         output[None], grad_inputs[None], g1, b1, gwq, gwk, gwv, g2, b2, gwo, g3, b3, gwu, gwd,
     )
@@ -1105,7 +1107,7 @@
 def takes_fast(mesh):
     seq, parts = mesh.shape["seq"], mesh.shape["rows"]
     chips = seq // 2
-    return seq % 2 == 0 and chips & (chips - 1) == 0 and parts & (parts - 1) == 0 and HEADS % max(chips, 1) == 0
+    return seq % 2 == 0 and chips & (chips - 1) == 0 and parts in (1, 2, 4) and HEADS % max(chips, 1) == 0
 
 
 def solution(mesh):

time: 148 us -> 207 us (1.40)
  local copies, waits for them, and re-layouts: 4.03 us -> 48.6 us
  waiting for transfers between devices: 43.3 us -> 66.6 us
  starting transfers between devices: 62.1 us -> 48.2 us
  Pallas kernels: 36.9 us -> 41 us
    unnamed x32 -> x160, local copies, waits for them, and re-layouts: 1.03 us -> 45.8 us
    ppermute x37 -> x22, starting transfers between devices: 60.3 us -> 31 us  [swap(): lax.ppermute(value, axis, [(k, k ^ bit) for k in range(lax.axis_size(axis...]
    ppermute x37 -> x22, waiting for transfers between devices: 38.6 us -> 58.5 us  [swap(): lax.ppermute(value, axis, [(k, k ^ bit) for k in range(lax.axis_size(axis...]
    all_to_all x0 -> x4, starting transfers between devices: none -> 15.4 us  [plane_trade(): return lax.all_to_all(messages, 'rows', 0, 0)]
    pallas_call x24, Pallas kernels: 36.9 us -> 41 us  [kernel(): pl.pallas_call(body, out_shape=outs if single else listed, in_specs=[smem...]
    all_to_all x0 -> x4, waiting for transfers between devices: none -> 3.7 us  [plane_trade(): return lax.all_to_all(messages, 'rows', 0, 0)]
  transfers between devices with their start and end apart: 44 -> 33, of which waited for: 17 -> 15; matrix products, arithmetic and copies ran while one was open for 2% -> 1% of each run, Pallas kernels for 18% -> 16%
where the time goes in v3:
time: 207 us; the launch traced here: 206 us
  waiting for transfers between devices  66.6 us (32%)
  local copies, waits for them, and re-layouts  48.6 us (23%)
  starting transfers between devices  48.2 us (23%)
  Pallas kernels  41 us (20%)
    ppermute x22, waiting for transfers between devices, swap(): lax.ppermute(value, axis, [(k, k ^ bit) for k in range(lax.axis_size(axis...  58.5 us
    unnamed x160, local copies, waits for them, and re-layouts  45.8 us
    pallas_call x24, Pallas kernels, kernel(): pl.pallas_call(body, out_shape=outs if single else listed, in_specs=[smem...  41 us
    ppermute x22, starting transfers between devices, swap(): lax.ppermute(value, axis, [(k, k ^ bit) for k in range(lax.axis_size(axis...  31 us
    all_to_all x4, starting transfers between devices, plane_trade(): return lax.all_to_all(messages, 'rows', 0, 0)  15.4 us
    ppermute x7, waiting for transfers between devices, swap_core(): return lax.ppermute(value, 'core', [(0, 1), (1, 0)])  4.44 us
  transfers between devices with their start and end apart: 33, of which 15 were waited for; matrix products, arithmetic and copies ran while one was open for 1% of the time, Pallas kernels for 16%

profile of v3, /device:TPU:0, one launch (start us, length us, event | category | flops | bytes accessed | tf_op | source)
XLA Modules:
  0.0 205.9 jit_solution(1560682287752120335)
XLA Ops:
  0.7 4.1 %collective-permute-start.1 = (bf16[128,768]{1,0:T(8,128)(2,1)}, bf16[128,768]{1,0:T(8,128)(2,1)}, u32[]{:S(2)}, u32[]{:S(2)}) collective-permute-start(bf16[128,768]{1,0:T(8,128)(2,1)} %bitcast.7), channel_id=1, source_target_pairs={{0,4},{2,6},{4,0},{6,2},{1,5},{3,7},{5,1},{7,3},{8,12},{10,14},{12... | collective-permute-start | bytes 589832 | tf_op jit(solution)/shard_map/gather_in/ppermute | solution.py:964
  4.8 1.6 collective-permute-start
  8.0 1.5 mask_grad.1
  10.2 3.7 %all-to-all-start = ((bf16[4,128,768]{2,1,0:T(8,128)(2,1)}), bf16[4,128,768]{2,1,0:T(8,128)(2,1)S(1)}, u32[]{:S(2)}, u32[]{:S(2)}) async-start(bf16[4,128,768]{2,1,0:T(8,128)(2,1)} %get-tuple-element.128), calls=%async_computation | async-start | bytes 1572864 | tf_op jit(solution)/shard_map/plane_out/all_to_all | solution.py:972
  13.9 1.6 constant_dynamic-slice_fusion
  17.9 1.6 qkv_heads.4
  20.8 2.1 %collective-permute-done.2.refs_0_ = bf16[128,768]{1,0:T(8,128)(2,1)S(1)} collective-permute-done((bf16[128,768]{1,0:T(8,128)(2,1)}, bf16[128,768]{1,0:T(8,128)(2,1)S(1)}, u32[]{:S(2)}, u32[]{:S(2)}) %collective-permute-start.2) | collective-permute-done | bytes 196640 | tf_op jit(solution)/shard_map/gather_in/ppermute | solution.py:964
  24.1 1.3 collective-permute-done.5.refs_8_
  25.4 4.2 %attend.1 = (f32[4,128,256]{2,1,0:T(8,128)S(1)}, bf16[4,2,384,512]{3,2,1,0:T(8,128)(2,1)S(1)}, bf16[4,128,256]{2,1,0:T(8,128)(2,1)S(1)}, bf16[4,128,512]{2,1,0:T...) custom-call(s32[3]{0:T(128)S(1)} %pad_add_fusion.place_ref, ...), custom_call_target="tpu_custom_call" | custom-call | flops 6000000 | bytes 6000 | tf_op jit(solution)/shard_map/attend/pallas_call | solution.py:350
  29.6 1.6 copy-done.4
  35.4 2.0 collective-permute-start.7
  37.4 1.9 collective-permute-start.8
  41.6 1.8 collective-permute-done.8.refs_3_
  49.2 1.4 norms.1
  50.6 2.3 %copy-done = bf16[768,3072]{1,0:T(8,128)(2,1)S(1)} copy-done((bf16[768,3072]{1,0:T(8,128)(2,1)S(1)}, bf16[768,3072]{1,0:T(8,128)(2,1)}, u32[]{:S(2)}) %copy-start) | copy-done | bytes 4718616
  53.0 1.9 up_gelu.1
  56.2 1.5 collective-permute-start.10
  57.8 1.5 collective-permute-start.9
  59.3 2.3 %copy-done.3 = bf16[3072,768]{1,0:T(8,128)(2,1)S(1)} copy-done((bf16[3072,768]{1,0:T(8,128)(2,1)S(1)}, bf16[3072,768]{1,0:T(8,128)(2,1)}, u32[]{:S(2)}) %copy-start.3) | copy-done | bytes 4718616
  61.6 5.8 %token_backward.1 = (bf16[128,768]{1,0:T(8,128)(2,1)}, f32[128,768]{1,0:T(8,128)S(1)}, bf16[4,128,2560]{2,1,0:T(8,128)(2,1)S(1)}, bf16[192,128]{1,0:T(8,128)(2,1...) custom-call(s32[3]{0:T(128)S(1)} %pad_add_fusion.place_ref, ...), custom_call_target="tpu_custom_call" | custom-call | flops 9000000 | bytes 9000 | tf_op jit(solution)/shard_map/token_backward/pallas_call | solution.py:350
  67.4 1.5 copy-done.6
  72.9 4.1 %collective-permute-done.11.refs_1_ = bf16[192,128]{1,0:T(8,128)(2,1)S(1)} collective-permute-done((bf16[192,128]{1,0:T(8,128)(2,1)S(1)}, bf16[192,128]{1,0:T(8,128)(2,1)S(1)}, u32[]{:S(2)}, u32[]{:S(2)}) %collective-permute-start.11) | collective-permute-done | bytes 49184 | tf_op jit(solution)/shard_map/chip_grad/ppermute | solution.py:964
  77.6 4.8 %all-to-all-start.2 = ((bf16[4,128,2560]{2,1,0:T(8,128)(2,1)}), bf16[4,128,2560]{2,1,0:T(8,128)(2,1)}, u32[]{:S(2)}, u32[]{:S(2)}) async-start(bf16[4,128,2560]{2,1,0:T(8,128)(2,1)} %copy-done.6), calls=%async_computation.2 | async-start | bytes 5242880 | tf_op jit(solution)/shard_map/plane_back/all_to_all | solution.py:972
  82.4 2.9 %collective-permute-start.15 = (bf16[128,768]{1,0:T(8,128)(2,1)S(1)}, bf16[128,768]{1,0:T(8,128)(2,1)S(1)}, u32[]{:S(2)}, u32[]{:S(2)}) collective-permute-start(bf16[128,768]{1,0:T(8,128)(2,1)S(1)} %copy-done.74), channel_id=1, source_target_pairs={{0,24},{8,16},{16,8},{24,0},{1,25},{9,17},{17,9},{25,1},{2,26},{10... | collective-permute-start | bytes 589832 | tf_op jit(solution)/shard_map/plane_act/ppermute | solution.py:964
  86.0 1.7 collective-permute-start.13
  87.7 27.8 %collective-permute-done.15.refs_3_ = bf16[128,768]{1,0:T(8,128)(2,1)S(1)} collective-permute-done((bf16[128,768]{1,0:T(8,128)(2,1)S(1)}, bf16[128,768]{1,0:T(8,128)(2,1)S(1)}, u32[]{:S(2)}, u32[]{:S(2)}) %collective-permute-start.15) | collective-permute-done | bytes 196640 | tf_op jit(solution)/shard_map/plane_act/ppermute | solution.py:964
  118.2 1.5 grad_down.1
  119.9 1.9 copy-done.5
  124.3 3.7 %attend_back.1 = (bf16[4,128,256]{2,1,0:T(8,128)(2,1)S(1)}, f32[4,128,512]{2,1,0:T(8,128)S(1)}, bf16[4,128,512]{2,1,0:T(8,128)(2,1)S(1)}) custom-call(s32[3]{0:T(128)S(1)} %pad_add_fusion.place_ref, bf16[4,128,256]{2,1,0:T(8,128)(2,1)S(1)} %copy-done.28, bf16[4,128,512]{2,1,0:T(8,128)(2,1)S(1)} %copy-done.16, bf16[4,128,512]{2,1,0:T(8,128)(2,1)S(1)} %copy-done.18, ...), custom_call_target="tpu_custom_call" | custom-call | flops 6000000 | bytes 6000 | tf_op jit(solution)/shard_map/attend_back/pallas_call | solution.py:350
  131.5 2.5 %grad_qkv.1 = (f32[4,96,768]{2,1,0:T(8,128)S(1)}, bf16[4,96,768]{2,1,0:T(8,128)(2,1)S(1)}) custom-call(s32[3]{0:T(128)S(1)} %pad_add_fusion.place_ref, bf16[1,128,768]{2,1,0:T(8,128)(2,1)S(1)} %get-tuple-element.178.refs_0_, bf16[2,128,768]{2,1,0:T(8,128)(2,1)S(1)} %copy-done.22, bf16[1,128,768]{2,1,0:T(8,128)(2,1)S(1)} %copy-done.30, ...), custom_call_target="tpu_custom_call" | custom-call | flops 4000000 | bytes 4000 | tf_op jit(solution)/shard_map/grad_qkv/pallas_call | solution.py:350
  134.7 1.7 collective-permute-start.17
  136.5 1.4 collective-permute-start.18
  139.1 8.4 %collective-permute-done.21.in_ref = bf16[2,96,768]{2,1,0:T(8,128)(2,1)S(1)} collective-permute-done((bf16[2,96,768]{2,1,0:T(8,128)(2,1)S(1)}, bf16[2,96,768]{2,1,0:T(8,128)(2,1)S(1)}, u32[]{:S(2)}, u32[]{:S(2)}) %collective-permute-start.21) | collective-permute-done | bytes 294944 | tf_op jit(solution)/shard_map/down_sum/ppermute | solution.py:964
  150.5 3.3 %collective-permute-done.19.refs_3_ = bf16[576,128]{1,0:T(8,128)(2,1)S(1)} collective-permute-done((bf16[576,128]{1,0:T(8,128)(2,1)S(1)}, bf16[576,128]{1,0:T(8,128)(2,1)S(1)}, u32[]{:S(2)}, u32[]{:S(2)}) %collective-permute-start.19) | collective-permute-done | bytes 147488 | tf_op jit(solution)/shard_map/chip_qkv/ppermute | solution.py:964
  155.4 2.9 %grad_up_out.1 = (f32[4,128,768]{2,1,0:T(8,128)S(1)}, bf16[4,128,768]{2,1,0:T(8,128)(2,1)S(1)}) custom-call(s32[3]{0:T(128)S(1)} %pad_add_fusion.place_ref, bf16[4,128,2560]{2,1,0:T(8,128)(2,1)} %all-to-all-done.2.back_ref), custom_call_target="tpu_custom_call" | custom-call | flops 4000000 | bytes 4000 | tf_op jit(solution)/shard_map/grad_up_out/pallas_call | solution.py:350
  158.4 2.3 %collective-permute-done.22.in_ref = bf16[4,128,768]{2,1,0:T(8,128)(2,1)S(1)} collective-permute-done((bf16[4,128,768]{2,1,0:T(8,128)(2,1)S(1)}, bf16[4,128,768]{2,1,0:T(8,128)(2,1)S(1)}, u32[]{:S(2)}, u32[]{:S(2)}) %collective-permute-start.22) | collective-permute-done | bytes 786464 | tf_op jit(solution)/shard_map/core_up/ppermute | solution.py:960
  160.7 1.4 halve.6
  163.0 3.6 %all-to-all-start.1 = ((bf16[4,96,768]{2,1,0:T(8,128)(2,1)}), bf16[4,96,768]{2,1,0:T(8,128)(2,1)S(1)}, u32[]{:S(2)}, u32[]{:S(2)}) async-start(bf16[4,96,768]{2,1,0:T(8,128)(2,1)} %spread.1), calls=%async_computation.1 | async-start | bytes 1179648 | tf_op jit(solution)/shard_map/plane_w/all_to_all | solution.py:972
  166.6 1.9 collective-permute-start.27
  168.5 6.9 %collective-permute-done.27.in_ref = bf16[1,96,768]{2,1,0:T(8,128)(2,1)S(1)} collective-permute-done((bf16[1,96,768]{2,1,0:T(8,128)(2,1)}, bf16[1,96,768]{2,1,0:T(8,128)(2,1)S(1)}, u32[]{:S(2)}, u32[]{:S(2)}) %collective-permute-start.27) | collective-permute-done | bytes 147488 | tf_op jit(solution)/shard_map/down_sum/ppermute | solution.py:964
  175.4 2.2 %collective-permute-done.26.in_ref = bf16[2,128,768]{2,1,0:T(8,128)(2,1)} collective-permute-done((bf16[2,128,768]{2,1,0:T(8,128)(2,1)}, bf16[2,128,768]{2,1,0:T(8,128)(2,1)}, u32[]{:S(2)}, u32[]{:S(2)}) %collective-permute-start.26) | collective-permute-done | bytes 393248 | tf_op jit(solution)/shard_map/up_sum/ppermute | solution.py:964
  178.7 1.7 halve.7
  185.0 2.5 %collective-permute-start.25 = (bf16[24,768]{1,0:T(8,128)(2,1)S(1)}, bf16[24,768]{1,0:T(8,128)(2,1)S(1)}, u32[]{:S(2)}, u32[]{:S(2)}) collective-permute-start(bf16[24,768]{1,0:T(8,128)(2,1)S(1)} %get-tuple-element.198), channel_id=1, source_target_pairs={{0,6},{2,4},{4,2},{6,0},{1,7},{3,5},{5,3},{7,1},{8,14},{10,12},{12... | collective-permute-start | bytes 110600 | tf_op jit(solution)/shard_map/chip_w/ppermute | solution.py:964
  187.5 1.3 copy-done.9
  192.5 2.7 %grad_inputs.1 = bf16[128,768]{1,0:T(8,128)(2,1)} custom-call(s32[3]{0:T(128)S(1)} %pad_add_fusion.place_ref, bf16[576,128]{1,0:T(8,128)(2,1)S(1)} %copy-done.41, bf16[576,128]{1,0:T(8,128)(2,1)S(1)} %copy-done.43, bf16[576,128]{1,0:T(8,128)(2,1)S(1)} %copy-done.45, bf16[576,128]{1,0:T(8,128)(2,1)S(1)} %copy-done.47, bf16[128,768]{1,0:T(8,128)(2,1)S(1)} %bitcast.11, ...), custom_call_target="tpu_custom_call" | custom-call | flops 3000000 | bytes 3000 | tf_op jit(solution)/shard_map/grad_inputs/pallas_call | solution.py:350
  196.7 3.3 %all-to-all-start.3 = ((bf16[4,24,768]{2,1,0:T(8,128)(2,1)}), bf16[4,24,768]{2,1,0:T(8,128)(2,1)S(1)}, u32[]{:S(2)}, u32[]{:S(2)}) async-start(bf16[4,24,768]{2,1,0:T(8,128)(2,1)} %get-tuple-element.215), calls=%async_computation.3 | async-start | bytes 294912 | tf_op jit(solution)/shard_map/plane_rows/all_to_all | solution.py:972
  200.1 1.3 finish_qkv.1
  201.4 3.7 %all-to-all-done.3.in_ref = bf16[4,24,768]{2,1,0:T(8,128)(2,1)S(1)} async-done(((bf16[4,24,768]{2,1,0:T(8,128)(2,1)}), bf16[4,24,768]{2,1,0:T(8,128)(2,1)S(1)}, u32[]{:S(2)}, u32[]{:S(2)}) %all-to-all-start.3) | async-done | bytes 147488 | tf_op jit(solution)/shard_map/plane_rows/all_to_all | solution.py:972
  (206 shorter events, 54.1 us)
Async XLA Ops:
  0.7 16.0 %collective-permute-start.1 = (bf16[128,768]{1,0:T(8,128)(2,1)}, bf16[128,768]{1,0:T(8,128)(2,1)}, u32[]{:S(2)}, u32[]{:S(2)}) collective-permute-start(bf16[128,768]{1,0:T(8,128)(2,1)} %bitcast.7), channel_id=1, source_target_pairs={{0,4},{2,6},{4,0},{6,2},{1,5},{3,7},{5,1},{7,3},{8,12},{10,14},{12... | collective-permute-start | bytes 589832 | tf_op jit(solution)/shard_map/gather_in/ppermute | solution.py:964
  4.8 12.6 %collective-permute-start = (bf16[128,768]{1,0:T(8,128)(2,1)}, bf16[128,768]{1,0:T(8,128)(2,1)S(1)}, u32[]{:S(2)}, u32[]{:S(2)}) collective-permute-start(bf16[128,768]{1,0:T(8,128)(2,1)} %bitcast.8), channel_id=1, source_target_pairs={{0,2},{2,0},{4,6},{6,4},{1,3},{3,1},{5,7},{7,5},{8,10},{10,8},{12,... | collective-permute-start | bytes 589832 | tf_op jit(solution)/shard_map/gather_in/ppermute | solution.py:964
  10.2 33.8 %all-to-all-start = ((bf16[4,128,768]{2,1,0:T(8,128)(2,1)}), bf16[4,128,768]{2,1,0:T(8,128)(2,1)S(1)}, u32[]{:S(2)}, u32[]{:S(2)}) async-start(bf16[4,128,768]{2,1,0:T(8,128)(2,1)} %get-tuple-element.128), calls=%async_computation | async-start | bytes 1572864 | tf_op jit(solution)/shard_map/plane_out/all_to_all | solution.py:972
  16.7 6.2 %collective-permute-start.2 = (bf16[128,768]{1,0:T(8,128)(2,1)}, bf16[128,768]{1,0:T(8,128)(2,1)S(1)}, u32[]{:S(2)}, u32[]{:S(2)}) collective-permute-start(bf16[128,768]{1,0:T(8,128)(2,1)} %collective-permute-done.1.refs_1_), channel_id=1, source_target_pairs={{0,2},{2,0},{4,6},{6,4},{1,3},{3,1},{5,7},{7,5},{8,10},{10,8},{12,... | collective-permute-start | bytes 589832 | tf_op jit(solution)/shard_map/gather_in/ppermute | solution.py:964
  19.6 4.5 %collective-permute-start.4 = (bf16[2,128,512]{2,1,0:T(8,128)(2,1)S(1)}, bf16[2,128,512]{2,1,0:T(8,128)(2,1)S(1)}, u32[]{:S(2)}, u32[]{:S(2)}) collective-permute-start(bf16[2,128,512]{2,1,0:T(8,128)(2,1)S(1)} %get-tuple-element.121.refs_4_), channel_id=1, source_target_pairs={{0,1},{1,0},{2,3},{3,2},{4,5},{5,4},{6,7},{7,6},{8,9},{9,8},{10,11... | collective-permute-start | bytes 786440 | tf_op jit(solution)/shard_map/core_kv/ppermute | solution.py:960
  20.2 23.8 %copy-start.2 = (bf16[768,768]{1,0:T(8,128)(2,1)S(1)}, bf16[768,768]{1,0:T(8,128)(2,1)}, u32[]{:S(2)}) copy-start(bf16[768,768]{1,0:T(8,128)(2,1)} %wo_ref.1) | copy-start | bytes 3538948
  20.2 23.8 %copy-start.64 = (f32[768]{0:T(1024)S(1)}, f32[768]{0:T(1024)}, u32[]{:S(2)}) copy-start(f32[768]{0:T(1024)} %g2.1) | copy-start | bytes 9220
  20.2 3.9 %collective-permute-start.3 = (bf16[1,128,512]{2,1,0:T(8,128)(2,1)S(1)}, bf16[1,128,512]{2,1,0:T(8,128)(2,1)S(1)}, u32[]{:S(2)}, u32[]{:S(2)}) collective-permute-start(bf16[1,128,512]{2,1,0:T(8,128)(2,1)S(1)} %get-tuple-element.120.refs_3_), channel_id=1, source_target_pairs={{0,1},{1,0},{2,3},{3,2},{4,5},{5,4},{6,7},{7,6},{8,9},{9,8},{10,11... | collective-permute-start | bytes 393224 | tf_op jit(solution)/shard_map/core_kv/ppermute | solution.py:960
  24.1 1.3 collective-permute-start.5
  34.9 4.6 %collective-permute-start.6 = (bf16[192,128]{1,0:T(8,128)(2,1)S(1)}, bf16[192,128]{1,0:T(8,128)(2,1)S(1)}, u32[]{:S(2)}, u32[]{:S(2)}) collective-permute-start(bf16[192,128]{1,0:T(8,128)(2,1)S(1)} %get-tuple-element.124), channel_id=1, source_target_pairs={{0,2},{2,0},{4,6},{6,4},{1,3},{3,1},{5,7},{7,5},{8,10},{10,8},{12,... | collective-permute-start | bytes 147464 | tf_op jit(solution)/shard_map/chip_attn/ppermute | solution.py:964
  35.4 5.5 %collective-permute-start.7 = (bf16[192,128]{1,0:T(8,128)(2,1)S(1)}, bf16[192,128]{1,0:T(8,128)(2,1)S(1)}, u32[]{:S(2)}, u32[]{:S(2)}) collective-permute-start(bf16[192,128]{1,0:T(8,128)(2,1)S(1)} %get-tuple-element.125), channel_id=1, source_target_pairs={{0,4},{2,6},{4,0},{6,2},{1,5},{3,7},{5,1},{7,3},{8,12},{10,14},{12... | collective-permute-start | bytes 147464 | tf_op jit(solution)/shard_map/chip_attn/ppermute | solution.py:964
  37.4 5.9 %collective-permute-start.8 = (bf16[192,128]{1,0:T(8,128)(2,1)S(1)}, bf16[192,128]{1,0:T(8,128)(2,1)S(1)}, u32[]{:S(2)}, u32[]{:S(2)}) collective-permute-start(bf16[192,128]{1,0:T(8,128)(2,1)S(1)} %get-tuple-element.126), channel_id=1, source_target_pairs={{0,6},{2,4},{4,2},{6,0},{1,7},{3,5},{5,3},{7,1},{8,14},{10,12},{12... | collective-permute-start | bytes 147464 | tf_op jit(solution)/shard_map/chip_attn/ppermute | solution.py:964
  53.0 6.3 %copy-start.39 = (bf16[128,768]{1,0:T(8,128)(2,1)S(1)}, bf16[128,768]{1,0:T(8,128)(2,1)}, u32[]{:S(2)}) copy-start(bf16[128,768]{1,0:T(8,128)(2,1)} %copy-done.38) | copy-start | bytes 589828
  53.0 6.3 %copy-start.66 = (f32[768]{0:T(1024)S(1)}, f32[768]{0:T(1024)}, u32[]{:S(2)}) copy-start(f32[768]{0:T(1024)} %b2.1) | copy-start | bytes 9220
  53.0 6.3 %copy-start.68 = (f32[768]{0:T(1024)S(1)}, f32[768]{0:T(1024)}, u32[]{:S(2)}) copy-start(f32[768]{0:T(1024)} %g3.1) | copy-start | bytes 9220
  53.0 6.3 %copy-start.70 = (f32[768]{0:T(1024)S(1)}, f32[768]{0:T(1024)}, u32[]{:S(2)}) copy-start(f32[768]{0:T(1024)} %b3.1) | copy-start | bytes 9220
  56.2 15.2 %collective-permute-start.10 = (bf16[128,768]{1,0:T(8,128)(2,1)S(1)}, bf16[128,768]{1,0:T(8,128)(2,1)S(1)}, u32[]{:S(2)}, u32[]{:S(2)}) collective-permute-start(bf16[128,768]{1,0:T(8,128)(2,1)S(1)} %get-tuple-element.147), channel_id=1, source_target_pairs={{0,16},{8,24},{16,0},{24,8},{1,17},{9,25},{17,1},{25,9},{2,18},{10... | collective-permute-start | bytes 589832 | tf_op jit(solution)/shard_map/plane_act/ppermute | solution.py:964
  57.8 14.4 %collective-permute-start.9 = (bf16[128,768]{1,0:T(8,128)(2,1)S(1)}, bf16[128,768]{1,0:T(8,128)(2,1)S(1)}, u32[]{:S(2)}, u32[]{:S(2)}) collective-permute-start(bf16[128,768]{1,0:T(8,128)(2,1)S(1)} %get-tuple-element.146), channel_id=1, source_target_pairs={{0,8},{8,0},{16,24},{24,16},{1,9},{9,1},{17,25},{25,17},{2,10},{10... | collective-permute-start | bytes 589832 | tf_op jit(solution)/shard_map/plane_act/ppermute | solution.py:964
  72.8 9.5 %copy-start.74 = (bf16[128,768]{1,0:T(8,128)(2,1)S(1)}, bf16[128,768]{1,0:T(8,128)(2,1)}, u32[]{:S(2)}) copy-start(bf16[128,768]{1,0:T(8,128)(2,1)} %copy-done.73) | copy-start | bytes 589828
  72.8 12.5 %copy-start.79 = (bf16[192,128]{1,0:T(8,128)(2,1)S(1)}, bf16[192,128]{1,0:T(8,128)(2,1)}, u32[]{:S(2)}) copy-start(bf16[192,128]{1,0:T(8,128)(2,1)} %copy-done.78) | copy-start | bytes 147460
  72.8 13.2 %copy-start.77 = (bf16[192,128]{1,0:T(8,128)(2,1)S(1)}, bf16[192,128]{1,0:T(8,128)(2,1)}, u32[]{:S(2)}) copy-start(bf16[192,128]{1,0:T(8,128)(2,1)} %copy-done.76) | copy-start | bytes 147460
  72.8 4.1 %collective-permute-start.11 = (bf16[192,128]{1,0:T(8,128)(2,1)S(1)}, bf16[192,128]{1,0:T(8,128)(2,1)S(1)}, u32[]{:S(2)}, u32[]{:S(2)}) collective-permute-start(bf16[192,128]{1,0:T(8,128)(2,1)S(1)} %get-tuple-element.154), channel_id=1, source_target_pairs={{0,2},{2,0},{4,6},{6,4},{1,3},{3,1},{5,7},{7,5},{8,10},{10,8},{12,... | collective-permute-start | bytes 147464 | tf_op jit(solution)/shard_map/chip_grad/ppermute | solution.py:964
  77.6 77.9 %all-to-all-start.2 = ((bf16[4,128,2560]{2,1,0:T(8,128)(2,1)}), bf16[4,128,2560]{2,1,0:T(8,128)(2,1)}, u32[]{:S(2)}, u32[]{:S(2)}) async-start(bf16[4,128,2560]{2,1,0:T(8,128)(2,1)} %copy-done.6), calls=%async_computation.2 | async-start | bytes 5242880 | tf_op jit(solution)/shard_map/plane_back/all_to_all | solution.py:972
  82.4 37.5 %copy-start.14 = (f32[4,128,256]{2,1,0:T(8,128)S(1)}, f32[4,128,256]{2,1,0:T(8,128)}, u32[]{:S(2)}) copy-start(f32[4,128,256]{2,1,0:T(8,128)} %copy-done.13) | copy-start | bytes 1572868
  82.4 37.5 %copy-start.16 = (bf16[4,128,512]{2,1,0:T(8,128)(2,1)S(1)}, bf16[4,128,512]{2,1,0:T(8,128)(2,1)}, u32[]{:S(2)}) copy-start(bf16[4,128,512]{2,1,0:T(8,128)(2,1)} %copy-done.15) | copy-start | bytes 1572868
  82.4 37.5 %copy-start.18 = (bf16[4,128,512]{2,1,0:T(8,128)(2,1)S(1)}, bf16[4,128,512]{2,1,0:T(8,128)(2,1)}, u32[]{:S(2)}) copy-start(bf16[4,128,512]{2,1,0:T(8,128)(2,1)} %copy-done.17) | copy-start | bytes 1572868
  82.4 33.0 %collective-permute-start.15 = (bf16[128,768]{1,0:T(8,128)(2,1)S(1)}, bf16[128,768]{1,0:T(8,128)(2,1)S(1)}, u32[]{:S(2)}, u32[]{:S(2)}) collective-permute-start(bf16[128,768]{1,0:T(8,128)(2,1)S(1)} %copy-done.74), channel_id=1, source_target_pairs={{0,24},{8,16},{16,8},{24,0},{1,25},{9,17},{17,9},{25,1},{2,26},{10... | collective-permute-start | bytes 589832 | tf_op jit(solution)/shard_map/plane_act/ppermute | solution.py:964
  85.3 30.1 %collective-permute-start.12 = (bf16[192,128]{1,0:T(8,128)(2,1)S(1)}, bf16[192,128]{1,0:T(8,128)(2,1)S(1)}, u32[]{:S(2)}, u32[]{:S(2)}) collective-permute-start(bf16[192,128]{1,0:T(8,128)(2,1)S(1)} %copy-done.79), channel_id=1, source_target_pairs={{0,4},{2,6},{4,0},{6,2},{1,5},{3,7},{5,1},{7,3},{8,12},{10,14},{12... | collective-permute-start | bytes 147464 | tf_op jit(solution)/shard_map/chip_grad/ppermute | solution.py:964
  86.0 29.4 %collective-permute-start.13 = (bf16[192,128]{1,0:T(8,128)(2,1)S(1)}, bf16[192,128]{1,0:T(8,128)(2,1)S(1)}, u32[]{:S(2)}, u32[]{:S(2)}) collective-permute-start(bf16[192,128]{1,0:T(8,128)(2,1)S(1)} %copy-done.77), channel_id=1, source_target_pairs={{0,6},{2,4},{4,2},{6,0},{1,7},{3,5},{5,3},{7,1},{8,14},{10,12},{12... | collective-permute-start | bytes 147464 | tf_op jit(solution)/shard_map/chip_grad/ppermute | solution.py:964
  119.7 8.8 %collective-permute-start.16 = (bf16[4,96,768]{2,1,0:T(8,128)(2,1)S(1)}, bf16[4,96,768]{2,1,0:T(8,128)(2,1)S(1)}, u32[]{:S(2)}, u32[]{:S(2)}) collective-permute-start(bf16[4,96,768]{2,1,0:T(8,128)(2,1)S(1)} %get-tuple-element.169), channel_id=1, source_target_pairs={{0,1},{1,0},{2,3},{3,2},{4,5},{5,4},{6,7},{7,6},{8,9},{9,8},{10,11... | collective-permute-start | bytes 1769480 | tf_op jit(solution)/shard_map/core_down/ppermute | solution.py:960
  128.0 2.1 %collective-permute-start.14 = (bf16[4,128,512]{2,1,0:T(8,128)(2,1)S(1)}, bf16[4,128,512]{2,1,0:T(8,128)(2,1)S(1)}, u32[]{:S(2)}, u32[]{:S(2)}) collective-permute-start(bf16[4,128,512]{2,1,0:T(8,128)(2,1)S(1)} %get-tuple-element.159), channel_id=1, source_target_pairs={{0,1},{1,0},{2,3},{3,2},{4,5},{5,4},{6,7},{7,6},{8,9},{9,8},{10,11... | collective-permute-start | bytes 1572872 | tf_op jit(solution)/shard_map/core_grad/ppermute | solution.py:960
  134.0 20.5 %collective-permute-start.20 = (bf16[4,96,768]{2,1,0:T(8,128)(2,1)S(1)}, bf16[4,96,768]{2,1,0:T(8,128)(2,1)S(1)}, u32[]{:S(2)}, u32[]{:S(2)}) collective-permute-start(bf16[4,96,768]{2,1,0:T(8,128)(2,1)S(1)} %get-tuple-element.183), channel_id=1, source_target_pairs={{0,1},{1,0},{2,3},{3,2},{4,5},{5,4},{6,7},{7,6},{8,9},{9,8},{10,11... | collective-permute-start | bytes 1769480 | tf_op jit(solution)/shard_map/core_w/ppermute | solution.py:960
  134.5 13.0 %collective-permute-start.21 = (bf16[2,96,768]{2,1,0:T(8,128)(2,1)S(1)}, bf16[2,96,768]{2,1,0:T(8,128)(2,1)S(1)}, u32[]{:S(2)}, u32[]{:S(2)}) collective-permute-start(bf16[2,96,768]{2,1,0:T(8,128)(2,1)S(1)} %get-tuple-element.184), channel_id=1, source_target_pairs={{0,2},{2,0},{4,6},{6,4},{1,3},{3,1},{5,7},{7,5},{8,10},{10,8},{12,... | collective-permute-start | bytes 884744 | tf_op jit(solution)/shard_map/down_sum/ppermute | solution.py:964
  134.7 15.1 %collective-permute-start.17 = (bf16[576,128]{1,0:T(8,128)(2,1)S(1)}, bf16[576,128]{1,0:T(8,128)(2,1)S(1)}, u32[]{:S(2)}, u32[]{:S(2)}) collective-permute-start(bf16[576,128]{1,0:T(8,128)(2,1)S(1)} %get-tuple-element.174), channel_id=1, source_target_pairs={{0,2},{2,0},{4,6},{6,4},{1,3},{3,1},{5,7},{7,5},{8,10},{10,8},{12,... | collective-permute-start | bytes 442376 | tf_op jit(solution)/shard_map/chip_qkv/ppermute | solution.py:964
  136.5 13.3 %collective-permute-start.18 = (bf16[576,128]{1,0:T(8,128)(2,1)S(1)}, bf16[576,128]{1,0:T(8,128)(2,1)S(1)}, u32[]{:S(2)}, u32[]{:S(2)}) collective-permute-start(bf16[576,128]{1,0:T(8,128)(2,1)S(1)} %get-tuple-element.175), channel_id=1, source_target_pairs={{0,4},{2,6},{4,0},{6,2},{1,5},{3,7},{5,1},{7,3},{8,12},{10,14},{12... | collective-permute-start | bytes 442376 | tf_op jit(solution)/shard_map/chip_qkv/ppermute | solution.py:964
  137.9 15.9 %collective-permute-start.19 = (bf16[576,128]{1,0:T(8,128)(2,1)S(1)}, bf16[576,128]{1,0:T(8,128)(2,1)S(1)}, u32[]{:S(2)}, u32[]{:S(2)}) collective-permute-start(bf16[576,128]{1,0:T(8,128)(2,1)S(1)} %get-tuple-element.176), channel_id=1, source_target_pairs={{0,6},{2,4},{4,2},{6,0},{1,7},{3,5},{5,3},{7,1},{8,14},{10,12},{12... | collective-permute-start | bytes 442376 | tf_op jit(solution)/shard_map/chip_qkv/ppermute | solution.py:964
  158.3 2.4 %collective-permute-start.22 = (bf16[4,128,768]{2,1,0:T(8,128)(2,1)S(1)}, bf16[4,128,768]{2,1,0:T(8,128)(2,1)S(1)}, u32[]{:S(2)}, u32[]{:S(2)}) collective-permute-start(bf16[4,128,768]{2,1,0:T(8,128)(2,1)S(1)} %get-tuple-element.192), channel_id=1, source_target_pairs={{0,1},{1,0},{2,3},{3,2},{4,5},{5,4},{6,7},{7,6},{8,9},{9,8},{10,11... | collective-permute-start | bytes 2359304 | tf_op jit(solution)/shard_map/core_up/ppermute | solution.py:960
  160.7 26.8 %copy-start.41 = (bf16[576,128]{1,0:T(8,128)(2,1)S(1)}, bf16[576,128]{1,0:T(8,128)(2,1)}, u32[]{:S(2)}) copy-start(bf16[576,128]{1,0:T(8,128)(2,1)} %copy-done.40) | copy-start | bytes 442372
  163.0 14.6 %collective-permute-start.26 = (bf16[2,128,768]{2,1,0:T(8,128)(2,1)}, bf16[2,128,768]{2,1,0:T(8,128)(2,1)}, u32[]{:S(2)}, u32[]{:S(2)}) collective-permute-start(bf16[2,128,768]{2,1,0:T(8,128)(2,1)} %get-tuple-element.193), channel_id=1, source_target_pairs={{0,2},{2,0},{4,6},{6,4},{1,3},{3,1},{5,7},{7,5},{8,10},{10,8},{12,... | collective-permute-start | bytes 1179656 | tf_op jit(solution)/shard_map/up_sum/ppermute | solution.py:964
  163.0 24.5 %copy-start.8 = (bf16[768,768]{1,0:T(8,128)(2,1)S(1)}, bf16[768,768]{1,0:T(8,128)(2,1)}, u32[]{:S(2)}) copy-start(bf16[768,768]{1,0:T(8,128)(2,1)} %refs_8_.3) | copy-start | bytes 3538948
  163.0 19.4 %all-to-all-start.1 = ((bf16[4,96,768]{2,1,0:T(8,128)(2,1)}), bf16[4,96,768]{2,1,0:T(8,128)(2,1)S(1)}, u32[]{:S(2)}, u32[]{:S(2)}) async-start(bf16[4,96,768]{2,1,0:T(8,128)(2,1)} %spread.1), calls=%async_computation.1 | async-start | bytes 1179648 | tf_op jit(solution)/shard_map/plane_w/all_to_all | solution.py:972
  166.6 20.9 %copy-start.7 = (bf16[768,768]{1,0:T(8,128)(2,1)S(1)}, bf16[768,768]{1,0:T(8,128)(2,1)}, u32[]{:S(2)}) copy-start(bf16[768,768]{1,0:T(8,128)(2,1)} %refs_9_.3) | copy-start | bytes 3538948
  166.6 8.8 %collective-permute-start.27 = (bf16[1,96,768]{2,1,0:T(8,128)(2,1)}, bf16[1,96,768]{2,1,0:T(8,128)(2,1)S(1)}, u32[]{:S(2)}, u32[]{:S(2)}) collective-permute-start(bf16[1,96,768]{2,1,0:T(8,128)(2,1)} %copy-done.75), channel_id=1, source_target_pairs={{0,4},{2,6},{4,0},{6,2},{1,5},{3,7},{5,1},{7,3},{8,12},{10,14},{12... | collective-permute-start | bytes 442376 | tf_op jit(solution)/shard_map/down_sum/ppermute | solution.py:964
  181.2 14.8 %collective-permute-start.28 = (bf16[1,128,768]{2,1,0:T(8,128)(2,1)}, bf16[1,128,768]{2,1,0:T(8,128)(2,1)S(1)}, u32[]{:S(2)}, u32[]{:S(2)}) collective-permute-start(bf16[1,128,768]{2,1,0:T(8,128)(2,1)} %get-tuple-element.208), channel_id=1, source_target_pairs={{0,4},{2,6},{4,0},{6,2},{1,5},{3,7},{5,1},{7,3},{8,12},{10,14},{12... | collective-permute-start | bytes 589832 | tf_op jit(solution)/shard_map/up_sum/ppermute | solution.py:964
  183.0 13.0 %collective-permute-start.23 = (bf16[24,768]{1,0:T(8,128)(2,1)S(1)}, bf16[24,768]{1,0:T(8,128)(2,1)S(1)}, u32[]{:S(2)}, u32[]{:S(2)}) collective-permute-start(bf16[24,768]{1,0:T(8,128)(2,1)S(1)} %get-tuple-element.196), channel_id=1, source_target_pairs={{0,2},{2,0},{4,6},{6,4},{1,3},{3,1},{5,7},{7,5},{8,10},{10,8},{12,... | collective-permute-start | bytes 110600 | tf_op jit(solution)/shard_map/chip_w/ppermute | solution.py:964
  183.8 12.2 %collective-permute-start.24 = (bf16[24,768]{1,0:T(8,128)(2,1)S(1)}, bf16[24,768]{1,0:T(8,128)(2,1)S(1)}, u32[]{:S(2)}, u32[]{:S(2)}) collective-permute-start(bf16[24,768]{1,0:T(8,128)(2,1)S(1)} %get-tuple-element.197), channel_id=1, source_target_pairs={{0,4},{2,6},{4,0},{6,2},{1,5},{3,7},{5,1},{7,3},{8,12},{10,14},{12... | collective-permute-start | bytes 110600 | tf_op jit(solution)/shard_map/chip_w/ppermute | solution.py:964
  185.0 11.0 %collective-permute-start.25 = (bf16[24,768]{1,0:T(8,128)(2,1)S(1)}, bf16[24,768]{1,0:T(8,128)(2,1)S(1)}, u32[]{:S(2)}, u32[]{:S(2)}) collective-permute-start(bf16[24,768]{1,0:T(8,128)(2,1)S(1)} %get-tuple-element.198), channel_id=1, source_target_pairs={{0,6},{2,4},{4,2},{6,0},{1,7},{3,5},{5,3},{7,1},{8,14},{10,12},{12... | collective-permute-start | bytes 110600 | tf_op jit(solution)/shard_map/chip_w/ppermute | solution.py:964
  196.7 8.4 %all-to-all-start.3 = ((bf16[4,24,768]{2,1,0:T(8,128)(2,1)}), bf16[4,24,768]{2,1,0:T(8,128)(2,1)S(1)}, u32[]{:S(2)}, u32[]{:S(2)}) async-start(bf16[4,24,768]{2,1,0:T(8,128)(2,1)} %get-tuple-element.215), calls=%async_computation.3 | async-start | bytes 294912 | tf_op jit(solution)/shard_map/plane_rows/all_to_all | solution.py:972
  (65 other events, 94.8 us)

commit v4 on v2

--- a/solution.py
+++ b/solution.py
@@ -637,36 +637,25 @@
     return jnp.concatenate([unpack(scr[k], rows, live) for k in range(len(pieces))], axis=1)
 
 
-def norms_call(place, pieces, layer_in, vectors, w_out, parts, live):
+def norms_call(place, pieces, layer_in, vectors, w_out, live):
     count, rows = len(pieces), layer_in.shape[0]
     model = w_out.shape[0]
-    quarter = model // parts
-    pad_q = -(-quarter // 128) * 128
 
     def body(place_ref, *refs):
-        in_ref, g2, b2, g3, b3, wo_ref, mid_ref, attn_ref = refs[count : count + 8]
-        msgs, (n2_scr, piece_scr) = refs[count + 8 : count + 8 + parts], refs[count + 8 + parts :]
+        in_ref, g2, b2, g3, b3, wo_ref, mid_ref, attn_ref, n3_ref, piece_scr = refs[count:]
         attn = gather_heads(place_ref, refs[:count], piece_scr, rows, live)
         attn_ref[...] = attn
         unit2, _ = unit_norm(attn.astype(F32))
         normed2 = (unit2 * row(g2) + row(b2)).astype(BF16)
-        for r in range(parts):
-            n2_scr[r, :, :quarter] = normed2[:, r * quarter : (r + 1) * quarter]
-            if pad_q > quarter:
-                n2_scr[r, :, quarter:] = jnp.zeros((rows, pad_q - quarter), BF16)
         middle = in_ref[...].astype(F32) + mm(normed2, wo_ref[...], NN)
         mid_ref[...] = middle
         unit3, _ = unit_norm(middle)
-        normed3 = (unit3 * row(g3) + row(b3)).astype(BF16)
-        for k in range(parts):
-            msgs[k][:, :model] = normed3
-            msgs[k][:, model:] = n2_scr[place_ref[2] ^ k]
-
-    outs = (shape(F32, rows, model), shape(BF16, rows, model)) + (shape(BF16, rows, model + pad_q),) * parts
+        n3_ref[...] = (unit3 * row(g3) + row(b3)).astype(BF16)
+
+    outs = (shape(F32, rows, model), shape(BF16, rows, model), shape(BF16, rows, model))
     operands = (*pieces, layer_in, *vectors, w_out)
-    scratch = (shape(BF16, parts, rows, pad_q), shape(BF16, count, *pieces[0].shape))
-    mid, attn, *msgs = kernel(body, outs, (place,), operands, scratch, micros=1.5, name="norms")
-    return mid, attn, msgs
+    scratch = (shape(BF16, count, *pieces[0].shape),)
+    return kernel(body, outs, (place,), operands, scratch, micros=1.5, name="norms")
 
 
 def up_call(place, normed3, w_up, parts):
@@ -674,7 +663,7 @@
     part = hidden // parts
 
     def body(place_ref, n3_ref, wu_ref, act_ref, slope_ref, *msgs):
-        normed = n3_ref[:, :model]
+        normed = n3_ref[...]
         for r in range(parts):
             upper = mm(normed, wu_ref[:, r * part : (r + 1) * part], NN)
             cumulative = 0.5 * (1.0 + lax.erf(upper * 0.7071067811865476))
@@ -689,10 +678,15 @@
     return act, slope, msgs
 
 
+def padded_quarter(quarter):
+    return -(-(quarter + 64) // 128) * 128
+
+
 def backward_call(place, attn, middle, act, slope, grad_out, vectors, w_out, w_up, w_down, parts, count, live):
     rows = attn.shape[0]
     model, hidden = w_up.shape
     part, quarter = hidden // parts, model // parts
+    pad_q = padded_quarter(quarter)
     message = shape(BF16, packed_rows(rows, live), 128)
 
     def body(
@@ -700,7 +694,7 @@
         out_ref, gmid_ref, *rest,
     ):
         msgs, heads = rest[:parts], rest[parts : parts + count]
-        up_scr, table_scr, head_scr = rest[parts + count :]
+        up_scr, n2_scr, head_scr = rest[parts + count :]
         here = place_ref[2]
         go = go_ref[...]
         middle = mid_ref[...]
@@ -730,24 +724,32 @@
             jnp.sum(grad3 * unit3, axis=0, keepdims=True),
             jnp.sum(grad3, axis=0, keepdims=True),
         ]
-        table = jnp.concatenate(sums + [jnp.zeros((12, model), F32)], axis=0).astype(BF16)
+        table = jnp.concatenate(sums + [jnp.zeros((4, model), F32)], axis=0)
+        normed2 = (unit2 * row(g2) + row(b2)).astype(BF16)
+        normed3 = (unit3 * row(g3) + row(b3)).astype(BF16)
+        spare, lines = pad_q - quarter, quarter // 64
         for r in range(parts):
-            table_scr[r, :, :quarter] = table[:, r * quarter : (r + 1) * quarter]
+            chunks = [table[:, r * quarter + 64 * j : r * quarter + 64 * (j + 1)] for j in range(lines)]
+            side = jnp.concatenate(chunks + [jnp.zeros((rows - 8 * lines, 64), F32)], axis=0).astype(BF16)
+            pieces = [normed2[:, r * quarter : (r + 1) * quarter], side]
+            if spare > 64:
+                pieces.append(jnp.zeros((rows, spare - 64), BF16))
+            n2_scr[r] = jnp.concatenate(pieces, axis=1)
         for k in range(parts):
-            msgs[k][:rows, :part] = up_scr[here ^ k]
-            msgs[k][:rows, part:] = proj
-            msgs[k][rows:, :] = jnp.zeros((16, part + model), BF16)
-            msgs[k][rows:, part : part + quarter] = table_scr[here ^ k, :, :quarter]
+            msgs[k][:, :part] = up_scr[here ^ k]
+            msgs[k][:, part : part + model] = proj
+            msgs[k][:, part + model : part + 2 * model] = normed3
+            msgs[k][:, part + 2 * model :] = n2_scr[here ^ k]
 
     outs = (
         shape(BF16, rows, model),
         shape(F32, rows, model),
     )
-    outs += (shape(BF16, rows + 16, part + model),) * parts + (message,) * count
+    outs += (shape(BF16, rows, part + 2 * model + pad_q),) * parts + (message,) * count
     operands = (attn, middle, act, slope, grad_out, *vectors, w_out, w_up, w_down)
     scratch = (
         shape(BF16, parts, rows, part),
-        shape(BF16, parts, 16, -(-quarter // 128) * 128),
+        shape(BF16, parts, rows, pad_q),
         shape(BF16, count, *message.shape),
     )
     found = kernel(body, outs, (place,), operands, scratch, micros=9.0, name="token_backward")
@@ -775,26 +777,27 @@
     return kernel(body, outs, (place,), (*acts, *grads), scratch, micros=3.0, name="grad_down")
 
 
-def up_grad_call(place, sent, back, chips, part, model):
-    parts = len(sent)
-    rows = sent[0].shape[0]
+def up_grad_call(place, back, chips, part, model):
+    parts = len(back)
     quarter = model // parts
     own = model // (parts * chips * 2)
     tall = (parts + 1) * own + 8
 
     def body(place_ref, *refs):
-        sent_refs, back_refs = refs[:parts], refs[parts : 2 * parts]
-        keep_ref, send_ref, up_scr, out_scr, vec_scr = refs[2 * parts :]
+        back_refs = refs[:parts]
+        keep_ref, send_ref, up_scr, out_scr, vec_scr = refs[parts:]
         core = place_ref[1]
-        normed3 = jnp.concatenate([ref[:, :model] for ref in sent_refs], axis=0)
-        normed2 = jnp.concatenate([ref[:, model:] for ref in sent_refs], axis=0)
-        grad_up = jnp.concatenate([ref[:rows, :part] for ref in back_refs], axis=0)
-        proj = jnp.concatenate([ref[:rows, part:] for ref in back_refs], axis=0)
+        ends = (0, part, part + model, part + 2 * model, back_refs[0].shape[1])
+        grad_up, proj, normed3, normed2 = (
+            jnp.concatenate([ref[:, lo:hi] for ref in back_refs], axis=0) for lo, hi in zip(ends, ends[1:])
+        )
         up_scr[...] = mm(normed3, grad_up, TN).reshape(parts, chips, 2, own, part)
         out_scr[...] = mm(normed2, proj, TN)[:quarter].reshape(chips, 2, own, model)
-        table = jnp.zeros((8, quarter), F32)
+        lines = quarter // 64
+        side = jnp.zeros((8 * lines, 64), F32)
         for ref in back_refs:
-            table = table + ref[rows:, part : part + quarter].astype(F32)[:8]
+            side = side + ref[:, ends[3] + quarter : ends[3] + quarter + 64].astype(F32)[: 8 * lines]
+        table = jnp.concatenate([side[8 * j : 8 * (j + 1)] for j in range(lines)], axis=1)
         vec_scr[...] = jnp.zeros_like(vec_scr)
         for k in range(chips):
             for side in range(2):
@@ -811,7 +814,7 @@
         shape(F32, chips, 2, own, model),
         shape(F32, chips, 2, 8, model),
     )
-    return kernel(body, outs, (place,), (*sent, *back), scratch, micros=4.0, name="grad_up_out")
+    return kernel(body, outs, (place,), tuple(back), scratch, micros=4.0, name="grad_up_out")
 
 
 def qkv_grad_call(place, groups, units, grads, gain, bias, weight, parts, live, width):
@@ -978,7 +981,8 @@
 
 
 def trade(messages, axis):
-    return [messages[0]] + [swap(messages[k], axis, k) for k in range(1, len(messages))]
+    found = {k: swap(messages[k], axis, k) for k in range(len(messages) - 1, 0, -1)}
+    return [messages[0]] + [found[k] for k in range(1, len(messages))]
 
 
 def gather_chips(block, chips):
@@ -997,6 +1001,10 @@
         arrived = swap(away, "chip", bit)
         bit *= 2
     return keep, arrived
+
+
+def after(values, *others):
+    return lax.optimization_barrier((values, others))[0]
 
 
 def fast_shards(
@@ -1033,70 +1041,79 @@
         place, doc_lengths, groups, queries, kv_own, kv_other, heads_here
     )
     fence = lax.optimization_barrier
-    messages, grad_out = fence((messages, grad_out))
     with scope("chip_attn"):
         pieces = trade(messages, "chip")
     with scope("plane_out"):
         grads_plane = trade([grad_out] * parts, "rows")
-    pieces, grads_plane = fence((pieces, grads_plane))
+    pieces = after(pieces, grads_plane)
 
     vectors = (ln2_gain, ln2_bias, ln3_gain, ln3_bias)
-    middle, attn, sent = norms_call(place, pieces, layer_in, vectors, w_out, parts, live)
-    act, slope, acts = up_call(place, sent[0], w_up, parts)
-    with scope("plane_norms"):
-        sent = trade(sent, "rows")
+    middle, attn, normed3 = norms_call(place, pieces, layer_in, vectors, w_out, live)
+    act, slope, acts = up_call(place, normed3, w_up, parts)
     with scope("plane_act"):
         acts = trade(acts, "rows")
     output, grad_mid, back, messages = backward_call(
         place, attn, middle, act, slope, grad_out, vectors, w_out, w_up, w_down, parts, chips, live
     )
+    back = after(back, acts[1:])
     with scope("chip_grad"):
         grad_heads = trade(messages, "chip")
-    grad_heads, sent = fence((grad_heads, sent))
+    with scope("plane_back"):
+        far = [swap(back[k], "rows", k) for k in range(3, parts)]
     grad_q, grad_kv, grad_kv_other = attend_back_call(
         place, queries, kv_own, kv_other, prob, attn_heads, grad_heads, heads_here
     )
-    grad_kv_other, acts = fence((grad_kv_other, acts))
-    down_keep, down_send = down_grad_call(place, acts, grads_plane, chips)
     with scope("core_grad"):
         grad_kv_other = swap_core(grad_kv_other)
+    down_keep, down_send = down_grad_call(place, after(acts, grad_q), grads_plane, chips)
+    grad_kv_other, down_send, far = fence((grad_kv_other, down_send, far))
     with scope("core_down"):
         down_recv = swap_core(down_send)
+    with scope("plane_back"):
+        near = after(back[1:3], far)
+        back = back[:1] + [swap(near[k], "rows", k + 1) for k in range(len(near))] + far
     grad_qkv, messages = join_call(place, grad_q, grad_kv, grad_kv_other, live)
-    down_keep, down_away = halve_call(place, down_keep, down_recv, 1)
-    messages, down_away, back, grad_qkv = fence((messages, down_away, back, grad_qkv))
+    with scope("down_sum"):
+        down_keep, down_away = halve_call(place, down_keep, after(down_recv, grad_qkv), 1)
+        grad_qkv, down_away = fence((grad_qkv, down_away))
+        down_recv = swap(down_away, "chip", 1)
     with scope("chip_qkv"):
         grad_pieces = trade(messages, "chip")
-    with scope("plane_back"):
-        back = trade(back, "rows")
-    with scope("down_one"):
-        down_recv = swap(down_away, "chip", 1)
     qkv_keep, qkv_send = qkv_grad_call(
         place, groups, units, grad_qkv, ln1_gain, ln1_bias, w_heads, parts, live, width
     )
-    qkv_send, down_recv, grad_pieces, back = fence((qkv_send, down_recv, grad_pieces, back))
-    up_keep, up_send = up_grad_call(place, sent, back, chips, part, model)
     with scope("core_w"):
         qkv_send = swap_core(qkv_send)
+    qkv_send = after(qkv_send, (grad_pieces, down_recv))
+    qkv_sums = spread_call(place, qkv_keep, qkv_send)
+    with scope("down_sum"):
+        down_keep, down_last = scatter_chips(place, down_keep, down_recv, chips, 2)
+    back = after(back, (down_keep, qkv_sums))
+    up_keep, up_send = up_grad_call(place, back, chips, part, model)
+    with scope("plane_w"):
+        traded = trade(qkv_sums, "rows")
     with scope("core_up"):
         up_recv = swap_core(up_send)
-    with scope("down_two"):
-        down_keep, down_last = scatter_chips(place, down_keep, down_recv, chips, 2)
-    with scope("plane_w"):
-        qkv_sums = trade(spread_call(place, qkv_keep, qkv_send), "rows")
+    up_keep, up_away = halve_call(place, up_keep, up_recv, 1)
     with scope("up_sum"):
-        up_keep, up_last = scatter_chips(place, up_keep, up_recv, chips, 1)
+        up_recv = swap(up_away, "chip", 1)
+    traded = after(traded, up_away)
     with scope("chip_w"):
-        qkv_all = trade(share_call(place, qkv_sums, chips), "chip")
+        shared = share_call(place, traded, chips)
+        qkv_all = trade(shared, "chip")
+    grad_inputs = input_grad_call(
+        place, grad_pieces, layer_in, grad_mid, ln1_gain, w_query, w_key, w_value, live
+    )
+    gwd = finish_down_call(down_keep, down_last)
+    up_recv = after(up_recv, (down_last, traded))
+    with scope("up_sum"):
+        up_keep, up_last = scatter_chips(place, up_keep, up_recv, chips, 2)
+    up_last = after(up_last, (qkv_all, gwd, grad_inputs))
     gwo, g2, b2, g3, b3, *up_rows = finish_up_call(place, up_keep, up_last, parts, own, part)
     with scope("plane_rows"):
         up_rows = trade(up_rows, "rows")
     gwq, gwk, gwv, g1, b1 = finish_qkv_call(place, qkv_all, model, live, width)
     gwu = place_up_call(place, up_rows)
-    gwd = finish_down_call(down_keep, down_last)
-    grad_inputs = input_grad_call(
-        place, grad_pieces, layer_in, grad_mid, ln1_gain, w_query, w_key, w_value, live
-    )
     return (
         output[None], grad_inputs[None], g1, b1, gwq, gwk, gwv, g2, b2, gwo, g3, b3, gwu, gwd,
     )
@@ -1105,7 +1122,7 @@
 def takes_fast(mesh):
     seq, parts = mesh.shape["seq"], mesh.shape["rows"]
     chips = seq // 2
-    return seq % 2 == 0 and chips & (chips - 1) == 0 and parts & (parts - 1) == 0 and HEADS % max(chips, 1) == 0
+    return seq % 2 == 0 and chips & (chips - 1) == 0 and parts in (1, 2, 4) and HEADS % max(chips, 1) == 0
 
 
 def solution(mesh):

time: 148 us -> 145 us (0.980)
  starting transfers between devices: 62.1 us -> 51.4 us
  waiting for transfers between devices: 43.3 us -> 51.5 us
    ppermute x37 -> x34, starting transfers between devices: 60.3 us -> 50.4 us  [swap(): lax.ppermute(value, axis, [(k, k ^ bit) for k in range(lax.axis_size(axis...]
    ppermute x37 -> x34, waiting for transfers between devices: 38.6 us -> 47.5 us  [swap(): lax.ppermute(value, axis, [(k, k ^ bit) for k in range(lax.axis_size(axis...]
  transfers between devices with their start and end apart: 44 -> 41, of which waited for: 17 -> 18; matrix products, arithmetic and copies ran while one was open for 2% -> 2% of each run, Pallas kernels for 18% -> 20%
where the time goes in v4:
time: 145 us
  waiting for transfers between devices  51.5 us (36%)
  starting transfers between devices  51.4 us (35%)
  Pallas kernels  37.4 us (26%)
  local copies, waits for them, and re-layouts  3.65 us (3%)
    ppermute x34, starting transfers between devices, swap(): lax.ppermute(value, axis, [(k, k ^ bit) for k in range(lax.axis_size(axis...  50.4 us
    ppermute x34, waiting for transfers between devices, swap(): lax.ppermute(value, axis, [(k, k ^ bit) for k in range(lax.axis_size(axis...  47.5 us
    pallas_call x24, Pallas kernels, kernel(): pl.pallas_call(body, out_shape=outs if single else listed, in_specs=[smem...  37.4 us
    ppermute x7, waiting for transfers between devices, swap_core(): return lax.ppermute(value, 'core', [(0, 1), (1, 0)])  4 us
  transfers between devices with their start and end apart: 41, of which 18 were waited for; matrix products, arithmetic and copies ran while one was open for 2% of the time, Pallas kernels for 20%

profile of v4, /device:TPU:0, one launch (start us, length us, event | category | flops | bytes accessed | tf_op | source)
XLA Modules:
  0.0 145.2 jit_solution(17472901112153842167)
XLA Ops:
  0.7 4.1 %collective-permute-start.1 = (bf16[128,768]{1,0:T(8,128)(2,1)}, bf16[128,768]{1,0:T(8,128)(2,1)S(1)}, u32[]{:S(2)}, u32[]{:S(2)}) collective-permute-start(bf16[128,768]{1,0:T(8,128)(2,1)} %bitcast.7), channel_id=1, source_target_pairs={{0,4},{2,6},{4,0},{6,2},{1,5},{3,7},{5,1},{7,3},{8,12},{10,14},{12... | collective-permute-start | bytes 589832 | tf_op jit(solution)/shard_map/gather_in/ppermute | solution.py:980
  4.8 1.6 %collective-permute-start = (bf16[128,768]{1,0:T(8,128)(2,1)}, bf16[128,768]{1,0:T(8,128)(2,1)S(1)}, u32[]{:S(2)}, u32[]{:S(2)}) collective-permute-start(bf16[128,768]{1,0:T(8,128)(2,1)} %bitcast.8), channel_id=1, source_target_pairs={{0,2},{2,0},{4,6},{6,4},{1,3},{3,1},{5,7},{7,5},{8,10},{10,8},{12,... | collective-permute-start | bytes 589832 | tf_op jit(solution)/shard_map/gather_in/ppermute | solution.py:980
  6.4 1.2 constant_dynamic-slice_fusion.2
  7.6 1.6 %constant_dynamic-slice_fusion = (bf16[768,192]{1,0:T(8,128)(2,1)S(1)}, bf16[768,192]{1,0:T(8,128)(2,1)S(1)}) fusion(bf16[768,768]{1,0:T(8,128)(2,1)} %refs_9_.3, s32[]{:T(128)S(6)} %select_n.2, bf16[768,768]{1,0:T(8,128)(2,1)} %refs_8_.3), kind=kLoop, calls=%fused_computation.10 | loop fusion | bytes 1179652 | tf_op jit(solution)/shard_map/dynamic_slice | solution.py:1027
  9.2 5.0 %collective-permute-done.1.refs_1_ = bf16[128,768]{1,0:T(8,128)(2,1)S(1)} collective-permute-done((bf16[128,768]{1,0:T(8,128)(2,1)}, bf16[128,768]{1,0:T(8,128)(2,1)S(1)}, u32[]{:S(2)}, u32[]{:S(2)}) %collective-permute-start.1) | collective-permute-done | bytes 196640 | tf_op jit(solution)/shard_map/gather_in/ppermute | solution.py:980
  18.4 2.5 %collective-permute-start.11 = (bf16[128,768]{1,0:T(8,128)(2,1)S(1)}, bf16[128,768]{1,0:T(8,128)(2,1)S(1)}, u32[]{:S(2)}, u32[]{:S(2)}) collective-permute-start(bf16[128,768]{1,0:T(8,128)(2,1)S(1)} %mask_grad.1.go_ref.refs_4_), channel_id=1, source_target_pairs={{0,24},{8,16},{16,8},{24,0},{1,25},{9,17},{17,9},{25,1},{2,26},{10... | collective-permute-start | bytes 589832 | tf_op jit(solution)/shard_map/plane_out/ppermute | solution.py:980
  22.6 1.3 collective-permute-done.5.refs_8_
  23.9 4.3 %attend.1 = (f32[4,128,256]{2,1,0:T(8,128)S(1)}, bf16[4,2,384,512]{3,2,1,0:T(8,128)(2,1)S(1)}, bf16[4,128,256]{2,1,0:T(8,128)(2,1)S(1)}, bf16[4,128,512]{2,1,0:T...) custom-call(s32[3]{0:T(128)S(1)} %pad_add_fusion.place_ref, ...), custom_call_target="tpu_custom_call" | custom-call | flops 6000000 | bytes 6000 | tf_op jit(solution)/shard_map/attend/pallas_call | solution.py:350
  28.2 1.4 collective-permute-start.6
  29.5 3.3 %collective-permute-start.7 = (bf16[192,128]{1,0:T(8,128)(2,1)S(1)}, bf16[192,128]{1,0:T(8,128)(2,1)S(1)}, u32[]{:S(2)}, u32[]{:S(2)}) collective-permute-start(bf16[192,128]{1,0:T(8,128)(2,1)S(1)} %get-tuple-element.139), channel_id=1, source_target_pairs={{0,4},{2,6},{4,0},{6,2},{1,5},{3,7},{5,1},{7,3},{8,12},{10,14},{12... | collective-permute-start | bytes 147464 | tf_op jit(solution)/shard_map/chip_attn/ppermute | solution.py:980
  33.0 2.9 %collective-permute-done.7.refs_2_ = bf16[192,128]{1,0:T(8,128)(2,1)S(1)} collective-permute-done((bf16[192,128]{1,0:T(8,128)(2,1)S(1)}, bf16[192,128]{1,0:T(8,128)(2,1)S(1)}, u32[]{:S(2)}, u32[]{:S(2)}) %collective-permute-start.7) | collective-permute-done | bytes 49184 | tf_op jit(solution)/shard_map/chip_attn/ppermute | solution.py:980
  35.9 2.8 %collective-permute-done.8.refs_3_ = bf16[192,128]{1,0:T(8,128)(2,1)S(1)} collective-permute-done((bf16[192,128]{1,0:T(8,128)(2,1)S(1)}, bf16[192,128]{1,0:T(8,128)(2,1)S(1)}, u32[]{:S(2)}, u32[]{:S(2)}) %collective-permute-start.8) | collective-permute-done | bytes 49184 | tf_op jit(solution)/shard_map/chip_attn/ppermute | solution.py:980
  38.7 1.4 norms.1
  40.1 1.9 %up_gelu.1 = (bf16[4,128,768]{2,1,0:T(8,128)(2,1)S(1)}, bf16[4,128,768]{2,1,0:T(8,128)(2,1)S(1)}, bf16[128,768]{1,0:T(8,128)(2,1)S(1)}, bf16[128,768]{1,0:T(8,12...) custom-call(s32[3]{0:T(128)S(1)} %pad_add_fusion.place_ref, ...), custom_call_target="tpu_custom_call" | custom-call | flops 2000000 | bytes 2000 | tf_op jit(solution)/shard_map/up_gelu/pallas_call | solution.py:350
  42.7 1.5 %collective-permute-start.17 = (bf16[128,768]{1,0:T(8,128)(2,1)S(1)}, bf16[128,768]{1,0:T(8,128)(2,1)S(1)}, u32[]{:S(2)}, u32[]{:S(2)}) collective-permute-start(bf16[128,768]{1,0:T(8,128)(2,1)S(1)} %get-tuple-element.166), channel_id=1, source_target_pairs={{0,16},{8,24},{16,0},{24,8},{1,17},{9,25},{17,1},{25,9},{2,18},{10... | collective-permute-start | bytes 589832 | tf_op jit(solution)/shard_map/plane_act/ppermute | solution.py:980
  44.2 1.4 collective-permute-start.18
  45.6 6.0 %token_backward.1 = (bf16[128,768]{1,0:T(8,128)(2,1)}, f32[128,768]{1,0:T(8,128)S(1)}, bf16[128,2560]{1,0:T(8,128)(2,1)S(1)}, bf16[128,2560]{1,0:T(8,128)(2,1)S(...) custom-call(s32[3]{0:T(128)S(1)} %pad_add_fusion.place_ref, ...), custom_call_target="tpu_custom_call" | custom-call | flops 9000000 | bytes 9000 | tf_op jit(solution)/shard_map/token_backward/pallas_call | solution.py:350
  52.6 1.8 %collective-permute-start.19 = (bf16[128,2560]{1,0:T(8,128)(2,1)S(1)}, bf16[128,2560]{1,0:T(8,128)(2,1)S(1)}, u32[]{:S(2)}, u32[]{:S(2)}) collective-permute-start(bf16[128,2560]{1,0:T(8,128)(2,1)S(1)} %get-tuple-element.177), channel_id=1, source_target_pairs={{0,24},{8,16},{16,8},{24,0},{1,25},{9,17},{17,9},{25,1},{2,26},{10... | collective-permute-start | bytes 1966088 | tf_op jit(solution)/shard_map/plane_back/ppermute | solution.py:980
  54.6 1.4 collective-permute-start.13
  56.0 2.8 %collective-permute-start.14 = (bf16[192,128]{1,0:T(8,128)(2,1)S(1)}, bf16[192,128]{1,0:T(8,128)(2,1)S(1)}, u32[]{:S(2)}, u32[]{:S(2)}) collective-permute-start(bf16[192,128]{1,0:T(8,128)(2,1)S(1)} %get-tuple-element.160), channel_id=1, source_target_pairs={{0,6},{2,4},{4,2},{6,0},{1,7},{3,5},{5,3},{7,1},{8,14},{10,12},{12... | collective-permute-start | bytes 147464 | tf_op jit(solution)/shard_map/chip_grad/ppermute | solution.py:980
  59.6 2.3 %collective-permute-done.14.refs_3_ = bf16[192,128]{1,0:T(8,128)(2,1)S(1)} collective-permute-done((bf16[192,128]{1,0:T(8,128)(2,1)S(1)}, bf16[192,128]{1,0:T(8,128)(2,1)S(1)}, u32[]{:S(2)}, u32[]{:S(2)}) %collective-permute-start.14) | collective-permute-done | bytes 49184 | tf_op jit(solution)/shard_map/chip_grad/ppermute | solution.py:980
  61.9 3.8 %attend_back.1 = (bf16[4,128,256]{2,1,0:T(8,128)(2,1)S(1)}, f32[4,128,512]{2,1,0:T(8,128)S(1)}, bf16[4,128,512]{2,1,0:T(8,128)(2,1)S(1)}) custom-call(s32[3]{0:T(128)S(1)} %pad_add_fusion.place_ref, bf16[4,128,256]{2,1,0:T(8,128)(2,1)S(1)} %get-tuple-element.152.q_ref, bf16[4,128,512]{2,1,0:T(8,128)(2,1)S(1)} %get-tuple-element.153.own_ref, ...), custom_call_target="tpu_custom_call" | custom-call | flops 6000000 | bytes 6000 | tf_op jit(solution)/shard_map/attend_back/pallas_call | solution.py:350
  65.8 1.5 %grad_down.1 = (f32[4,96,768]{2,1,0:T(8,128)S(1)}, bf16[4,96,768]{2,1,0:T(8,128)(2,1)S(1)}) custom-call(s32[3]{0:T(128)S(1)} %pad_add_fusion.place_ref, bf16[128,768]{1,0:T(8,128)(2,1)S(1)} %get-tuple-element.168.refs_0_, bf16[128,768]{1,0:T(8,128)(2,1)S(1)} %collective-permute-done.16.refs_1_, bf16[128,768]{1,0:T(8,128)(2,1)S(1)} %collective-permute-done.17.refs_2_, ...), custom_call_target="tpu_custom_call" | custom-call | flops 3000000 | bytes 3000 | tf_op jit(solution)/shard_map/grad_down/pallas_call | solution.py:350
  67.9 1.4 collective-permute-start.29
  71.4 2.5 %grad_qkv.1 = (f32[4,96,768]{2,1,0:T(8,128)S(1)}, bf16[4,96,768]{2,1,0:T(8,128)(2,1)S(1)}) custom-call(s32[3]{0:T(128)S(1)} %pad_add_fusion.place_ref, bf16[1,128,768]{2,1,0:T(8,128)(2,1)S(1)} %get-tuple-element.184.refs_0_, bf16[2,128,768]{2,1,0:T(8,128)(2,1)S(1)} %get-tuple-element.185.refs_1_, bf16[1,128,768]{2,1,0:T(8,128)(2,1)S(1)} %get-tuple-element.186.refs_2_, ...), custom_call_target="tpu_custom_call" | custom-call | flops 4000000 | bytes 4000 | tf_op jit(solution)/shard_map/grad_qkv/pallas_call | solution.py:350
  74.0 1.6 %collective-permute-start.25 = (bf16[2,96,768]{2,1,0:T(8,128)(2,1)S(1)}, bf16[2,96,768]{2,1,0:T(8,128)(2,1)S(1)}, u32[]{:S(2)}, u32[]{:S(2)}) collective-permute-start(bf16[2,96,768]{2,1,0:T(8,128)(2,1)S(1)} %get-tuple-element.195), channel_id=1, source_target_pairs={{0,2},{2,0},{4,6},{6,4},{1,3},{3,1},{5,7},{7,5},{8,10},{10,8},{12,... | collective-permute-start | bytes 884744 | tf_op jit(solution)/shard_map/down_sum/ppermute | solution.py:980
  76.1 10.5 %collective-permute-done.20.refs_1_ = bf16[576,128]{1,0:T(8,128)(2,1)S(1)} collective-permute-done((bf16[576,128]{1,0:T(8,128)(2,1)S(1)}, bf16[576,128]{1,0:T(8,128)(2,1)S(1)}, u32[]{:S(2)}, u32[]{:S(2)}) %collective-permute-start.20) | collective-permute-done | bytes 147488 | tf_op jit(solution)/shard_map/chip_qkv/ppermute | solution.py:980
  86.5 1.9 %collective-permute-start.21 = (bf16[576,128]{1,0:T(8,128)(2,1)S(1)}, bf16[576,128]{1,0:T(8,128)(2,1)S(1)}, u32[]{:S(2)}, u32[]{:S(2)}) collective-permute-start(bf16[576,128]{1,0:T(8,128)(2,1)S(1)} %get-tuple-element.181), channel_id=1, source_target_pairs={{0,4},{2,6},{4,0},{6,2},{1,5},{3,7},{5,1},{7,3},{8,12},{10,14},{12... | collective-permute-start | bytes 442376 | tf_op jit(solution)/shard_map/chip_qkv/ppermute | solution.py:980
  88.4 2.0 %collective-permute-start.22 = (bf16[576,128]{1,0:T(8,128)(2,1)S(1)}, bf16[576,128]{1,0:T(8,128)(2,1)S(1)}, u32[]{:S(2)}, u32[]{:S(2)}) collective-permute-start(bf16[576,128]{1,0:T(8,128)(2,1)S(1)} %get-tuple-element.182), channel_id=1, source_target_pairs={{0,6},{2,4},{4,2},{6,0},{1,7},{3,5},{5,3},{7,1},{8,14},{10,12},{12... | collective-permute-start | bytes 442376 | tf_op jit(solution)/shard_map/chip_qkv/ppermute | solution.py:980
  91.1 9.1 %collective-permute-done.21.refs_2_ = bf16[576,128]{1,0:T(8,128)(2,1)S(1)} collective-permute-done((bf16[576,128]{1,0:T(8,128)(2,1)S(1)}, bf16[576,128]{1,0:T(8,128)(2,1)S(1)}, u32[]{:S(2)}, u32[]{:S(2)}) %collective-permute-start.21) | collective-permute-done | bytes 147488 | tf_op jit(solution)/shard_map/chip_qkv/ppermute | solution.py:980
  100.9 1.7 %grad_up_out.1 = (f32[4,128,768]{2,1,0:T(8,128)S(1)}, bf16[4,128,768]{2,1,0:T(8,128)(2,1)S(1)}) custom-call(s32[3]{0:T(128)S(1)} %pad_add_fusion.place_ref, bf16[128,2560]{1,0:T(8,128)(2,1)S(1)} %get-tuple-element.209.refs_0_, bf16[128,2560]{1,0:T(8,128)(2,1)S(1)} %collective-permute-done.29.refs_1_, bf16[128,2560]{1,0:T(8,128)(2,1)S(1)} %collective-permute-done.30.refs_2_, ...), custom_call_target="tpu_custom_call" | custom-call | flops 4000000 | bytes 4000 | tf_op jit(solution)/shard_map/grad_up_out/pallas_call | solution.py:350
  102.7 2.3 %collective-permute-done.31.in_ref = bf16[4,128,768]{2,1,0:T(8,128)(2,1)S(1)} collective-permute-done((bf16[4,128,768]{2,1,0:T(8,128)(2,1)S(1)}, bf16[4,128,768]{2,1,0:T(8,128)(2,1)S(1)}, u32[]{:S(2)}, u32[]{:S(2)}) %collective-permute-start.31) | collective-permute-done | bytes 786464 | tf_op jit(solution)/shard_map/core_up/ppermute | solution.py:976
  105.6 2.7 %collective-permute-start.35 = (bf16[2,128,768]{2,1,0:T(8,128)(2,1)S(1)}, bf16[2,128,768]{2,1,0:T(8,128)(2,1)S(1)}, u32[]{:S(2)}, u32[]{:S(2)}) collective-permute-start(bf16[2,128,768]{2,1,0:T(8,128)(2,1)S(1)} %get-tuple-element.215), channel_id=1, source_target_pairs={{0,2},{2,0},{4,6},{6,4},{1,3},{3,1},{5,7},{7,5},{8,10},{10,8},{12,... | collective-permute-start | bytes 1179656 | tf_op jit(solution)/shard_map/up_sum/ppermute | solution.py:980
  108.3 1.8 %collective-permute-start.26 = (bf16[96,768]{1,0:T(8,128)(2,1)S(1)}, bf16[96,768]{1,0:T(8,128)(2,1)S(1)}, u32[]{:S(2)}, u32[]{:S(2)}) collective-permute-start(bf16[96,768]{1,0:T(8,128)(2,1)S(1)} %get-tuple-element.198), channel_id=1, source_target_pairs={{0,8},{8,0},{16,24},{24,16},{1,9},{9,1},{17,25},{25,17},{2,10},{10... | collective-permute-start | bytes 442376 | tf_op jit(solution)/shard_map/plane_w/ppermute | solution.py:980
  110.3 1.5 %collective-permute-start.28 = (bf16[96,768]{1,0:T(8,128)(2,1)S(1)}, bf16[96,768]{1,0:T(8,128)(2,1)S(1)}, u32[]{:S(2)}, u32[]{:S(2)}) collective-permute-start(bf16[96,768]{1,0:T(8,128)(2,1)S(1)} %get-tuple-element.200), channel_id=1, source_target_pairs={{0,24},{8,16},{16,8},{24,0},{1,25},{9,17},{17,9},{25,1},{2,26},{10... | collective-permute-start | bytes 442376 | tf_op jit(solution)/shard_map/plane_w/ppermute | solution.py:980
  112.9 1.6 %collective-permute-done.26.refs_1_ = bf16[96,768]{1,0:T(8,128)(2,1)S(1)} collective-permute-done((bf16[96,768]{1,0:T(8,128)(2,1)S(1)}, bf16[96,768]{1,0:T(8,128)(2,1)S(1)}, u32[]{:S(2)}, u32[]{:S(2)}) %collective-permute-start.26) | collective-permute-done | bytes 147488 | tf_op jit(solution)/shard_map/plane_w/ppermute | solution.py:980
  114.5 4.1 %collective-permute-done.27.refs_2_ = bf16[96,768]{1,0:T(8,128)(2,1)S(1)} collective-permute-done((bf16[96,768]{1,0:T(8,128)(2,1)S(1)}, bf16[96,768]{1,0:T(8,128)(2,1)S(1)}, u32[]{:S(2)}, u32[]{:S(2)}) %collective-permute-start.27) | collective-permute-done | bytes 147488 | tf_op jit(solution)/shard_map/plane_w/ppermute | solution.py:980
  118.6 1.6 %collective-permute-done.36.in_ref = bf16[1,96,768]{2,1,0:T(8,128)(2,1)S(1)} collective-permute-done((bf16[1,96,768]{2,1,0:T(8,128)(2,1)S(1)}, bf16[1,96,768]{2,1,0:T(8,128)(2,1)S(1)}, u32[]{:S(2)}, u32[]{:S(2)}) %collective-permute-start.36) | collective-permute-done | bytes 147488 | tf_op jit(solution)/shard_map/down_sum/ppermute | solution.py:980
  121.6 2.7 %collective-permute-start.37 = (bf16[1,128,768]{2,1,0:T(8,128)(2,1)S(1)}, bf16[1,128,768]{2,1,0:T(8,128)(2,1)S(1)}, u32[]{:S(2)}, u32[]{:S(2)}) collective-permute-start(bf16[1,128,768]{2,1,0:T(8,128)(2,1)S(1)} %get-tuple-element.233), channel_id=1, source_target_pairs={{0,4},{2,6},{4,0},{6,2},{1,5},{3,7},{5,1},{7,3},{8,12},{10,14},{12... | collective-permute-start | bytes 589832 | tf_op jit(solution)/shard_map/up_sum/ppermute | solution.py:980
  125.4 2.6 %collective-permute-start.33 = (bf16[24,768]{1,0:T(8,128)(2,1)S(1)}, bf16[24,768]{1,0:T(8,128)(2,1)S(1)}, u32[]{:S(2)}, u32[]{:S(2)}) collective-permute-start(bf16[24,768]{1,0:T(8,128)(2,1)S(1)} %get-tuple-element.222), channel_id=1, source_target_pairs={{0,4},{2,6},{4,0},{6,2},{1,5},{3,7},{5,1},{7,3},{8,12},{10,14},{12... | collective-permute-start | bytes 110600 | tf_op jit(solution)/shard_map/chip_w/ppermute | solution.py:980
  128.0 1.4 collective-permute-start.34
  129.4 2.7 %grad_inputs.1 = bf16[128,768]{1,0:T(8,128)(2,1)} custom-call(s32[3]{0:T(128)S(1)} %pad_add_fusion.place_ref, bf16[576,128]{1,0:T(8,128)(2,1)S(1)} %get-tuple-element.179.refs_0_, bf16[576,128]{1,0:T(8,128)(2,1)S(1)} %collective-permute-done.20.refs_1_, bf16[576,128]{1,0:T(8,128)(2,1)S(1)} %collective-permute-done.21.refs_2_, ...), custom_call_target="tpu_custom_call" | custom-call | flops 3000000 | bytes 3000 | tf_op jit(solution)/shard_map/grad_inputs/pallas_call | solution.py:350
  132.9 3.0 %collective-permute-done.33.refs_2_ = bf16[24,768]{1,0:T(8,128)(2,1)S(1)} collective-permute-done((bf16[24,768]{1,0:T(8,128)(2,1)S(1)}, bf16[24,768]{1,0:T(8,128)(2,1)S(1)}, u32[]{:S(2)}, u32[]{:S(2)}) %collective-permute-start.33) | collective-permute-done | bytes 36896 | tf_op jit(solution)/shard_map/chip_w/ppermute | solution.py:980
  135.9 1.2 finish_up.1
  137.1 1.8 %collective-permute-start.38 = (bf16[24,768]{1,0:T(8,128)(2,1)S(1)}, bf16[24,768]{1,0:T(8,128)(2,1)S(1)}, u32[]{:S(2)}, u32[]{:S(2)}) collective-permute-start(bf16[24,768]{1,0:T(8,128)(2,1)S(1)} %get-tuple-element.241), channel_id=1, source_target_pairs={{0,8},{8,0},{16,24},{24,16},{1,9},{9,1},{17,25},{25,17},{2,10},{10... | collective-permute-start | bytes 110600 | tf_op jit(solution)/shard_map/plane_rows/ppermute | solution.py:980
  139.1 1.5 %collective-permute-start.40 = (bf16[24,768]{1,0:T(8,128)(2,1)S(1)}, bf16[24,768]{1,0:T(8,128)(2,1)S(1)}, u32[]{:S(2)}, u32[]{:S(2)}) collective-permute-start(bf16[24,768]{1,0:T(8,128)(2,1)S(1)} %get-tuple-element.243), channel_id=1, source_target_pairs={{0,24},{8,16},{16,8},{24,0},{1,25},{9,17},{17,9},{25,1},{2,26},{10... | collective-permute-start | bytes 110600 | tf_op jit(solution)/shard_map/plane_rows/ppermute | solution.py:980
  140.6 1.3 finish_qkv.1
  144.0 1.3 place_up.1
  (92 shorter events, 20.7 us)
Async XLA Ops:
  0.7 13.5 %collective-permute-start.1 = (bf16[128,768]{1,0:T(8,128)(2,1)}, bf16[128,768]{1,0:T(8,128)(2,1)S(1)}, u32[]{:S(2)}, u32[]{:S(2)}) collective-permute-start(bf16[128,768]{1,0:T(8,128)(2,1)} %bitcast.7), channel_id=1, source_target_pairs={{0,4},{2,6},{4,0},{6,2},{1,5},{3,7},{5,1},{7,3},{8,12},{10,14},{12... | collective-permute-start | bytes 589832 | tf_op jit(solution)/shard_map/gather_in/ppermute | solution.py:980
  4.8 11.7 %collective-permute-start = (bf16[128,768]{1,0:T(8,128)(2,1)}, bf16[128,768]{1,0:T(8,128)(2,1)S(1)}, u32[]{:S(2)}, u32[]{:S(2)}) collective-permute-start(bf16[128,768]{1,0:T(8,128)(2,1)} %bitcast.8), channel_id=1, source_target_pairs={{0,2},{2,0},{4,6},{6,4},{1,3},{3,1},{5,7},{7,5},{8,10},{10,8},{12,... | collective-permute-start | bytes 589832 | tf_op jit(solution)/shard_map/gather_in/ppermute | solution.py:980
  14.2 7.2 %collective-permute-start.2 = (bf16[128,768]{1,0:T(8,128)(2,1)S(1)}, bf16[128,768]{1,0:T(8,128)(2,1)S(1)}, u32[]{:S(2)}, u32[]{:S(2)}) collective-permute-start(bf16[128,768]{1,0:T(8,128)(2,1)S(1)} %collective-permute-done.1.refs_1_), channel_id=1, source_target_pairs={{0,2},{2,0},{4,6},{6,4},{1,3},{3,1},{5,7},{7,5},{8,10},{10,8},{12,... | collective-permute-start | bytes 589832 | tf_op jit(solution)/shard_map/gather_in/ppermute | solution.py:980
  16.4 6.1 %collective-permute-start.3 = (bf16[1,128,512]{2,1,0:T(8,128)(2,1)S(1)}, bf16[1,128,512]{2,1,0:T(8,128)(2,1)S(1)}, u32[]{:S(2)}, u32[]{:S(2)}) collective-permute-start(bf16[1,128,512]{2,1,0:T(8,128)(2,1)S(1)} %get-tuple-element.134.refs_3_), channel_id=1, source_target_pairs={{0,1},{1,0},{2,3},{3,2},{4,5},{5,4},{6,7},{7,6},{8,9},{9,8},{10,11... | collective-permute-start | bytes 393224 | tf_op jit(solution)/shard_map/core_kv/ppermute | solution.py:976
  16.5 22.2 %copy-start.1 = (bf16[768,768]{1,0:T(8,128)(2,1)S(1)}, bf16[768,768]{1,0:T(8,128)(2,1)}, u32[]{:S(2)}) copy-start(bf16[768,768]{1,0:T(8,128)(2,1)} %wo_ref.1) | copy-start | bytes 3538948
  16.5 22.2 %copy-start.10 = (f32[768]{0:T(1024)S(1)}, f32[768]{0:T(1024)}, u32[]{:S(2)}) copy-start(f32[768]{0:T(1024)} %g2.1) | copy-start | bytes 9220
  16.5 22.2 %copy-start.11 = (f32[768]{0:T(1024)S(1)}, f32[768]{0:T(1024)}, u32[]{:S(2)}) copy-start(f32[768]{0:T(1024)} %b2.1) | copy-start | bytes 9220
  16.5 23.6 %copy-start = (bf16[768,3072]{1,0:T(8,128)(2,1)S(1)}, bf16[768,3072]{1,0:T(8,128)(2,1)}, u32[]{:S(2)}) copy-start(bf16[768,3072]{1,0:T(8,128)(2,1)} %wu_ref.3) | copy-start | bytes 14155780
  17.3 5.3 %collective-permute-start.4 = (bf16[2,128,512]{2,1,0:T(8,128)(2,1)S(1)}, bf16[2,128,512]{2,1,0:T(8,128)(2,1)S(1)}, u32[]{:S(2)}, u32[]{:S(2)}) collective-permute-start(bf16[2,128,512]{2,1,0:T(8,128)(2,1)S(1)} %get-tuple-element.135.refs_4_), channel_id=1, source_target_pairs={{0,1},{1,0},{2,3},{3,2},{4,5},{5,4},{6,7},{7,6},{8,9},{9,8},{10,11... | collective-permute-start | bytes 786440 | tf_op jit(solution)/shard_map/core_kv/ppermute | solution.py:976
  18.4 14.4 %collective-permute-start.11 = (bf16[128,768]{1,0:T(8,128)(2,1)S(1)}, bf16[128,768]{1,0:T(8,128)(2,1)S(1)}, u32[]{:S(2)}, u32[]{:S(2)}) collective-permute-start(bf16[128,768]{1,0:T(8,128)(2,1)S(1)} %mask_grad.1.go_ref.refs_4_), channel_id=1, source_target_pairs={{0,24},{8,16},{16,8},{24,0},{1,25},{9,17},{17,9},{25,1},{2,26},{10... | collective-permute-start | bytes 589832 | tf_op jit(solution)/shard_map/plane_out/ppermute | solution.py:980
  20.9 12.1 %collective-permute-start.10 = (bf16[128,768]{1,0:T(8,128)(2,1)S(1)}, bf16[128,768]{1,0:T(8,128)(2,1)S(1)}, u32[]{:S(2)}, u32[]{:S(2)}) collective-permute-start(bf16[128,768]{1,0:T(8,128)(2,1)S(1)} %mask_grad.1.go_ref.refs_4_), channel_id=1, source_target_pairs={{0,16},{8,24},{16,0},{24,8},{1,17},{9,25},{17,1},{25,9},{2,18},{10... | collective-permute-start | bytes 589832 | tf_op jit(solution)/shard_map/plane_out/ppermute | solution.py:980
  21.4 11.5 %collective-permute-start.9 = (bf16[128,768]{1,0:T(8,128)(2,1)S(1)}, bf16[128,768]{1,0:T(8,128)(2,1)S(1)}, u32[]{:S(2)}, u32[]{:S(2)}) collective-permute-start(bf16[128,768]{1,0:T(8,128)(2,1)S(1)} %mask_grad.1.go_ref.refs_4_), channel_id=1, source_target_pairs={{0,8},{8,0},{16,24},{24,16},{1,9},{9,1},{17,25},{25,17},{2,10},{10... | collective-permute-start | bytes 589832 | tf_op jit(solution)/shard_map/plane_out/ppermute | solution.py:980
  22.5 1.4 collective-permute-start.5
  28.2 4.8 %collective-permute-start.6 = (bf16[192,128]{1,0:T(8,128)(2,1)S(1)}, bf16[192,128]{1,0:T(8,128)(2,1)S(1)}, u32[]{:S(2)}, u32[]{:S(2)}) collective-permute-start(bf16[192,128]{1,0:T(8,128)(2,1)S(1)} %get-tuple-element.138), channel_id=1, source_target_pairs={{0,2},{2,0},{4,6},{6,4},{1,3},{3,1},{5,7},{7,5},{8,10},{10,8},{12,... | collective-permute-start | bytes 147464 | tf_op jit(solution)/shard_map/chip_attn/ppermute | solution.py:980
  29.5 6.4 %collective-permute-start.7 = (bf16[192,128]{1,0:T(8,128)(2,1)S(1)}, bf16[192,128]{1,0:T(8,128)(2,1)S(1)}, u32[]{:S(2)}, u32[]{:S(2)}) collective-permute-start(bf16[192,128]{1,0:T(8,128)(2,1)S(1)} %get-tuple-element.139), channel_id=1, source_target_pairs={{0,4},{2,6},{4,0},{6,2},{1,5},{3,7},{5,1},{7,3},{8,12},{10,14},{12... | collective-permute-start | bytes 147464 | tf_op jit(solution)/shard_map/chip_attn/ppermute | solution.py:980
  32.8 5.9 %collective-permute-start.8 = (bf16[192,128]{1,0:T(8,128)(2,1)S(1)}, bf16[192,128]{1,0:T(8,128)(2,1)S(1)}, u32[]{:S(2)}, u32[]{:S(2)}) collective-permute-start(bf16[192,128]{1,0:T(8,128)(2,1)S(1)} %get-tuple-element.140), channel_id=1, source_target_pairs={{0,6},{2,4},{4,2},{6,0},{1,7},{3,5},{5,3},{7,1},{8,14},{10,12},{12... | collective-permute-start | bytes 147464 | tf_op jit(solution)/shard_map/chip_attn/ppermute | solution.py:980
  42.0 9.6 %collective-permute-start.16 = (bf16[128,768]{1,0:T(8,128)(2,1)S(1)}, bf16[128,768]{1,0:T(8,128)(2,1)S(1)}, u32[]{:S(2)}, u32[]{:S(2)}) collective-permute-start(bf16[128,768]{1,0:T(8,128)(2,1)S(1)} %get-tuple-element.165), channel_id=1, source_target_pairs={{0,8},{8,0},{16,24},{24,16},{1,9},{9,1},{17,25},{25,17},{2,10},{10... | collective-permute-start | bytes 589832 | tf_op jit(solution)/shard_map/plane_act/ppermute | solution.py:980
  42.7 9.0 %collective-permute-start.17 = (bf16[128,768]{1,0:T(8,128)(2,1)S(1)}, bf16[128,768]{1,0:T(8,128)(2,1)S(1)}, u32[]{:S(2)}, u32[]{:S(2)}) collective-permute-start(bf16[128,768]{1,0:T(8,128)(2,1)S(1)} %get-tuple-element.166), channel_id=1, source_target_pairs={{0,16},{8,24},{16,0},{24,8},{1,17},{9,25},{17,1},{25,9},{2,18},{10... | collective-permute-start | bytes 589832 | tf_op jit(solution)/shard_map/plane_act/ppermute | solution.py:980
  44.2 8.4 %collective-permute-start.18 = (bf16[128,768]{1,0:T(8,128)(2,1)S(1)}, bf16[128,768]{1,0:T(8,128)(2,1)S(1)}, u32[]{:S(2)}, u32[]{:S(2)}) collective-permute-start(bf16[128,768]{1,0:T(8,128)(2,1)S(1)} %get-tuple-element.167), channel_id=1, source_target_pairs={{0,24},{8,16},{16,8},{24,0},{1,25},{9,17},{17,9},{25,1},{2,26},{10... | collective-permute-start | bytes 589832 | tf_op jit(solution)/shard_map/plane_act/ppermute | solution.py:980
  52.6 15.1 %collective-permute-start.19 = (bf16[128,2560]{1,0:T(8,128)(2,1)S(1)}, bf16[128,2560]{1,0:T(8,128)(2,1)S(1)}, u32[]{:S(2)}, u32[]{:S(2)}) collective-permute-start(bf16[128,2560]{1,0:T(8,128)(2,1)S(1)} %get-tuple-element.177), channel_id=1, source_target_pairs={{0,24},{8,16},{16,8},{24,0},{1,25},{9,17},{17,9},{25,1},{2,26},{10... | collective-permute-start | bytes 1966088 | tf_op jit(solution)/shard_map/plane_back/ppermute | solution.py:980
  54.4 4.4 %collective-permute-start.12 = (bf16[192,128]{1,0:T(8,128)(2,1)S(1)}, bf16[192,128]{1,0:T(8,128)(2,1)S(1)}, u32[]{:S(2)}, u32[]{:S(2)}) collective-permute-start(bf16[192,128]{1,0:T(8,128)(2,1)S(1)} %get-tuple-element.158), channel_id=1, source_target_pairs={{0,2},{2,0},{4,6},{6,4},{1,3},{3,1},{5,7},{7,5},{8,10},{10,8},{12,... | collective-permute-start | bytes 147464 | tf_op jit(solution)/shard_map/chip_grad/ppermute | solution.py:980
  54.6 5.0 %collective-permute-start.13 = (bf16[192,128]{1,0:T(8,128)(2,1)S(1)}, bf16[192,128]{1,0:T(8,128)(2,1)S(1)}, u32[]{:S(2)}, u32[]{:S(2)}) collective-permute-start(bf16[192,128]{1,0:T(8,128)(2,1)S(1)} %get-tuple-element.159), channel_id=1, source_target_pairs={{0,4},{2,6},{4,0},{6,2},{1,5},{3,7},{5,1},{7,3},{8,12},{10,14},{12... | collective-permute-start | bytes 147464 | tf_op jit(solution)/shard_map/chip_grad/ppermute | solution.py:980
  56.0 5.9 %collective-permute-start.14 = (bf16[192,128]{1,0:T(8,128)(2,1)S(1)}, bf16[192,128]{1,0:T(8,128)(2,1)S(1)}, u32[]{:S(2)}, u32[]{:S(2)}) collective-permute-start(bf16[192,128]{1,0:T(8,128)(2,1)S(1)} %get-tuple-element.160), channel_id=1, source_target_pairs={{0,6},{2,4},{4,2},{6,0},{1,7},{3,5},{5,3},{7,1},{8,14},{10,12},{12... | collective-permute-start | bytes 147464 | tf_op jit(solution)/shard_map/chip_grad/ppermute | solution.py:980
  65.7 2.0 %collective-permute-start.15 = (bf16[4,128,512]{2,1,0:T(8,128)(2,1)S(1)}, bf16[4,128,512]{2,1,0:T(8,128)(2,1)S(1)}, u32[]{:S(2)}, u32[]{:S(2)}) collective-permute-start(bf16[4,128,512]{2,1,0:T(8,128)(2,1)S(1)} %get-tuple-element.163), channel_id=1, source_target_pairs={{0,1},{1,0},{2,3},{3,2},{4,5},{5,4},{6,7},{7,6},{8,9},{9,8},{10,11... | collective-permute-start | bytes 1572872 | tf_op jit(solution)/shard_map/core_grad/ppermute | solution.py:976
  67.7 3.0 %collective-permute-start.23 = (bf16[4,96,768]{2,1,0:T(8,128)(2,1)S(1)}, bf16[4,96,768]{2,1,0:T(8,128)(2,1)S(1)}, u32[]{:S(2)}, u32[]{:S(2)}) collective-permute-start(bf16[4,96,768]{2,1,0:T(8,128)(2,1)S(1)} %get-tuple-element.189), channel_id=1, source_target_pairs={{0,1},{1,0},{2,3},{3,2},{4,5},{5,4},{6,7},{7,6},{8,9},{9,8},{10,11... | collective-permute-start | bytes 1769480 | tf_op jit(solution)/shard_map/core_down/ppermute | solution.py:976
  67.9 33.0 %collective-permute-start.29 = (bf16[128,2560]{1,0:T(8,128)(2,1)S(1)}, bf16[128,2560]{1,0:T(8,128)(2,1)S(1)}, u32[]{:S(2)}, u32[]{:S(2)}) collective-permute-start(bf16[128,2560]{1,0:T(8,128)(2,1)S(1)} %get-tuple-element.205), channel_id=1, source_target_pairs={{0,8},{8,0},{16,24},{24,16},{1,9},{9,1},{17,25},{25,17},{2,10},{10... | collective-permute-start | bytes 1966088 | tf_op jit(solution)/shard_map/plane_back/ppermute | solution.py:980
  69.3 31.6 %collective-permute-start.30 = (bf16[128,2560]{1,0:T(8,128)(2,1)S(1)}, bf16[128,2560]{1,0:T(8,128)(2,1)S(1)}, u32[]{:S(2)}, u32[]{:S(2)}) collective-permute-start(bf16[128,2560]{1,0:T(8,128)(2,1)S(1)} %get-tuple-element.206), channel_id=1, source_target_pairs={{0,16},{8,24},{16,0},{24,8},{1,17},{9,25},{17,1},{25,9},{2,18},{10... | collective-permute-start | bytes 1966088 | tf_op jit(solution)/shard_map/plane_back/ppermute | solution.py:980
  73.9 26.3 %collective-permute-start.24 = (bf16[4,96,768]{2,1,0:T(8,128)(2,1)S(1)}, bf16[4,96,768]{2,1,0:T(8,128)(2,1)S(1)}, u32[]{:S(2)}, u32[]{:S(2)}) collective-permute-start(bf16[4,96,768]{2,1,0:T(8,128)(2,1)S(1)} %get-tuple-element.194), channel_id=1, source_target_pairs={{0,1},{1,0},{2,3},{3,2},{4,5},{5,4},{6,7},{7,6},{8,9},{9,8},{10,11... | collective-permute-start | bytes 1769480 | tf_op jit(solution)/shard_map/core_w/ppermute | solution.py:976
  74.0 14.5 %collective-permute-start.25 = (bf16[2,96,768]{2,1,0:T(8,128)(2,1)S(1)}, bf16[2,96,768]{2,1,0:T(8,128)(2,1)S(1)}, u32[]{:S(2)}, u32[]{:S(2)}) collective-permute-start(bf16[2,96,768]{2,1,0:T(8,128)(2,1)S(1)} %get-tuple-element.195), channel_id=1, source_target_pairs={{0,2},{2,0},{4,6},{6,4},{1,3},{3,1},{5,7},{7,5},{8,10},{10,8},{12,... | collective-permute-start | bytes 884744 | tf_op jit(solution)/shard_map/down_sum/ppermute | solution.py:980
  75.6 11.0 %collective-permute-start.20 = (bf16[576,128]{1,0:T(8,128)(2,1)S(1)}, bf16[576,128]{1,0:T(8,128)(2,1)S(1)}, u32[]{:S(2)}, u32[]{:S(2)}) collective-permute-start(bf16[576,128]{1,0:T(8,128)(2,1)S(1)} %get-tuple-element.180), channel_id=1, source_target_pairs={{0,2},{2,0},{4,6},{6,4},{1,3},{3,1},{5,7},{7,5},{8,10},{10,8},{12,... | collective-permute-start | bytes 442376 | tf_op jit(solution)/shard_map/chip_qkv/ppermute | solution.py:980
  86.5 13.6 %collective-permute-start.21 = (bf16[576,128]{1,0:T(8,128)(2,1)S(1)}, bf16[576,128]{1,0:T(8,128)(2,1)S(1)}, u32[]{:S(2)}, u32[]{:S(2)}) collective-permute-start(bf16[576,128]{1,0:T(8,128)(2,1)S(1)} %get-tuple-element.181), channel_id=1, source_target_pairs={{0,4},{2,6},{4,0},{6,2},{1,5},{3,7},{5,1},{7,3},{8,12},{10,14},{12... | collective-permute-start | bytes 442376 | tf_op jit(solution)/shard_map/chip_qkv/ppermute | solution.py:980
  88.4 11.7 %collective-permute-start.22 = (bf16[576,128]{1,0:T(8,128)(2,1)S(1)}, bf16[576,128]{1,0:T(8,128)(2,1)S(1)}, u32[]{:S(2)}, u32[]{:S(2)}) collective-permute-start(bf16[576,128]{1,0:T(8,128)(2,1)S(1)} %get-tuple-element.182), channel_id=1, source_target_pairs={{0,6},{2,4},{4,2},{6,0},{1,7},{3,5},{5,3},{7,1},{8,14},{10,12},{12... | collective-permute-start | bytes 442376 | tf_op jit(solution)/shard_map/chip_qkv/ppermute | solution.py:980
  102.6 2.4 %collective-permute-start.31 = (bf16[4,128,768]{2,1,0:T(8,128)(2,1)S(1)}, bf16[4,128,768]{2,1,0:T(8,128)(2,1)S(1)}, u32[]{:S(2)}, u32[]{:S(2)}) collective-permute-start(bf16[4,128,768]{2,1,0:T(8,128)(2,1)S(1)} %get-tuple-element.214), channel_id=1, source_target_pairs={{0,1},{1,0},{2,3},{3,2},{4,5},{5,4},{6,7},{7,6},{8,9},{9,8},{10,11... | collective-permute-start | bytes 2359304 | tf_op jit(solution)/shard_map/core_up/ppermute | solution.py:976
  104.9 24.5 %copy-start.4 = (bf16[768,768]{1,0:T(8,128)(2,1)S(1)}, bf16[768,768]{1,0:T(8,128)(2,1)}, u32[]{:S(2)}) copy-start(bf16[768,768]{1,0:T(8,128)(2,1)} %refs_8_.3) | copy-start | bytes 3538948
  104.9 24.5 %copy-start.5 = (bf16[768,768]{1,0:T(8,128)(2,1)S(1)}, bf16[768,768]{1,0:T(8,128)(2,1)}, u32[]{:S(2)}) copy-start(bf16[768,768]{1,0:T(8,128)(2,1)} %refs_7_.3) | copy-start | bytes 3538948
  105.6 23.8 %copy-start.3 = (bf16[768,768]{1,0:T(8,128)(2,1)S(1)}, bf16[768,768]{1,0:T(8,128)(2,1)}, u32[]{:S(2)}) copy-start(bf16[768,768]{1,0:T(8,128)(2,1)} %refs_9_.3) | copy-start | bytes 3538948
  105.6 15.3 %collective-permute-start.35 = (bf16[2,128,768]{2,1,0:T(8,128)(2,1)S(1)}, bf16[2,128,768]{2,1,0:T(8,128)(2,1)S(1)}, u32[]{:S(2)}, u32[]{:S(2)}) collective-permute-start(bf16[2,128,768]{2,1,0:T(8,128)(2,1)S(1)} %get-tuple-element.215), channel_id=1, source_target_pairs={{0,2},{2,0},{4,6},{6,4},{1,3},{3,1},{5,7},{7,5},{8,10},{10,8},{12,... | collective-permute-start | bytes 1179656 | tf_op jit(solution)/shard_map/up_sum/ppermute | solution.py:980
  108.3 6.1 %collective-permute-start.26 = (bf16[96,768]{1,0:T(8,128)(2,1)S(1)}, bf16[96,768]{1,0:T(8,128)(2,1)S(1)}, u32[]{:S(2)}, u32[]{:S(2)}) collective-permute-start(bf16[96,768]{1,0:T(8,128)(2,1)S(1)} %get-tuple-element.198), channel_id=1, source_target_pairs={{0,8},{8,0},{16,24},{24,16},{1,9},{9,1},{17,25},{25,17},{2,10},{10... | collective-permute-start | bytes 442376 | tf_op jit(solution)/shard_map/plane_w/ppermute | solution.py:980
  110.1 8.5 %collective-permute-start.27 = (bf16[96,768]{1,0:T(8,128)(2,1)S(1)}, bf16[96,768]{1,0:T(8,128)(2,1)S(1)}, u32[]{:S(2)}, u32[]{:S(2)}) collective-permute-start(bf16[96,768]{1,0:T(8,128)(2,1)S(1)} %get-tuple-element.199), channel_id=1, source_target_pairs={{0,16},{8,24},{16,0},{24,8},{1,17},{9,25},{17,1},{25,9},{2,18},{10... | collective-permute-start | bytes 442376 | tf_op jit(solution)/shard_map/plane_w/ppermute | solution.py:980
  110.3 8.3 %collective-permute-start.28 = (bf16[96,768]{1,0:T(8,128)(2,1)S(1)}, bf16[96,768]{1,0:T(8,128)(2,1)S(1)}, u32[]{:S(2)}, u32[]{:S(2)}) collective-permute-start(bf16[96,768]{1,0:T(8,128)(2,1)S(1)} %get-tuple-element.200), channel_id=1, source_target_pairs={{0,24},{8,16},{16,8},{24,0},{1,25},{9,17},{17,9},{25,1},{2,26},{10... | collective-permute-start | bytes 442376 | tf_op jit(solution)/shard_map/plane_w/ppermute | solution.py:980
  111.8 8.3 %collective-permute-start.36 = (bf16[1,96,768]{2,1,0:T(8,128)(2,1)S(1)}, bf16[1,96,768]{2,1,0:T(8,128)(2,1)S(1)}, u32[]{:S(2)}, u32[]{:S(2)}) collective-permute-start(bf16[1,96,768]{2,1,0:T(8,128)(2,1)S(1)} %get-tuple-element.230), channel_id=1, source_target_pairs={{0,4},{2,6},{4,0},{6,2},{1,5},{3,7},{5,1},{7,3},{8,12},{10,14},{12... | collective-permute-start | bytes 442376 | tf_op jit(solution)/shard_map/down_sum/ppermute | solution.py:980
  121.6 14.3 %collective-permute-start.37 = (bf16[1,128,768]{2,1,0:T(8,128)(2,1)S(1)}, bf16[1,128,768]{2,1,0:T(8,128)(2,1)S(1)}, u32[]{:S(2)}, u32[]{:S(2)}) collective-permute-start(bf16[1,128,768]{2,1,0:T(8,128)(2,1)S(1)} %get-tuple-element.233), channel_id=1, source_target_pairs={{0,4},{2,6},{4,0},{6,2},{1,5},{3,7},{5,1},{7,3},{8,12},{10,14},{12... | collective-permute-start | bytes 589832 | tf_op jit(solution)/shard_map/up_sum/ppermute | solution.py:980
  124.9 8.0 %collective-permute-start.32 = (bf16[24,768]{1,0:T(8,128)(2,1)S(1)}, bf16[24,768]{1,0:T(8,128)(2,1)S(1)}, u32[]{:S(2)}, u32[]{:S(2)}) collective-permute-start(bf16[24,768]{1,0:T(8,128)(2,1)S(1)} %get-tuple-element.221), channel_id=1, source_target_pairs={{0,2},{2,0},{4,6},{6,4},{1,3},{3,1},{5,7},{7,5},{8,10},{10,8},{12,... | collective-permute-start | bytes 110600 | tf_op jit(solution)/shard_map/chip_w/ppermute | solution.py:980
  125.4 10.5 %collective-permute-start.33 = (bf16[24,768]{1,0:T(8,128)(2,1)S(1)}, bf16[24,768]{1,0:T(8,128)(2,1)S(1)}, u32[]{:S(2)}, u32[]{:S(2)}) collective-permute-start(bf16[24,768]{1,0:T(8,128)(2,1)S(1)} %get-tuple-element.222), channel_id=1, source_target_pairs={{0,4},{2,6},{4,0},{6,2},{1,5},{3,7},{5,1},{7,3},{8,12},{10,14},{12... | collective-permute-start | bytes 110600 | tf_op jit(solution)/shard_map/chip_w/ppermute | solution.py:980
  128.0 7.9 %collective-permute-start.34 = (bf16[24,768]{1,0:T(8,128)(2,1)S(1)}, bf16[24,768]{1,0:T(8,128)(2,1)S(1)}, u32[]{:S(2)}, u32[]{:S(2)}) collective-permute-start(bf16[24,768]{1,0:T(8,128)(2,1)S(1)} %get-tuple-element.223), channel_id=1, source_target_pairs={{0,6},{2,4},{4,2},{6,0},{1,7},{3,5},{5,3},{7,1},{8,14},{10,12},{12... | collective-permute-start | bytes 110600 | tf_op jit(solution)/shard_map/chip_w/ppermute | solution.py:980
  137.1 4.8 %collective-permute-start.38 = (bf16[24,768]{1,0:T(8,128)(2,1)S(1)}, bf16[24,768]{1,0:T(8,128)(2,1)S(1)}, u32[]{:S(2)}, u32[]{:S(2)}) collective-permute-start(bf16[24,768]{1,0:T(8,128)(2,1)S(1)} %get-tuple-element.241), channel_id=1, source_target_pairs={{0,8},{8,0},{16,24},{24,16},{1,9},{9,1},{17,25},{25,17},{2,10},{10... | collective-permute-start | bytes 110600 | tf_op jit(solution)/shard_map/plane_rows/ppermute | solution.py:980
  138.9 4.0 %collective-permute-start.39 = (bf16[24,768]{1,0:T(8,128)(2,1)S(1)}, bf16[24,768]{1,0:T(8,128)(2,1)S(1)}, u32[]{:S(2)}, u32[]{:S(2)}) collective-permute-start(bf16[24,768]{1,0:T(8,128)(2,1)S(1)} %get-tuple-element.242), channel_id=1, source_target_pairs={{0,16},{8,24},{16,0},{24,8},{1,17},{9,25},{17,1},{25,9},{2,18},{10... | collective-permute-start | bytes 110600 | tf_op jit(solution)/shard_map/plane_rows/ppermute | solution.py:980
  139.1 4.9 %collective-permute-start.40 = (bf16[24,768]{1,0:T(8,128)(2,1)S(1)}, bf16[24,768]{1,0:T(8,128)(2,1)S(1)}, u32[]{:S(2)}, u32[]{:S(2)}) collective-permute-start(bf16[24,768]{1,0:T(8,128)(2,1)S(1)} %get-tuple-element.243), channel_id=1, source_target_pairs={{0,24},{8,16},{16,8},{24,0},{1,25},{9,17},{17,9},{25,1},{2,26},{10... | collective-permute-start | bytes 110600 | tf_op jit(solution)/shard_map/plane_rows/ppermute | solution.py:980
  (8 other events, 56.5 us)

commit v5 on v4

--- a/solution.py
+++ b/solution.py
@@ -1082,13 +1082,13 @@
     qkv_keep, qkv_send = qkv_grad_call(
         place, groups, units, grad_qkv, ln1_gain, ln1_bias, w_heads, parts, live, width
     )
+    down_recv = after(down_recv, qkv_send)
     with scope("core_w"):
         qkv_send = swap_core(qkv_send)
-    qkv_send = after(qkv_send, (grad_pieces, down_recv))
     qkv_sums = spread_call(place, qkv_keep, qkv_send)
     with scope("down_sum"):
         down_keep, down_last = scatter_chips(place, down_keep, down_recv, chips, 2)
-    back = after(back, (down_keep, qkv_sums))
+    back = after(back, (down_keep, grad_pieces[2:]))
     up_keep, up_send = up_grad_call(place, back, chips, part, model)
     with scope("plane_w"):
         traded = trade(qkv_sums, "rows")
@@ -1105,7 +1105,7 @@
         place, grad_pieces, layer_in, grad_mid, ln1_gain, w_query, w_key, w_value, live
     )
     gwd = finish_down_call(down_keep, down_last)
-    up_recv = after(up_recv, (down_last, traded))
+    up_recv = after(up_recv, (grad_pieces, shared, down_last))
     with scope("up_sum"):
         up_keep, up_last = scatter_chips(place, up_keep, up_recv, chips, 2)
     up_last = after(up_last, (qkv_all, gwd, grad_inputs))

time: 145 us -> 135 us (0.931)
  waiting for transfers between devices: 51.5 us -> 42.6 us
  starting transfers between devices: 51.4 us -> 49.6 us
    ppermute x34, waiting for transfers between devices: 47.5 us -> 39.1 us  [swap(): lax.ppermute(value, axis, [(k, k ^ bit) for k in range(lax.axis_size(axis...]
    ppermute x34, starting transfers between devices: 50.4 us -> 48.1 us  [swap(): lax.ppermute(value, axis, [(k, k ^ bit) for k in range(lax.axis_size(axis...]
  transfers between devices with their start and end apart: 41 -> 41, of which waited for: 18 -> 17; matrix products, arithmetic and copies ran while one was open for 2% -> 2% of each run, Pallas kernels for 20% -> 22%
where the time goes in v5:
time: 135 us; the launch traced here: 134 us
  starting transfers between devices  49.6 us (37%)
  waiting for transfers between devices  42.6 us (32%)
  Pallas kernels  37.4 us (28%)
  local copies, waits for them, and re-layouts  3.65 us (3%)
    ppermute x34, starting transfers between devices, swap(): lax.ppermute(value, axis, [(k, k ^ bit) for k in range(lax.axis_size(axis...  48.1 us
    ppermute x34, waiting for transfers between devices, swap(): lax.ppermute(value, axis, [(k, k ^ bit) for k in range(lax.axis_size(axis...  39.1 us
    pallas_call x24, Pallas kernels, kernel(): pl.pallas_call(body, out_shape=outs if single else listed, in_specs=[smem...  37.4 us
    ppermute x7, waiting for transfers between devices, swap_core(): return lax.ppermute(value, 'core', [(0, 1), (1, 0)])  3.5 us
    dynamic_slice x2, local copies, waits for them, and re-layouts, columns(): mine = lax.dynamic_slice_in_dim(weight, z_index * live, live, 1)  2.82 us
  transfers between devices with their start and end apart: 41, of which 17 were waited for; matrix products, arithmetic and copies ran while one was open for 2% of the time, Pallas kernels for 22%

profile of v5, /device:TPU:0, one launch (start us, length us, event | category | flops | bytes accessed | tf_op | source)
XLA Modules:
  0.0 134.5 jit_solution(16804389550851988058)
XLA Ops:
  0.7 4.1 %collective-permute-start.1 = (bf16[128,768]{1,0:T(8,128)(2,1)}, bf16[128,768]{1,0:T(8,128)(2,1)S(1)}, u32[]{:S(2)}, u32[]{:S(2)}) collective-permute-start(bf16[128,768]{1,0:T(8,128)(2,1)} %bitcast.7), channel_id=1, source_target_pairs={{0,4},{2,6},{4,0},{6,2},{1,5},{3,7},{5,1},{7,3},{8,12},{10,14},{12... | collective-permute-start | bytes 589832 | tf_op jit(solution)/shard_map/gather_in/ppermute | solution.py:980
  4.8 1.6 %collective-permute-start = (bf16[128,768]{1,0:T(8,128)(2,1)}, bf16[128,768]{1,0:T(8,128)(2,1)S(1)}, u32[]{:S(2)}, u32[]{:S(2)}) collective-permute-start(bf16[128,768]{1,0:T(8,128)(2,1)} %bitcast.8), channel_id=1, source_target_pairs={{0,2},{2,0},{4,6},{6,4},{1,3},{3,1},{5,7},{7,5},{8,10},{10,8},{12,... | collective-permute-start | bytes 589832 | tf_op jit(solution)/shard_map/gather_in/ppermute | solution.py:980
  7.6 1.6 %constant_dynamic-slice_fusion = (bf16[768,192]{1,0:T(8,128)(2,1)S(1)}, bf16[768,192]{1,0:T(8,128)(2,1)S(1)}) fusion(bf16[768,768]{1,0:T(8,128)(2,1)} %refs_9_.3, s32[]{:T(128)S(6)} %select_n.2, bf16[768,768]{1,0:T(8,128)(2,1)} %refs_8_.3), kind=kLoop, calls=%fused_computation.10 | loop fusion | bytes 1179652 | tf_op jit(solution)/shard_map/dynamic_slice | solution.py:1027
  9.2 5.0 %collective-permute-done.1.refs_1_ = bf16[128,768]{1,0:T(8,128)(2,1)S(1)} collective-permute-done((bf16[128,768]{1,0:T(8,128)(2,1)}, bf16[128,768]{1,0:T(8,128)(2,1)S(1)}, u32[]{:S(2)}, u32[]{:S(2)}) %collective-permute-start.1) | collective-permute-done | bytes 196640 | tf_op jit(solution)/shard_map/gather_in/ppermute | solution.py:980
  18.4 2.5 %collective-permute-start.11 = (bf16[128,768]{1,0:T(8,128)(2,1)S(1)}, bf16[128,768]{1,0:T(8,128)(2,1)S(1)}, u32[]{:S(2)}, u32[]{:S(2)}) collective-permute-start(bf16[128,768]{1,0:T(8,128)(2,1)S(1)} %mask_grad.1.go_ref.refs_4_), channel_id=1, source_target_pairs={{0,24},{8,16},{16,8},{24,0},{1,25},{9,17},{17,9},{25,1},{2,26},{10... | collective-permute-start | bytes 589832 | tf_op jit(solution)/shard_map/plane_out/ppermute | solution.py:980
  22.6 1.3 collective-permute-done.5.refs_8_
  23.9 4.3 %attend.1 = (f32[4,128,256]{2,1,0:T(8,128)S(1)}, bf16[4,2,384,512]{3,2,1,0:T(8,128)(2,1)S(1)}, bf16[4,128,256]{2,1,0:T(8,128)(2,1)S(1)}, bf16[4,128,512]{2,1,0:T...) custom-call(s32[3]{0:T(128)S(1)} %pad_add_fusion.place_ref, ...), custom_call_target="tpu_custom_call" | custom-call | flops 6000000 | bytes 6000 | tf_op jit(solution)/shard_map/attend/pallas_call | solution.py:350
  28.2 1.4 %collective-permute-start.6 = (bf16[192,128]{1,0:T(8,128)(2,1)S(1)}, bf16[192,128]{1,0:T(8,128)(2,1)S(1)}, u32[]{:S(2)}, u32[]{:S(2)}) collective-permute-start(bf16[192,128]{1,0:T(8,128)(2,1)S(1)} %get-tuple-element.138), channel_id=1, source_target_pairs={{0,2},{2,0},{4,6},{6,4},{1,3},{3,1},{5,7},{7,5},{8,10},{10,8},{12,... | collective-permute-start | bytes 147464 | tf_op jit(solution)/shard_map/chip_attn/ppermute | solution.py:980
  29.5 3.3 %collective-permute-start.7 = (bf16[192,128]{1,0:T(8,128)(2,1)S(1)}, bf16[192,128]{1,0:T(8,128)(2,1)S(1)}, u32[]{:S(2)}, u32[]{:S(2)}) collective-permute-start(bf16[192,128]{1,0:T(8,128)(2,1)S(1)} %get-tuple-element.139), channel_id=1, source_target_pairs={{0,4},{2,6},{4,0},{6,2},{1,5},{3,7},{5,1},{7,3},{8,12},{10,14},{12... | collective-permute-start | bytes 147464 | tf_op jit(solution)/shard_map/chip_attn/ppermute | solution.py:980
  33.0 2.9 %collective-permute-done.7.refs_2_ = bf16[192,128]{1,0:T(8,128)(2,1)S(1)} collective-permute-done((bf16[192,128]{1,0:T(8,128)(2,1)S(1)}, bf16[192,128]{1,0:T(8,128)(2,1)S(1)}, u32[]{:S(2)}, u32[]{:S(2)}) %collective-permute-start.7) | collective-permute-done | bytes 49184 | tf_op jit(solution)/shard_map/chip_attn/ppermute | solution.py:980
  35.9 2.8 %collective-permute-done.8.refs_3_ = bf16[192,128]{1,0:T(8,128)(2,1)S(1)} collective-permute-done((bf16[192,128]{1,0:T(8,128)(2,1)S(1)}, bf16[192,128]{1,0:T(8,128)(2,1)S(1)}, u32[]{:S(2)}, u32[]{:S(2)}) %collective-permute-start.8) | collective-permute-done | bytes 49184 | tf_op jit(solution)/shard_map/chip_attn/ppermute | solution.py:980
  38.7 1.4 %norms.1 = (f32[128,768]{1,0:T(8,128)S(1)}, bf16[128,768]{1,0:T(8,128)(2,1)S(1)}, bf16[128,768]{1,0:T(8,128)(2,1)S(1)}) custom-call(s32[3]{0:T(128)S(1)} %pad_add_fusion.place_ref, bf16[192,128]{1,0:T(8,128)(2,1)S(1)} %get-tuple-element.142.refs_0_, bf16[192,128]{1,0:T(8,128)(2,1)S(1)} %collective-permute-done.6.refs_1_, ...), custom_call_target="tpu_custom_call" | custom-call | flops 1500000 | bytes 1500 | tf_op jit(solution)/shard_map/norms/pallas_call | solution.py:350
  40.1 1.9 %up_gelu.1 = (bf16[4,128,768]{2,1,0:T(8,128)(2,1)S(1)}, bf16[4,128,768]{2,1,0:T(8,128)(2,1)S(1)}, bf16[128,768]{1,0:T(8,128)(2,1)S(1)}, bf16[128,768]{1,0:T(8,12...) custom-call(s32[3]{0:T(128)S(1)} %pad_add_fusion.place_ref, ...), custom_call_target="tpu_custom_call" | custom-call | flops 2000000 | bytes 2000 | tf_op jit(solution)/shard_map/up_gelu/pallas_call | solution.py:350
  42.7 1.5 %collective-permute-start.17 = (bf16[128,768]{1,0:T(8,128)(2,1)S(1)}, bf16[128,768]{1,0:T(8,128)(2,1)S(1)}, u32[]{:S(2)}, u32[]{:S(2)}) collective-permute-start(bf16[128,768]{1,0:T(8,128)(2,1)S(1)} %get-tuple-element.166), channel_id=1, source_target_pairs={{0,16},{8,24},{16,0},{24,8},{1,17},{9,25},{17,1},{25,9},{2,18},{10... | collective-permute-start | bytes 589832 | tf_op jit(solution)/shard_map/plane_act/ppermute | solution.py:980
  44.2 1.4 %collective-permute-start.18 = (bf16[128,768]{1,0:T(8,128)(2,1)S(1)}, bf16[128,768]{1,0:T(8,128)(2,1)S(1)}, u32[]{:S(2)}, u32[]{:S(2)}) collective-permute-start(bf16[128,768]{1,0:T(8,128)(2,1)S(1)} %get-tuple-element.167), channel_id=1, source_target_pairs={{0,24},{8,16},{16,8},{24,0},{1,25},{9,17},{17,9},{25,1},{2,26},{10... | collective-permute-start | bytes 589832 | tf_op jit(solution)/shard_map/plane_act/ppermute | solution.py:980
  45.6 6.0 %token_backward.1 = (bf16[128,768]{1,0:T(8,128)(2,1)}, f32[128,768]{1,0:T(8,128)S(1)}, bf16[128,2560]{1,0:T(8,128)(2,1)S(1)}, bf16[128,2560]{1,0:T(8,128)(2,1)S(...) custom-call(s32[3]{0:T(128)S(1)} %pad_add_fusion.place_ref, ...), custom_call_target="tpu_custom_call" | custom-call | flops 9000000 | bytes 9000 | tf_op jit(solution)/shard_map/token_backward/pallas_call | solution.py:350
  52.6 1.8 %collective-permute-start.19 = (bf16[128,2560]{1,0:T(8,128)(2,1)S(1)}, bf16[128,2560]{1,0:T(8,128)(2,1)S(1)}, u32[]{:S(2)}, u32[]{:S(2)}) collective-permute-start(bf16[128,2560]{1,0:T(8,128)(2,1)S(1)} %get-tuple-element.177), channel_id=1, source_target_pairs={{0,24},{8,16},{16,8},{24,0},{1,25},{9,17},{17,9},{25,1},{2,26},{10... | collective-permute-start | bytes 1966088 | tf_op jit(solution)/shard_map/plane_back/ppermute | solution.py:980
  54.6 1.4 %collective-permute-start.13 = (bf16[192,128]{1,0:T(8,128)(2,1)S(1)}, bf16[192,128]{1,0:T(8,128)(2,1)S(1)}, u32[]{:S(2)}, u32[]{:S(2)}) collective-permute-start(bf16[192,128]{1,0:T(8,128)(2,1)S(1)} %get-tuple-element.159), channel_id=1, source_target_pairs={{0,4},{2,6},{4,0},{6,2},{1,5},{3,7},{5,1},{7,3},{8,12},{10,14},{12... | collective-permute-start | bytes 147464 | tf_op jit(solution)/shard_map/chip_grad/ppermute | solution.py:980
  56.0 2.8 %collective-permute-start.14 = (bf16[192,128]{1,0:T(8,128)(2,1)S(1)}, bf16[192,128]{1,0:T(8,128)(2,1)S(1)}, u32[]{:S(2)}, u32[]{:S(2)}) collective-permute-start(bf16[192,128]{1,0:T(8,128)(2,1)S(1)} %get-tuple-element.160), channel_id=1, source_target_pairs={{0,6},{2,4},{4,2},{6,0},{1,7},{3,5},{5,3},{7,1},{8,14},{10,12},{12... | collective-permute-start | bytes 147464 | tf_op jit(solution)/shard_map/chip_grad/ppermute | solution.py:980
  59.6 2.3 %collective-permute-done.14.refs_3_ = bf16[192,128]{1,0:T(8,128)(2,1)S(1)} collective-permute-done((bf16[192,128]{1,0:T(8,128)(2,1)S(1)}, bf16[192,128]{1,0:T(8,128)(2,1)S(1)}, u32[]{:S(2)}, u32[]{:S(2)}) %collective-permute-start.14) | collective-permute-done | bytes 49184 | tf_op jit(solution)/shard_map/chip_grad/ppermute | solution.py:980
  61.9 3.8 %attend_back.1 = (bf16[4,128,256]{2,1,0:T(8,128)(2,1)S(1)}, f32[4,128,512]{2,1,0:T(8,128)S(1)}, bf16[4,128,512]{2,1,0:T(8,128)(2,1)S(1)}) custom-call(s32[3]{0:T(128)S(1)} %pad_add_fusion.place_ref, bf16[4,128,256]{2,1,0:T(8,128)(2,1)S(1)} %get-tuple-element.152.q_ref, bf16[4,128,512]{2,1,0:T(8,128)(2,1)S(1)} %get-tuple-element.153.own_ref, ...), custom_call_target="tpu_custom_call" | custom-call | flops 6000000 | bytes 6000 | tf_op jit(solution)/shard_map/attend_back/pallas_call | solution.py:350
  65.8 1.5 %grad_down.1 = (f32[4,96,768]{2,1,0:T(8,128)S(1)}, bf16[4,96,768]{2,1,0:T(8,128)(2,1)S(1)}) custom-call(s32[3]{0:T(128)S(1)} %pad_add_fusion.place_ref, bf16[128,768]{1,0:T(8,128)(2,1)S(1)} %get-tuple-element.168.refs_0_, bf16[128,768]{1,0:T(8,128)(2,1)S(1)} %collective-permute-done.16.refs_1_, bf16[128,768]{1,0:T(8,128)(2,1)S(1)} %collective-permute-done.17.refs_2_, ...), custom_call_target="tpu_custom_call" | custom-call | flops 3000000 | bytes 3000 | tf_op jit(solution)/shard_map/grad_down/pallas_call | solution.py:350
  67.9 1.4 %collective-permute-start.28 = (bf16[128,2560]{1,0:T(8,128)(2,1)S(1)}, bf16[128,2560]{1,0:T(8,128)(2,1)S(1)}, u32[]{:S(2)}, u32[]{:S(2)}) collective-permute-start(bf16[128,2560]{1,0:T(8,128)(2,1)S(1)} %get-tuple-element.203), channel_id=1, source_target_pairs={{0,8},{8,0},{16,24},{24,16},{1,9},{9,1},{17,25},{25,17},{2,10},{10... | collective-permute-start | bytes 1966088 | tf_op jit(solution)/shard_map/plane_back/ppermute | solution.py:980
  71.4 1.6 %collective-permute-start.30 = (bf16[2,96,768]{2,1,0:T(8,128)(2,1)S(1)}, bf16[2,96,768]{2,1,0:T(8,128)(2,1)S(1)}, u32[]{:S(2)}, u32[]{:S(2)}) collective-permute-start(bf16[2,96,768]{2,1,0:T(8,128)(2,1)S(1)} %get-tuple-element.206), channel_id=1, source_target_pairs={{0,2},{2,0},{4,6},{6,4},{1,3},{3,1},{5,7},{7,5},{8,10},{10,8},{12,... | collective-permute-start | bytes 884744 | tf_op jit(solution)/shard_map/down_sum/ppermute | solution.py:980
  73.0 1.4 %collective-permute-start.21 = (bf16[576,128]{1,0:T(8,128)(2,1)S(1)}, bf16[576,128]{1,0:T(8,128)(2,1)S(1)}, u32[]{:S(2)}, u32[]{:S(2)}) collective-permute-start(bf16[576,128]{1,0:T(8,128)(2,1)S(1)} %get-tuple-element.181), channel_id=1, source_target_pairs={{0,4},{2,6},{4,0},{6,2},{1,5},{3,7},{5,1},{7,3},{8,12},{10,14},{12... | collective-permute-start | bytes 442376 | tf_op jit(solution)/shard_map/chip_qkv/ppermute | solution.py:980
  74.4 1.4 %collective-permute-start.22 = (bf16[576,128]{1,0:T(8,128)(2,1)S(1)}, bf16[576,128]{1,0:T(8,128)(2,1)S(1)}, u32[]{:S(2)}, u32[]{:S(2)}) collective-permute-start(bf16[576,128]{1,0:T(8,128)(2,1)S(1)} %get-tuple-element.182), channel_id=1, source_target_pairs={{0,6},{2,4},{4,2},{6,0},{1,7},{3,5},{5,3},{7,1},{8,14},{10,12},{12... | collective-permute-start | bytes 442376 | tf_op jit(solution)/shard_map/chip_qkv/ppermute | solution.py:980
  75.8 2.5 %grad_qkv.1 = (f32[4,96,768]{2,1,0:T(8,128)S(1)}, bf16[4,96,768]{2,1,0:T(8,128)(2,1)S(1)}) custom-call(s32[3]{0:T(128)S(1)} %pad_add_fusion.place_ref, bf16[1,128,768]{2,1,0:T(8,128)(2,1)S(1)} %get-tuple-element.184.refs_0_, bf16[2,128,768]{2,1,0:T(8,128)(2,1)S(1)} %get-tuple-element.185.refs_1_, bf16[1,128,768]{2,1,0:T(8,128)(2,1)S(1)} %get-tuple-element.186.refs_2_, ...), custom_call_target="tpu_custom_call" | custom-call | flops 4000000 | bytes 4000 | tf_op jit(solution)/shard_map/grad_qkv/pallas_call | solution.py:350
  78.3 4.9 %collective-permute-done.30.in_ref = bf16[2,96,768]{2,1,0:T(8,128)(2,1)S(1)} collective-permute-done((bf16[2,96,768]{2,1,0:T(8,128)(2,1)S(1)}, bf16[2,96,768]{2,1,0:T(8,128)(2,1)S(1)}, u32[]{:S(2)}, u32[]{:S(2)}) %collective-permute-start.30) | collective-permute-done | bytes 294944 | tf_op jit(solution)/shard_map/down_sum/ppermute | solution.py:980
  83.9 4.1 %collective-permute-done.22.refs_3_ = bf16[576,128]{1,0:T(8,128)(2,1)S(1)} collective-permute-done((bf16[576,128]{1,0:T(8,128)(2,1)S(1)}, bf16[576,128]{1,0:T(8,128)(2,1)S(1)}, u32[]{:S(2)}, u32[]{:S(2)}) %collective-permute-start.22) | collective-permute-done | bytes 147488 | tf_op jit(solution)/shard_map/chip_qkv/ppermute | solution.py:980
  88.1 1.7 %grad_up_out.1 = (f32[4,128,768]{2,1,0:T(8,128)S(1)}, bf16[4,128,768]{2,1,0:T(8,128)(2,1)S(1)}) custom-call(s32[3]{0:T(128)S(1)} %pad_add_fusion.place_ref, bf16[128,2560]{1,0:T(8,128)(2,1)S(1)} %get-tuple-element.209.refs_0_, bf16[128,2560]{1,0:T(8,128)(2,1)S(1)} %collective-permute-done.28.refs_1_, bf16[128,2560]{1,0:T(8,128)(2,1)S(1)} %collective-permute-done.29.refs_2_, ...), custom_call_target="tpu_custom_call" | custom-call | flops 4000000 | bytes 4000 | tf_op jit(solution)/shard_map/grad_up_out/pallas_call | solution.py:350
  90.4 1.8 %collective-permute-done.31.in_ref = bf16[4,128,768]{2,1,0:T(8,128)(2,1)S(1)} collective-permute-done((bf16[4,128,768]{2,1,0:T(8,128)(2,1)S(1)}, bf16[4,128,768]{2,1,0:T(8,128)(2,1)S(1)}, u32[]{:S(2)}, u32[]{:S(2)}) %collective-permute-start.31) | collective-permute-done | bytes 786464 | tf_op jit(solution)/shard_map/core_up/ppermute | solution.py:976
  92.8 1.4 %collective-permute-start.35 = (bf16[2,128,768]{2,1,0:T(8,128)(2,1)S(1)}, bf16[2,128,768]{2,1,0:T(8,128)(2,1)S(1)}, u32[]{:S(2)}, u32[]{:S(2)}) collective-permute-start(bf16[2,128,768]{2,1,0:T(8,128)(2,1)S(1)} %get-tuple-element.215), channel_id=1, source_target_pairs={{0,2},{2,0},{4,6},{6,4},{1,3},{3,1},{5,7},{7,5},{8,10},{10,8},{12,... | collective-permute-start | bytes 1179656 | tf_op jit(solution)/shard_map/up_sum/ppermute | solution.py:980
  94.9 1.7 %collective-permute-start.25 = (bf16[96,768]{1,0:T(8,128)(2,1)S(1)}, bf16[96,768]{1,0:T(8,128)(2,1)S(1)}, u32[]{:S(2)}, u32[]{:S(2)}) collective-permute-start(bf16[96,768]{1,0:T(8,128)(2,1)S(1)} %get-tuple-element.196), channel_id=1, source_target_pairs={{0,8},{8,0},{16,24},{24,16},{1,9},{9,1},{17,25},{25,17},{2,10},{10... | collective-permute-start | bytes 442376 | tf_op jit(solution)/shard_map/plane_w/ppermute | solution.py:980
  97.0 1.5 %collective-permute-start.27 = (bf16[96,768]{1,0:T(8,128)(2,1)S(1)}, bf16[96,768]{1,0:T(8,128)(2,1)S(1)}, u32[]{:S(2)}, u32[]{:S(2)}) collective-permute-start(bf16[96,768]{1,0:T(8,128)(2,1)S(1)} %get-tuple-element.198), channel_id=1, source_target_pairs={{0,24},{8,16},{16,8},{24,0},{1,25},{9,17},{17,9},{25,1},{2,26},{10... | collective-permute-start | bytes 442376 | tf_op jit(solution)/shard_map/plane_w/ppermute | solution.py:980
  99.2 2.0 %collective-permute-done.25.refs_1_ = bf16[96,768]{1,0:T(8,128)(2,1)S(1)} collective-permute-done((bf16[96,768]{1,0:T(8,128)(2,1)S(1)}, bf16[96,768]{1,0:T(8,128)(2,1)S(1)}, u32[]{:S(2)}, u32[]{:S(2)}) %collective-permute-start.25) | collective-permute-done | bytes 147488 | tf_op jit(solution)/shard_map/plane_w/ppermute | solution.py:980
  101.2 1.3 collective-permute-start.36
  102.5 2.7 %collective-permute-done.26.refs_2_ = bf16[96,768]{1,0:T(8,128)(2,1)S(1)} collective-permute-done((bf16[96,768]{1,0:T(8,128)(2,1)S(1)}, bf16[96,768]{1,0:T(8,128)(2,1)S(1)}, u32[]{:S(2)}, u32[]{:S(2)}) %collective-permute-start.26) | collective-permute-done | bytes 147488 | tf_op jit(solution)/shard_map/plane_w/ppermute | solution.py:980
  105.8 4.5 %collective-permute-done.20.refs_1_ = bf16[576,128]{1,0:T(8,128)(2,1)S(1)} collective-permute-done((bf16[576,128]{1,0:T(8,128)(2,1)S(1)}, bf16[576,128]{1,0:T(8,128)(2,1)S(1)}, u32[]{:S(2)}, u32[]{:S(2)}) %collective-permute-start.20) | collective-permute-done | bytes 147488 | tf_op jit(solution)/shard_map/chip_qkv/ppermute | solution.py:980
  111.0 2.3 %collective-permute-start.37 = (bf16[1,128,768]{2,1,0:T(8,128)(2,1)S(1)}, bf16[1,128,768]{2,1,0:T(8,128)(2,1)S(1)}, u32[]{:S(2)}, u32[]{:S(2)}) collective-permute-start(bf16[1,128,768]{2,1,0:T(8,128)(2,1)S(1)} %get-tuple-element.233), channel_id=1, source_target_pairs={{0,4},{2,6},{4,0},{6,2},{1,5},{3,7},{5,1},{7,3},{8,12},{10,14},{12... | collective-permute-start | bytes 589832 | tf_op jit(solution)/shard_map/up_sum/ppermute | solution.py:980
  113.7 2.0 %collective-permute-start.33 = (bf16[24,768]{1,0:T(8,128)(2,1)S(1)}, bf16[24,768]{1,0:T(8,128)(2,1)S(1)}, u32[]{:S(2)}, u32[]{:S(2)}) collective-permute-start(bf16[24,768]{1,0:T(8,128)(2,1)S(1)} %get-tuple-element.222), channel_id=1, source_target_pairs={{0,4},{2,6},{4,0},{6,2},{1,5},{3,7},{5,1},{7,3},{8,12},{10,14},{12... | collective-permute-start | bytes 110600 | tf_op jit(solution)/shard_map/chip_w/ppermute | solution.py:980
  115.7 2.0 %collective-permute-start.34 = (bf16[24,768]{1,0:T(8,128)(2,1)S(1)}, bf16[24,768]{1,0:T(8,128)(2,1)S(1)}, u32[]{:S(2)}, u32[]{:S(2)}) collective-permute-start(bf16[24,768]{1,0:T(8,128)(2,1)S(1)} %get-tuple-element.223), channel_id=1, source_target_pairs={{0,6},{2,4},{4,2},{6,0},{1,7},{3,5},{5,3},{7,1},{8,14},{10,12},{12... | collective-permute-start | bytes 110600 | tf_op jit(solution)/shard_map/chip_w/ppermute | solution.py:980
  117.7 2.7 %grad_inputs.1 = bf16[128,768]{1,0:T(8,128)(2,1)} custom-call(s32[3]{0:T(128)S(1)} %pad_add_fusion.place_ref, bf16[576,128]{1,0:T(8,128)(2,1)S(1)} %get-tuple-element.179.refs_0_, bf16[576,128]{1,0:T(8,128)(2,1)S(1)} %collective-permute-done.20.refs_1_, bf16[576,128]{1,0:T(8,128)(2,1)S(1)} %collective-permute-done.21.refs_2_, ...), custom_call_target="tpu_custom_call" | custom-call | flops 3000000 | bytes 3000 | tf_op jit(solution)/shard_map/grad_inputs/pallas_call | solution.py:350
  121.2 3.8 %collective-permute-done.33.refs_2_ = bf16[24,768]{1,0:T(8,128)(2,1)S(1)} collective-permute-done((bf16[24,768]{1,0:T(8,128)(2,1)S(1)}, bf16[24,768]{1,0:T(8,128)(2,1)S(1)}, u32[]{:S(2)}, u32[]{:S(2)}) %collective-permute-start.33) | collective-permute-done | bytes 36896 | tf_op jit(solution)/shard_map/chip_w/ppermute | solution.py:980
  126.3 1.3 collective-permute-start.38
  128.3 1.4 %collective-permute-start.40 = (bf16[24,768]{1,0:T(8,128)(2,1)S(1)}, bf16[24,768]{1,0:T(8,128)(2,1)S(1)}, u32[]{:S(2)}, u32[]{:S(2)}) collective-permute-start(bf16[24,768]{1,0:T(8,128)(2,1)S(1)} %get-tuple-element.243), channel_id=1, source_target_pairs={{0,24},{8,16},{16,8},{24,0},{1,25},{9,17},{17,9},{25,1},{2,26},{10... | collective-permute-start | bytes 110600 | tf_op jit(solution)/shard_map/plane_rows/ppermute | solution.py:980
  129.8 1.3 finish_qkv.1
  131.5 1.7 %collective-permute-done.40.refs_3_ = bf16[24,768]{1,0:T(8,128)(2,1)S(1)} collective-permute-done((bf16[24,768]{1,0:T(8,128)(2,1)S(1)}, bf16[24,768]{1,0:T(8,128)(2,1)S(1)}, u32[]{:S(2)}, u32[]{:S(2)}) %collective-permute-start.40) | collective-permute-done | bytes 36896 | tf_op jit(solution)/shard_map/plane_rows/ppermute | solution.py:980
  133.2 1.3 place_up.1
  (92 shorter events, 20.9 us)
Async XLA Ops:
  0.7 13.5 %collective-permute-start.1 = (bf16[128,768]{1,0:T(8,128)(2,1)}, bf16[128,768]{1,0:T(8,128)(2,1)S(1)}, u32[]{:S(2)}, u32[]{:S(2)}) collective-permute-start(bf16[128,768]{1,0:T(8,128)(2,1)} %bitcast.7), channel_id=1, source_target_pairs={{0,4},{2,6},{4,0},{6,2},{1,5},{3,7},{5,1},{7,3},{8,12},{10,14},{12... | collective-permute-start | bytes 589832 | tf_op jit(solution)/shard_map/gather_in/ppermute | solution.py:980
  4.8 11.7 %collective-permute-start = (bf16[128,768]{1,0:T(8,128)(2,1)}, bf16[128,768]{1,0:T(8,128)(2,1)S(1)}, u32[]{:S(2)}, u32[]{:S(2)}) collective-permute-start(bf16[128,768]{1,0:T(8,128)(2,1)} %bitcast.8), channel_id=1, source_target_pairs={{0,2},{2,0},{4,6},{6,4},{1,3},{3,1},{5,7},{7,5},{8,10},{10,8},{12,... | collective-permute-start | bytes 589832 | tf_op jit(solution)/shard_map/gather_in/ppermute | solution.py:980
  14.2 7.2 %collective-permute-start.2 = (bf16[128,768]{1,0:T(8,128)(2,1)S(1)}, bf16[128,768]{1,0:T(8,128)(2,1)S(1)}, u32[]{:S(2)}, u32[]{:S(2)}) collective-permute-start(bf16[128,768]{1,0:T(8,128)(2,1)S(1)} %collective-permute-done.1.refs_1_), channel_id=1, source_target_pairs={{0,2},{2,0},{4,6},{6,4},{1,3},{3,1},{5,7},{7,5},{8,10},{10,8},{12,... | collective-permute-start | bytes 589832 | tf_op jit(solution)/shard_map/gather_in/ppermute | solution.py:980
  16.4 6.1 %collective-permute-start.3 = (bf16[1,128,512]{2,1,0:T(8,128)(2,1)S(1)}, bf16[1,128,512]{2,1,0:T(8,128)(2,1)S(1)}, u32[]{:S(2)}, u32[]{:S(2)}) collective-permute-start(bf16[1,128,512]{2,1,0:T(8,128)(2,1)S(1)} %get-tuple-element.134.refs_3_), channel_id=1, source_target_pairs={{0,1},{1,0},{2,3},{3,2},{4,5},{5,4},{6,7},{7,6},{8,9},{9,8},{10,11... | collective-permute-start | bytes 393224 | tf_op jit(solution)/shard_map/core_kv/ppermute | solution.py:976
  16.5 22.2 %copy-start.1 = (bf16[768,768]{1,0:T(8,128)(2,1)S(1)}, bf16[768,768]{1,0:T(8,128)(2,1)}, u32[]{:S(2)}) copy-start(bf16[768,768]{1,0:T(8,128)(2,1)} %wo_ref.1) | copy-start | bytes 3538948
  16.5 22.2 %copy-start.10 = (f32[768]{0:T(1024)S(1)}, f32[768]{0:T(1024)}, u32[]{:S(2)}) copy-start(f32[768]{0:T(1024)} %g2.1) | copy-start | bytes 9220
  16.5 22.2 %copy-start.11 = (f32[768]{0:T(1024)S(1)}, f32[768]{0:T(1024)}, u32[]{:S(2)}) copy-start(f32[768]{0:T(1024)} %b2.1) | copy-start | bytes 9220
  16.5 23.6 %copy-start = (bf16[768,3072]{1,0:T(8,128)(2,1)S(1)}, bf16[768,3072]{1,0:T(8,128)(2,1)}, u32[]{:S(2)}) copy-start(bf16[768,3072]{1,0:T(8,128)(2,1)} %wu_ref.3) | copy-start | bytes 14155780
  17.3 5.3 %collective-permute-start.4 = (bf16[2,128,512]{2,1,0:T(8,128)(2,1)S(1)}, bf16[2,128,512]{2,1,0:T(8,128)(2,1)S(1)}, u32[]{:S(2)}, u32[]{:S(2)}) collective-permute-start(bf16[2,128,512]{2,1,0:T(8,128)(2,1)S(1)} %get-tuple-element.135.refs_4_), channel_id=1, source_target_pairs={{0,1},{1,0},{2,3},{3,2},{4,5},{5,4},{6,7},{7,6},{8,9},{9,8},{10,11... | collective-permute-start | bytes 786440 | tf_op jit(solution)/shard_map/core_kv/ppermute | solution.py:976
  18.4 14.4 %collective-permute-start.11 = (bf16[128,768]{1,0:T(8,128)(2,1)S(1)}, bf16[128,768]{1,0:T(8,128)(2,1)S(1)}, u32[]{:S(2)}, u32[]{:S(2)}) collective-permute-start(bf16[128,768]{1,0:T(8,128)(2,1)S(1)} %mask_grad.1.go_ref.refs_4_), channel_id=1, source_target_pairs={{0,24},{8,16},{16,8},{24,0},{1,25},{9,17},{17,9},{25,1},{2,26},{10... | collective-permute-start | bytes 589832 | tf_op jit(solution)/shard_map/plane_out/ppermute | solution.py:980
  20.9 12.1 %collective-permute-start.10 = (bf16[128,768]{1,0:T(8,128)(2,1)S(1)}, bf16[128,768]{1,0:T(8,128)(2,1)S(1)}, u32[]{:S(2)}, u32[]{:S(2)}) collective-permute-start(bf16[128,768]{1,0:T(8,128)(2,1)S(1)} %mask_grad.1.go_ref.refs_4_), channel_id=1, source_target_pairs={{0,16},{8,24},{16,0},{24,8},{1,17},{9,25},{17,1},{25,9},{2,18},{10... | collective-permute-start | bytes 589832 | tf_op jit(solution)/shard_map/plane_out/ppermute | solution.py:980
  21.4 11.5 %collective-permute-start.9 = (bf16[128,768]{1,0:T(8,128)(2,1)S(1)}, bf16[128,768]{1,0:T(8,128)(2,1)S(1)}, u32[]{:S(2)}, u32[]{:S(2)}) collective-permute-start(bf16[128,768]{1,0:T(8,128)(2,1)S(1)} %mask_grad.1.go_ref.refs_4_), channel_id=1, source_target_pairs={{0,8},{8,0},{16,24},{24,16},{1,9},{9,1},{17,25},{25,17},{2,10},{10... | collective-permute-start | bytes 589832 | tf_op jit(solution)/shard_map/plane_out/ppermute | solution.py:980
  22.5 1.4 %collective-permute-start.5 = (bf16[1,128,512]{2,1,0:T(8,128)(2,1)S(1)}, bf16[1,128,512]{2,1,0:T(8,128)(2,1)S(1)}, u32[]{:S(2)}, u32[]{:S(2)}) collective-permute-start(bf16[1,128,512]{2,1,0:T(8,128)(2,1)S(1)} %get-tuple-element.136.refs_5_), channel_id=1, source_target_pairs={{0,1},{1,0},{2,3},{3,2},{4,5},{5,4},{6,7},{7,6},{8,9},{9,8},{10,11... | collective-permute-start | bytes 393224 | tf_op jit(solution)/shard_map/core_kv/ppermute | solution.py:976
  28.2 4.8 %collective-permute-start.6 = (bf16[192,128]{1,0:T(8,128)(2,1)S(1)}, bf16[192,128]{1,0:T(8,128)(2,1)S(1)}, u32[]{:S(2)}, u32[]{:S(2)}) collective-permute-start(bf16[192,128]{1,0:T(8,128)(2,1)S(1)} %get-tuple-element.138), channel_id=1, source_target_pairs={{0,2},{2,0},{4,6},{6,4},{1,3},{3,1},{5,7},{7,5},{8,10},{10,8},{12,... | collective-permute-start | bytes 147464 | tf_op jit(solution)/shard_map/chip_attn/ppermute | solution.py:980
  29.5 6.4 %collective-permute-start.7 = (bf16[192,128]{1,0:T(8,128)(2,1)S(1)}, bf16[192,128]{1,0:T(8,128)(2,1)S(1)}, u32[]{:S(2)}, u32[]{:S(2)}) collective-permute-start(bf16[192,128]{1,0:T(8,128)(2,1)S(1)} %get-tuple-element.139), channel_id=1, source_target_pairs={{0,4},{2,6},{4,0},{6,2},{1,5},{3,7},{5,1},{7,3},{8,12},{10,14},{12... | collective-permute-start | bytes 147464 | tf_op jit(solution)/shard_map/chip_attn/ppermute | solution.py:980
  32.8 5.9 %collective-permute-start.8 = (bf16[192,128]{1,0:T(8,128)(2,1)S(1)}, bf16[192,128]{1,0:T(8,128)(2,1)S(1)}, u32[]{:S(2)}, u32[]{:S(2)}) collective-permute-start(bf16[192,128]{1,0:T(8,128)(2,1)S(1)} %get-tuple-element.140), channel_id=1, source_target_pairs={{0,6},{2,4},{4,2},{6,0},{1,7},{3,5},{5,3},{7,1},{8,14},{10,12},{12... | collective-permute-start | bytes 147464 | tf_op jit(solution)/shard_map/chip_attn/ppermute | solution.py:980
  42.0 9.6 %collective-permute-start.16 = (bf16[128,768]{1,0:T(8,128)(2,1)S(1)}, bf16[128,768]{1,0:T(8,128)(2,1)S(1)}, u32[]{:S(2)}, u32[]{:S(2)}) collective-permute-start(bf16[128,768]{1,0:T(8,128)(2,1)S(1)} %get-tuple-element.165), channel_id=1, source_target_pairs={{0,8},{8,0},{16,24},{24,16},{1,9},{9,1},{17,25},{25,17},{2,10},{10... | collective-permute-start | bytes 589832 | tf_op jit(solution)/shard_map/plane_act/ppermute | solution.py:980
  42.7 9.0 %collective-permute-start.17 = (bf16[128,768]{1,0:T(8,128)(2,1)S(1)}, bf16[128,768]{1,0:T(8,128)(2,1)S(1)}, u32[]{:S(2)}, u32[]{:S(2)}) collective-permute-start(bf16[128,768]{1,0:T(8,128)(2,1)S(1)} %get-tuple-element.166), channel_id=1, source_target_pairs={{0,16},{8,24},{16,0},{24,8},{1,17},{9,25},{17,1},{25,9},{2,18},{10... | collective-permute-start | bytes 589832 | tf_op jit(solution)/shard_map/plane_act/ppermute | solution.py:980
  44.2 8.4 %collective-permute-start.18 = (bf16[128,768]{1,0:T(8,128)(2,1)S(1)}, bf16[128,768]{1,0:T(8,128)(2,1)S(1)}, u32[]{:S(2)}, u32[]{:S(2)}) collective-permute-start(bf16[128,768]{1,0:T(8,128)(2,1)S(1)} %get-tuple-element.167), channel_id=1, source_target_pairs={{0,24},{8,16},{16,8},{24,0},{1,25},{9,17},{17,9},{25,1},{2,26},{10... | collective-permute-start | bytes 589832 | tf_op jit(solution)/shard_map/plane_act/ppermute | solution.py:980
  52.6 15.1 %collective-permute-start.19 = (bf16[128,2560]{1,0:T(8,128)(2,1)S(1)}, bf16[128,2560]{1,0:T(8,128)(2,1)S(1)}, u32[]{:S(2)}, u32[]{:S(2)}) collective-permute-start(bf16[128,2560]{1,0:T(8,128)(2,1)S(1)} %get-tuple-element.177), channel_id=1, source_target_pairs={{0,24},{8,16},{16,8},{24,0},{1,25},{9,17},{17,9},{25,1},{2,26},{10... | collective-permute-start | bytes 1966088 | tf_op jit(solution)/shard_map/plane_back/ppermute | solution.py:980
  54.4 4.4 %collective-permute-start.12 = (bf16[192,128]{1,0:T(8,128)(2,1)S(1)}, bf16[192,128]{1,0:T(8,128)(2,1)S(1)}, u32[]{:S(2)}, u32[]{:S(2)}) collective-permute-start(bf16[192,128]{1,0:T(8,128)(2,1)S(1)} %get-tuple-element.158), channel_id=1, source_target_pairs={{0,2},{2,0},{4,6},{6,4},{1,3},{3,1},{5,7},{7,5},{8,10},{10,8},{12,... | collective-permute-start | bytes 147464 | tf_op jit(solution)/shard_map/chip_grad/ppermute | solution.py:980
  54.6 5.0 %collective-permute-start.13 = (bf16[192,128]{1,0:T(8,128)(2,1)S(1)}, bf16[192,128]{1,0:T(8,128)(2,1)S(1)}, u32[]{:S(2)}, u32[]{:S(2)}) collective-permute-start(bf16[192,128]{1,0:T(8,128)(2,1)S(1)} %get-tuple-element.159), channel_id=1, source_target_pairs={{0,4},{2,6},{4,0},{6,2},{1,5},{3,7},{5,1},{7,3},{8,12},{10,14},{12... | collective-permute-start | bytes 147464 | tf_op jit(solution)/shard_map/chip_grad/ppermute | solution.py:980
  56.0 5.9 %collective-permute-start.14 = (bf16[192,128]{1,0:T(8,128)(2,1)S(1)}, bf16[192,128]{1,0:T(8,128)(2,1)S(1)}, u32[]{:S(2)}, u32[]{:S(2)}) collective-permute-start(bf16[192,128]{1,0:T(8,128)(2,1)S(1)} %get-tuple-element.160), channel_id=1, source_target_pairs={{0,6},{2,4},{4,2},{6,0},{1,7},{3,5},{5,3},{7,1},{8,14},{10,12},{12... | collective-permute-start | bytes 147464 | tf_op jit(solution)/shard_map/chip_grad/ppermute | solution.py:980
  65.7 2.0 %collective-permute-start.15 = (bf16[4,128,512]{2,1,0:T(8,128)(2,1)S(1)}, bf16[4,128,512]{2,1,0:T(8,128)(2,1)S(1)}, u32[]{:S(2)}, u32[]{:S(2)}) collective-permute-start(bf16[4,128,512]{2,1,0:T(8,128)(2,1)S(1)} %get-tuple-element.163), channel_id=1, source_target_pairs={{0,1},{1,0},{2,3},{3,2},{4,5},{5,4},{6,7},{7,6},{8,9},{9,8},{10,11... | collective-permute-start | bytes 1572872 | tf_op jit(solution)/shard_map/core_grad/ppermute | solution.py:976
  67.7 3.0 %collective-permute-start.23 = (bf16[4,96,768]{2,1,0:T(8,128)(2,1)S(1)}, bf16[4,96,768]{2,1,0:T(8,128)(2,1)S(1)}, u32[]{:S(2)}, u32[]{:S(2)}) collective-permute-start(bf16[4,96,768]{2,1,0:T(8,128)(2,1)S(1)} %get-tuple-element.189), channel_id=1, source_target_pairs={{0,1},{1,0},{2,3},{3,2},{4,5},{5,4},{6,7},{7,6},{8,9},{9,8},{10,11... | collective-permute-start | bytes 1769480 | tf_op jit(solution)/shard_map/core_down/ppermute | solution.py:976
  67.9 20.2 %collective-permute-start.28 = (bf16[128,2560]{1,0:T(8,128)(2,1)S(1)}, bf16[128,2560]{1,0:T(8,128)(2,1)S(1)}, u32[]{:S(2)}, u32[]{:S(2)}) collective-permute-start(bf16[128,2560]{1,0:T(8,128)(2,1)S(1)} %get-tuple-element.203), channel_id=1, source_target_pairs={{0,8},{8,0},{16,24},{24,16},{1,9},{9,1},{17,25},{25,17},{2,10},{10... | collective-permute-start | bytes 1966088 | tf_op jit(solution)/shard_map/plane_back/ppermute | solution.py:980
  69.3 18.8 %collective-permute-start.29 = (bf16[128,2560]{1,0:T(8,128)(2,1)S(1)}, bf16[128,2560]{1,0:T(8,128)(2,1)S(1)}, u32[]{:S(2)}, u32[]{:S(2)}) collective-permute-start(bf16[128,2560]{1,0:T(8,128)(2,1)S(1)} %get-tuple-element.204), channel_id=1, source_target_pairs={{0,16},{8,24},{16,0},{24,8},{1,17},{9,25},{17,1},{25,9},{2,18},{10... | collective-permute-start | bytes 1966088 | tf_op jit(solution)/shard_map/plane_back/ppermute | solution.py:980
  71.4 11.9 %collective-permute-start.30 = (bf16[2,96,768]{2,1,0:T(8,128)(2,1)S(1)}, bf16[2,96,768]{2,1,0:T(8,128)(2,1)S(1)}, u32[]{:S(2)}, u32[]{:S(2)}) collective-permute-start(bf16[2,96,768]{2,1,0:T(8,128)(2,1)S(1)} %get-tuple-element.206), channel_id=1, source_target_pairs={{0,2},{2,0},{4,6},{6,4},{1,3},{3,1},{5,7},{7,5},{8,10},{10,8},{12,... | collective-permute-start | bytes 884744 | tf_op jit(solution)/shard_map/down_sum/ppermute | solution.py:980
  73.0 10.9 %collective-permute-start.21 = (bf16[576,128]{1,0:T(8,128)(2,1)S(1)}, bf16[576,128]{1,0:T(8,128)(2,1)S(1)}, u32[]{:S(2)}, u32[]{:S(2)}) collective-permute-start(bf16[576,128]{1,0:T(8,128)(2,1)S(1)} %get-tuple-element.181), channel_id=1, source_target_pairs={{0,4},{2,6},{4,0},{6,2},{1,5},{3,7},{5,1},{7,3},{8,12},{10,14},{12... | collective-permute-start | bytes 442376 | tf_op jit(solution)/shard_map/chip_qkv/ppermute | solution.py:980
  74.4 13.6 %collective-permute-start.22 = (bf16[576,128]{1,0:T(8,128)(2,1)S(1)}, bf16[576,128]{1,0:T(8,128)(2,1)S(1)}, u32[]{:S(2)}, u32[]{:S(2)}) collective-permute-start(bf16[576,128]{1,0:T(8,128)(2,1)S(1)} %get-tuple-element.182), channel_id=1, source_target_pairs={{0,6},{2,4},{4,2},{6,0},{1,7},{3,5},{5,3},{7,1},{8,14},{10,12},{12... | collective-permute-start | bytes 442376 | tf_op jit(solution)/shard_map/chip_qkv/ppermute | solution.py:980
  89.8 2.4 %collective-permute-start.31 = (bf16[4,128,768]{2,1,0:T(8,128)(2,1)S(1)}, bf16[4,128,768]{2,1,0:T(8,128)(2,1)S(1)}, u32[]{:S(2)}, u32[]{:S(2)}) collective-permute-start(bf16[4,128,768]{2,1,0:T(8,128)(2,1)S(1)} %get-tuple-element.214), channel_id=1, source_target_pairs={{0,1},{1,0},{2,3},{3,2},{4,5},{5,4},{6,7},{7,6},{8,9},{9,8},{10,11... | collective-permute-start | bytes 2359304 | tf_op jit(solution)/shard_map/core_up/ppermute | solution.py:976
  89.9 4.4 %collective-permute-start.24 = (bf16[4,96,768]{2,1,0:T(8,128)(2,1)S(1)}, bf16[4,96,768]{2,1,0:T(8,128)(2,1)S(1)}, u32[]{:S(2)}, u32[]{:S(2)}) collective-permute-start(bf16[4,96,768]{2,1,0:T(8,128)(2,1)S(1)} %get-tuple-element.194), channel_id=1, source_target_pairs={{0,1},{1,0},{2,3},{3,2},{4,5},{5,4},{6,7},{7,6},{8,9},{9,8},{10,11... | collective-permute-start | bytes 1769480 | tf_op jit(solution)/shard_map/core_w/ppermute | solution.py:976
  92.8 17.5 %collective-permute-start.35 = (bf16[2,128,768]{2,1,0:T(8,128)(2,1)S(1)}, bf16[2,128,768]{2,1,0:T(8,128)(2,1)S(1)}, u32[]{:S(2)}, u32[]{:S(2)}) collective-permute-start(bf16[2,128,768]{2,1,0:T(8,128)(2,1)S(1)} %get-tuple-element.215), channel_id=1, source_target_pairs={{0,2},{2,0},{4,6},{6,4},{1,3},{3,1},{5,7},{7,5},{8,10},{10,8},{12,... | collective-permute-start | bytes 1179656 | tf_op jit(solution)/shard_map/up_sum/ppermute | solution.py:980
  94.2 23.5 %copy-start.4 = (bf16[768,768]{1,0:T(8,128)(2,1)S(1)}, bf16[768,768]{1,0:T(8,128)(2,1)}, u32[]{:S(2)}) copy-start(bf16[768,768]{1,0:T(8,128)(2,1)} %refs_8_.3) | copy-start | bytes 3538948
  94.2 23.5 %copy-start.5 = (bf16[768,768]{1,0:T(8,128)(2,1)S(1)}, bf16[768,768]{1,0:T(8,128)(2,1)}, u32[]{:S(2)}) copy-start(bf16[768,768]{1,0:T(8,128)(2,1)} %refs_7_.3) | copy-start | bytes 3538948
  94.9 22.8 %copy-start.3 = (bf16[768,768]{1,0:T(8,128)(2,1)S(1)}, bf16[768,768]{1,0:T(8,128)(2,1)}, u32[]{:S(2)}) copy-start(bf16[768,768]{1,0:T(8,128)(2,1)} %refs_9_.3) | copy-start | bytes 3538948
  94.9 6.2 %collective-permute-start.25 = (bf16[96,768]{1,0:T(8,128)(2,1)S(1)}, bf16[96,768]{1,0:T(8,128)(2,1)S(1)}, u32[]{:S(2)}, u32[]{:S(2)}) collective-permute-start(bf16[96,768]{1,0:T(8,128)(2,1)S(1)} %get-tuple-element.196), channel_id=1, source_target_pairs={{0,8},{8,0},{16,24},{24,16},{1,9},{9,1},{17,25},{25,17},{2,10},{10... | collective-permute-start | bytes 442376 | tf_op jit(solution)/shard_map/plane_w/ppermute | solution.py:980
  96.7 8.5 %collective-permute-start.26 = (bf16[96,768]{1,0:T(8,128)(2,1)S(1)}, bf16[96,768]{1,0:T(8,128)(2,1)S(1)}, u32[]{:S(2)}, u32[]{:S(2)}) collective-permute-start(bf16[96,768]{1,0:T(8,128)(2,1)S(1)} %get-tuple-element.197), channel_id=1, source_target_pairs={{0,16},{8,24},{16,0},{24,8},{1,17},{9,25},{17,1},{25,9},{2,18},{10... | collective-permute-start | bytes 442376 | tf_op jit(solution)/shard_map/plane_w/ppermute | solution.py:980
  97.0 8.2 %collective-permute-start.27 = (bf16[96,768]{1,0:T(8,128)(2,1)S(1)}, bf16[96,768]{1,0:T(8,128)(2,1)S(1)}, u32[]{:S(2)}, u32[]{:S(2)}) collective-permute-start(bf16[96,768]{1,0:T(8,128)(2,1)S(1)} %get-tuple-element.198), channel_id=1, source_target_pairs={{0,24},{8,16},{16,8},{24,0},{1,25},{9,17},{17,9},{25,1},{2,26},{10... | collective-permute-start | bytes 442376 | tf_op jit(solution)/shard_map/plane_w/ppermute | solution.py:980
  98.5 11.9 %collective-permute-start.20 = (bf16[576,128]{1,0:T(8,128)(2,1)S(1)}, bf16[576,128]{1,0:T(8,128)(2,1)S(1)}, u32[]{:S(2)}, u32[]{:S(2)}) collective-permute-start(bf16[576,128]{1,0:T(8,128)(2,1)S(1)} %get-tuple-element.180), channel_id=1, source_target_pairs={{0,2},{2,0},{4,6},{6,4},{1,3},{3,1},{5,7},{7,5},{8,10},{10,8},{12,... | collective-permute-start | bytes 442376 | tf_op jit(solution)/shard_map/chip_qkv/ppermute | solution.py:980
  101.2 9.2 %collective-permute-start.36 = (bf16[1,96,768]{2,1,0:T(8,128)(2,1)S(1)}, bf16[1,96,768]{2,1,0:T(8,128)(2,1)S(1)}, u32[]{:S(2)}, u32[]{:S(2)}) collective-permute-start(bf16[1,96,768]{2,1,0:T(8,128)(2,1)S(1)} %get-tuple-element.230), channel_id=1, source_target_pairs={{0,4},{2,6},{4,0},{6,2},{1,5},{3,7},{5,1},{7,3},{8,12},{10,14},{12... | collective-permute-start | bytes 442376 | tf_op jit(solution)/shard_map/down_sum/ppermute | solution.py:980
  111.0 14.0 %collective-permute-start.37 = (bf16[1,128,768]{2,1,0:T(8,128)(2,1)S(1)}, bf16[1,128,768]{2,1,0:T(8,128)(2,1)S(1)}, u32[]{:S(2)}, u32[]{:S(2)}) collective-permute-start(bf16[1,128,768]{2,1,0:T(8,128)(2,1)S(1)} %get-tuple-element.233), channel_id=1, source_target_pairs={{0,4},{2,6},{4,0},{6,2},{1,5},{3,7},{5,1},{7,3},{8,12},{10,14},{12... | collective-permute-start | bytes 589832 | tf_op jit(solution)/shard_map/up_sum/ppermute | solution.py:980
  113.3 7.9 %collective-permute-start.32 = (bf16[24,768]{1,0:T(8,128)(2,1)S(1)}, bf16[24,768]{1,0:T(8,128)(2,1)S(1)}, u32[]{:S(2)}, u32[]{:S(2)}) collective-permute-start(bf16[24,768]{1,0:T(8,128)(2,1)S(1)} %get-tuple-element.221), channel_id=1, source_target_pairs={{0,2},{2,0},{4,6},{6,4},{1,3},{3,1},{5,7},{7,5},{8,10},{10,8},{12,... | collective-permute-start | bytes 110600 | tf_op jit(solution)/shard_map/chip_w/ppermute | solution.py:980
  113.7 11.4 %collective-permute-start.33 = (bf16[24,768]{1,0:T(8,128)(2,1)S(1)}, bf16[24,768]{1,0:T(8,128)(2,1)S(1)}, u32[]{:S(2)}, u32[]{:S(2)}) collective-permute-start(bf16[24,768]{1,0:T(8,128)(2,1)S(1)} %get-tuple-element.222), channel_id=1, source_target_pairs={{0,4},{2,6},{4,0},{6,2},{1,5},{3,7},{5,1},{7,3},{8,12},{10,14},{12... | collective-permute-start | bytes 110600 | tf_op jit(solution)/shard_map/chip_w/ppermute | solution.py:980
  115.7 9.4 %collective-permute-start.34 = (bf16[24,768]{1,0:T(8,128)(2,1)S(1)}, bf16[24,768]{1,0:T(8,128)(2,1)S(1)}, u32[]{:S(2)}, u32[]{:S(2)}) collective-permute-start(bf16[24,768]{1,0:T(8,128)(2,1)S(1)} %get-tuple-element.223), channel_id=1, source_target_pairs={{0,6},{2,4},{4,2},{6,0},{1,7},{3,5},{5,3},{7,1},{8,14},{10,12},{12... | collective-permute-start | bytes 110600 | tf_op jit(solution)/shard_map/chip_w/ppermute | solution.py:980
  126.3 4.8 %collective-permute-start.38 = (bf16[24,768]{1,0:T(8,128)(2,1)S(1)}, bf16[24,768]{1,0:T(8,128)(2,1)S(1)}, u32[]{:S(2)}, u32[]{:S(2)}) collective-permute-start(bf16[24,768]{1,0:T(8,128)(2,1)S(1)} %get-tuple-element.241), channel_id=1, source_target_pairs={{0,8},{8,0},{16,24},{24,16},{1,9},{9,1},{17,25},{25,17},{2,10},{10... | collective-permute-start | bytes 110600 | tf_op jit(solution)/shard_map/plane_rows/ppermute | solution.py:980
  127.6 4.0 %collective-permute-start.39 = (bf16[24,768]{1,0:T(8,128)(2,1)S(1)}, bf16[24,768]{1,0:T(8,128)(2,1)S(1)}, u32[]{:S(2)}, u32[]{:S(2)}) collective-permute-start(bf16[24,768]{1,0:T(8,128)(2,1)S(1)} %get-tuple-element.242), channel_id=1, source_target_pairs={{0,16},{8,24},{16,0},{24,8},{1,17},{9,25},{17,1},{25,9},{2,18},{10... | collective-permute-start | bytes 110600 | tf_op jit(solution)/shard_map/plane_rows/ppermute | solution.py:980
  128.3 4.9 %collective-permute-start.40 = (bf16[24,768]{1,0:T(8,128)(2,1)S(1)}, bf16[24,768]{1,0:T(8,128)(2,1)S(1)}, u32[]{:S(2)}, u32[]{:S(2)}) collective-permute-start(bf16[24,768]{1,0:T(8,128)(2,1)S(1)} %get-tuple-element.243), channel_id=1, source_target_pairs={{0,24},{8,16},{16,8},{24,0},{1,25},{9,17},{17,9},{25,1},{2,26},{10... | collective-permute-start | bytes 110600 | tf_op jit(solution)/shard_map/plane_rows/ppermute | solution.py:980
  (8 other events, 56.5 us)

commit v6 on v5

--- a/solution.py
+++ b/solution.py
@@ -1092,6 +1092,7 @@
     up_keep, up_send = up_grad_call(place, back, chips, part, model)
     with scope("plane_w"):
         traded = trade(qkv_sums, "rows")
+    up_send = after(up_send, (down_last, grad_pieces[1:2]))
     with scope("core_up"):
         up_recv = swap_core(up_send)
     up_keep, up_away = halve_call(place, up_keep, up_recv, 1)

time: 135 us -> 134 us (level)
  transfers between devices with their start and end apart: 41 -> 41, of which waited for: 17 -> 19; matrix products, arithmetic and copies ran while one was open for 2% -> 2% of each run, Pallas kernels for 22% -> 23%
where the time goes in v6:
time: 134 us
  starting transfers between devices  48.7 us (36%)
  waiting for transfers between devices  43.1 us (32%)
  Pallas kernels  37.4 us (28%)
  local copies, waits for them, and re-layouts  3.65 us (3%)
    ppermute x34, starting transfers between devices, swap(): lax.ppermute(value, axis, [(k, k ^ bit) for k in range(lax.axis_size(axis...  47.2 us
    ppermute x34, waiting for transfers between devices, swap(): lax.ppermute(value, axis, [(k, k ^ bit) for k in range(lax.axis_size(axis...  39.5 us
    pallas_call x24, Pallas kernels, kernel(): pl.pallas_call(body, out_shape=outs if single else listed, in_specs=[smem...  37.4 us
    ppermute x7, waiting for transfers between devices, swap_core(): return lax.ppermute(value, 'core', [(0, 1), (1, 0)])  3.58 us
    dynamic_slice x2, local copies, waits for them, and re-layouts, columns(): mine = lax.dynamic_slice_in_dim(weight, z_index * live, live, 1)  2.82 us
  transfers between devices with their start and end apart: 41, of which 19 were waited for; matrix products, arithmetic and copies ran while one was open for 2% of the time, Pallas kernels for 23%

profile of v6, /device:TPU:0, one launch (start us, length us, event | category | flops | bytes accessed | tf_op | source)
XLA Modules:
  0.0 134.0 jit_solution(9344487042258870722)
XLA Ops:
  0.7 4.1 %collective-permute-start.1 = (bf16[128,768]{1,0:T(8,128)(2,1)}, bf16[128,768]{1,0:T(8,128)(2,1)S(1)}, u32[]{:S(2)}, u32[]{:S(2)}) collective-permute-start(bf16[128,768]{1,0:T(8,128)(2,1)} %bitcast.7), channel_id=1, source_target_pairs={{0,4},{2,6},{4,0},{6,2},{1,5},{3,7},{5,1},{7,3},{8,12},{10,14},{12... | collective-permute-start | bytes 589832 | tf_op jit(solution)/shard_map/gather_in/ppermute | solution.py:980
  4.8 1.6 %collective-permute-start = (bf16[128,768]{1,0:T(8,128)(2,1)}, bf16[128,768]{1,0:T(8,128)(2,1)S(1)}, u32[]{:S(2)}, u32[]{:S(2)}) collective-permute-start(bf16[128,768]{1,0:T(8,128)(2,1)} %bitcast.8), channel_id=1, source_target_pairs={{0,2},{2,0},{4,6},{6,4},{1,3},{3,1},{5,7},{7,5},{8,10},{10,8},{12,... | collective-permute-start | bytes 589832 | tf_op jit(solution)/shard_map/gather_in/ppermute | solution.py:980
  6.4 1.2 constant_dynamic-slice_fusion.2
  7.6 1.6 %constant_dynamic-slice_fusion = (bf16[768,192]{1,0:T(8,128)(2,1)S(1)}, bf16[768,192]{1,0:T(8,128)(2,1)S(1)}) fusion(bf16[768,768]{1,0:T(8,128)(2,1)} %refs_9_.3, s32[]{:T(128)S(6)} %select_n.2, bf16[768,768]{1,0:T(8,128)(2,1)} %refs_8_.3), kind=kLoop, calls=%fused_computation.10 | loop fusion | bytes 1179652 | tf_op jit(solution)/shard_map/dynamic_slice | solution.py:1027
  9.2 5.0 %collective-permute-done.1.refs_1_ = bf16[128,768]{1,0:T(8,128)(2,1)S(1)} collective-permute-done((bf16[128,768]{1,0:T(8,128)(2,1)}, bf16[128,768]{1,0:T(8,128)(2,1)S(1)}, u32[]{:S(2)}, u32[]{:S(2)}) %collective-permute-start.1) | collective-permute-done | bytes 196640 | tf_op jit(solution)/shard_map/gather_in/ppermute | solution.py:980
  18.4 2.5 %collective-permute-start.11 = (bf16[128,768]{1,0:T(8,128)(2,1)S(1)}, bf16[128,768]{1,0:T(8,128)(2,1)S(1)}, u32[]{:S(2)}, u32[]{:S(2)}) collective-permute-start(bf16[128,768]{1,0:T(8,128)(2,1)S(1)} %mask_grad.1.go_ref.refs_4_), channel_id=1, source_target_pairs={{0,24},{8,16},{16,8},{24,0},{1,25},{9,17},{17,9},{25,1},{2,26},{10... | collective-permute-start | bytes 589832 | tf_op jit(solution)/shard_map/plane_out/ppermute | solution.py:980
  22.6 1.3 collective-permute-done.5.refs_8_
  23.9 4.3 %attend.1 = (f32[4,128,256]{2,1,0:T(8,128)S(1)}, bf16[4,2,384,512]{3,2,1,0:T(8,128)(2,1)S(1)}, bf16[4,128,256]{2,1,0:T(8,128)(2,1)S(1)}, bf16[4,128,512]{2,1,0:T...) custom-call(s32[3]{0:T(128)S(1)} %pad_add_fusion.place_ref, ...), custom_call_target="tpu_custom_call" | custom-call | flops 6000000 | bytes 6000 | tf_op jit(solution)/shard_map/attend/pallas_call | solution.py:350
  28.2 1.4 %collective-permute-start.6 = (bf16[192,128]{1,0:T(8,128)(2,1)S(1)}, bf16[192,128]{1,0:T(8,128)(2,1)S(1)}, u32[]{:S(2)}, u32[]{:S(2)}) collective-permute-start(bf16[192,128]{1,0:T(8,128)(2,1)S(1)} %get-tuple-element.139), channel_id=1, source_target_pairs={{0,2},{2,0},{4,6},{6,4},{1,3},{3,1},{5,7},{7,5},{8,10},{10,8},{12,... | collective-permute-start | bytes 147464 | tf_op jit(solution)/shard_map/chip_attn/ppermute | solution.py:980
  29.5 3.3 %collective-permute-start.7 = (bf16[192,128]{1,0:T(8,128)(2,1)S(1)}, bf16[192,128]{1,0:T(8,128)(2,1)S(1)}, u32[]{:S(2)}, u32[]{:S(2)}) collective-permute-start(bf16[192,128]{1,0:T(8,128)(2,1)S(1)} %get-tuple-element.140), channel_id=1, source_target_pairs={{0,4},{2,6},{4,0},{6,2},{1,5},{3,7},{5,1},{7,3},{8,12},{10,14},{12... | collective-permute-start | bytes 147464 | tf_op jit(solution)/shard_map/chip_attn/ppermute | solution.py:980
  33.0 2.9 %collective-permute-done.7.refs_2_ = bf16[192,128]{1,0:T(8,128)(2,1)S(1)} collective-permute-done((bf16[192,128]{1,0:T(8,128)(2,1)S(1)}, bf16[192,128]{1,0:T(8,128)(2,1)S(1)}, u32[]{:S(2)}, u32[]{:S(2)}) %collective-permute-start.7) | collective-permute-done | bytes 49184 | tf_op jit(solution)/shard_map/chip_attn/ppermute | solution.py:980
  35.9 2.8 %collective-permute-done.8.refs_3_ = bf16[192,128]{1,0:T(8,128)(2,1)S(1)} collective-permute-done((bf16[192,128]{1,0:T(8,128)(2,1)S(1)}, bf16[192,128]{1,0:T(8,128)(2,1)S(1)}, u32[]{:S(2)}, u32[]{:S(2)}) %collective-permute-start.8) | collective-permute-done | bytes 49184 | tf_op jit(solution)/shard_map/chip_attn/ppermute | solution.py:980
  38.7 1.4 %norms.1 = (f32[128,768]{1,0:T(8,128)S(1)}, bf16[128,768]{1,0:T(8,128)(2,1)S(1)}, bf16[128,768]{1,0:T(8,128)(2,1)S(1)}) custom-call(s32[3]{0:T(128)S(1)} %pad_add_fusion.place_ref, bf16[192,128]{1,0:T(8,128)(2,1)S(1)} %get-tuple-element.143.refs_0_, bf16[192,128]{1,0:T(8,128)(2,1)S(1)} %collective-permute-done.6.refs_1_, ...), custom_call_target="tpu_custom_call" | custom-call | flops 1500000 | bytes 1500 | tf_op jit(solution)/shard_map/norms/pallas_call | solution.py:350
  40.1 1.9 %up_gelu.1 = (bf16[4,128,768]{2,1,0:T(8,128)(2,1)S(1)}, bf16[4,128,768]{2,1,0:T(8,128)(2,1)S(1)}, bf16[128,768]{1,0:T(8,128)(2,1)S(1)}, bf16[128,768]{1,0:T(8,12...) custom-call(s32[3]{0:T(128)S(1)} %pad_add_fusion.place_ref, ...), custom_call_target="tpu_custom_call" | custom-call | flops 2000000 | bytes 2000 | tf_op jit(solution)/shard_map/up_gelu/pallas_call | solution.py:350
  42.7 1.5 %collective-permute-start.17 = (bf16[128,768]{1,0:T(8,128)(2,1)S(1)}, bf16[128,768]{1,0:T(8,128)(2,1)S(1)}, u32[]{:S(2)}, u32[]{:S(2)}) collective-permute-start(bf16[128,768]{1,0:T(8,128)(2,1)S(1)} %get-tuple-element.167), channel_id=1, source_target_pairs={{0,16},{8,24},{16,0},{24,8},{1,17},{9,25},{17,1},{25,9},{2,18},{10... | collective-permute-start | bytes 589832 | tf_op jit(solution)/shard_map/plane_act/ppermute | solution.py:980
  44.2 1.4 %collective-permute-start.18 = (bf16[128,768]{1,0:T(8,128)(2,1)S(1)}, bf16[128,768]{1,0:T(8,128)(2,1)S(1)}, u32[]{:S(2)}, u32[]{:S(2)}) collective-permute-start(bf16[128,768]{1,0:T(8,128)(2,1)S(1)} %get-tuple-element.168), channel_id=1, source_target_pairs={{0,24},{8,16},{16,8},{24,0},{1,25},{9,17},{17,9},{25,1},{2,26},{10... | collective-permute-start | bytes 589832 | tf_op jit(solution)/shard_map/plane_act/ppermute | solution.py:980
  45.6 6.0 %token_backward.1 = (bf16[128,768]{1,0:T(8,128)(2,1)}, f32[128,768]{1,0:T(8,128)S(1)}, bf16[128,2560]{1,0:T(8,128)(2,1)S(1)}, bf16[128,2560]{1,0:T(8,128)(2,1)S(...) custom-call(s32[3]{0:T(128)S(1)} %pad_add_fusion.place_ref, ...), custom_call_target="tpu_custom_call" | custom-call | flops 9000000 | bytes 9000 | tf_op jit(solution)/shard_map/token_backward/pallas_call | solution.py:350
  52.6 1.8 %collective-permute-start.19 = (bf16[128,2560]{1,0:T(8,128)(2,1)S(1)}, bf16[128,2560]{1,0:T(8,128)(2,1)S(1)}, u32[]{:S(2)}, u32[]{:S(2)}) collective-permute-start(bf16[128,2560]{1,0:T(8,128)(2,1)S(1)} %get-tuple-element.178), channel_id=1, source_target_pairs={{0,24},{8,16},{16,8},{24,0},{1,25},{9,17},{17,9},{25,1},{2,26},{10... | collective-permute-start | bytes 1966088 | tf_op jit(solution)/shard_map/plane_back/ppermute | solution.py:980
  54.6 1.4 %collective-permute-start.13 = (bf16[192,128]{1,0:T(8,128)(2,1)S(1)}, bf16[192,128]{1,0:T(8,128)(2,1)S(1)}, u32[]{:S(2)}, u32[]{:S(2)}) collective-permute-start(bf16[192,128]{1,0:T(8,128)(2,1)S(1)} %get-tuple-element.160), channel_id=1, source_target_pairs={{0,4},{2,6},{4,0},{6,2},{1,5},{3,7},{5,1},{7,3},{8,12},{10,14},{12... | collective-permute-start | bytes 147464 | tf_op jit(solution)/shard_map/chip_grad/ppermute | solution.py:980
  56.0 2.8 %collective-permute-start.14 = (bf16[192,128]{1,0:T(8,128)(2,1)S(1)}, bf16[192,128]{1,0:T(8,128)(2,1)S(1)}, u32[]{:S(2)}, u32[]{:S(2)}) collective-permute-start(bf16[192,128]{1,0:T(8,128)(2,1)S(1)} %get-tuple-element.161), channel_id=1, source_target_pairs={{0,6},{2,4},{4,2},{6,0},{1,7},{3,5},{5,3},{7,1},{8,14},{10,12},{12... | collective-permute-start | bytes 147464 | tf_op jit(solution)/shard_map/chip_grad/ppermute | solution.py:980
  59.6 2.3 %collective-permute-done.14.refs_3_ = bf16[192,128]{1,0:T(8,128)(2,1)S(1)} collective-permute-done((bf16[192,128]{1,0:T(8,128)(2,1)S(1)}, bf16[192,128]{1,0:T(8,128)(2,1)S(1)}, u32[]{:S(2)}, u32[]{:S(2)}) %collective-permute-start.14) | collective-permute-done | bytes 49184 | tf_op jit(solution)/shard_map/chip_grad/ppermute | solution.py:980
  61.9 3.8 %attend_back.1 = (bf16[4,128,256]{2,1,0:T(8,128)(2,1)S(1)}, f32[4,128,512]{2,1,0:T(8,128)S(1)}, bf16[4,128,512]{2,1,0:T(8,128)(2,1)S(1)}) custom-call(s32[3]{0:T(128)S(1)} %pad_add_fusion.place_ref, bf16[4,128,256]{2,1,0:T(8,128)(2,1)S(1)} %get-tuple-element.153.q_ref, bf16[4,128,512]{2,1,0:T(8,128)(2,1)S(1)} %get-tuple-element.154.own_ref, ...), custom_call_target="tpu_custom_call" | custom-call | flops 6000000 | bytes 6000 | tf_op jit(solution)/shard_map/attend_back/pallas_call | solution.py:350
  65.8 1.5 %grad_down.1 = (f32[4,96,768]{2,1,0:T(8,128)S(1)}, bf16[4,96,768]{2,1,0:T(8,128)(2,1)S(1)}) custom-call(s32[3]{0:T(128)S(1)} %pad_add_fusion.place_ref, bf16[128,768]{1,0:T(8,128)(2,1)S(1)} %get-tuple-element.169.refs_0_, bf16[128,768]{1,0:T(8,128)(2,1)S(1)} %collective-permute-done.16.refs_1_, bf16[128,768]{1,0:T(8,128)(2,1)S(1)} %collective-permute-done.17.refs_2_, ...), custom_call_target="tpu_custom_call" | custom-call | flops 3000000 | bytes 3000 | tf_op jit(solution)/shard_map/grad_down/pallas_call | solution.py:350
  67.9 1.4 %collective-permute-start.28 = (bf16[128,2560]{1,0:T(8,128)(2,1)S(1)}, bf16[128,2560]{1,0:T(8,128)(2,1)S(1)}, u32[]{:S(2)}, u32[]{:S(2)}) collective-permute-start(bf16[128,2560]{1,0:T(8,128)(2,1)S(1)} %get-tuple-element.204), channel_id=1, source_target_pairs={{0,8},{8,0},{16,24},{24,16},{1,9},{9,1},{17,25},{25,17},{2,10},{10... | collective-permute-start | bytes 1966088 | tf_op jit(solution)/shard_map/plane_back/ppermute | solution.py:980
  71.4 1.6 %collective-permute-start.30 = (bf16[2,96,768]{2,1,0:T(8,128)(2,1)S(1)}, bf16[2,96,768]{2,1,0:T(8,128)(2,1)S(1)}, u32[]{:S(2)}, u32[]{:S(2)}) collective-permute-start(bf16[2,96,768]{2,1,0:T(8,128)(2,1)S(1)} %get-tuple-element.207), channel_id=1, source_target_pairs={{0,2},{2,0},{4,6},{6,4},{1,3},{3,1},{5,7},{7,5},{8,10},{10,8},{12,... | collective-permute-start | bytes 884744 | tf_op jit(solution)/shard_map/down_sum/ppermute | solution.py:980
  73.0 1.4 %collective-permute-start.21 = (bf16[576,128]{1,0:T(8,128)(2,1)S(1)}, bf16[576,128]{1,0:T(8,128)(2,1)S(1)}, u32[]{:S(2)}, u32[]{:S(2)}) collective-permute-start(bf16[576,128]{1,0:T(8,128)(2,1)S(1)} %get-tuple-element.182), channel_id=1, source_target_pairs={{0,4},{2,6},{4,0},{6,2},{1,5},{3,7},{5,1},{7,3},{8,12},{10,14},{12... | collective-permute-start | bytes 442376 | tf_op jit(solution)/shard_map/chip_qkv/ppermute | solution.py:980
  74.4 1.4 %collective-permute-start.22 = (bf16[576,128]{1,0:T(8,128)(2,1)S(1)}, bf16[576,128]{1,0:T(8,128)(2,1)S(1)}, u32[]{:S(2)}, u32[]{:S(2)}) collective-permute-start(bf16[576,128]{1,0:T(8,128)(2,1)S(1)} %get-tuple-element.183), channel_id=1, source_target_pairs={{0,6},{2,4},{4,2},{6,0},{1,7},{3,5},{5,3},{7,1},{8,14},{10,12},{12... | collective-permute-start | bytes 442376 | tf_op jit(solution)/shard_map/chip_qkv/ppermute | solution.py:980
  75.8 2.5 %grad_qkv.1 = (f32[4,96,768]{2,1,0:T(8,128)S(1)}, bf16[4,96,768]{2,1,0:T(8,128)(2,1)S(1)}) custom-call(s32[3]{0:T(128)S(1)} %pad_add_fusion.place_ref, bf16[1,128,768]{2,1,0:T(8,128)(2,1)S(1)} %get-tuple-element.185.refs_0_, bf16[2,128,768]{2,1,0:T(8,128)(2,1)S(1)} %get-tuple-element.186.refs_1_, bf16[1,128,768]{2,1,0:T(8,128)(2,1)S(1)} %get-tuple-element.187.refs_2_, ...), custom_call_target="tpu_custom_call" | custom-call | flops 4000000 | bytes 4000 | tf_op jit(solution)/shard_map/grad_qkv/pallas_call | solution.py:350
  78.3 4.9 %collective-permute-done.30.in_ref = bf16[2,96,768]{2,1,0:T(8,128)(2,1)S(1)} collective-permute-done((bf16[2,96,768]{2,1,0:T(8,128)(2,1)S(1)}, bf16[2,96,768]{2,1,0:T(8,128)(2,1)S(1)}, u32[]{:S(2)}, u32[]{:S(2)}) %collective-permute-start.30) | collective-permute-done | bytes 294944 | tf_op jit(solution)/shard_map/down_sum/ppermute | solution.py:980
  83.9 3.1 %collective-permute-start.31 = (bf16[1,96,768]{2,1,0:T(8,128)(2,1)S(1)}, bf16[1,96,768]{2,1,0:T(8,128)(2,1)S(1)}, u32[]{:S(2)}, u32[]{:S(2)}) collective-permute-start(bf16[1,96,768]{2,1,0:T(8,128)(2,1)S(1)} %get-tuple-element.216), channel_id=1, source_target_pairs={{0,4},{2,6},{4,0},{6,2},{1,5},{3,7},{5,1},{7,3},{8,12},{10,14},{12... | collective-permute-start | bytes 442376 | tf_op jit(solution)/shard_map/down_sum/ppermute | solution.py:980
  87.0 2.0 %collective-permute-done.22.refs_3_ = bf16[576,128]{1,0:T(8,128)(2,1)S(1)} collective-permute-done((bf16[576,128]{1,0:T(8,128)(2,1)S(1)}, bf16[576,128]{1,0:T(8,128)(2,1)S(1)}, u32[]{:S(2)}, u32[]{:S(2)}) %collective-permute-start.22) | collective-permute-done | bytes 147488 | tf_op jit(solution)/shard_map/chip_qkv/ppermute | solution.py:980
  89.0 1.7 %grad_up_out.1 = (f32[4,128,768]{2,1,0:T(8,128)S(1)}, bf16[4,128,768]{2,1,0:T(8,128)(2,1)S(1)}) custom-call(s32[3]{0:T(128)S(1)} %pad_add_fusion.place_ref, bf16[128,2560]{1,0:T(8,128)(2,1)S(1)} %get-tuple-element.210.refs_0_, bf16[128,2560]{1,0:T(8,128)(2,1)S(1)} %collective-permute-done.28.refs_1_, bf16[128,2560]{1,0:T(8,128)(2,1)S(1)} %collective-permute-done.29.refs_2_, ...), custom_call_target="tpu_custom_call" | custom-call | flops 4000000 | bytes 4000 | tf_op jit(solution)/shard_map/grad_up_out/pallas_call | solution.py:350
  90.7 2.3 %collective-permute-done.20.refs_1_ = bf16[576,128]{1,0:T(8,128)(2,1)S(1)} collective-permute-done((bf16[576,128]{1,0:T(8,128)(2,1)S(1)}, bf16[576,128]{1,0:T(8,128)(2,1)S(1)}, u32[]{:S(2)}, u32[]{:S(2)}) %collective-permute-start.20) | collective-permute-done | bytes 147488 | tf_op jit(solution)/shard_map/chip_qkv/ppermute | solution.py:980
  93.0 2.2 %collective-permute-done.31.in_ref = bf16[1,96,768]{2,1,0:T(8,128)(2,1)S(1)} collective-permute-done((bf16[1,96,768]{2,1,0:T(8,128)(2,1)S(1)}, bf16[1,96,768]{2,1,0:T(8,128)(2,1)S(1)}, u32[]{:S(2)}, u32[]{:S(2)}) %collective-permute-start.31) | collective-permute-done | bytes 147488 | tf_op jit(solution)/shard_map/down_sum/ppermute | solution.py:980
  95.7 1.8 %collective-permute-done.32.in_ref = bf16[4,128,768]{2,1,0:T(8,128)(2,1)S(1)} collective-permute-done((bf16[4,128,768]{2,1,0:T(8,128)(2,1)S(1)}, bf16[4,128,768]{2,1,0:T(8,128)(2,1)S(1)}, u32[]{:S(2)}, u32[]{:S(2)}) %collective-permute-start.32) | collective-permute-done | bytes 786464 | tf_op jit(solution)/shard_map/core_up/ppermute | solution.py:976
  99.0 1.7 %collective-permute-start.25 = (bf16[96,768]{1,0:T(8,128)(2,1)S(1)}, bf16[96,768]{1,0:T(8,128)(2,1)S(1)}, u32[]{:S(2)}, u32[]{:S(2)}) collective-permute-start(bf16[96,768]{1,0:T(8,128)(2,1)S(1)} %get-tuple-element.197), channel_id=1, source_target_pairs={{0,8},{8,0},{16,24},{24,16},{1,9},{9,1},{17,25},{25,17},{2,10},{10... | collective-permute-start | bytes 442376 | tf_op jit(solution)/shard_map/plane_w/ppermute | solution.py:980
  101.1 1.5 %collective-permute-start.27 = (bf16[96,768]{1,0:T(8,128)(2,1)S(1)}, bf16[96,768]{1,0:T(8,128)(2,1)S(1)}, u32[]{:S(2)}, u32[]{:S(2)}) collective-permute-start(bf16[96,768]{1,0:T(8,128)(2,1)S(1)} %get-tuple-element.199), channel_id=1, source_target_pairs={{0,24},{8,16},{16,8},{24,0},{1,25},{9,17},{17,9},{25,1},{2,26},{10... | collective-permute-start | bytes 442376 | tf_op jit(solution)/shard_map/plane_w/ppermute | solution.py:980
  102.6 3.0 %collective-permute-done.25.refs_1_ = bf16[96,768]{1,0:T(8,128)(2,1)S(1)} collective-permute-done((bf16[96,768]{1,0:T(8,128)(2,1)S(1)}, bf16[96,768]{1,0:T(8,128)(2,1)S(1)}, u32[]{:S(2)}, u32[]{:S(2)}) %collective-permute-start.25) | collective-permute-done | bytes 147488 | tf_op jit(solution)/shard_map/plane_w/ppermute | solution.py:980
  105.6 3.9 %collective-permute-done.26.refs_2_ = bf16[96,768]{1,0:T(8,128)(2,1)S(1)} collective-permute-done((bf16[96,768]{1,0:T(8,128)(2,1)S(1)}, bf16[96,768]{1,0:T(8,128)(2,1)S(1)}, u32[]{:S(2)}, u32[]{:S(2)}) %collective-permute-start.26) | collective-permute-done | bytes 147488 | tf_op jit(solution)/shard_map/plane_w/ppermute | solution.py:980
  110.8 1.7 %collective-permute-start.37 = (bf16[1,128,768]{2,1,0:T(8,128)(2,1)S(1)}, bf16[1,128,768]{2,1,0:T(8,128)(2,1)S(1)}, u32[]{:S(2)}, u32[]{:S(2)}) collective-permute-start(bf16[1,128,768]{2,1,0:T(8,128)(2,1)S(1)} %get-tuple-element.235), channel_id=1, source_target_pairs={{0,4},{2,6},{4,0},{6,2},{1,5},{3,7},{5,1},{7,3},{8,12},{10,14},{12... | collective-permute-start | bytes 589832 | tf_op jit(solution)/shard_map/up_sum/ppermute | solution.py:980
  112.9 2.6 %collective-permute-start.34 = (bf16[24,768]{1,0:T(8,128)(2,1)S(1)}, bf16[24,768]{1,0:T(8,128)(2,1)S(1)}, u32[]{:S(2)}, u32[]{:S(2)}) collective-permute-start(bf16[24,768]{1,0:T(8,128)(2,1)S(1)} %get-tuple-element.225), channel_id=1, source_target_pairs={{0,4},{2,6},{4,0},{6,2},{1,5},{3,7},{5,1},{7,3},{8,12},{10,14},{12... | collective-permute-start | bytes 110600 | tf_op jit(solution)/shard_map/chip_w/ppermute | solution.py:980
  115.5 1.4 %collective-permute-start.35 = (bf16[24,768]{1,0:T(8,128)(2,1)S(1)}, bf16[24,768]{1,0:T(8,128)(2,1)S(1)}, u32[]{:S(2)}, u32[]{:S(2)}) collective-permute-start(bf16[24,768]{1,0:T(8,128)(2,1)S(1)} %get-tuple-element.226), channel_id=1, source_target_pairs={{0,6},{2,4},{4,2},{6,0},{1,7},{3,5},{5,3},{7,1},{8,14},{10,12},{12... | collective-permute-start | bytes 110600 | tf_op jit(solution)/shard_map/chip_w/ppermute | solution.py:980
  116.9 2.7 %grad_inputs.1 = bf16[128,768]{1,0:T(8,128)(2,1)} custom-call(s32[3]{0:T(128)S(1)} %pad_add_fusion.place_ref, bf16[576,128]{1,0:T(8,128)(2,1)S(1)} %get-tuple-element.180.refs_0_, bf16[576,128]{1,0:T(8,128)(2,1)S(1)} %collective-permute-done.20.refs_1_, bf16[576,128]{1,0:T(8,128)(2,1)S(1)} %collective-permute-done.21.refs_2_, ...), custom_call_target="tpu_custom_call" | custom-call | flops 3000000 | bytes 3000 | tf_op jit(solution)/shard_map/grad_inputs/pallas_call | solution.py:350
  120.4 4.1 %collective-permute-done.34.refs_2_ = bf16[24,768]{1,0:T(8,128)(2,1)S(1)} collective-permute-done((bf16[24,768]{1,0:T(8,128)(2,1)S(1)}, bf16[24,768]{1,0:T(8,128)(2,1)S(1)}, u32[]{:S(2)}, u32[]{:S(2)}) %collective-permute-start.34) | collective-permute-done | bytes 36896 | tf_op jit(solution)/shard_map/chip_w/ppermute | solution.py:980
  127.9 1.3 collective-permute-start.40
  129.2 1.3 finish_qkv.1
  130.8 1.9 %collective-permute-done.40.refs_3_ = bf16[24,768]{1,0:T(8,128)(2,1)S(1)} collective-permute-done((bf16[24,768]{1,0:T(8,128)(2,1)S(1)}, bf16[24,768]{1,0:T(8,128)(2,1)S(1)}, u32[]{:S(2)}, u32[]{:S(2)}) %collective-permute-start.40) | collective-permute-done | bytes 36896 | tf_op jit(solution)/shard_map/plane_rows/ppermute | solution.py:980
  132.7 1.3 place_up.1
  (92 shorter events, 20.4 us)
Async XLA Ops:
  0.7 13.5 %collective-permute-start.1 = (bf16[128,768]{1,0:T(8,128)(2,1)}, bf16[128,768]{1,0:T(8,128)(2,1)S(1)}, u32[]{:S(2)}, u32[]{:S(2)}) collective-permute-start(bf16[128,768]{1,0:T(8,128)(2,1)} %bitcast.7), channel_id=1, source_target_pairs={{0,4},{2,6},{4,0},{6,2},{1,5},{3,7},{5,1},{7,3},{8,12},{10,14},{12... | collective-permute-start | bytes 589832 | tf_op jit(solution)/shard_map/gather_in/ppermute | solution.py:980
  4.8 11.7 %collective-permute-start = (bf16[128,768]{1,0:T(8,128)(2,1)}, bf16[128,768]{1,0:T(8,128)(2,1)S(1)}, u32[]{:S(2)}, u32[]{:S(2)}) collective-permute-start(bf16[128,768]{1,0:T(8,128)(2,1)} %bitcast.8), channel_id=1, source_target_pairs={{0,2},{2,0},{4,6},{6,4},{1,3},{3,1},{5,7},{7,5},{8,10},{10,8},{12,... | collective-permute-start | bytes 589832 | tf_op jit(solution)/shard_map/gather_in/ppermute | solution.py:980
  14.2 7.2 %collective-permute-start.2 = (bf16[128,768]{1,0:T(8,128)(2,1)S(1)}, bf16[128,768]{1,0:T(8,128)(2,1)S(1)}, u32[]{:S(2)}, u32[]{:S(2)}) collective-permute-start(bf16[128,768]{1,0:T(8,128)(2,1)S(1)} %collective-permute-done.1.refs_1_), channel_id=1, source_target_pairs={{0,2},{2,0},{4,6},{6,4},{1,3},{3,1},{5,7},{7,5},{8,10},{10,8},{12,... | collective-permute-start | bytes 589832 | tf_op jit(solution)/shard_map/gather_in/ppermute | solution.py:980
  16.4 6.1 %collective-permute-start.3 = (bf16[1,128,512]{2,1,0:T(8,128)(2,1)S(1)}, bf16[1,128,512]{2,1,0:T(8,128)(2,1)S(1)}, u32[]{:S(2)}, u32[]{:S(2)}) collective-permute-start(bf16[1,128,512]{2,1,0:T(8,128)(2,1)S(1)} %get-tuple-element.135.refs_3_), channel_id=1, source_target_pairs={{0,1},{1,0},{2,3},{3,2},{4,5},{5,4},{6,7},{7,6},{8,9},{9,8},{10,11... | collective-permute-start | bytes 393224 | tf_op jit(solution)/shard_map/core_kv/ppermute | solution.py:976
  16.5 22.2 %copy-start.1 = (bf16[768,768]{1,0:T(8,128)(2,1)S(1)}, bf16[768,768]{1,0:T(8,128)(2,1)}, u32[]{:S(2)}) copy-start(bf16[768,768]{1,0:T(8,128)(2,1)} %wo_ref.1) | copy-start | bytes 3538948
  16.5 22.2 %copy-start.10 = (f32[768]{0:T(1024)S(1)}, f32[768]{0:T(1024)}, u32[]{:S(2)}) copy-start(f32[768]{0:T(1024)} %g2.1) | copy-start | bytes 9220
  16.5 22.2 %copy-start.11 = (f32[768]{0:T(1024)S(1)}, f32[768]{0:T(1024)}, u32[]{:S(2)}) copy-start(f32[768]{0:T(1024)} %b2.1) | copy-start | bytes 9220
  16.5 22.2 %copy-start.12 = (f32[768]{0:T(1024)S(1)}, f32[768]{0:T(1024)}, u32[]{:S(2)}) copy-start(f32[768]{0:T(1024)} %g3.1) | copy-start | bytes 9220
  16.5 22.2 %copy-start.13 = (f32[768]{0:T(1024)S(1)}, f32[768]{0:T(1024)}, u32[]{:S(2)}) copy-start(f32[768]{0:T(1024)} %b3.1) | copy-start | bytes 9220
  16.5 23.6 %copy-start = (bf16[768,3072]{1,0:T(8,128)(2,1)S(1)}, bf16[768,3072]{1,0:T(8,128)(2,1)}, u32[]{:S(2)}) copy-start(bf16[768,3072]{1,0:T(8,128)(2,1)} %wu_ref.3) | copy-start | bytes 14155780
  17.3 5.3 %collective-permute-start.4 = (bf16[2,128,512]{2,1,0:T(8,128)(2,1)S(1)}, bf16[2,128,512]{2,1,0:T(8,128)(2,1)S(1)}, u32[]{:S(2)}, u32[]{:S(2)}) collective-permute-start(bf16[2,128,512]{2,1,0:T(8,128)(2,1)S(1)} %get-tuple-element.136.refs_4_), channel_id=1, source_target_pairs={{0,1},{1,0},{2,3},{3,2},{4,5},{5,4},{6,7},{7,6},{8,9},{9,8},{10,11... | collective-permute-start | bytes 786440 | tf_op jit(solution)/shard_map/core_kv/ppermute | solution.py:976
  18.4 14.4 %collective-permute-start.11 = (bf16[128,768]{1,0:T(8,128)(2,1)S(1)}, bf16[128,768]{1,0:T(8,128)(2,1)S(1)}, u32[]{:S(2)}, u32[]{:S(2)}) collective-permute-start(bf16[128,768]{1,0:T(8,128)(2,1)S(1)} %mask_grad.1.go_ref.refs_4_), channel_id=1, source_target_pairs={{0,24},{8,16},{16,8},{24,0},{1,25},{9,17},{17,9},{25,1},{2,26},{10... | collective-permute-start | bytes 589832 | tf_op jit(solution)/shard_map/plane_out/ppermute | solution.py:980
  20.9 12.1 %collective-permute-start.10 = (bf16[128,768]{1,0:T(8,128)(2,1)S(1)}, bf16[128,768]{1,0:T(8,128)(2,1)S(1)}, u32[]{:S(2)}, u32[]{:S(2)}) collective-permute-start(bf16[128,768]{1,0:T(8,128)(2,1)S(1)} %mask_grad.1.go_ref.refs_4_), channel_id=1, source_target_pairs={{0,16},{8,24},{16,0},{24,8},{1,17},{9,25},{17,1},{25,9},{2,18},{10... | collective-permute-start | bytes 589832 | tf_op jit(solution)/shard_map/plane_out/ppermute | solution.py:980
  21.4 11.5 %collective-permute-start.9 = (bf16[128,768]{1,0:T(8,128)(2,1)S(1)}, bf16[128,768]{1,0:T(8,128)(2,1)S(1)}, u32[]{:S(2)}, u32[]{:S(2)}) collective-permute-start(bf16[128,768]{1,0:T(8,128)(2,1)S(1)} %mask_grad.1.go_ref.refs_4_), channel_id=1, source_target_pairs={{0,8},{8,0},{16,24},{24,16},{1,9},{9,1},{17,25},{25,17},{2,10},{10... | collective-permute-start | bytes 589832 | tf_op jit(solution)/shard_map/plane_out/ppermute | solution.py:980
  22.5 1.4 %collective-permute-start.5 = (bf16[1,128,512]{2,1,0:T(8,128)(2,1)S(1)}, bf16[1,128,512]{2,1,0:T(8,128)(2,1)S(1)}, u32[]{:S(2)}, u32[]{:S(2)}) collective-permute-start(bf16[1,128,512]{2,1,0:T(8,128)(2,1)S(1)} %get-tuple-element.137.refs_5_), channel_id=1, source_target_pairs={{0,1},{1,0},{2,3},{3,2},{4,5},{5,4},{6,7},{7,6},{8,9},{9,8},{10,11... | collective-permute-start | bytes 393224 | tf_op jit(solution)/shard_map/core_kv/ppermute | solution.py:976
  28.2 4.8 %collective-permute-start.6 = (bf16[192,128]{1,0:T(8,128)(2,1)S(1)}, bf16[192,128]{1,0:T(8,128)(2,1)S(1)}, u32[]{:S(2)}, u32[]{:S(2)}) collective-permute-start(bf16[192,128]{1,0:T(8,128)(2,1)S(1)} %get-tuple-element.139), channel_id=1, source_target_pairs={{0,2},{2,0},{4,6},{6,4},{1,3},{3,1},{5,7},{7,5},{8,10},{10,8},{12,... | collective-permute-start | bytes 147464 | tf_op jit(solution)/shard_map/chip_attn/ppermute | solution.py:980
  29.5 6.4 %collective-permute-start.7 = (bf16[192,128]{1,0:T(8,128)(2,1)S(1)}, bf16[192,128]{1,0:T(8,128)(2,1)S(1)}, u32[]{:S(2)}, u32[]{:S(2)}) collective-permute-start(bf16[192,128]{1,0:T(8,128)(2,1)S(1)} %get-tuple-element.140), channel_id=1, source_target_pairs={{0,4},{2,6},{4,0},{6,2},{1,5},{3,7},{5,1},{7,3},{8,12},{10,14},{12... | collective-permute-start | bytes 147464 | tf_op jit(solution)/shard_map/chip_attn/ppermute | solution.py:980
  32.8 5.9 %collective-permute-start.8 = (bf16[192,128]{1,0:T(8,128)(2,1)S(1)}, bf16[192,128]{1,0:T(8,128)(2,1)S(1)}, u32[]{:S(2)}, u32[]{:S(2)}) collective-permute-start(bf16[192,128]{1,0:T(8,128)(2,1)S(1)} %get-tuple-element.141), channel_id=1, source_target_pairs={{0,6},{2,4},{4,2},{6,0},{1,7},{3,5},{5,3},{7,1},{8,14},{10,12},{12... | collective-permute-start | bytes 147464 | tf_op jit(solution)/shard_map/chip_attn/ppermute | solution.py:980
  42.0 9.6 %collective-permute-start.16 = (bf16[128,768]{1,0:T(8,128)(2,1)S(1)}, bf16[128,768]{1,0:T(8,128)(2,1)S(1)}, u32[]{:S(2)}, u32[]{:S(2)}) collective-permute-start(bf16[128,768]{1,0:T(8,128)(2,1)S(1)} %get-tuple-element.166), channel_id=1, source_target_pairs={{0,8},{8,0},{16,24},{24,16},{1,9},{9,1},{17,25},{25,17},{2,10},{10... | collective-permute-start | bytes 589832 | tf_op jit(solution)/shard_map/plane_act/ppermute | solution.py:980
  42.7 9.0 %collective-permute-start.17 = (bf16[128,768]{1,0:T(8,128)(2,1)S(1)}, bf16[128,768]{1,0:T(8,128)(2,1)S(1)}, u32[]{:S(2)}, u32[]{:S(2)}) collective-permute-start(bf16[128,768]{1,0:T(8,128)(2,1)S(1)} %get-tuple-element.167), channel_id=1, source_target_pairs={{0,16},{8,24},{16,0},{24,8},{1,17},{9,25},{17,1},{25,9},{2,18},{10... | collective-permute-start | bytes 589832 | tf_op jit(solution)/shard_map/plane_act/ppermute | solution.py:980
  44.2 8.4 %collective-permute-start.18 = (bf16[128,768]{1,0:T(8,128)(2,1)S(1)}, bf16[128,768]{1,0:T(8,128)(2,1)S(1)}, u32[]{:S(2)}, u32[]{:S(2)}) collective-permute-start(bf16[128,768]{1,0:T(8,128)(2,1)S(1)} %get-tuple-element.168), channel_id=1, source_target_pairs={{0,24},{8,16},{16,8},{24,0},{1,25},{9,17},{17,9},{25,1},{2,26},{10... | collective-permute-start | bytes 589832 | tf_op jit(solution)/shard_map/plane_act/ppermute | solution.py:980
  52.6 15.1 %collective-permute-start.19 = (bf16[128,2560]{1,0:T(8,128)(2,1)S(1)}, bf16[128,2560]{1,0:T(8,128)(2,1)S(1)}, u32[]{:S(2)}, u32[]{:S(2)}) collective-permute-start(bf16[128,2560]{1,0:T(8,128)(2,1)S(1)} %get-tuple-element.178), channel_id=1, source_target_pairs={{0,24},{8,16},{16,8},{24,0},{1,25},{9,17},{17,9},{25,1},{2,26},{10... | collective-permute-start | bytes 1966088 | tf_op jit(solution)/shard_map/plane_back/ppermute | solution.py:980
  54.4 4.4 %collective-permute-start.12 = (bf16[192,128]{1,0:T(8,128)(2,1)S(1)}, bf16[192,128]{1,0:T(8,128)(2,1)S(1)}, u32[]{:S(2)}, u32[]{:S(2)}) collective-permute-start(bf16[192,128]{1,0:T(8,128)(2,1)S(1)} %get-tuple-element.159), channel_id=1, source_target_pairs={{0,2},{2,0},{4,6},{6,4},{1,3},{3,1},{5,7},{7,5},{8,10},{10,8},{12,... | collective-permute-start | bytes 147464 | tf_op jit(solution)/shard_map/chip_grad/ppermute | solution.py:980
  54.6 5.0 %collective-permute-start.13 = (bf16[192,128]{1,0:T(8,128)(2,1)S(1)}, bf16[192,128]{1,0:T(8,128)(2,1)S(1)}, u32[]{:S(2)}, u32[]{:S(2)}) collective-permute-start(bf16[192,128]{1,0:T(8,128)(2,1)S(1)} %get-tuple-element.160), channel_id=1, source_target_pairs={{0,4},{2,6},{4,0},{6,2},{1,5},{3,7},{5,1},{7,3},{8,12},{10,14},{12... | collective-permute-start | bytes 147464 | tf_op jit(solution)/shard_map/chip_grad/ppermute | solution.py:980
  56.0 5.9 %collective-permute-start.14 = (bf16[192,128]{1,0:T(8,128)(2,1)S(1)}, bf16[192,128]{1,0:T(8,128)(2,1)S(1)}, u32[]{:S(2)}, u32[]{:S(2)}) collective-permute-start(bf16[192,128]{1,0:T(8,128)(2,1)S(1)} %get-tuple-element.161), channel_id=1, source_target_pairs={{0,6},{2,4},{4,2},{6,0},{1,7},{3,5},{5,3},{7,1},{8,14},{10,12},{12... | collective-permute-start | bytes 147464 | tf_op jit(solution)/shard_map/chip_grad/ppermute | solution.py:980
  65.7 2.0 %collective-permute-start.15 = (bf16[4,128,512]{2,1,0:T(8,128)(2,1)S(1)}, bf16[4,128,512]{2,1,0:T(8,128)(2,1)S(1)}, u32[]{:S(2)}, u32[]{:S(2)}) collective-permute-start(bf16[4,128,512]{2,1,0:T(8,128)(2,1)S(1)} %get-tuple-element.164), channel_id=1, source_target_pairs={{0,1},{1,0},{2,3},{3,2},{4,5},{5,4},{6,7},{7,6},{8,9},{9,8},{10,11... | collective-permute-start | bytes 1572872 | tf_op jit(solution)/shard_map/core_grad/ppermute | solution.py:976
  67.7 3.0 %collective-permute-start.23 = (bf16[4,96,768]{2,1,0:T(8,128)(2,1)S(1)}, bf16[4,96,768]{2,1,0:T(8,128)(2,1)S(1)}, u32[]{:S(2)}, u32[]{:S(2)}) collective-permute-start(bf16[4,96,768]{2,1,0:T(8,128)(2,1)S(1)} %get-tuple-element.190), channel_id=1, source_target_pairs={{0,1},{1,0},{2,3},{3,2},{4,5},{5,4},{6,7},{7,6},{8,9},{9,8},{10,11... | collective-permute-start | bytes 1769480 | tf_op jit(solution)/shard_map/core_down/ppermute | solution.py:976
  67.9 21.2 %collective-permute-start.28 = (bf16[128,2560]{1,0:T(8,128)(2,1)S(1)}, bf16[128,2560]{1,0:T(8,128)(2,1)S(1)}, u32[]{:S(2)}, u32[]{:S(2)}) collective-permute-start(bf16[128,2560]{1,0:T(8,128)(2,1)S(1)} %get-tuple-element.204), channel_id=1, source_target_pairs={{0,8},{8,0},{16,24},{24,16},{1,9},{9,1},{17,25},{25,17},{2,10},{10... | collective-permute-start | bytes 1966088 | tf_op jit(solution)/shard_map/plane_back/ppermute | solution.py:980
  69.3 19.7 %collective-permute-start.29 = (bf16[128,2560]{1,0:T(8,128)(2,1)S(1)}, bf16[128,2560]{1,0:T(8,128)(2,1)S(1)}, u32[]{:S(2)}, u32[]{:S(2)}) collective-permute-start(bf16[128,2560]{1,0:T(8,128)(2,1)S(1)} %get-tuple-element.205), channel_id=1, source_target_pairs={{0,16},{8,24},{16,0},{24,8},{1,17},{9,25},{17,1},{25,9},{2,18},{10... | collective-permute-start | bytes 1966088 | tf_op jit(solution)/shard_map/plane_back/ppermute | solution.py:980
  71.4 11.9 %collective-permute-start.30 = (bf16[2,96,768]{2,1,0:T(8,128)(2,1)S(1)}, bf16[2,96,768]{2,1,0:T(8,128)(2,1)S(1)}, u32[]{:S(2)}, u32[]{:S(2)}) collective-permute-start(bf16[2,96,768]{2,1,0:T(8,128)(2,1)S(1)} %get-tuple-element.207), channel_id=1, source_target_pairs={{0,2},{2,0},{4,6},{6,4},{1,3},{3,1},{5,7},{7,5},{8,10},{10,8},{12,... | collective-permute-start | bytes 884744 | tf_op jit(solution)/shard_map/down_sum/ppermute | solution.py:980
  73.0 10.9 %collective-permute-start.21 = (bf16[576,128]{1,0:T(8,128)(2,1)S(1)}, bf16[576,128]{1,0:T(8,128)(2,1)S(1)}, u32[]{:S(2)}, u32[]{:S(2)}) collective-permute-start(bf16[576,128]{1,0:T(8,128)(2,1)S(1)} %get-tuple-element.182), channel_id=1, source_target_pairs={{0,4},{2,6},{4,0},{6,2},{1,5},{3,7},{5,1},{7,3},{8,12},{10,14},{12... | collective-permute-start | bytes 442376 | tf_op jit(solution)/shard_map/chip_qkv/ppermute | solution.py:980
  74.4 14.6 %collective-permute-start.22 = (bf16[576,128]{1,0:T(8,128)(2,1)S(1)}, bf16[576,128]{1,0:T(8,128)(2,1)S(1)}, u32[]{:S(2)}, u32[]{:S(2)}) collective-permute-start(bf16[576,128]{1,0:T(8,128)(2,1)S(1)} %get-tuple-element.183), channel_id=1, source_target_pairs={{0,6},{2,4},{4,2},{6,0},{1,7},{3,5},{5,3},{7,1},{8,14},{10,12},{12... | collective-permute-start | bytes 442376 | tf_op jit(solution)/shard_map/chip_qkv/ppermute | solution.py:980
  83.3 9.7 %collective-permute-start.20 = (bf16[576,128]{1,0:T(8,128)(2,1)S(1)}, bf16[576,128]{1,0:T(8,128)(2,1)S(1)}, u32[]{:S(2)}, u32[]{:S(2)}) collective-permute-start(bf16[576,128]{1,0:T(8,128)(2,1)S(1)} %get-tuple-element.181), channel_id=1, source_target_pairs={{0,2},{2,0},{4,6},{6,4},{1,3},{3,1},{5,7},{7,5},{8,10},{10,8},{12,... | collective-permute-start | bytes 442376 | tf_op jit(solution)/shard_map/chip_qkv/ppermute | solution.py:980
  83.9 11.3 %collective-permute-start.31 = (bf16[1,96,768]{2,1,0:T(8,128)(2,1)S(1)}, bf16[1,96,768]{2,1,0:T(8,128)(2,1)S(1)}, u32[]{:S(2)}, u32[]{:S(2)}) collective-permute-start(bf16[1,96,768]{2,1,0:T(8,128)(2,1)S(1)} %get-tuple-element.216), channel_id=1, source_target_pairs={{0,4},{2,6},{4,0},{6,2},{1,5},{3,7},{5,1},{7,3},{8,12},{10,14},{12... | collective-permute-start | bytes 442376 | tf_op jit(solution)/shard_map/down_sum/ppermute | solution.py:980
  95.2 2.3 %collective-permute-start.32 = (bf16[4,128,768]{2,1,0:T(8,128)(2,1)S(1)}, bf16[4,128,768]{2,1,0:T(8,128)(2,1)S(1)}, u32[]{:S(2)}, u32[]{:S(2)}) collective-permute-start(bf16[4,128,768]{2,1,0:T(8,128)(2,1)S(1)} %get-tuple-element.217), channel_id=1, source_target_pairs={{0,1},{1,0},{2,3},{3,2},{4,5},{5,4},{6,7},{7,6},{8,9},{9,8},{10,11... | collective-permute-start | bytes 2359304 | tf_op jit(solution)/shard_map/core_up/ppermute | solution.py:976
  95.2 3.1 %collective-permute-start.24 = (bf16[4,96,768]{2,1,0:T(8,128)(2,1)S(1)}, bf16[4,96,768]{2,1,0:T(8,128)(2,1)S(1)}, u32[]{:S(2)}, u32[]{:S(2)}) collective-permute-start(bf16[4,96,768]{2,1,0:T(8,128)(2,1)S(1)} %get-tuple-element.195), channel_id=1, source_target_pairs={{0,1},{1,0},{2,3},{3,2},{4,5},{5,4},{6,7},{7,6},{8,9},{9,8},{10,11... | collective-permute-start | bytes 1769480 | tf_op jit(solution)/shard_map/core_w/ppermute | solution.py:976
  98.2 12.0 %collective-permute-start.36 = (bf16[2,128,768]{2,1,0:T(8,128)(2,1)S(1)}, bf16[2,128,768]{2,1,0:T(8,128)(2,1)S(1)}, u32[]{:S(2)}, u32[]{:S(2)}) collective-permute-start(bf16[2,128,768]{2,1,0:T(8,128)(2,1)S(1)} %get-tuple-element.218), channel_id=1, source_target_pairs={{0,2},{2,0},{4,6},{6,4},{1,3},{3,1},{5,7},{7,5},{8,10},{10,8},{12,... | collective-permute-start | bytes 1179656 | tf_op jit(solution)/shard_map/up_sum/ppermute | solution.py:980
  98.3 18.6 %copy-start.5 = (bf16[768,768]{1,0:T(8,128)(2,1)S(1)}, bf16[768,768]{1,0:T(8,128)(2,1)}, u32[]{:S(2)}) copy-start(bf16[768,768]{1,0:T(8,128)(2,1)} %refs_7_.3) | copy-start | bytes 3538948
  99.0 6.6 %collective-permute-start.25 = (bf16[96,768]{1,0:T(8,128)(2,1)S(1)}, bf16[96,768]{1,0:T(8,128)(2,1)S(1)}, u32[]{:S(2)}, u32[]{:S(2)}) collective-permute-start(bf16[96,768]{1,0:T(8,128)(2,1)S(1)} %get-tuple-element.197), channel_id=1, source_target_pairs={{0,8},{8,0},{16,24},{24,16},{1,9},{9,1},{17,25},{25,17},{2,10},{10... | collective-permute-start | bytes 442376 | tf_op jit(solution)/shard_map/plane_w/ppermute | solution.py:980
  100.7 8.8 %collective-permute-start.26 = (bf16[96,768]{1,0:T(8,128)(2,1)S(1)}, bf16[96,768]{1,0:T(8,128)(2,1)S(1)}, u32[]{:S(2)}, u32[]{:S(2)}) collective-permute-start(bf16[96,768]{1,0:T(8,128)(2,1)S(1)} %get-tuple-element.198), channel_id=1, source_target_pairs={{0,16},{8,24},{16,0},{24,8},{1,17},{9,25},{17,1},{25,9},{2,18},{10... | collective-permute-start | bytes 442376 | tf_op jit(solution)/shard_map/plane_w/ppermute | solution.py:980
  101.1 8.4 %collective-permute-start.27 = (bf16[96,768]{1,0:T(8,128)(2,1)S(1)}, bf16[96,768]{1,0:T(8,128)(2,1)S(1)}, u32[]{:S(2)}, u32[]{:S(2)}) collective-permute-start(bf16[96,768]{1,0:T(8,128)(2,1)S(1)} %get-tuple-element.199), channel_id=1, source_target_pairs={{0,24},{8,16},{16,8},{24,0},{1,25},{9,17},{17,9},{25,1},{2,26},{10... | collective-permute-start | bytes 442376 | tf_op jit(solution)/shard_map/plane_w/ppermute | solution.py:980
  110.8 13.6 %collective-permute-start.37 = (bf16[1,128,768]{2,1,0:T(8,128)(2,1)S(1)}, bf16[1,128,768]{2,1,0:T(8,128)(2,1)S(1)}, u32[]{:S(2)}, u32[]{:S(2)}) collective-permute-start(bf16[1,128,768]{2,1,0:T(8,128)(2,1)S(1)} %get-tuple-element.235), channel_id=1, source_target_pairs={{0,4},{2,6},{4,0},{6,2},{1,5},{3,7},{5,1},{7,3},{8,12},{10,14},{12... | collective-permute-start | bytes 589832 | tf_op jit(solution)/shard_map/up_sum/ppermute | solution.py:980
  112.5 7.9 %collective-permute-start.33 = (bf16[24,768]{1,0:T(8,128)(2,1)S(1)}, bf16[24,768]{1,0:T(8,128)(2,1)S(1)}, u32[]{:S(2)}, u32[]{:S(2)}) collective-permute-start(bf16[24,768]{1,0:T(8,128)(2,1)S(1)} %get-tuple-element.224), channel_id=1, source_target_pairs={{0,2},{2,0},{4,6},{6,4},{1,3},{3,1},{5,7},{7,5},{8,10},{10,8},{12,... | collective-permute-start | bytes 110600 | tf_op jit(solution)/shard_map/chip_w/ppermute | solution.py:980
  112.9 11.6 %collective-permute-start.34 = (bf16[24,768]{1,0:T(8,128)(2,1)S(1)}, bf16[24,768]{1,0:T(8,128)(2,1)S(1)}, u32[]{:S(2)}, u32[]{:S(2)}) collective-permute-start(bf16[24,768]{1,0:T(8,128)(2,1)S(1)} %get-tuple-element.225), channel_id=1, source_target_pairs={{0,4},{2,6},{4,0},{6,2},{1,5},{3,7},{5,1},{7,3},{8,12},{10,14},{12... | collective-permute-start | bytes 110600 | tf_op jit(solution)/shard_map/chip_w/ppermute | solution.py:980
  115.5 9.0 %collective-permute-start.35 = (bf16[24,768]{1,0:T(8,128)(2,1)S(1)}, bf16[24,768]{1,0:T(8,128)(2,1)S(1)}, u32[]{:S(2)}, u32[]{:S(2)}) collective-permute-start(bf16[24,768]{1,0:T(8,128)(2,1)S(1)} %get-tuple-element.226), channel_id=1, source_target_pairs={{0,6},{2,4},{4,2},{6,0},{1,7},{3,5},{5,3},{7,1},{8,14},{10,12},{12... | collective-permute-start | bytes 110600 | tf_op jit(solution)/shard_map/chip_w/ppermute | solution.py:980
  125.7 4.8 %collective-permute-start.38 = (bf16[24,768]{1,0:T(8,128)(2,1)S(1)}, bf16[24,768]{1,0:T(8,128)(2,1)S(1)}, u32[]{:S(2)}, u32[]{:S(2)}) collective-permute-start(bf16[24,768]{1,0:T(8,128)(2,1)S(1)} %get-tuple-element.243), channel_id=1, source_target_pairs={{0,8},{8,0},{16,24},{24,16},{1,9},{9,1},{17,25},{25,17},{2,10},{10... | collective-permute-start | bytes 110600 | tf_op jit(solution)/shard_map/plane_rows/ppermute | solution.py:980
  126.8 4.0 %collective-permute-start.39 = (bf16[24,768]{1,0:T(8,128)(2,1)S(1)}, bf16[24,768]{1,0:T(8,128)(2,1)S(1)}, u32[]{:S(2)}, u32[]{:S(2)}) collective-permute-start(bf16[24,768]{1,0:T(8,128)(2,1)S(1)} %get-tuple-element.244), channel_id=1, source_target_pairs={{0,16},{8,24},{16,0},{24,8},{1,17},{9,25},{17,1},{25,9},{2,18},{10... | collective-permute-start | bytes 110600 | tf_op jit(solution)/shard_map/plane_rows/ppermute | solution.py:980
  127.9 4.9 %collective-permute-start.40 = (bf16[24,768]{1,0:T(8,128)(2,1)S(1)}, bf16[24,768]{1,0:T(8,128)(2,1)S(1)}, u32[]{:S(2)}, u32[]{:S(2)}) collective-permute-start(bf16[24,768]{1,0:T(8,128)(2,1)S(1)} %get-tuple-element.245), channel_id=1, source_target_pairs={{0,24},{8,16},{16,8},{24,0},{1,25},{9,17},{17,9},{25,1},{2,26},{10... | collective-permute-start | bytes 110600 | tf_op jit(solution)/shard_map/plane_rows/ppermute | solution.py:980
  (8 other events, 48.5 us)

commit v7 on v5

--- a/solution.py
+++ b/solution.py
@@ -1083,15 +1083,17 @@
         place, groups, units, grad_qkv, ln1_gain, ln1_bias, w_heads, parts, live, width
     )
     down_recv = after(down_recv, qkv_send)
+    with scope("down_sum"):
+        down_keep, down_last = scatter_chips(place, down_keep, down_recv, chips, 2)
+    qkv_send = after(qkv_send, (down_keep, grad_pieces[2:3]))
     with scope("core_w"):
         qkv_send = swap_core(qkv_send)
     qkv_sums = spread_call(place, qkv_keep, qkv_send)
-    with scope("down_sum"):
-        down_keep, down_last = scatter_chips(place, down_keep, down_recv, chips, 2)
-    back = after(back, (down_keep, grad_pieces[2:]))
+    back = after(back, (down_keep, grad_pieces[2:3]))
     up_keep, up_send = up_grad_call(place, back, chips, part, model)
     with scope("plane_w"):
         traded = trade(qkv_sums, "rows")
+    up_send = after(up_send, (down_last, grad_pieces[1:2], qkv_sums))
     with scope("core_up"):
         up_recv = swap_core(up_send)
     up_keep, up_away = halve_call(place, up_keep, up_recv, 1)

time: 135 us -> 136 us (level)
  waiting for transfers between devices: 42.6 us -> 45.6 us
  starting transfers between devices: 49.6 us -> 47.8 us
    ppermute x7, waiting for transfers between devices: 3.5 us -> 5.07 us  [swap_core(): return lax.ppermute(value, 'core', [(0, 1), (1, 0)])]
    ppermute x34, waiting for transfers between devices: 39.1 us -> 40.6 us  [swap(): lax.ppermute(value, axis, [(k, k ^ bit) for k in range(lax.axis_size(axis...]
  transfers between devices with their start and end apart: 41 -> 41, of which waited for: 17 -> 20; matrix products, arithmetic and copies ran while one was open for 2% -> 2% of each run, Pallas kernels for 22% -> 22%
where the time goes in v7:
time: 136 us
  starting transfers between devices  47.8 us (35%)
  waiting for transfers between devices  45.6 us (34%)
  Pallas kernels  37.4 us (28%)
  local copies, waits for them, and re-layouts  3.65 us (3%)
    ppermute x34, starting transfers between devices, swap(): lax.ppermute(value, axis, [(k, k ^ bit) for k in range(lax.axis_size(axis...  46.8 us
    ppermute x34, waiting for transfers between devices, swap(): lax.ppermute(value, axis, [(k, k ^ bit) for k in range(lax.axis_size(axis...  40.6 us
    pallas_call x24, Pallas kernels, kernel(): pl.pallas_call(body, out_shape=outs if single else listed, in_specs=[smem...  37.4 us
    ppermute x7, waiting for transfers between devices, swap_core(): return lax.ppermute(value, 'core', [(0, 1), (1, 0)])  5.07 us
    dynamic_slice x2, local copies, waits for them, and re-layouts, columns(): mine = lax.dynamic_slice_in_dim(weight, z_index * live, live, 1)  2.82 us
  transfers between devices with their start and end apart: 41, of which 20 were waited for; matrix products, arithmetic and copies ran while one was open for 2% of the time, Pallas kernels for 22%

profile of v7, /device:TPU:0, one launch (start us, length us, event | category | flops | bytes accessed | tf_op | source)
XLA Modules:
  0.0 135.7 jit_solution(1839061263189917955)
XLA Ops:
  0.7 4.1 %collective-permute-start.1 = (bf16[128,768]{1,0:T(8,128)(2,1)}, bf16[128,768]{1,0:T(8,128)(2,1)S(1)}, u32[]{:S(2)}, u32[]{:S(2)}) collective-permute-start(bf16[128,768]{1,0:T(8,128)(2,1)} %bitcast.7), channel_id=1, source_target_pairs={{0,4},{2,6},{4,0},{6,2},{1,5},{3,7},{5,1},{7,3},{8,12},{10,14},{12... | collective-permute-start | bytes 589832 | tf_op jit(solution)/shard_map/gather_in/ppermute | solution.py:980
  4.8 1.6 %collective-permute-start = (bf16[128,768]{1,0:T(8,128)(2,1)}, bf16[128,768]{1,0:T(8,128)(2,1)S(1)}, u32[]{:S(2)}, u32[]{:S(2)}) collective-permute-start(bf16[128,768]{1,0:T(8,128)(2,1)} %bitcast.8), channel_id=1, source_target_pairs={{0,2},{2,0},{4,6},{6,4},{1,3},{3,1},{5,7},{7,5},{8,10},{10,8},{12,... | collective-permute-start | bytes 589832 | tf_op jit(solution)/shard_map/gather_in/ppermute | solution.py:980
  6.4 1.2 constant_dynamic-slice_fusion.2
  7.6 1.6 %constant_dynamic-slice_fusion = (bf16[768,192]{1,0:T(8,128)(2,1)S(1)}, bf16[768,192]{1,0:T(8,128)(2,1)S(1)}) fusion(bf16[768,768]{1,0:T(8,128)(2,1)} %refs_9_.3, s32[]{:T(128)S(6)} %select_n.2, bf16[768,768]{1,0:T(8,128)(2,1)} %refs_8_.3), kind=kLoop, calls=%fused_computation.10 | loop fusion | bytes 1179652 | tf_op jit(solution)/shard_map/dynamic_slice | solution.py:1027
  9.2 5.0 %collective-permute-done.1.refs_1_ = bf16[128,768]{1,0:T(8,128)(2,1)S(1)} collective-permute-done((bf16[128,768]{1,0:T(8,128)(2,1)}, bf16[128,768]{1,0:T(8,128)(2,1)S(1)}, u32[]{:S(2)}, u32[]{:S(2)}) %collective-permute-start.1) | collective-permute-done | bytes 196640 | tf_op jit(solution)/shard_map/gather_in/ppermute | solution.py:980
  18.4 2.5 %collective-permute-start.11 = (bf16[128,768]{1,0:T(8,128)(2,1)S(1)}, bf16[128,768]{1,0:T(8,128)(2,1)S(1)}, u32[]{:S(2)}, u32[]{:S(2)}) collective-permute-start(bf16[128,768]{1,0:T(8,128)(2,1)S(1)} %mask_grad.1.go_ref.refs_4_), channel_id=1, source_target_pairs={{0,24},{8,16},{16,8},{24,0},{1,25},{9,17},{17,9},{25,1},{2,26},{10... | collective-permute-start | bytes 589832 | tf_op jit(solution)/shard_map/plane_out/ppermute | solution.py:980
  22.6 1.3 collective-permute-done.5.refs_8_
  23.9 4.3 %attend.1 = (f32[4,128,256]{2,1,0:T(8,128)S(1)}, bf16[4,2,384,512]{3,2,1,0:T(8,128)(2,1)S(1)}, bf16[4,128,256]{2,1,0:T(8,128)(2,1)S(1)}, bf16[4,128,512]{2,1,0:T...) custom-call(s32[3]{0:T(128)S(1)} %pad_add_fusion.place_ref, ...), custom_call_target="tpu_custom_call" | custom-call | flops 6000000 | bytes 6000 | tf_op jit(solution)/shard_map/attend/pallas_call | solution.py:350
  28.2 1.4 %collective-permute-start.6 = (bf16[192,128]{1,0:T(8,128)(2,1)S(1)}, bf16[192,128]{1,0:T(8,128)(2,1)S(1)}, u32[]{:S(2)}, u32[]{:S(2)}) collective-permute-start(bf16[192,128]{1,0:T(8,128)(2,1)S(1)} %get-tuple-element.140), channel_id=1, source_target_pairs={{0,2},{2,0},{4,6},{6,4},{1,3},{3,1},{5,7},{7,5},{8,10},{10,8},{12,... | collective-permute-start | bytes 147464 | tf_op jit(solution)/shard_map/chip_attn/ppermute | solution.py:980
  29.5 3.3 %collective-permute-start.7 = (bf16[192,128]{1,0:T(8,128)(2,1)S(1)}, bf16[192,128]{1,0:T(8,128)(2,1)S(1)}, u32[]{:S(2)}, u32[]{:S(2)}) collective-permute-start(bf16[192,128]{1,0:T(8,128)(2,1)S(1)} %get-tuple-element.141), channel_id=1, source_target_pairs={{0,4},{2,6},{4,0},{6,2},{1,5},{3,7},{5,1},{7,3},{8,12},{10,14},{12... | collective-permute-start | bytes 147464 | tf_op jit(solution)/shard_map/chip_attn/ppermute | solution.py:980
  33.0 2.9 %collective-permute-done.7.refs_2_ = bf16[192,128]{1,0:T(8,128)(2,1)S(1)} collective-permute-done((bf16[192,128]{1,0:T(8,128)(2,1)S(1)}, bf16[192,128]{1,0:T(8,128)(2,1)S(1)}, u32[]{:S(2)}, u32[]{:S(2)}) %collective-permute-start.7) | collective-permute-done | bytes 49184 | tf_op jit(solution)/shard_map/chip_attn/ppermute | solution.py:980
  35.9 2.8 %collective-permute-done.8.refs_3_ = bf16[192,128]{1,0:T(8,128)(2,1)S(1)} collective-permute-done((bf16[192,128]{1,0:T(8,128)(2,1)S(1)}, bf16[192,128]{1,0:T(8,128)(2,1)S(1)}, u32[]{:S(2)}, u32[]{:S(2)}) %collective-permute-start.8) | collective-permute-done | bytes 49184 | tf_op jit(solution)/shard_map/chip_attn/ppermute | solution.py:980
  38.7 1.4 %norms.1 = (f32[128,768]{1,0:T(8,128)S(1)}, bf16[128,768]{1,0:T(8,128)(2,1)S(1)}, bf16[128,768]{1,0:T(8,128)(2,1)S(1)}) custom-call(s32[3]{0:T(128)S(1)} %pad_add_fusion.place_ref, bf16[192,128]{1,0:T(8,128)(2,1)S(1)} %get-tuple-element.144.refs_0_, bf16[192,128]{1,0:T(8,128)(2,1)S(1)} %collective-permute-done.6.refs_1_, ...), custom_call_target="tpu_custom_call" | custom-call | flops 1500000 | bytes 1500 | tf_op jit(solution)/shard_map/norms/pallas_call | solution.py:350
  40.1 1.9 %up_gelu.1 = (bf16[4,128,768]{2,1,0:T(8,128)(2,1)S(1)}, bf16[4,128,768]{2,1,0:T(8,128)(2,1)S(1)}, bf16[128,768]{1,0:T(8,128)(2,1)S(1)}, bf16[128,768]{1,0:T(8,12...) custom-call(s32[3]{0:T(128)S(1)} %pad_add_fusion.place_ref, ...), custom_call_target="tpu_custom_call" | custom-call | flops 2000000 | bytes 2000 | tf_op jit(solution)/shard_map/up_gelu/pallas_call | solution.py:350
  42.7 1.5 %collective-permute-start.17 = (bf16[128,768]{1,0:T(8,128)(2,1)S(1)}, bf16[128,768]{1,0:T(8,128)(2,1)S(1)}, u32[]{:S(2)}, u32[]{:S(2)}) collective-permute-start(bf16[128,768]{1,0:T(8,128)(2,1)S(1)} %get-tuple-element.168), channel_id=1, source_target_pairs={{0,16},{8,24},{16,0},{24,8},{1,17},{9,25},{17,1},{25,9},{2,18},{10... | collective-permute-start | bytes 589832 | tf_op jit(solution)/shard_map/plane_act/ppermute | solution.py:980
  44.2 1.4 %collective-permute-start.18 = (bf16[128,768]{1,0:T(8,128)(2,1)S(1)}, bf16[128,768]{1,0:T(8,128)(2,1)S(1)}, u32[]{:S(2)}, u32[]{:S(2)}) collective-permute-start(bf16[128,768]{1,0:T(8,128)(2,1)S(1)} %get-tuple-element.169), channel_id=1, source_target_pairs={{0,24},{8,16},{16,8},{24,0},{1,25},{9,17},{17,9},{25,1},{2,26},{10... | collective-permute-start | bytes 589832 | tf_op jit(solution)/shard_map/plane_act/ppermute | solution.py:980
  45.6 6.0 %token_backward.1 = (bf16[128,768]{1,0:T(8,128)(2,1)}, f32[128,768]{1,0:T(8,128)S(1)}, bf16[128,2560]{1,0:T(8,128)(2,1)S(1)}, bf16[128,2560]{1,0:T(8,128)(2,1)S(...) custom-call(s32[3]{0:T(128)S(1)} %pad_add_fusion.place_ref, ...), custom_call_target="tpu_custom_call" | custom-call | flops 9000000 | bytes 9000 | tf_op jit(solution)/shard_map/token_backward/pallas_call | solution.py:350
  52.6 1.8 %collective-permute-start.19 = (bf16[128,2560]{1,0:T(8,128)(2,1)S(1)}, bf16[128,2560]{1,0:T(8,128)(2,1)S(1)}, u32[]{:S(2)}, u32[]{:S(2)}) collective-permute-start(bf16[128,2560]{1,0:T(8,128)(2,1)S(1)} %get-tuple-element.179), channel_id=1, source_target_pairs={{0,24},{8,16},{16,8},{24,0},{1,25},{9,17},{17,9},{25,1},{2,26},{10... | collective-permute-start | bytes 1966088 | tf_op jit(solution)/shard_map/plane_back/ppermute | solution.py:980
  54.6 1.4 %collective-permute-start.13 = (bf16[192,128]{1,0:T(8,128)(2,1)S(1)}, bf16[192,128]{1,0:T(8,128)(2,1)S(1)}, u32[]{:S(2)}, u32[]{:S(2)}) collective-permute-start(bf16[192,128]{1,0:T(8,128)(2,1)S(1)} %get-tuple-element.161), channel_id=1, source_target_pairs={{0,4},{2,6},{4,0},{6,2},{1,5},{3,7},{5,1},{7,3},{8,12},{10,14},{12... | collective-permute-start | bytes 147464 | tf_op jit(solution)/shard_map/chip_grad/ppermute | solution.py:980
  56.0 2.8 %collective-permute-start.14 = (bf16[192,128]{1,0:T(8,128)(2,1)S(1)}, bf16[192,128]{1,0:T(8,128)(2,1)S(1)}, u32[]{:S(2)}, u32[]{:S(2)}) collective-permute-start(bf16[192,128]{1,0:T(8,128)(2,1)S(1)} %get-tuple-element.162), channel_id=1, source_target_pairs={{0,6},{2,4},{4,2},{6,0},{1,7},{3,5},{5,3},{7,1},{8,14},{10,12},{12... | collective-permute-start | bytes 147464 | tf_op jit(solution)/shard_map/chip_grad/ppermute | solution.py:980
  59.6 2.3 %collective-permute-done.14.refs_3_ = bf16[192,128]{1,0:T(8,128)(2,1)S(1)} collective-permute-done((bf16[192,128]{1,0:T(8,128)(2,1)S(1)}, bf16[192,128]{1,0:T(8,128)(2,1)S(1)}, u32[]{:S(2)}, u32[]{:S(2)}) %collective-permute-start.14) | collective-permute-done | bytes 49184 | tf_op jit(solution)/shard_map/chip_grad/ppermute | solution.py:980
  61.9 3.8 %attend_back.1 = (bf16[4,128,256]{2,1,0:T(8,128)(2,1)S(1)}, f32[4,128,512]{2,1,0:T(8,128)S(1)}, bf16[4,128,512]{2,1,0:T(8,128)(2,1)S(1)}) custom-call(s32[3]{0:T(128)S(1)} %pad_add_fusion.place_ref, bf16[4,128,256]{2,1,0:T(8,128)(2,1)S(1)} %get-tuple-element.154.q_ref, bf16[4,128,512]{2,1,0:T(8,128)(2,1)S(1)} %get-tuple-element.155.own_ref, ...), custom_call_target="tpu_custom_call" | custom-call | flops 6000000 | bytes 6000 | tf_op jit(solution)/shard_map/attend_back/pallas_call | solution.py:350
  65.8 1.5 %grad_down.1 = (f32[4,96,768]{2,1,0:T(8,128)S(1)}, bf16[4,96,768]{2,1,0:T(8,128)(2,1)S(1)}) custom-call(s32[3]{0:T(128)S(1)} %pad_add_fusion.place_ref, bf16[128,768]{1,0:T(8,128)(2,1)S(1)} %get-tuple-element.170.refs_0_, bf16[128,768]{1,0:T(8,128)(2,1)S(1)} %collective-permute-done.16.refs_1_, bf16[128,768]{1,0:T(8,128)(2,1)S(1)} %collective-permute-done.17.refs_2_, ...), custom_call_target="tpu_custom_call" | custom-call | flops 3000000 | bytes 3000 | tf_op jit(solution)/shard_map/grad_down/pallas_call | solution.py:350
  70.4 1.2 collective-permute-start.24
  71.6 2.1 %collective-permute-start.21 = (bf16[576,128]{1,0:T(8,128)(2,1)S(1)}, bf16[576,128]{1,0:T(8,128)(2,1)S(1)}, u32[]{:S(2)}, u32[]{:S(2)}) collective-permute-start(bf16[576,128]{1,0:T(8,128)(2,1)S(1)} %get-tuple-element.183), channel_id=1, source_target_pairs={{0,4},{2,6},{4,0},{6,2},{1,5},{3,7},{5,1},{7,3},{8,12},{10,14},{12... | collective-permute-start | bytes 442376 | tf_op jit(solution)/shard_map/chip_qkv/ppermute | solution.py:980
  75.5 2.5 %grad_qkv.1 = (f32[4,96,768]{2,1,0:T(8,128)S(1)}, bf16[4,96,768]{2,1,0:T(8,128)(2,1)S(1)}) custom-call(s32[3]{0:T(128)S(1)} %pad_add_fusion.place_ref, bf16[1,128,768]{2,1,0:T(8,128)(2,1)S(1)} %get-tuple-element.186.refs_0_, bf16[2,128,768]{2,1,0:T(8,128)(2,1)S(1)} %get-tuple-element.187.refs_1_, bf16[1,128,768]{2,1,0:T(8,128)(2,1)S(1)} %get-tuple-element.188.refs_2_, ...), custom_call_target="tpu_custom_call" | custom-call | flops 4000000 | bytes 4000 | tf_op jit(solution)/shard_map/grad_qkv/pallas_call | solution.py:350
  78.0 4.7 %collective-permute-done.24.in_ref = bf16[2,96,768]{2,1,0:T(8,128)(2,1)S(1)} collective-permute-done((bf16[2,96,768]{2,1,0:T(8,128)(2,1)S(1)}, bf16[2,96,768]{2,1,0:T(8,128)(2,1)S(1)}, u32[]{:S(2)}, u32[]{:S(2)}) %collective-permute-start.24) | collective-permute-done | bytes 294944 | tf_op jit(solution)/shard_map/down_sum/ppermute | solution.py:980
  83.4 1.4 %collective-permute-start.20 = (bf16[576,128]{1,0:T(8,128)(2,1)S(1)}, bf16[576,128]{1,0:T(8,128)(2,1)S(1)}, u32[]{:S(2)}, u32[]{:S(2)}) collective-permute-start(bf16[576,128]{1,0:T(8,128)(2,1)S(1)} %get-tuple-element.182), channel_id=1, source_target_pairs={{0,2},{2,0},{4,6},{6,4},{1,3},{3,1},{5,7},{7,5},{8,10},{10,8},{12,... | collective-permute-start | bytes 442376 | tf_op jit(solution)/shard_map/chip_qkv/ppermute | solution.py:980
  84.8 2.0 %collective-permute-start.31 = (bf16[1,96,768]{2,1,0:T(8,128)(2,1)S(1)}, bf16[1,96,768]{2,1,0:T(8,128)(2,1)S(1)}, u32[]{:S(2)}, u32[]{:S(2)}) collective-permute-start(bf16[1,96,768]{2,1,0:T(8,128)(2,1)S(1)} %get-tuple-element.218), channel_id=1, source_target_pairs={{0,4},{2,6},{4,0},{6,2},{1,5},{3,7},{5,1},{7,3},{8,12},{10,14},{12... | collective-permute-start | bytes 442376 | tf_op jit(solution)/shard_map/down_sum/ppermute | solution.py:980
  86.8 3.2 %collective-permute-done.29.refs_1_ = bf16[128,2560]{1,0:T(8,128)(2,1)S(1)} collective-permute-done((bf16[128,2560]{1,0:T(8,128)(2,1)S(1)}, bf16[128,2560]{1,0:T(8,128)(2,1)S(1)}, u32[]{:S(2)}, u32[]{:S(2)}) %collective-permute-start.29) | collective-permute-done | bytes 655392 | tf_op jit(solution)/shard_map/plane_back/ppermute | solution.py:980
  90.4 1.7 %grad_up_out.1 = (f32[4,128,768]{2,1,0:T(8,128)S(1)}, bf16[4,128,768]{2,1,0:T(8,128)(2,1)S(1)}) custom-call(s32[3]{0:T(128)S(1)} %pad_add_fusion.place_ref, bf16[128,2560]{1,0:T(8,128)(2,1)S(1)} %get-tuple-element.212.refs_0_, bf16[128,2560]{1,0:T(8,128)(2,1)S(1)} %collective-permute-done.29.refs_1_, bf16[128,2560]{1,0:T(8,128)(2,1)S(1)} %collective-permute-done.30.refs_2_, ...), custom_call_target="tpu_custom_call" | custom-call | flops 4000000 | bytes 4000 | tf_op jit(solution)/shard_map/grad_up_out/pallas_call | solution.py:350
  92.8 2.1 %collective-permute-done.31.in_ref = bf16[1,96,768]{2,1,0:T(8,128)(2,1)S(1)} collective-permute-done((bf16[1,96,768]{2,1,0:T(8,128)(2,1)S(1)}, bf16[1,96,768]{2,1,0:T(8,128)(2,1)S(1)}, u32[]{:S(2)}, u32[]{:S(2)}) %collective-permute-start.31) | collective-permute-done | bytes 147488 | tf_op jit(solution)/shard_map/down_sum/ppermute | solution.py:980
  94.9 2.3 %collective-permute-done.32.in_ref = bf16[4,128,768]{2,1,0:T(8,128)(2,1)S(1)} collective-permute-done((bf16[4,128,768]{2,1,0:T(8,128)(2,1)S(1)}, bf16[4,128,768]{2,1,0:T(8,128)(2,1)S(1)}, u32[]{:S(2)}, u32[]{:S(2)}) %collective-permute-start.32) | collective-permute-done | bytes 786464 | tf_op jit(solution)/shard_map/core_up/ppermute | solution.py:976
  97.9 1.6 %collective-permute-start.26 = (bf16[96,768]{1,0:T(8,128)(2,1)S(1)}, bf16[96,768]{1,0:T(8,128)(2,1)S(1)}, u32[]{:S(2)}, u32[]{:S(2)}) collective-permute-start(bf16[96,768]{1,0:T(8,128)(2,1)S(1)} %get-tuple-element.203), channel_id=1, source_target_pairs={{0,8},{8,0},{16,24},{24,16},{1,9},{9,1},{17,25},{25,17},{2,10},{10... | collective-permute-start | bytes 442376 | tf_op jit(solution)/shard_map/plane_w/ppermute | solution.py:980
  100.0 1.5 %collective-permute-start.28 = (bf16[96,768]{1,0:T(8,128)(2,1)S(1)}, bf16[96,768]{1,0:T(8,128)(2,1)S(1)}, u32[]{:S(2)}, u32[]{:S(2)}) collective-permute-start(bf16[96,768]{1,0:T(8,128)(2,1)S(1)} %get-tuple-element.205), channel_id=1, source_target_pairs={{0,24},{8,16},{16,8},{24,0},{1,25},{9,17},{17,9},{25,1},{2,26},{10... | collective-permute-start | bytes 442376 | tf_op jit(solution)/shard_map/plane_w/ppermute | solution.py:980
  101.5 1.7 %collective-permute-start.22 = (bf16[576,128]{1,0:T(8,128)(2,1)S(1)}, bf16[576,128]{1,0:T(8,128)(2,1)S(1)}, u32[]{:S(2)}, u32[]{:S(2)}) collective-permute-start(bf16[576,128]{1,0:T(8,128)(2,1)S(1)} %get-tuple-element.184), channel_id=1, source_target_pairs={{0,6},{2,4},{4,2},{6,0},{1,7},{3,5},{5,3},{7,1},{8,14},{10,12},{12... | collective-permute-start | bytes 442376 | tf_op jit(solution)/shard_map/chip_qkv/ppermute | solution.py:980
  103.2 1.4 %collective-permute-done.26.refs_1_ = bf16[96,768]{1,0:T(8,128)(2,1)S(1)} collective-permute-done((bf16[96,768]{1,0:T(8,128)(2,1)S(1)}, bf16[96,768]{1,0:T(8,128)(2,1)S(1)}, u32[]{:S(2)}, u32[]{:S(2)}) %collective-permute-start.26) | collective-permute-done | bytes 147488 | tf_op jit(solution)/shard_map/plane_w/ppermute | solution.py:980
  104.6 3.6 %collective-permute-done.27.refs_2_ = bf16[96,768]{1,0:T(8,128)(2,1)S(1)} collective-permute-done((bf16[96,768]{1,0:T(8,128)(2,1)S(1)}, bf16[96,768]{1,0:T(8,128)(2,1)S(1)}, u32[]{:S(2)}, u32[]{:S(2)}) %collective-permute-start.27) | collective-permute-done | bytes 147488 | tf_op jit(solution)/shard_map/plane_w/ppermute | solution.py:980
  108.9 3.3 %collective-permute-done.22.refs_3_ = bf16[576,128]{1,0:T(8,128)(2,1)S(1)} collective-permute-done((bf16[576,128]{1,0:T(8,128)(2,1)S(1)}, bf16[576,128]{1,0:T(8,128)(2,1)S(1)}, u32[]{:S(2)}, u32[]{:S(2)}) %collective-permute-start.22) | collective-permute-done | bytes 147488 | tf_op jit(solution)/shard_map/chip_qkv/ppermute | solution.py:980
  113.0 2.6 %collective-permute-start.33 = (bf16[24,768]{1,0:T(8,128)(2,1)S(1)}, bf16[24,768]{1,0:T(8,128)(2,1)S(1)}, u32[]{:S(2)}, u32[]{:S(2)}) collective-permute-start(bf16[24,768]{1,0:T(8,128)(2,1)S(1)} %get-tuple-element.226), channel_id=1, source_target_pairs={{0,2},{2,0},{4,6},{6,4},{1,3},{3,1},{5,7},{7,5},{8,10},{10,8},{12,... | collective-permute-start | bytes 110600 | tf_op jit(solution)/shard_map/chip_w/ppermute | solution.py:980
  115.9 2.1 %collective-permute-start.35 = (bf16[24,768]{1,0:T(8,128)(2,1)S(1)}, bf16[24,768]{1,0:T(8,128)(2,1)S(1)}, u32[]{:S(2)}, u32[]{:S(2)}) collective-permute-start(bf16[24,768]{1,0:T(8,128)(2,1)S(1)} %get-tuple-element.228), channel_id=1, source_target_pairs={{0,6},{2,4},{4,2},{6,0},{1,7},{3,5},{5,3},{7,1},{8,14},{10,12},{12... | collective-permute-start | bytes 110600 | tf_op jit(solution)/shard_map/chip_w/ppermute | solution.py:980
  118.0 2.7 %grad_inputs.1 = bf16[128,768]{1,0:T(8,128)(2,1)} custom-call(s32[3]{0:T(128)S(1)} %pad_add_fusion.place_ref, bf16[576,128]{1,0:T(8,128)(2,1)S(1)} %get-tuple-element.181.refs_0_, bf16[576,128]{1,0:T(8,128)(2,1)S(1)} %collective-permute-done.20.refs_1_, bf16[576,128]{1,0:T(8,128)(2,1)S(1)} %collective-permute-done.21.refs_2_, ...), custom_call_target="tpu_custom_call" | custom-call | flops 3000000 | bytes 3000 | tf_op jit(solution)/shard_map/grad_inputs/pallas_call | solution.py:350
  121.5 4.9 %collective-permute-done.34.refs_2_ = bf16[24,768]{1,0:T(8,128)(2,1)S(1)} collective-permute-done((bf16[24,768]{1,0:T(8,128)(2,1)S(1)}, bf16[24,768]{1,0:T(8,128)(2,1)S(1)}, u32[]{:S(2)}, u32[]{:S(2)}) %collective-permute-start.34) | collective-permute-done | bytes 36896 | tf_op jit(solution)/shard_map/chip_w/ppermute | solution.py:980
  126.4 1.2 finish_up.1
  127.6 1.5 %collective-permute-start.38 = (bf16[24,768]{1,0:T(8,128)(2,1)S(1)}, bf16[24,768]{1,0:T(8,128)(2,1)S(1)}, u32[]{:S(2)}, u32[]{:S(2)}) collective-permute-start(bf16[24,768]{1,0:T(8,128)(2,1)S(1)} %get-tuple-element.245), channel_id=1, source_target_pairs={{0,8},{8,0},{16,24},{24,16},{1,9},{9,1},{17,25},{25,17},{2,10},{10... | collective-permute-start | bytes 110600 | tf_op jit(solution)/shard_map/plane_rows/ppermute | solution.py:980
  129.6 1.5 %collective-permute-start.40 = (bf16[24,768]{1,0:T(8,128)(2,1)S(1)}, bf16[24,768]{1,0:T(8,128)(2,1)S(1)}, u32[]{:S(2)}, u32[]{:S(2)}) collective-permute-start(bf16[24,768]{1,0:T(8,128)(2,1)S(1)} %get-tuple-element.247), channel_id=1, source_target_pairs={{0,24},{8,16},{16,8},{24,0},{1,25},{9,17},{17,9},{25,1},{2,26},{10... | collective-permute-start | bytes 110600 | tf_op jit(solution)/shard_map/plane_rows/ppermute | solution.py:980
  131.1 1.3 finish_qkv.1
  134.4 1.3 place_up.1
  (92 shorter events, 21.3 us)
Async XLA Ops:
  0.7 13.5 %collective-permute-start.1 = (bf16[128,768]{1,0:T(8,128)(2,1)}, bf16[128,768]{1,0:T(8,128)(2,1)S(1)}, u32[]{:S(2)}, u32[]{:S(2)}) collective-permute-start(bf16[128,768]{1,0:T(8,128)(2,1)} %bitcast.7), channel_id=1, source_target_pairs={{0,4},{2,6},{4,0},{6,2},{1,5},{3,7},{5,1},{7,3},{8,12},{10,14},{12... | collective-permute-start | bytes 589832 | tf_op jit(solution)/shard_map/gather_in/ppermute | solution.py:980
  4.8 11.7 %collective-permute-start = (bf16[128,768]{1,0:T(8,128)(2,1)}, bf16[128,768]{1,0:T(8,128)(2,1)S(1)}, u32[]{:S(2)}, u32[]{:S(2)}) collective-permute-start(bf16[128,768]{1,0:T(8,128)(2,1)} %bitcast.8), channel_id=1, source_target_pairs={{0,2},{2,0},{4,6},{6,4},{1,3},{3,1},{5,7},{7,5},{8,10},{10,8},{12,... | collective-permute-start | bytes 589832 | tf_op jit(solution)/shard_map/gather_in/ppermute | solution.py:980
  14.2 7.2 %collective-permute-start.2 = (bf16[128,768]{1,0:T(8,128)(2,1)S(1)}, bf16[128,768]{1,0:T(8,128)(2,1)S(1)}, u32[]{:S(2)}, u32[]{:S(2)}) collective-permute-start(bf16[128,768]{1,0:T(8,128)(2,1)S(1)} %collective-permute-done.1.refs_1_), channel_id=1, source_target_pairs={{0,2},{2,0},{4,6},{6,4},{1,3},{3,1},{5,7},{7,5},{8,10},{10,8},{12,... | collective-permute-start | bytes 589832 | tf_op jit(solution)/shard_map/gather_in/ppermute | solution.py:980
  16.4 6.1 %collective-permute-start.3 = (bf16[1,128,512]{2,1,0:T(8,128)(2,1)S(1)}, bf16[1,128,512]{2,1,0:T(8,128)(2,1)S(1)}, u32[]{:S(2)}, u32[]{:S(2)}) collective-permute-start(bf16[1,128,512]{2,1,0:T(8,128)(2,1)S(1)} %get-tuple-element.136.refs_3_), channel_id=1, source_target_pairs={{0,1},{1,0},{2,3},{3,2},{4,5},{5,4},{6,7},{7,6},{8,9},{9,8},{10,11... | collective-permute-start | bytes 393224 | tf_op jit(solution)/shard_map/core_kv/ppermute | solution.py:976
  16.5 22.2 %copy-start.1 = (bf16[768,768]{1,0:T(8,128)(2,1)S(1)}, bf16[768,768]{1,0:T(8,128)(2,1)}, u32[]{:S(2)}) copy-start(bf16[768,768]{1,0:T(8,128)(2,1)} %wo_ref.1) | copy-start | bytes 3538948
  16.5 22.2 %copy-start.10 = (f32[768]{0:T(1024)S(1)}, f32[768]{0:T(1024)}, u32[]{:S(2)}) copy-start(f32[768]{0:T(1024)} %g2.1) | copy-start | bytes 9220
  16.5 22.2 %copy-start.11 = (f32[768]{0:T(1024)S(1)}, f32[768]{0:T(1024)}, u32[]{:S(2)}) copy-start(f32[768]{0:T(1024)} %b2.1) | copy-start | bytes 9220
  16.5 22.2 %copy-start.12 = (f32[768]{0:T(1024)S(1)}, f32[768]{0:T(1024)}, u32[]{:S(2)}) copy-start(f32[768]{0:T(1024)} %g3.1) | copy-start | bytes 9220
  16.5 22.2 %copy-start.13 = (f32[768]{0:T(1024)S(1)}, f32[768]{0:T(1024)}, u32[]{:S(2)}) copy-start(f32[768]{0:T(1024)} %b3.1) | copy-start | bytes 9220
  16.5 23.6 %copy-start = (bf16[768,3072]{1,0:T(8,128)(2,1)S(1)}, bf16[768,3072]{1,0:T(8,128)(2,1)}, u32[]{:S(2)}) copy-start(bf16[768,3072]{1,0:T(8,128)(2,1)} %wu_ref.3) | copy-start | bytes 14155780
  17.3 5.3 %collective-permute-start.4 = (bf16[2,128,512]{2,1,0:T(8,128)(2,1)S(1)}, bf16[2,128,512]{2,1,0:T(8,128)(2,1)S(1)}, u32[]{:S(2)}, u32[]{:S(2)}) collective-permute-start(bf16[2,128,512]{2,1,0:T(8,128)(2,1)S(1)} %get-tuple-element.137.refs_4_), channel_id=1, source_target_pairs={{0,1},{1,0},{2,3},{3,2},{4,5},{5,4},{6,7},{7,6},{8,9},{9,8},{10,11... | collective-permute-start | bytes 786440 | tf_op jit(solution)/shard_map/core_kv/ppermute | solution.py:976
  18.4 14.4 %collective-permute-start.11 = (bf16[128,768]{1,0:T(8,128)(2,1)S(1)}, bf16[128,768]{1,0:T(8,128)(2,1)S(1)}, u32[]{:S(2)}, u32[]{:S(2)}) collective-permute-start(bf16[128,768]{1,0:T(8,128)(2,1)S(1)} %mask_grad.1.go_ref.refs_4_), channel_id=1, source_target_pairs={{0,24},{8,16},{16,8},{24,0},{1,25},{9,17},{17,9},{25,1},{2,26},{10... | collective-permute-start | bytes 589832 | tf_op jit(solution)/shard_map/plane_out/ppermute | solution.py:980
  20.9 12.1 %collective-permute-start.10 = (bf16[128,768]{1,0:T(8,128)(2,1)S(1)}, bf16[128,768]{1,0:T(8,128)(2,1)S(1)}, u32[]{:S(2)}, u32[]{:S(2)}) collective-permute-start(bf16[128,768]{1,0:T(8,128)(2,1)S(1)} %mask_grad.1.go_ref.refs_4_), channel_id=1, source_target_pairs={{0,16},{8,24},{16,0},{24,8},{1,17},{9,25},{17,1},{25,9},{2,18},{10... | collective-permute-start | bytes 589832 | tf_op jit(solution)/shard_map/plane_out/ppermute | solution.py:980
  21.4 11.5 %collective-permute-start.9 = (bf16[128,768]{1,0:T(8,128)(2,1)S(1)}, bf16[128,768]{1,0:T(8,128)(2,1)S(1)}, u32[]{:S(2)}, u32[]{:S(2)}) collective-permute-start(bf16[128,768]{1,0:T(8,128)(2,1)S(1)} %mask_grad.1.go_ref.refs_4_), channel_id=1, source_target_pairs={{0,8},{8,0},{16,24},{24,16},{1,9},{9,1},{17,25},{25,17},{2,10},{10... | collective-permute-start | bytes 589832 | tf_op jit(solution)/shard_map/plane_out/ppermute | solution.py:980
  22.5 1.4 %collective-permute-start.5 = (bf16[1,128,512]{2,1,0:T(8,128)(2,1)S(1)}, bf16[1,128,512]{2,1,0:T(8,128)(2,1)S(1)}, u32[]{:S(2)}, u32[]{:S(2)}) collective-permute-start(bf16[1,128,512]{2,1,0:T(8,128)(2,1)S(1)} %get-tuple-element.138.refs_5_), channel_id=1, source_target_pairs={{0,1},{1,0},{2,3},{3,2},{4,5},{5,4},{6,7},{7,6},{8,9},{9,8},{10,11... | collective-permute-start | bytes 393224 | tf_op jit(solution)/shard_map/core_kv/ppermute | solution.py:976
  28.2 4.8 %collective-permute-start.6 = (bf16[192,128]{1,0:T(8,128)(2,1)S(1)}, bf16[192,128]{1,0:T(8,128)(2,1)S(1)}, u32[]{:S(2)}, u32[]{:S(2)}) collective-permute-start(bf16[192,128]{1,0:T(8,128)(2,1)S(1)} %get-tuple-element.140), channel_id=1, source_target_pairs={{0,2},{2,0},{4,6},{6,4},{1,3},{3,1},{5,7},{7,5},{8,10},{10,8},{12,... | collective-permute-start | bytes 147464 | tf_op jit(solution)/shard_map/chip_attn/ppermute | solution.py:980
  29.5 6.4 %collective-permute-start.7 = (bf16[192,128]{1,0:T(8,128)(2,1)S(1)}, bf16[192,128]{1,0:T(8,128)(2,1)S(1)}, u32[]{:S(2)}, u32[]{:S(2)}) collective-permute-start(bf16[192,128]{1,0:T(8,128)(2,1)S(1)} %get-tuple-element.141), channel_id=1, source_target_pairs={{0,4},{2,6},{4,0},{6,2},{1,5},{3,7},{5,1},{7,3},{8,12},{10,14},{12... | collective-permute-start | bytes 147464 | tf_op jit(solution)/shard_map/chip_attn/ppermute | solution.py:980
  32.8 5.9 %collective-permute-start.8 = (bf16[192,128]{1,0:T(8,128)(2,1)S(1)}, bf16[192,128]{1,0:T(8,128)(2,1)S(1)}, u32[]{:S(2)}, u32[]{:S(2)}) collective-permute-start(bf16[192,128]{1,0:T(8,128)(2,1)S(1)} %get-tuple-element.142), channel_id=1, source_target_pairs={{0,6},{2,4},{4,2},{6,0},{1,7},{3,5},{5,3},{7,1},{8,14},{10,12},{12... | collective-permute-start | bytes 147464 | tf_op jit(solution)/shard_map/chip_attn/ppermute | solution.py:980
  42.0 9.6 %collective-permute-start.16 = (bf16[128,768]{1,0:T(8,128)(2,1)S(1)}, bf16[128,768]{1,0:T(8,128)(2,1)S(1)}, u32[]{:S(2)}, u32[]{:S(2)}) collective-permute-start(bf16[128,768]{1,0:T(8,128)(2,1)S(1)} %get-tuple-element.167), channel_id=1, source_target_pairs={{0,8},{8,0},{16,24},{24,16},{1,9},{9,1},{17,25},{25,17},{2,10},{10... | collective-permute-start | bytes 589832 | tf_op jit(solution)/shard_map/plane_act/ppermute | solution.py:980
  42.7 9.0 %collective-permute-start.17 = (bf16[128,768]{1,0:T(8,128)(2,1)S(1)}, bf16[128,768]{1,0:T(8,128)(2,1)S(1)}, u32[]{:S(2)}, u32[]{:S(2)}) collective-permute-start(bf16[128,768]{1,0:T(8,128)(2,1)S(1)} %get-tuple-element.168), channel_id=1, source_target_pairs={{0,16},{8,24},{16,0},{24,8},{1,17},{9,25},{17,1},{25,9},{2,18},{10... | collective-permute-start | bytes 589832 | tf_op jit(solution)/shard_map/plane_act/ppermute | solution.py:980
  44.2 8.4 %collective-permute-start.18 = (bf16[128,768]{1,0:T(8,128)(2,1)S(1)}, bf16[128,768]{1,0:T(8,128)(2,1)S(1)}, u32[]{:S(2)}, u32[]{:S(2)}) collective-permute-start(bf16[128,768]{1,0:T(8,128)(2,1)S(1)} %get-tuple-element.169), channel_id=1, source_target_pairs={{0,24},{8,16},{16,8},{24,0},{1,25},{9,17},{17,9},{25,1},{2,26},{10... | collective-permute-start | bytes 589832 | tf_op jit(solution)/shard_map/plane_act/ppermute | solution.py:980
  52.6 15.1 %collective-permute-start.19 = (bf16[128,2560]{1,0:T(8,128)(2,1)S(1)}, bf16[128,2560]{1,0:T(8,128)(2,1)S(1)}, u32[]{:S(2)}, u32[]{:S(2)}) collective-permute-start(bf16[128,2560]{1,0:T(8,128)(2,1)S(1)} %get-tuple-element.179), channel_id=1, source_target_pairs={{0,24},{8,16},{16,8},{24,0},{1,25},{9,17},{17,9},{25,1},{2,26},{10... | collective-permute-start | bytes 1966088 | tf_op jit(solution)/shard_map/plane_back/ppermute | solution.py:980
  54.4 4.4 %collective-permute-start.12 = (bf16[192,128]{1,0:T(8,128)(2,1)S(1)}, bf16[192,128]{1,0:T(8,128)(2,1)S(1)}, u32[]{:S(2)}, u32[]{:S(2)}) collective-permute-start(bf16[192,128]{1,0:T(8,128)(2,1)S(1)} %get-tuple-element.160), channel_id=1, source_target_pairs={{0,2},{2,0},{4,6},{6,4},{1,3},{3,1},{5,7},{7,5},{8,10},{10,8},{12,... | collective-permute-start | bytes 147464 | tf_op jit(solution)/shard_map/chip_grad/ppermute | solution.py:980
  54.6 5.0 %collective-permute-start.13 = (bf16[192,128]{1,0:T(8,128)(2,1)S(1)}, bf16[192,128]{1,0:T(8,128)(2,1)S(1)}, u32[]{:S(2)}, u32[]{:S(2)}) collective-permute-start(bf16[192,128]{1,0:T(8,128)(2,1)S(1)} %get-tuple-element.161), channel_id=1, source_target_pairs={{0,4},{2,6},{4,0},{6,2},{1,5},{3,7},{5,1},{7,3},{8,12},{10,14},{12... | collective-permute-start | bytes 147464 | tf_op jit(solution)/shard_map/chip_grad/ppermute | solution.py:980
  56.0 5.9 %collective-permute-start.14 = (bf16[192,128]{1,0:T(8,128)(2,1)S(1)}, bf16[192,128]{1,0:T(8,128)(2,1)S(1)}, u32[]{:S(2)}, u32[]{:S(2)}) collective-permute-start(bf16[192,128]{1,0:T(8,128)(2,1)S(1)} %get-tuple-element.162), channel_id=1, source_target_pairs={{0,6},{2,4},{4,2},{6,0},{1,7},{3,5},{5,3},{7,1},{8,14},{10,12},{12... | collective-permute-start | bytes 147464 | tf_op jit(solution)/shard_map/chip_grad/ppermute | solution.py:980
  65.7 2.0 %collective-permute-start.15 = (bf16[4,128,512]{2,1,0:T(8,128)(2,1)S(1)}, bf16[4,128,512]{2,1,0:T(8,128)(2,1)S(1)}, u32[]{:S(2)}, u32[]{:S(2)}) collective-permute-start(bf16[4,128,512]{2,1,0:T(8,128)(2,1)S(1)} %get-tuple-element.165), channel_id=1, source_target_pairs={{0,1},{1,0},{2,3},{3,2},{4,5},{5,4},{6,7},{7,6},{8,9},{9,8},{10,11... | collective-permute-start | bytes 1572872 | tf_op jit(solution)/shard_map/core_grad/ppermute | solution.py:976
  67.7 2.0 %collective-permute-start.23 = (bf16[4,96,768]{2,1,0:T(8,128)(2,1)S(1)}, bf16[4,96,768]{2,1,0:T(8,128)(2,1)S(1)}, u32[]{:S(2)}, u32[]{:S(2)}) collective-permute-start(bf16[4,96,768]{2,1,0:T(8,128)(2,1)S(1)} %get-tuple-element.191), channel_id=1, source_target_pairs={{0,1},{1,0},{2,3},{3,2},{4,5},{5,4},{6,7},{7,6},{8,9},{9,8},{10,11... | collective-permute-start | bytes 1769480 | tf_op jit(solution)/shard_map/core_down/ppermute | solution.py:976
  70.4 12.3 %collective-permute-start.24 = (bf16[2,96,768]{2,1,0:T(8,128)(2,1)S(1)}, bf16[2,96,768]{2,1,0:T(8,128)(2,1)S(1)}, u32[]{:S(2)}, u32[]{:S(2)}) collective-permute-start(bf16[2,96,768]{2,1,0:T(8,128)(2,1)S(1)} %get-tuple-element.198), channel_id=1, source_target_pairs={{0,2},{2,0},{4,6},{6,4},{1,3},{3,1},{5,7},{7,5},{8,10},{10,8},{12,... | collective-permute-start | bytes 884744 | tf_op jit(solution)/shard_map/down_sum/ppermute | solution.py:980
  71.6 11.7 %collective-permute-start.21 = (bf16[576,128]{1,0:T(8,128)(2,1)S(1)}, bf16[576,128]{1,0:T(8,128)(2,1)S(1)}, u32[]{:S(2)}, u32[]{:S(2)}) collective-permute-start(bf16[576,128]{1,0:T(8,128)(2,1)S(1)} %get-tuple-element.183), channel_id=1, source_target_pairs={{0,4},{2,6},{4,0},{6,2},{1,5},{3,7},{5,1},{7,3},{8,12},{10,14},{12... | collective-permute-start | bytes 442376 | tf_op jit(solution)/shard_map/chip_qkv/ppermute | solution.py:980
  73.8 16.3 %collective-permute-start.29 = (bf16[128,2560]{1,0:T(8,128)(2,1)S(1)}, bf16[128,2560]{1,0:T(8,128)(2,1)S(1)}, u32[]{:S(2)}, u32[]{:S(2)}) collective-permute-start(bf16[128,2560]{1,0:T(8,128)(2,1)S(1)} %get-tuple-element.210), channel_id=1, source_target_pairs={{0,8},{8,0},{16,24},{24,16},{1,9},{9,1},{17,25},{25,17},{2,10},{10... | collective-permute-start | bytes 1966088 | tf_op jit(solution)/shard_map/plane_back/ppermute | solution.py:980
  74.3 16.1 %collective-permute-start.30 = (bf16[128,2560]{1,0:T(8,128)(2,1)S(1)}, bf16[128,2560]{1,0:T(8,128)(2,1)S(1)}, u32[]{:S(2)}, u32[]{:S(2)}) collective-permute-start(bf16[128,2560]{1,0:T(8,128)(2,1)S(1)} %get-tuple-element.211), channel_id=1, source_target_pairs={{0,16},{8,24},{16,0},{24,8},{1,17},{9,25},{17,1},{25,9},{2,18},{10... | collective-permute-start | bytes 1966088 | tf_op jit(solution)/shard_map/plane_back/ppermute | solution.py:980
  83.3 8.8 %collective-permute-start.25 = (bf16[4,96,768]{2,1,0:T(8,128)(2,1)S(1)}, bf16[4,96,768]{2,1,0:T(8,128)(2,1)S(1)}, u32[]{:S(2)}, u32[]{:S(2)}) collective-permute-start(bf16[4,96,768]{2,1,0:T(8,128)(2,1)S(1)} %get-tuple-element.201), channel_id=1, source_target_pairs={{0,1},{1,0},{2,3},{3,2},{4,5},{5,4},{6,7},{7,6},{8,9},{9,8},{10,11... | collective-permute-start | bytes 1769480 | tf_op jit(solution)/shard_map/core_w/ppermute | solution.py:976
  83.4 9.4 %collective-permute-start.20 = (bf16[576,128]{1,0:T(8,128)(2,1)S(1)}, bf16[576,128]{1,0:T(8,128)(2,1)S(1)}, u32[]{:S(2)}, u32[]{:S(2)}) collective-permute-start(bf16[576,128]{1,0:T(8,128)(2,1)S(1)} %get-tuple-element.182), channel_id=1, source_target_pairs={{0,2},{2,0},{4,6},{6,4},{1,3},{3,1},{5,7},{7,5},{8,10},{10,8},{12,... | collective-permute-start | bytes 442376 | tf_op jit(solution)/shard_map/chip_qkv/ppermute | solution.py:980
  84.8 10.1 %collective-permute-start.31 = (bf16[1,96,768]{2,1,0:T(8,128)(2,1)S(1)}, bf16[1,96,768]{2,1,0:T(8,128)(2,1)S(1)}, u32[]{:S(2)}, u32[]{:S(2)}) collective-permute-start(bf16[1,96,768]{2,1,0:T(8,128)(2,1)S(1)} %get-tuple-element.218), channel_id=1, source_target_pairs={{0,4},{2,6},{4,0},{6,2},{1,5},{3,7},{5,1},{7,3},{8,12},{10,14},{12... | collective-permute-start | bytes 442376 | tf_op jit(solution)/shard_map/down_sum/ppermute | solution.py:980
  94.9 2.3 %collective-permute-start.32 = (bf16[4,128,768]{2,1,0:T(8,128)(2,1)S(1)}, bf16[4,128,768]{2,1,0:T(8,128)(2,1)S(1)}, u32[]{:S(2)}, u32[]{:S(2)}) collective-permute-start(bf16[4,128,768]{2,1,0:T(8,128)(2,1)S(1)} %get-tuple-element.219), channel_id=1, source_target_pairs={{0,1},{1,0},{2,3},{3,2},{4,5},{5,4},{6,7},{7,6},{8,9},{9,8},{10,11... | collective-permute-start | bytes 2359304 | tf_op jit(solution)/shard_map/core_up/ppermute | solution.py:976
  97.2 20.8 %copy-start.5 = (bf16[768,768]{1,0:T(8,128)(2,1)S(1)}, bf16[768,768]{1,0:T(8,128)(2,1)}, u32[]{:S(2)}) copy-start(bf16[768,768]{1,0:T(8,128)(2,1)} %refs_7_.3) | copy-start | bytes 3538948
  97.9 14.4 %collective-permute-start.36 = (bf16[2,128,768]{2,1,0:T(8,128)(2,1)S(1)}, bf16[2,128,768]{2,1,0:T(8,128)(2,1)S(1)}, u32[]{:S(2)}, u32[]{:S(2)}) collective-permute-start(bf16[2,128,768]{2,1,0:T(8,128)(2,1)S(1)} %get-tuple-element.220), channel_id=1, source_target_pairs={{0,2},{2,0},{4,6},{6,4},{1,3},{3,1},{5,7},{7,5},{8,10},{10,8},{12,... | collective-permute-start | bytes 1179656 | tf_op jit(solution)/shard_map/up_sum/ppermute | solution.py:980
  97.9 6.7 %collective-permute-start.26 = (bf16[96,768]{1,0:T(8,128)(2,1)S(1)}, bf16[96,768]{1,0:T(8,128)(2,1)S(1)}, u32[]{:S(2)}, u32[]{:S(2)}) collective-permute-start(bf16[96,768]{1,0:T(8,128)(2,1)S(1)} %get-tuple-element.203), channel_id=1, source_target_pairs={{0,8},{8,0},{16,24},{24,16},{1,9},{9,1},{17,25},{25,17},{2,10},{10... | collective-permute-start | bytes 442376 | tf_op jit(solution)/shard_map/plane_w/ppermute | solution.py:980
  99.5 8.8 %collective-permute-start.27 = (bf16[96,768]{1,0:T(8,128)(2,1)S(1)}, bf16[96,768]{1,0:T(8,128)(2,1)S(1)}, u32[]{:S(2)}, u32[]{:S(2)}) collective-permute-start(bf16[96,768]{1,0:T(8,128)(2,1)S(1)} %get-tuple-element.204), channel_id=1, source_target_pairs={{0,16},{8,24},{16,0},{24,8},{1,17},{9,25},{17,1},{25,9},{2,18},{10... | collective-permute-start | bytes 442376 | tf_op jit(solution)/shard_map/plane_w/ppermute | solution.py:980
  100.0 8.3 %collective-permute-start.28 = (bf16[96,768]{1,0:T(8,128)(2,1)S(1)}, bf16[96,768]{1,0:T(8,128)(2,1)S(1)}, u32[]{:S(2)}, u32[]{:S(2)}) collective-permute-start(bf16[96,768]{1,0:T(8,128)(2,1)S(1)} %get-tuple-element.205), channel_id=1, source_target_pairs={{0,24},{8,16},{16,8},{24,0},{1,25},{9,17},{17,9},{25,1},{2,26},{10... | collective-permute-start | bytes 442376 | tf_op jit(solution)/shard_map/plane_w/ppermute | solution.py:980
  101.5 10.7 %collective-permute-start.22 = (bf16[576,128]{1,0:T(8,128)(2,1)S(1)}, bf16[576,128]{1,0:T(8,128)(2,1)S(1)}, u32[]{:S(2)}, u32[]{:S(2)}) collective-permute-start(bf16[576,128]{1,0:T(8,128)(2,1)S(1)} %get-tuple-element.184), channel_id=1, source_target_pairs={{0,6},{2,4},{4,2},{6,0},{1,7},{3,5},{5,3},{7,1},{8,14},{10,12},{12... | collective-permute-start | bytes 442376 | tf_op jit(solution)/shard_map/chip_qkv/ppermute | solution.py:980
  112.9 13.5 %collective-permute-start.37 = (bf16[1,128,768]{2,1,0:T(8,128)(2,1)S(1)}, bf16[1,128,768]{2,1,0:T(8,128)(2,1)S(1)}, u32[]{:S(2)}, u32[]{:S(2)}) collective-permute-start(bf16[1,128,768]{2,1,0:T(8,128)(2,1)S(1)} %get-tuple-element.237), channel_id=1, source_target_pairs={{0,4},{2,6},{4,0},{6,2},{1,5},{3,7},{5,1},{7,3},{8,12},{10,14},{12... | collective-permute-start | bytes 589832 | tf_op jit(solution)/shard_map/up_sum/ppermute | solution.py:980
  113.0 8.5 %collective-permute-start.33 = (bf16[24,768]{1,0:T(8,128)(2,1)S(1)}, bf16[24,768]{1,0:T(8,128)(2,1)S(1)}, u32[]{:S(2)}, u32[]{:S(2)}) collective-permute-start(bf16[24,768]{1,0:T(8,128)(2,1)S(1)} %get-tuple-element.226), channel_id=1, source_target_pairs={{0,2},{2,0},{4,6},{6,4},{1,3},{3,1},{5,7},{7,5},{8,10},{10,8},{12,... | collective-permute-start | bytes 110600 | tf_op jit(solution)/shard_map/chip_w/ppermute | solution.py:980
  115.6 10.7 %collective-permute-start.34 = (bf16[24,768]{1,0:T(8,128)(2,1)S(1)}, bf16[24,768]{1,0:T(8,128)(2,1)S(1)}, u32[]{:S(2)}, u32[]{:S(2)}) collective-permute-start(bf16[24,768]{1,0:T(8,128)(2,1)S(1)} %get-tuple-element.227), channel_id=1, source_target_pairs={{0,4},{2,6},{4,0},{6,2},{1,5},{3,7},{5,1},{7,3},{8,12},{10,14},{12... | collective-permute-start | bytes 110600 | tf_op jit(solution)/shard_map/chip_w/ppermute | solution.py:980
  115.9 10.5 %collective-permute-start.35 = (bf16[24,768]{1,0:T(8,128)(2,1)S(1)}, bf16[24,768]{1,0:T(8,128)(2,1)S(1)}, u32[]{:S(2)}, u32[]{:S(2)}) collective-permute-start(bf16[24,768]{1,0:T(8,128)(2,1)S(1)} %get-tuple-element.228), channel_id=1, source_target_pairs={{0,6},{2,4},{4,2},{6,0},{1,7},{3,5},{5,3},{7,1},{8,14},{10,12},{12... | collective-permute-start | bytes 110600 | tf_op jit(solution)/shard_map/chip_w/ppermute | solution.py:980
  127.6 4.8 %collective-permute-start.38 = (bf16[24,768]{1,0:T(8,128)(2,1)S(1)}, bf16[24,768]{1,0:T(8,128)(2,1)S(1)}, u32[]{:S(2)}, u32[]{:S(2)}) collective-permute-start(bf16[24,768]{1,0:T(8,128)(2,1)S(1)} %get-tuple-element.245), channel_id=1, source_target_pairs={{0,8},{8,0},{16,24},{24,16},{1,9},{9,1},{17,25},{25,17},{2,10},{10... | collective-permute-start | bytes 110600 | tf_op jit(solution)/shard_map/plane_rows/ppermute | solution.py:980
  129.1 4.1 %collective-permute-start.39 = (bf16[24,768]{1,0:T(8,128)(2,1)S(1)}, bf16[24,768]{1,0:T(8,128)(2,1)S(1)}, u32[]{:S(2)}, u32[]{:S(2)}) collective-permute-start(bf16[24,768]{1,0:T(8,128)(2,1)S(1)} %get-tuple-element.246), channel_id=1, source_target_pairs={{0,16},{8,24},{16,0},{24,8},{1,17},{9,25},{17,1},{25,9},{2,18},{10... | collective-permute-start | bytes 110600 | tf_op jit(solution)/shard_map/plane_rows/ppermute | solution.py:980
  129.6 4.9 %collective-permute-start.40 = (bf16[24,768]{1,0:T(8,128)(2,1)S(1)}, bf16[24,768]{1,0:T(8,128)(2,1)S(1)}, u32[]{:S(2)}, u32[]{:S(2)}) collective-permute-start(bf16[24,768]{1,0:T(8,128)(2,1)S(1)} %get-tuple-element.247), channel_id=1, source_target_pairs={{0,24},{8,16},{16,8},{24,0},{1,25},{9,17},{17,9},{25,1},{2,26},{10... | collective-permute-start | bytes 110600 | tf_op jit(solution)/shard_map/plane_rows/ppermute | solution.py:980
  (8 other events, 53.1 us)

commit v8 on v7

--- a/solution.py
+++ b/solution.py
@@ -1085,11 +1085,11 @@
     down_recv = after(down_recv, qkv_send)
     with scope("down_sum"):
         down_keep, down_last = scatter_chips(place, down_keep, down_recv, chips, 2)
-    qkv_send = after(qkv_send, (down_keep, grad_pieces[2:3]))
+    qkv_send = after(qkv_send, (down_keep, grad_pieces[2:]))
     with scope("core_w"):
         qkv_send = swap_core(qkv_send)
     qkv_sums = spread_call(place, qkv_keep, qkv_send)
-    back = after(back, (down_keep, grad_pieces[2:3]))
+    back = after(back, (down_keep, grad_pieces[2:]))
     up_keep, up_send = up_grad_call(place, back, chips, part, model)
     with scope("plane_w"):
         traded = trade(qkv_sums, "rows")

time: 136 us -> 137 us (level)
  waiting for transfers between devices: 45.6 us -> 47.1 us
    ppermute x34, waiting for transfers between devices: 40.6 us -> 42.1 us  [swap(): lax.ppermute(value, axis, [(k, k ^ bit) for k in range(lax.axis_size(axis...]
  transfers between devices with their start and end apart: 41 -> 41, of which waited for: 20 -> 22; matrix products, arithmetic and copies ran while one was open for 2% -> 2% of each run, Pallas kernels for 22% -> 22%
where the time goes in v8:
time: 137 us
  starting transfers between devices  47.8 us (35%)
  waiting for transfers between devices  47.1 us (34%)
  Pallas kernels  37.4 us (27%)
  local copies, waits for them, and re-layouts  3.65 us (3%)
    ppermute x34, starting transfers between devices, swap(): lax.ppermute(value, axis, [(k, k ^ bit) for k in range(lax.axis_size(axis...  46.8 us
    ppermute x34, waiting for transfers between devices, swap(): lax.ppermute(value, axis, [(k, k ^ bit) for k in range(lax.axis_size(axis...  42.1 us
    pallas_call x24, Pallas kernels, kernel(): pl.pallas_call(body, out_shape=outs if single else listed, in_specs=[smem...  37.4 us
    ppermute x7, waiting for transfers between devices, swap_core(): return lax.ppermute(value, 'core', [(0, 1), (1, 0)])  5.07 us
    dynamic_slice x2, local copies, waits for them, and re-layouts, columns(): mine = lax.dynamic_slice_in_dim(weight, z_index * live, live, 1)  2.82 us
  transfers between devices with their start and end apart: 41, of which 22 were waited for; matrix products, arithmetic and copies ran while one was open for 2% of the time, Pallas kernels for 22%

profile of v8, /device:TPU:0, one launch (start us, length us, event | category | flops | bytes accessed | tf_op | source)
XLA Modules:
  0.0 137.2 jit_solution(9113713806997218902)
XLA Ops:
  0.7 4.1 %collective-permute-start.1 = (bf16[128,768]{1,0:T(8,128)(2,1)}, bf16[128,768]{1,0:T(8,128)(2,1)S(1)}, u32[]{:S(2)}, u32[]{:S(2)}) collective-permute-start(bf16[128,768]{1,0:T(8,128)(2,1)} %bitcast.7), channel_id=1, source_target_pairs={{0,4},{2,6},{4,0},{6,2},{1,5},{3,7},{5,1},{7,3},{8,12},{10,14},{12... | collective-permute-start | bytes 589832 | tf_op jit(solution)/shard_map/gather_in/ppermute | solution.py:980
  4.8 1.6 %collective-permute-start = (bf16[128,768]{1,0:T(8,128)(2,1)}, bf16[128,768]{1,0:T(8,128)(2,1)S(1)}, u32[]{:S(2)}, u32[]{:S(2)}) collective-permute-start(bf16[128,768]{1,0:T(8,128)(2,1)} %bitcast.8), channel_id=1, source_target_pairs={{0,2},{2,0},{4,6},{6,4},{1,3},{3,1},{5,7},{7,5},{8,10},{10,8},{12,... | collective-permute-start | bytes 589832 | tf_op jit(solution)/shard_map/gather_in/ppermute | solution.py:980
  7.6 1.6 %constant_dynamic-slice_fusion = (bf16[768,192]{1,0:T(8,128)(2,1)S(1)}, bf16[768,192]{1,0:T(8,128)(2,1)S(1)}) fusion(bf16[768,768]{1,0:T(8,128)(2,1)} %refs_9_.3, s32[]{:T(128)S(6)} %select_n.2, bf16[768,768]{1,0:T(8,128)(2,1)} %refs_8_.3), kind=kLoop, calls=%fused_computation.10 | loop fusion | bytes 1179652 | tf_op jit(solution)/shard_map/dynamic_slice | solution.py:1027
  9.2 5.0 %collective-permute-done.1.refs_1_ = bf16[128,768]{1,0:T(8,128)(2,1)S(1)} collective-permute-done((bf16[128,768]{1,0:T(8,128)(2,1)}, bf16[128,768]{1,0:T(8,128)(2,1)S(1)}, u32[]{:S(2)}, u32[]{:S(2)}) %collective-permute-start.1) | collective-permute-done | bytes 196640 | tf_op jit(solution)/shard_map/gather_in/ppermute | solution.py:980
  18.4 2.5 %collective-permute-start.11 = (bf16[128,768]{1,0:T(8,128)(2,1)S(1)}, bf16[128,768]{1,0:T(8,128)(2,1)S(1)}, u32[]{:S(2)}, u32[]{:S(2)}) collective-permute-start(bf16[128,768]{1,0:T(8,128)(2,1)S(1)} %mask_grad.1.go_ref.refs_4_), channel_id=1, source_target_pairs={{0,24},{8,16},{16,8},{24,0},{1,25},{9,17},{17,9},{25,1},{2,26},{10... | collective-permute-start | bytes 589832 | tf_op jit(solution)/shard_map/plane_out/ppermute | solution.py:980
  22.6 1.3 collective-permute-done.5.refs_8_
  23.9 4.3 %attend.1 = (f32[4,128,256]{2,1,0:T(8,128)S(1)}, bf16[4,2,384,512]{3,2,1,0:T(8,128)(2,1)S(1)}, bf16[4,128,256]{2,1,0:T(8,128)(2,1)S(1)}, bf16[4,128,512]{2,1,0:T...) custom-call(s32[3]{0:T(128)S(1)} %pad_add_fusion.place_ref, ...), custom_call_target="tpu_custom_call" | custom-call | flops 6000000 | bytes 6000 | tf_op jit(solution)/shard_map/attend/pallas_call | solution.py:350
  28.2 1.4 %collective-permute-start.6 = (bf16[192,128]{1,0:T(8,128)(2,1)S(1)}, bf16[192,128]{1,0:T(8,128)(2,1)S(1)}, u32[]{:S(2)}, u32[]{:S(2)}) collective-permute-start(bf16[192,128]{1,0:T(8,128)(2,1)S(1)} %get-tuple-element.140), channel_id=1, source_target_pairs={{0,2},{2,0},{4,6},{6,4},{1,3},{3,1},{5,7},{7,5},{8,10},{10,8},{12,... | collective-permute-start | bytes 147464 | tf_op jit(solution)/shard_map/chip_attn/ppermute | solution.py:980
  29.5 3.3 %collective-permute-start.7 = (bf16[192,128]{1,0:T(8,128)(2,1)S(1)}, bf16[192,128]{1,0:T(8,128)(2,1)S(1)}, u32[]{:S(2)}, u32[]{:S(2)}) collective-permute-start(bf16[192,128]{1,0:T(8,128)(2,1)S(1)} %get-tuple-element.141), channel_id=1, source_target_pairs={{0,4},{2,6},{4,0},{6,2},{1,5},{3,7},{5,1},{7,3},{8,12},{10,14},{12... | collective-permute-start | bytes 147464 | tf_op jit(solution)/shard_map/chip_attn/ppermute | solution.py:980
  33.0 2.9 %collective-permute-done.7.refs_2_ = bf16[192,128]{1,0:T(8,128)(2,1)S(1)} collective-permute-done((bf16[192,128]{1,0:T(8,128)(2,1)S(1)}, bf16[192,128]{1,0:T(8,128)(2,1)S(1)}, u32[]{:S(2)}, u32[]{:S(2)}) %collective-permute-start.7) | collective-permute-done | bytes 49184 | tf_op jit(solution)/shard_map/chip_attn/ppermute | solution.py:980
  35.9 2.8 %collective-permute-done.8.refs_3_ = bf16[192,128]{1,0:T(8,128)(2,1)S(1)} collective-permute-done((bf16[192,128]{1,0:T(8,128)(2,1)S(1)}, bf16[192,128]{1,0:T(8,128)(2,1)S(1)}, u32[]{:S(2)}, u32[]{:S(2)}) %collective-permute-start.8) | collective-permute-done | bytes 49184 | tf_op jit(solution)/shard_map/chip_attn/ppermute | solution.py:980
  38.7 1.4 %norms.1 = (f32[128,768]{1,0:T(8,128)S(1)}, bf16[128,768]{1,0:T(8,128)(2,1)S(1)}, bf16[128,768]{1,0:T(8,128)(2,1)S(1)}) custom-call(s32[3]{0:T(128)S(1)} %pad_add_fusion.place_ref, bf16[192,128]{1,0:T(8,128)(2,1)S(1)} %get-tuple-element.144.refs_0_, bf16[192,128]{1,0:T(8,128)(2,1)S(1)} %collective-permute-done.6.refs_1_, ...), custom_call_target="tpu_custom_call" | custom-call | flops 1500000 | bytes 1500 | tf_op jit(solution)/shard_map/norms/pallas_call | solution.py:350
  40.1 1.9 %up_gelu.1 = (bf16[4,128,768]{2,1,0:T(8,128)(2,1)S(1)}, bf16[4,128,768]{2,1,0:T(8,128)(2,1)S(1)}, bf16[128,768]{1,0:T(8,128)(2,1)S(1)}, bf16[128,768]{1,0:T(8,12...) custom-call(s32[3]{0:T(128)S(1)} %pad_add_fusion.place_ref, ...), custom_call_target="tpu_custom_call" | custom-call | flops 2000000 | bytes 2000 | tf_op jit(solution)/shard_map/up_gelu/pallas_call | solution.py:350
  42.7 1.5 %collective-permute-start.17 = (bf16[128,768]{1,0:T(8,128)(2,1)S(1)}, bf16[128,768]{1,0:T(8,128)(2,1)S(1)}, u32[]{:S(2)}, u32[]{:S(2)}) collective-permute-start(bf16[128,768]{1,0:T(8,128)(2,1)S(1)} %get-tuple-element.168), channel_id=1, source_target_pairs={{0,16},{8,24},{16,0},{24,8},{1,17},{9,25},{17,1},{25,9},{2,18},{10... | collective-permute-start | bytes 589832 | tf_op jit(solution)/shard_map/plane_act/ppermute | solution.py:980
  44.2 1.4 %collective-permute-start.18 = (bf16[128,768]{1,0:T(8,128)(2,1)S(1)}, bf16[128,768]{1,0:T(8,128)(2,1)S(1)}, u32[]{:S(2)}, u32[]{:S(2)}) collective-permute-start(bf16[128,768]{1,0:T(8,128)(2,1)S(1)} %get-tuple-element.169), channel_id=1, source_target_pairs={{0,24},{8,16},{16,8},{24,0},{1,25},{9,17},{17,9},{25,1},{2,26},{10... | collective-permute-start | bytes 589832 | tf_op jit(solution)/shard_map/plane_act/ppermute | solution.py:980
  45.6 6.0 %token_backward.1 = (bf16[128,768]{1,0:T(8,128)(2,1)}, f32[128,768]{1,0:T(8,128)S(1)}, bf16[128,2560]{1,0:T(8,128)(2,1)S(1)}, bf16[128,2560]{1,0:T(8,128)(2,1)S(...) custom-call(s32[3]{0:T(128)S(1)} %pad_add_fusion.place_ref, ...), custom_call_target="tpu_custom_call" | custom-call | flops 9000000 | bytes 9000 | tf_op jit(solution)/shard_map/token_backward/pallas_call | solution.py:350
  52.6 1.8 %collective-permute-start.19 = (bf16[128,2560]{1,0:T(8,128)(2,1)S(1)}, bf16[128,2560]{1,0:T(8,128)(2,1)S(1)}, u32[]{:S(2)}, u32[]{:S(2)}) collective-permute-start(bf16[128,2560]{1,0:T(8,128)(2,1)S(1)} %get-tuple-element.179), channel_id=1, source_target_pairs={{0,24},{8,16},{16,8},{24,0},{1,25},{9,17},{17,9},{25,1},{2,26},{10... | collective-permute-start | bytes 1966088 | tf_op jit(solution)/shard_map/plane_back/ppermute | solution.py:980
  54.6 1.4 %collective-permute-start.13 = (bf16[192,128]{1,0:T(8,128)(2,1)S(1)}, bf16[192,128]{1,0:T(8,128)(2,1)S(1)}, u32[]{:S(2)}, u32[]{:S(2)}) collective-permute-start(bf16[192,128]{1,0:T(8,128)(2,1)S(1)} %get-tuple-element.161), channel_id=1, source_target_pairs={{0,4},{2,6},{4,0},{6,2},{1,5},{3,7},{5,1},{7,3},{8,12},{10,14},{12... | collective-permute-start | bytes 147464 | tf_op jit(solution)/shard_map/chip_grad/ppermute | solution.py:980
  56.0 2.8 %collective-permute-start.14 = (bf16[192,128]{1,0:T(8,128)(2,1)S(1)}, bf16[192,128]{1,0:T(8,128)(2,1)S(1)}, u32[]{:S(2)}, u32[]{:S(2)}) collective-permute-start(bf16[192,128]{1,0:T(8,128)(2,1)S(1)} %get-tuple-element.162), channel_id=1, source_target_pairs={{0,6},{2,4},{4,2},{6,0},{1,7},{3,5},{5,3},{7,1},{8,14},{10,12},{12... | collective-permute-start | bytes 147464 | tf_op jit(solution)/shard_map/chip_grad/ppermute | solution.py:980
  59.6 2.3 %collective-permute-done.14.refs_3_ = bf16[192,128]{1,0:T(8,128)(2,1)S(1)} collective-permute-done((bf16[192,128]{1,0:T(8,128)(2,1)S(1)}, bf16[192,128]{1,0:T(8,128)(2,1)S(1)}, u32[]{:S(2)}, u32[]{:S(2)}) %collective-permute-start.14) | collective-permute-done | bytes 49184 | tf_op jit(solution)/shard_map/chip_grad/ppermute | solution.py:980
  61.9 3.8 %attend_back.1 = (bf16[4,128,256]{2,1,0:T(8,128)(2,1)S(1)}, f32[4,128,512]{2,1,0:T(8,128)S(1)}, bf16[4,128,512]{2,1,0:T(8,128)(2,1)S(1)}) custom-call(s32[3]{0:T(128)S(1)} %pad_add_fusion.place_ref, bf16[4,128,256]{2,1,0:T(8,128)(2,1)S(1)} %get-tuple-element.154.q_ref, bf16[4,128,512]{2,1,0:T(8,128)(2,1)S(1)} %get-tuple-element.155.own_ref, ...), custom_call_target="tpu_custom_call" | custom-call | flops 6000000 | bytes 6000 | tf_op jit(solution)/shard_map/attend_back/pallas_call | solution.py:350
  65.8 1.5 %grad_down.1 = (f32[4,96,768]{2,1,0:T(8,128)S(1)}, bf16[4,96,768]{2,1,0:T(8,128)(2,1)S(1)}) custom-call(s32[3]{0:T(128)S(1)} %pad_add_fusion.place_ref, bf16[128,768]{1,0:T(8,128)(2,1)S(1)} %get-tuple-element.170.refs_0_, bf16[128,768]{1,0:T(8,128)(2,1)S(1)} %collective-permute-done.16.refs_1_, bf16[128,768]{1,0:T(8,128)(2,1)S(1)} %collective-permute-done.17.refs_2_, ...), custom_call_target="tpu_custom_call" | custom-call | flops 3000000 | bytes 3000 | tf_op jit(solution)/shard_map/grad_down/pallas_call | solution.py:350
  70.4 1.2 collective-permute-start.24
  71.6 2.1 %collective-permute-start.21 = (bf16[576,128]{1,0:T(8,128)(2,1)S(1)}, bf16[576,128]{1,0:T(8,128)(2,1)S(1)}, u32[]{:S(2)}, u32[]{:S(2)}) collective-permute-start(bf16[576,128]{1,0:T(8,128)(2,1)S(1)} %get-tuple-element.183), channel_id=1, source_target_pairs={{0,4},{2,6},{4,0},{6,2},{1,5},{3,7},{5,1},{7,3},{8,12},{10,14},{12... | collective-permute-start | bytes 442376 | tf_op jit(solution)/shard_map/chip_qkv/ppermute | solution.py:980
  74.8 1.4 %collective-permute-start.29 = (bf16[128,2560]{1,0:T(8,128)(2,1)S(1)}, bf16[128,2560]{1,0:T(8,128)(2,1)S(1)}, u32[]{:S(2)}, u32[]{:S(2)}) collective-permute-start(bf16[128,2560]{1,0:T(8,128)(2,1)S(1)} %get-tuple-element.210), channel_id=1, source_target_pairs={{0,8},{8,0},{16,24},{24,16},{1,9},{9,1},{17,25},{25,17},{2,10},{10... | collective-permute-start | bytes 1966088 | tf_op jit(solution)/shard_map/plane_back/ppermute | solution.py:980
  76.9 2.5 %grad_qkv.1 = (f32[4,96,768]{2,1,0:T(8,128)S(1)}, bf16[4,96,768]{2,1,0:T(8,128)(2,1)S(1)}) custom-call(s32[3]{0:T(128)S(1)} %pad_add_fusion.place_ref, bf16[1,128,768]{2,1,0:T(8,128)(2,1)S(1)} %get-tuple-element.186.refs_0_, bf16[2,128,768]{2,1,0:T(8,128)(2,1)S(1)} %get-tuple-element.187.refs_1_, bf16[1,128,768]{2,1,0:T(8,128)(2,1)S(1)} %get-tuple-element.188.refs_2_, ...), custom_call_target="tpu_custom_call" | custom-call | flops 4000000 | bytes 4000 | tf_op jit(solution)/shard_map/grad_qkv/pallas_call | solution.py:350
  79.4 3.3 %collective-permute-done.24.in_ref = bf16[2,96,768]{2,1,0:T(8,128)(2,1)S(1)} collective-permute-done((bf16[2,96,768]{2,1,0:T(8,128)(2,1)S(1)}, bf16[2,96,768]{2,1,0:T(8,128)(2,1)S(1)}, u32[]{:S(2)}, u32[]{:S(2)}) %collective-permute-start.24) | collective-permute-done | bytes 294944 | tf_op jit(solution)/shard_map/down_sum/ppermute | solution.py:980
  83.3 4.2 %collective-permute-done.22.refs_3_ = bf16[576,128]{1,0:T(8,128)(2,1)S(1)} collective-permute-done((bf16[576,128]{1,0:T(8,128)(2,1)S(1)}, bf16[576,128]{1,0:T(8,128)(2,1)S(1)}, u32[]{:S(2)}, u32[]{:S(2)}) %collective-permute-start.22) | collective-permute-done | bytes 147488 | tf_op jit(solution)/shard_map/chip_qkv/ppermute | solution.py:980
  89.5 1.4 collective-permute-done.29.refs_1_
  90.8 1.3 collective-permute-done.30.refs_2_
  92.1 1.7 %grad_up_out.1 = (f32[4,128,768]{2,1,0:T(8,128)S(1)}, bf16[4,128,768]{2,1,0:T(8,128)(2,1)S(1)}) custom-call(s32[3]{0:T(128)S(1)} %pad_add_fusion.place_ref, bf16[128,2560]{1,0:T(8,128)(2,1)S(1)} %get-tuple-element.212.refs_0_, bf16[128,2560]{1,0:T(8,128)(2,1)S(1)} %collective-permute-done.29.refs_1_, bf16[128,2560]{1,0:T(8,128)(2,1)S(1)} %collective-permute-done.30.refs_2_, ...), custom_call_target="tpu_custom_call" | custom-call | flops 4000000 | bytes 4000 | tf_op jit(solution)/shard_map/grad_up_out/pallas_call | solution.py:350
  94.4 2.3 %collective-permute-done.20.refs_1_ = bf16[576,128]{1,0:T(8,128)(2,1)S(1)} collective-permute-done((bf16[576,128]{1,0:T(8,128)(2,1)S(1)}, bf16[576,128]{1,0:T(8,128)(2,1)S(1)}, u32[]{:S(2)}, u32[]{:S(2)}) %collective-permute-start.20) | collective-permute-done | bytes 147488 | tf_op jit(solution)/shard_map/chip_qkv/ppermute | solution.py:980
  96.7 1.6 %collective-permute-done.31.in_ref = bf16[1,96,768]{2,1,0:T(8,128)(2,1)S(1)} collective-permute-done((bf16[1,96,768]{2,1,0:T(8,128)(2,1)S(1)}, bf16[1,96,768]{2,1,0:T(8,128)(2,1)S(1)}, u32[]{:S(2)}, u32[]{:S(2)}) %collective-permute-start.31) | collective-permute-done | bytes 147488 | tf_op jit(solution)/shard_map/down_sum/ppermute | solution.py:980
  98.3 2.3 %collective-permute-done.32.in_ref = bf16[4,128,768]{2,1,0:T(8,128)(2,1)S(1)} collective-permute-done((bf16[4,128,768]{2,1,0:T(8,128)(2,1)S(1)}, bf16[4,128,768]{2,1,0:T(8,128)(2,1)S(1)}, u32[]{:S(2)}, u32[]{:S(2)}) %collective-permute-start.32) | collective-permute-done | bytes 786464 | tf_op jit(solution)/shard_map/core_up/ppermute | solution.py:976
  101.8 1.8 %collective-permute-start.26 = (bf16[96,768]{1,0:T(8,128)(2,1)S(1)}, bf16[96,768]{1,0:T(8,128)(2,1)S(1)}, u32[]{:S(2)}, u32[]{:S(2)}) collective-permute-start(bf16[96,768]{1,0:T(8,128)(2,1)S(1)} %get-tuple-element.203), channel_id=1, source_target_pairs={{0,8},{8,0},{16,24},{24,16},{1,9},{9,1},{17,25},{25,17},{2,10},{10... | collective-permute-start | bytes 442376 | tf_op jit(solution)/shard_map/plane_w/ppermute | solution.py:980
  105.2 2.9 %collective-permute-done.26.refs_1_ = bf16[96,768]{1,0:T(8,128)(2,1)S(1)} collective-permute-done((bf16[96,768]{1,0:T(8,128)(2,1)S(1)}, bf16[96,768]{1,0:T(8,128)(2,1)S(1)}, u32[]{:S(2)}, u32[]{:S(2)}) %collective-permute-start.26) | collective-permute-done | bytes 147488 | tf_op jit(solution)/shard_map/plane_w/ppermute | solution.py:980
  108.2 2.2 %collective-permute-done.27.refs_2_ = bf16[96,768]{1,0:T(8,128)(2,1)S(1)} collective-permute-done((bf16[96,768]{1,0:T(8,128)(2,1)S(1)}, bf16[96,768]{1,0:T(8,128)(2,1)S(1)}, u32[]{:S(2)}, u32[]{:S(2)}) %collective-permute-start.27) | collective-permute-done | bytes 147488 | tf_op jit(solution)/shard_map/plane_w/ppermute | solution.py:980
  110.4 1.9 %collective-permute-done.28.refs_3_ = bf16[96,768]{1,0:T(8,128)(2,1)S(1)} collective-permute-done((bf16[96,768]{1,0:T(8,128)(2,1)S(1)}, bf16[96,768]{1,0:T(8,128)(2,1)S(1)}, u32[]{:S(2)}, u32[]{:S(2)}) %collective-permute-start.28) | collective-permute-done | bytes 147488 | tf_op jit(solution)/shard_map/plane_w/ppermute | solution.py:980
  113.6 2.1 %collective-permute-start.37 = (bf16[1,128,768]{2,1,0:T(8,128)(2,1)S(1)}, bf16[1,128,768]{2,1,0:T(8,128)(2,1)S(1)}, u32[]{:S(2)}, u32[]{:S(2)}) collective-permute-start(bf16[1,128,768]{2,1,0:T(8,128)(2,1)S(1)} %get-tuple-element.237), channel_id=1, source_target_pairs={{0,4},{2,6},{4,0},{6,2},{1,5},{3,7},{5,1},{7,3},{8,12},{10,14},{12... | collective-permute-start | bytes 589832 | tf_op jit(solution)/shard_map/up_sum/ppermute | solution.py:980
  116.2 2.0 %collective-permute-start.34 = (bf16[24,768]{1,0:T(8,128)(2,1)S(1)}, bf16[24,768]{1,0:T(8,128)(2,1)S(1)}, u32[]{:S(2)}, u32[]{:S(2)}) collective-permute-start(bf16[24,768]{1,0:T(8,128)(2,1)S(1)} %get-tuple-element.227), channel_id=1, source_target_pairs={{0,4},{2,6},{4,0},{6,2},{1,5},{3,7},{5,1},{7,3},{8,12},{10,14},{12... | collective-permute-start | bytes 110600 | tf_op jit(solution)/shard_map/chip_w/ppermute | solution.py:980
  118.3 1.9 %collective-permute-start.35 = (bf16[24,768]{1,0:T(8,128)(2,1)S(1)}, bf16[24,768]{1,0:T(8,128)(2,1)S(1)}, u32[]{:S(2)}, u32[]{:S(2)}) collective-permute-start(bf16[24,768]{1,0:T(8,128)(2,1)S(1)} %get-tuple-element.228), channel_id=1, source_target_pairs={{0,6},{2,4},{4,2},{6,0},{1,7},{3,5},{5,3},{7,1},{8,14},{10,12},{12... | collective-permute-start | bytes 110600 | tf_op jit(solution)/shard_map/chip_w/ppermute | solution.py:980
  120.1 2.7 %grad_inputs.1 = bf16[128,768]{1,0:T(8,128)(2,1)} custom-call(s32[3]{0:T(128)S(1)} %pad_add_fusion.place_ref, bf16[576,128]{1,0:T(8,128)(2,1)S(1)} %get-tuple-element.181.refs_0_, bf16[576,128]{1,0:T(8,128)(2,1)S(1)} %collective-permute-done.20.refs_1_, bf16[576,128]{1,0:T(8,128)(2,1)S(1)} %collective-permute-done.21.refs_2_, ...), custom_call_target="tpu_custom_call" | custom-call | flops 3000000 | bytes 3000 | tf_op jit(solution)/shard_map/grad_inputs/pallas_call | solution.py:350
  123.6 4.0 %collective-permute-done.34.refs_2_ = bf16[24,768]{1,0:T(8,128)(2,1)S(1)} collective-permute-done((bf16[24,768]{1,0:T(8,128)(2,1)S(1)}, bf16[24,768]{1,0:T(8,128)(2,1)S(1)}, u32[]{:S(2)}, u32[]{:S(2)}) %collective-permute-start.34) | collective-permute-done | bytes 36896 | tf_op jit(solution)/shard_map/chip_w/ppermute | solution.py:980
  128.8 1.4 %collective-permute-start.38 = (bf16[24,768]{1,0:T(8,128)(2,1)S(1)}, bf16[24,768]{1,0:T(8,128)(2,1)S(1)}, u32[]{:S(2)}, u32[]{:S(2)}) collective-permute-start(bf16[24,768]{1,0:T(8,128)(2,1)S(1)} %get-tuple-element.245), channel_id=1, source_target_pairs={{0,8},{8,0},{16,24},{24,16},{1,9},{9,1},{17,25},{25,17},{2,10},{10... | collective-permute-start | bytes 110600 | tf_op jit(solution)/shard_map/plane_rows/ppermute | solution.py:980
  131.0 1.3 collective-permute-start.40
  132.3 1.3 finish_qkv.1
  134.4 1.5 %collective-permute-done.40.refs_3_ = bf16[24,768]{1,0:T(8,128)(2,1)S(1)} collective-permute-done((bf16[24,768]{1,0:T(8,128)(2,1)S(1)}, bf16[24,768]{1,0:T(8,128)(2,1)S(1)}, u32[]{:S(2)}, u32[]{:S(2)}) %collective-permute-start.40) | collective-permute-done | bytes 36896 | tf_op jit(solution)/shard_map/plane_rows/ppermute | solution.py:980
  135.9 1.3 place_up.1
  (92 shorter events, 26.2 us)
Async XLA Ops:
  0.7 13.5 %collective-permute-start.1 = (bf16[128,768]{1,0:T(8,128)(2,1)}, bf16[128,768]{1,0:T(8,128)(2,1)S(1)}, u32[]{:S(2)}, u32[]{:S(2)}) collective-permute-start(bf16[128,768]{1,0:T(8,128)(2,1)} %bitcast.7), channel_id=1, source_target_pairs={{0,4},{2,6},{4,0},{6,2},{1,5},{3,7},{5,1},{7,3},{8,12},{10,14},{12... | collective-permute-start | bytes 589832 | tf_op jit(solution)/shard_map/gather_in/ppermute | solution.py:980
  4.8 11.7 %collective-permute-start = (bf16[128,768]{1,0:T(8,128)(2,1)}, bf16[128,768]{1,0:T(8,128)(2,1)S(1)}, u32[]{:S(2)}, u32[]{:S(2)}) collective-permute-start(bf16[128,768]{1,0:T(8,128)(2,1)} %bitcast.8), channel_id=1, source_target_pairs={{0,2},{2,0},{4,6},{6,4},{1,3},{3,1},{5,7},{7,5},{8,10},{10,8},{12,... | collective-permute-start | bytes 589832 | tf_op jit(solution)/shard_map/gather_in/ppermute | solution.py:980
  14.2 7.2 %collective-permute-start.2 = (bf16[128,768]{1,0:T(8,128)(2,1)S(1)}, bf16[128,768]{1,0:T(8,128)(2,1)S(1)}, u32[]{:S(2)}, u32[]{:S(2)}) collective-permute-start(bf16[128,768]{1,0:T(8,128)(2,1)S(1)} %collective-permute-done.1.refs_1_), channel_id=1, source_target_pairs={{0,2},{2,0},{4,6},{6,4},{1,3},{3,1},{5,7},{7,5},{8,10},{10,8},{12,... | collective-permute-start | bytes 589832 | tf_op jit(solution)/shard_map/gather_in/ppermute | solution.py:980
  16.4 6.1 %collective-permute-start.3 = (bf16[1,128,512]{2,1,0:T(8,128)(2,1)S(1)}, bf16[1,128,512]{2,1,0:T(8,128)(2,1)S(1)}, u32[]{:S(2)}, u32[]{:S(2)}) collective-permute-start(bf16[1,128,512]{2,1,0:T(8,128)(2,1)S(1)} %get-tuple-element.136.refs_3_), channel_id=1, source_target_pairs={{0,1},{1,0},{2,3},{3,2},{4,5},{5,4},{6,7},{7,6},{8,9},{9,8},{10,11... | collective-permute-start | bytes 393224 | tf_op jit(solution)/shard_map/core_kv/ppermute | solution.py:976
  16.5 22.2 %copy-start.1 = (bf16[768,768]{1,0:T(8,128)(2,1)S(1)}, bf16[768,768]{1,0:T(8,128)(2,1)}, u32[]{:S(2)}) copy-start(bf16[768,768]{1,0:T(8,128)(2,1)} %wo_ref.1) | copy-start | bytes 3538948
  16.5 22.2 %copy-start.10 = (f32[768]{0:T(1024)S(1)}, f32[768]{0:T(1024)}, u32[]{:S(2)}) copy-start(f32[768]{0:T(1024)} %g2.1) | copy-start | bytes 9220
  16.5 22.2 %copy-start.11 = (f32[768]{0:T(1024)S(1)}, f32[768]{0:T(1024)}, u32[]{:S(2)}) copy-start(f32[768]{0:T(1024)} %b2.1) | copy-start | bytes 9220
  16.5 22.2 %copy-start.12 = (f32[768]{0:T(1024)S(1)}, f32[768]{0:T(1024)}, u32[]{:S(2)}) copy-start(f32[768]{0:T(1024)} %g3.1) | copy-start | bytes 9220
  16.5 22.2 %copy-start.13 = (f32[768]{0:T(1024)S(1)}, f32[768]{0:T(1024)}, u32[]{:S(2)}) copy-start(f32[768]{0:T(1024)} %b3.1) | copy-start | bytes 9220
  16.5 23.6 %copy-start = (bf16[768,3072]{1,0:T(8,128)(2,1)S(1)}, bf16[768,3072]{1,0:T(8,128)(2,1)}, u32[]{:S(2)}) copy-start(bf16[768,3072]{1,0:T(8,128)(2,1)} %wu_ref.3) | copy-start | bytes 14155780
  17.3 5.3 %collective-permute-start.4 = (bf16[2,128,512]{2,1,0:T(8,128)(2,1)S(1)}, bf16[2,128,512]{2,1,0:T(8,128)(2,1)S(1)}, u32[]{:S(2)}, u32[]{:S(2)}) collective-permute-start(bf16[2,128,512]{2,1,0:T(8,128)(2,1)S(1)} %get-tuple-element.137.refs_4_), channel_id=1, source_target_pairs={{0,1},{1,0},{2,3},{3,2},{4,5},{5,4},{6,7},{7,6},{8,9},{9,8},{10,11... | collective-permute-start | bytes 786440 | tf_op jit(solution)/shard_map/core_kv/ppermute | solution.py:976
  18.4 14.4 %collective-permute-start.11 = (bf16[128,768]{1,0:T(8,128)(2,1)S(1)}, bf16[128,768]{1,0:T(8,128)(2,1)S(1)}, u32[]{:S(2)}, u32[]{:S(2)}) collective-permute-start(bf16[128,768]{1,0:T(8,128)(2,1)S(1)} %mask_grad.1.go_ref.refs_4_), channel_id=1, source_target_pairs={{0,24},{8,16},{16,8},{24,0},{1,25},{9,17},{17,9},{25,1},{2,26},{10... | collective-permute-start | bytes 589832 | tf_op jit(solution)/shard_map/plane_out/ppermute | solution.py:980
  20.9 12.1 %collective-permute-start.10 = (bf16[128,768]{1,0:T(8,128)(2,1)S(1)}, bf16[128,768]{1,0:T(8,128)(2,1)S(1)}, u32[]{:S(2)}, u32[]{:S(2)}) collective-permute-start(bf16[128,768]{1,0:T(8,128)(2,1)S(1)} %mask_grad.1.go_ref.refs_4_), channel_id=1, source_target_pairs={{0,16},{8,24},{16,0},{24,8},{1,17},{9,25},{17,1},{25,9},{2,18},{10... | collective-permute-start | bytes 589832 | tf_op jit(solution)/shard_map/plane_out/ppermute | solution.py:980
  21.4 11.5 %collective-permute-start.9 = (bf16[128,768]{1,0:T(8,128)(2,1)S(1)}, bf16[128,768]{1,0:T(8,128)(2,1)S(1)}, u32[]{:S(2)}, u32[]{:S(2)}) collective-permute-start(bf16[128,768]{1,0:T(8,128)(2,1)S(1)} %mask_grad.1.go_ref.refs_4_), channel_id=1, source_target_pairs={{0,8},{8,0},{16,24},{24,16},{1,9},{9,1},{17,25},{25,17},{2,10},{10... | collective-permute-start | bytes 589832 | tf_op jit(solution)/shard_map/plane_out/ppermute | solution.py:980
  22.5 1.4 %collective-permute-start.5 = (bf16[1,128,512]{2,1,0:T(8,128)(2,1)S(1)}, bf16[1,128,512]{2,1,0:T(8,128)(2,1)S(1)}, u32[]{:S(2)}, u32[]{:S(2)}) collective-permute-start(bf16[1,128,512]{2,1,0:T(8,128)(2,1)S(1)} %get-tuple-element.138.refs_5_), channel_id=1, source_target_pairs={{0,1},{1,0},{2,3},{3,2},{4,5},{5,4},{6,7},{7,6},{8,9},{9,8},{10,11... | collective-permute-start | bytes 393224 | tf_op jit(solution)/shard_map/core_kv/ppermute | solution.py:976
  28.2 4.8 %collective-permute-start.6 = (bf16[192,128]{1,0:T(8,128)(2,1)S(1)}, bf16[192,128]{1,0:T(8,128)(2,1)S(1)}, u32[]{:S(2)}, u32[]{:S(2)}) collective-permute-start(bf16[192,128]{1,0:T(8,128)(2,1)S(1)} %get-tuple-element.140), channel_id=1, source_target_pairs={{0,2},{2,0},{4,6},{6,4},{1,3},{3,1},{5,7},{7,5},{8,10},{10,8},{12,... | collective-permute-start | bytes 147464 | tf_op jit(solution)/shard_map/chip_attn/ppermute | solution.py:980
  29.5 6.4 %collective-permute-start.7 = (bf16[192,128]{1,0:T(8,128)(2,1)S(1)}, bf16[192,128]{1,0:T(8,128)(2,1)S(1)}, u32[]{:S(2)}, u32[]{:S(2)}) collective-permute-start(bf16[192,128]{1,0:T(8,128)(2,1)S(1)} %get-tuple-element.141), channel_id=1, source_target_pairs={{0,4},{2,6},{4,0},{6,2},{1,5},{3,7},{5,1},{7,3},{8,12},{10,14},{12... | collective-permute-start | bytes 147464 | tf_op jit(solution)/shard_map/chip_attn/ppermute | solution.py:980
  32.8 5.9 %collective-permute-start.8 = (bf16[192,128]{1,0:T(8,128)(2,1)S(1)}, bf16[192,128]{1,0:T(8,128)(2,1)S(1)}, u32[]{:S(2)}, u32[]{:S(2)}) collective-permute-start(bf16[192,128]{1,0:T(8,128)(2,1)S(1)} %get-tuple-element.142), channel_id=1, source_target_pairs={{0,6},{2,4},{4,2},{6,0},{1,7},{3,5},{5,3},{7,1},{8,14},{10,12},{12... | collective-permute-start | bytes 147464 | tf_op jit(solution)/shard_map/chip_attn/ppermute | solution.py:980
  42.0 9.6 %collective-permute-start.16 = (bf16[128,768]{1,0:T(8,128)(2,1)S(1)}, bf16[128,768]{1,0:T(8,128)(2,1)S(1)}, u32[]{:S(2)}, u32[]{:S(2)}) collective-permute-start(bf16[128,768]{1,0:T(8,128)(2,1)S(1)} %get-tuple-element.167), channel_id=1, source_target_pairs={{0,8},{8,0},{16,24},{24,16},{1,9},{9,1},{17,25},{25,17},{2,10},{10... | collective-permute-start | bytes 589832 | tf_op jit(solution)/shard_map/plane_act/ppermute | solution.py:980
  42.7 9.0 %collective-permute-start.17 = (bf16[128,768]{1,0:T(8,128)(2,1)S(1)}, bf16[128,768]{1,0:T(8,128)(2,1)S(1)}, u32[]{:S(2)}, u32[]{:S(2)}) collective-permute-start(bf16[128,768]{1,0:T(8,128)(2,1)S(1)} %get-tuple-element.168), channel_id=1, source_target_pairs={{0,16},{8,24},{16,0},{24,8},{1,17},{9,25},{17,1},{25,9},{2,18},{10... | collective-permute-start | bytes 589832 | tf_op jit(solution)/shard_map/plane_act/ppermute | solution.py:980
  44.2 8.4 %collective-permute-start.18 = (bf16[128,768]{1,0:T(8,128)(2,1)S(1)}, bf16[128,768]{1,0:T(8,128)(2,1)S(1)}, u32[]{:S(2)}, u32[]{:S(2)}) collective-permute-start(bf16[128,768]{1,0:T(8,128)(2,1)S(1)} %get-tuple-element.169), channel_id=1, source_target_pairs={{0,24},{8,16},{16,8},{24,0},{1,25},{9,17},{17,9},{25,1},{2,26},{10... | collective-permute-start | bytes 589832 | tf_op jit(solution)/shard_map/plane_act/ppermute | solution.py:980
  52.6 15.1 %collective-permute-start.19 = (bf16[128,2560]{1,0:T(8,128)(2,1)S(1)}, bf16[128,2560]{1,0:T(8,128)(2,1)S(1)}, u32[]{:S(2)}, u32[]{:S(2)}) collective-permute-start(bf16[128,2560]{1,0:T(8,128)(2,1)S(1)} %get-tuple-element.179), channel_id=1, source_target_pairs={{0,24},{8,16},{16,8},{24,0},{1,25},{9,17},{17,9},{25,1},{2,26},{10... | collective-permute-start | bytes 1966088 | tf_op jit(solution)/shard_map/plane_back/ppermute | solution.py:980
  54.4 4.4 %collective-permute-start.12 = (bf16[192,128]{1,0:T(8,128)(2,1)S(1)}, bf16[192,128]{1,0:T(8,128)(2,1)S(1)}, u32[]{:S(2)}, u32[]{:S(2)}) collective-permute-start(bf16[192,128]{1,0:T(8,128)(2,1)S(1)} %get-tuple-element.160), channel_id=1, source_target_pairs={{0,2},{2,0},{4,6},{6,4},{1,3},{3,1},{5,7},{7,5},{8,10},{10,8},{12,... | collective-permute-start | bytes 147464 | tf_op jit(solution)/shard_map/chip_grad/ppermute | solution.py:980
  54.6 5.0 %collective-permute-start.13 = (bf16[192,128]{1,0:T(8,128)(2,1)S(1)}, bf16[192,128]{1,0:T(8,128)(2,1)S(1)}, u32[]{:S(2)}, u32[]{:S(2)}) collective-permute-start(bf16[192,128]{1,0:T(8,128)(2,1)S(1)} %get-tuple-element.161), channel_id=1, source_target_pairs={{0,4},{2,6},{4,0},{6,2},{1,5},{3,7},{5,1},{7,3},{8,12},{10,14},{12... | collective-permute-start | bytes 147464 | tf_op jit(solution)/shard_map/chip_grad/ppermute | solution.py:980
  56.0 5.9 %collective-permute-start.14 = (bf16[192,128]{1,0:T(8,128)(2,1)S(1)}, bf16[192,128]{1,0:T(8,128)(2,1)S(1)}, u32[]{:S(2)}, u32[]{:S(2)}) collective-permute-start(bf16[192,128]{1,0:T(8,128)(2,1)S(1)} %get-tuple-element.162), channel_id=1, source_target_pairs={{0,6},{2,4},{4,2},{6,0},{1,7},{3,5},{5,3},{7,1},{8,14},{10,12},{12... | collective-permute-start | bytes 147464 | tf_op jit(solution)/shard_map/chip_grad/ppermute | solution.py:980
  65.7 2.0 %collective-permute-start.15 = (bf16[4,128,512]{2,1,0:T(8,128)(2,1)S(1)}, bf16[4,128,512]{2,1,0:T(8,128)(2,1)S(1)}, u32[]{:S(2)}, u32[]{:S(2)}) collective-permute-start(bf16[4,128,512]{2,1,0:T(8,128)(2,1)S(1)} %get-tuple-element.165), channel_id=1, source_target_pairs={{0,1},{1,0},{2,3},{3,2},{4,5},{5,4},{6,7},{7,6},{8,9},{9,8},{10,11... | collective-permute-start | bytes 1572872 | tf_op jit(solution)/shard_map/core_grad/ppermute | solution.py:976
  67.7 2.0 %collective-permute-start.23 = (bf16[4,96,768]{2,1,0:T(8,128)(2,1)S(1)}, bf16[4,96,768]{2,1,0:T(8,128)(2,1)S(1)}, u32[]{:S(2)}, u32[]{:S(2)}) collective-permute-start(bf16[4,96,768]{2,1,0:T(8,128)(2,1)S(1)} %get-tuple-element.191), channel_id=1, source_target_pairs={{0,1},{1,0},{2,3},{3,2},{4,5},{5,4},{6,7},{7,6},{8,9},{9,8},{10,11... | collective-permute-start | bytes 1769480 | tf_op jit(solution)/shard_map/core_down/ppermute | solution.py:976
  70.4 12.3 %collective-permute-start.24 = (bf16[2,96,768]{2,1,0:T(8,128)(2,1)S(1)}, bf16[2,96,768]{2,1,0:T(8,128)(2,1)S(1)}, u32[]{:S(2)}, u32[]{:S(2)}) collective-permute-start(bf16[2,96,768]{2,1,0:T(8,128)(2,1)S(1)} %get-tuple-element.198), channel_id=1, source_target_pairs={{0,2},{2,0},{4,6},{6,4},{1,3},{3,1},{5,7},{7,5},{8,10},{10,8},{12,... | collective-permute-start | bytes 884744 | tf_op jit(solution)/shard_map/down_sum/ppermute | solution.py:980
  71.6 11.7 %collective-permute-start.21 = (bf16[576,128]{1,0:T(8,128)(2,1)S(1)}, bf16[576,128]{1,0:T(8,128)(2,1)S(1)}, u32[]{:S(2)}, u32[]{:S(2)}) collective-permute-start(bf16[576,128]{1,0:T(8,128)(2,1)S(1)} %get-tuple-element.183), channel_id=1, source_target_pairs={{0,4},{2,6},{4,0},{6,2},{1,5},{3,7},{5,1},{7,3},{8,12},{10,14},{12... | collective-permute-start | bytes 442376 | tf_op jit(solution)/shard_map/chip_qkv/ppermute | solution.py:980
  73.8 13.7 %collective-permute-start.22 = (bf16[576,128]{1,0:T(8,128)(2,1)S(1)}, bf16[576,128]{1,0:T(8,128)(2,1)S(1)}, u32[]{:S(2)}, u32[]{:S(2)}) collective-permute-start(bf16[576,128]{1,0:T(8,128)(2,1)S(1)} %get-tuple-element.184), channel_id=1, source_target_pairs={{0,6},{2,4},{4,2},{6,0},{1,7},{3,5},{5,3},{7,1},{8,14},{10,12},{12... | collective-permute-start | bytes 442376 | tf_op jit(solution)/shard_map/chip_qkv/ppermute | solution.py:980
  74.8 16.0 %collective-permute-start.29 = (bf16[128,2560]{1,0:T(8,128)(2,1)S(1)}, bf16[128,2560]{1,0:T(8,128)(2,1)S(1)}, u32[]{:S(2)}, u32[]{:S(2)}) collective-permute-start(bf16[128,2560]{1,0:T(8,128)(2,1)S(1)} %get-tuple-element.210), channel_id=1, source_target_pairs={{0,8},{8,0},{16,24},{24,16},{1,9},{9,1},{17,25},{25,17},{2,10},{10... | collective-permute-start | bytes 1966088 | tf_op jit(solution)/shard_map/plane_back/ppermute | solution.py:980
  76.2 15.8 %collective-permute-start.30 = (bf16[128,2560]{1,0:T(8,128)(2,1)S(1)}, bf16[128,2560]{1,0:T(8,128)(2,1)S(1)}, u32[]{:S(2)}, u32[]{:S(2)}) collective-permute-start(bf16[128,2560]{1,0:T(8,128)(2,1)S(1)} %get-tuple-element.211), channel_id=1, source_target_pairs={{0,16},{8,24},{16,0},{24,8},{1,17},{9,25},{17,1},{25,9},{2,18},{10... | collective-permute-start | bytes 1966088 | tf_op jit(solution)/shard_map/plane_back/ppermute | solution.py:980
  87.5 6.3 %collective-permute-start.25 = (bf16[4,96,768]{2,1,0:T(8,128)(2,1)S(1)}, bf16[4,96,768]{2,1,0:T(8,128)(2,1)S(1)}, u32[]{:S(2)}, u32[]{:S(2)}) collective-permute-start(bf16[4,96,768]{2,1,0:T(8,128)(2,1)S(1)} %get-tuple-element.201), channel_id=1, source_target_pairs={{0,1},{1,0},{2,3},{3,2},{4,5},{5,4},{6,7},{7,6},{8,9},{9,8},{10,11... | collective-permute-start | bytes 1769480 | tf_op jit(solution)/shard_map/core_w/ppermute | solution.py:976
  87.5 9.3 %collective-permute-start.20 = (bf16[576,128]{1,0:T(8,128)(2,1)S(1)}, bf16[576,128]{1,0:T(8,128)(2,1)S(1)}, u32[]{:S(2)}, u32[]{:S(2)}) collective-permute-start(bf16[576,128]{1,0:T(8,128)(2,1)S(1)} %get-tuple-element.182), channel_id=1, source_target_pairs={{0,2},{2,0},{4,6},{6,4},{1,3},{3,1},{5,7},{7,5},{8,10},{10,8},{12,... | collective-permute-start | bytes 442376 | tf_op jit(solution)/shard_map/chip_qkv/ppermute | solution.py:980
  88.2 10.1 %collective-permute-start.31 = (bf16[1,96,768]{2,1,0:T(8,128)(2,1)S(1)}, bf16[1,96,768]{2,1,0:T(8,128)(2,1)S(1)}, u32[]{:S(2)}, u32[]{:S(2)}) collective-permute-start(bf16[1,96,768]{2,1,0:T(8,128)(2,1)S(1)} %get-tuple-element.218), channel_id=1, source_target_pairs={{0,4},{2,6},{4,0},{6,2},{1,5},{3,7},{5,1},{7,3},{8,12},{10,14},{12... | collective-permute-start | bytes 442376 | tf_op jit(solution)/shard_map/down_sum/ppermute | solution.py:980
  98.3 2.3 %collective-permute-start.32 = (bf16[4,128,768]{2,1,0:T(8,128)(2,1)S(1)}, bf16[4,128,768]{2,1,0:T(8,128)(2,1)S(1)}, u32[]{:S(2)}, u32[]{:S(2)}) collective-permute-start(bf16[4,128,768]{2,1,0:T(8,128)(2,1)S(1)} %get-tuple-element.219), channel_id=1, source_target_pairs={{0,1},{1,0},{2,3},{3,2},{4,5},{5,4},{6,7},{7,6},{8,9},{9,8},{10,11... | collective-permute-start | bytes 2359304 | tf_op jit(solution)/shard_map/core_up/ppermute | solution.py:976
  100.6 19.5 %copy-start.5 = (bf16[768,768]{1,0:T(8,128)(2,1)S(1)}, bf16[768,768]{1,0:T(8,128)(2,1)}, u32[]{:S(2)}) copy-start(bf16[768,768]{1,0:T(8,128)(2,1)} %refs_7_.3) | copy-start | bytes 3538948
  101.3 11.7 %collective-permute-start.36 = (bf16[2,128,768]{2,1,0:T(8,128)(2,1)S(1)}, bf16[2,128,768]{2,1,0:T(8,128)(2,1)S(1)}, u32[]{:S(2)}, u32[]{:S(2)}) collective-permute-start(bf16[2,128,768]{2,1,0:T(8,128)(2,1)S(1)} %get-tuple-element.220), channel_id=1, source_target_pairs={{0,2},{2,0},{4,6},{6,4},{1,3},{3,1},{5,7},{7,5},{8,10},{10,8},{12,... | collective-permute-start | bytes 1179656 | tf_op jit(solution)/shard_map/up_sum/ppermute | solution.py:980
  101.8 6.4 %collective-permute-start.26 = (bf16[96,768]{1,0:T(8,128)(2,1)S(1)}, bf16[96,768]{1,0:T(8,128)(2,1)S(1)}, u32[]{:S(2)}, u32[]{:S(2)}) collective-permute-start(bf16[96,768]{1,0:T(8,128)(2,1)S(1)} %get-tuple-element.203), channel_id=1, source_target_pairs={{0,8},{8,0},{16,24},{24,16},{1,9},{9,1},{17,25},{25,17},{2,10},{10... | collective-permute-start | bytes 442376 | tf_op jit(solution)/shard_map/plane_w/ppermute | solution.py:980
  103.5 6.9 %collective-permute-start.27 = (bf16[96,768]{1,0:T(8,128)(2,1)S(1)}, bf16[96,768]{1,0:T(8,128)(2,1)S(1)}, u32[]{:S(2)}, u32[]{:S(2)}) collective-permute-start(bf16[96,768]{1,0:T(8,128)(2,1)S(1)} %get-tuple-element.204), channel_id=1, source_target_pairs={{0,16},{8,24},{16,0},{24,8},{1,17},{9,25},{17,1},{25,9},{2,18},{10... | collective-permute-start | bytes 442376 | tf_op jit(solution)/shard_map/plane_w/ppermute | solution.py:980
  104.0 8.2 %collective-permute-start.28 = (bf16[96,768]{1,0:T(8,128)(2,1)S(1)}, bf16[96,768]{1,0:T(8,128)(2,1)S(1)}, u32[]{:S(2)}, u32[]{:S(2)}) collective-permute-start(bf16[96,768]{1,0:T(8,128)(2,1)S(1)} %get-tuple-element.205), channel_id=1, source_target_pairs={{0,24},{8,16},{16,8},{24,0},{1,25},{9,17},{17,9},{25,1},{2,26},{10... | collective-permute-start | bytes 442376 | tf_op jit(solution)/shard_map/plane_w/ppermute | solution.py:980
  113.6 14.0 %collective-permute-start.37 = (bf16[1,128,768]{2,1,0:T(8,128)(2,1)S(1)}, bf16[1,128,768]{2,1,0:T(8,128)(2,1)S(1)}, u32[]{:S(2)}, u32[]{:S(2)}) collective-permute-start(bf16[1,128,768]{2,1,0:T(8,128)(2,1)S(1)} %get-tuple-element.237), channel_id=1, source_target_pairs={{0,4},{2,6},{4,0},{6,2},{1,5},{3,7},{5,1},{7,3},{8,12},{10,14},{12... | collective-permute-start | bytes 589832 | tf_op jit(solution)/shard_map/up_sum/ppermute | solution.py:980
  115.7 7.9 %collective-permute-start.33 = (bf16[24,768]{1,0:T(8,128)(2,1)S(1)}, bf16[24,768]{1,0:T(8,128)(2,1)S(1)}, u32[]{:S(2)}, u32[]{:S(2)}) collective-permute-start(bf16[24,768]{1,0:T(8,128)(2,1)S(1)} %get-tuple-element.226), channel_id=1, source_target_pairs={{0,2},{2,0},{4,6},{6,4},{1,3},{3,1},{5,7},{7,5},{8,10},{10,8},{12,... | collective-permute-start | bytes 110600 | tf_op jit(solution)/shard_map/chip_w/ppermute | solution.py:980
  116.2 11.4 %collective-permute-start.34 = (bf16[24,768]{1,0:T(8,128)(2,1)S(1)}, bf16[24,768]{1,0:T(8,128)(2,1)S(1)}, u32[]{:S(2)}, u32[]{:S(2)}) collective-permute-start(bf16[24,768]{1,0:T(8,128)(2,1)S(1)} %get-tuple-element.227), channel_id=1, source_target_pairs={{0,4},{2,6},{4,0},{6,2},{1,5},{3,7},{5,1},{7,3},{8,12},{10,14},{12... | collective-permute-start | bytes 110600 | tf_op jit(solution)/shard_map/chip_w/ppermute | solution.py:980
  118.3 9.3 %collective-permute-start.35 = (bf16[24,768]{1,0:T(8,128)(2,1)S(1)}, bf16[24,768]{1,0:T(8,128)(2,1)S(1)}, u32[]{:S(2)}, u32[]{:S(2)}) collective-permute-start(bf16[24,768]{1,0:T(8,128)(2,1)S(1)} %get-tuple-element.228), channel_id=1, source_target_pairs={{0,6},{2,4},{4,2},{6,0},{1,7},{3,5},{5,3},{7,1},{8,14},{10,12},{12... | collective-permute-start | bytes 110600 | tf_op jit(solution)/shard_map/chip_w/ppermute | solution.py:980
  128.8 4.8 %collective-permute-start.38 = (bf16[24,768]{1,0:T(8,128)(2,1)S(1)}, bf16[24,768]{1,0:T(8,128)(2,1)S(1)}, u32[]{:S(2)}, u32[]{:S(2)}) collective-permute-start(bf16[24,768]{1,0:T(8,128)(2,1)S(1)} %get-tuple-element.245), channel_id=1, source_target_pairs={{0,8},{8,0},{16,24},{24,16},{1,9},{9,1},{17,25},{25,17},{2,10},{10... | collective-permute-start | bytes 110600 | tf_op jit(solution)/shard_map/plane_rows/ppermute | solution.py:980
  130.2 4.2 %collective-permute-start.39 = (bf16[24,768]{1,0:T(8,128)(2,1)S(1)}, bf16[24,768]{1,0:T(8,128)(2,1)S(1)}, u32[]{:S(2)}, u32[]{:S(2)}) collective-permute-start(bf16[24,768]{1,0:T(8,128)(2,1)S(1)} %get-tuple-element.246), channel_id=1, source_target_pairs={{0,16},{8,24},{16,0},{24,8},{1,17},{9,25},{17,1},{25,9},{2,18},{10... | collective-permute-start | bytes 110600 | tf_op jit(solution)/shard_map/plane_rows/ppermute | solution.py:980
  131.0 4.9 %collective-permute-start.40 = (bf16[24,768]{1,0:T(8,128)(2,1)S(1)}, bf16[24,768]{1,0:T(8,128)(2,1)S(1)}, u32[]{:S(2)}, u32[]{:S(2)}) collective-permute-start(bf16[24,768]{1,0:T(8,128)(2,1)S(1)} %get-tuple-element.247), channel_id=1, source_target_pairs={{0,24},{8,16},{16,8},{24,0},{1,25},{9,17},{17,9},{25,1},{2,26},{10... | collective-permute-start | bytes 110600 | tf_op jit(solution)/shard_map/plane_rows/ppermute | solution.py:980
  (8 other events, 50.5 us)

commit v9 on v6

--- a/solution.py
+++ b/solution.py
@@ -821,6 +821,7 @@
     count, rows = grads.shape[:2]
     model = weight.shape[0]
     own = model // (parts * count * 2)
+    lanes = -(-(3 * live + 2) // 128) * 128
     n = len(units)
 
     def body(place_ref, *refs):
@@ -837,16 +838,17 @@
         weight_f = weight_ref[...].astype(F32)
         grad_gain = jnp.sum(weight_f * cross, axis=1, keepdims=True)
         grad_bias = jnp.sum(weight_f * total, axis=1, keepdims=True)
-        lane = lax.broadcasted_iota(jnp.int32, (1, 3 * width), 1)
+        lane = lax.broadcasted_iota(jnp.int32, (1, lanes - 3 * live), 1)
         made = columns[:, 0:1] * cross + columns[:, 1:2] * total
-        made = jnp.where(lane == live, grad_gain, jnp.where(lane == live + 1, grad_bias, made))
-        scr[...] = made.reshape(parts, count, 2, own, 3 * width)
+        spare = jnp.where(lane == 0, grad_gain, jnp.where(lane == 1, grad_bias, 0.0))
+        pieces = [made[:, at * width : at * width + live] for at in range(3)] + [spare]
+        scr[...] = jnp.concatenate(pieces, axis=1).reshape(parts, count, 2, own, lanes)
         for r in range(parts):
             keep_ref[r] = jnp.concatenate([scr[r, k, core] for k in range(count)], axis=0)
             send_ref[r] = jnp.concatenate([scr[r, k, 1 - core] for k in range(count)], axis=0).astype(BF16)
 
-    outs = (shape(F32, parts, count * own, 3 * width), shape(BF16, parts, count * own, 3 * width))
-    scratch = (shape(BF16, count, rows, model), shape(F32, parts, count, 2, own, 3 * width))
+    outs = (shape(F32, parts, count * own, lanes), shape(BF16, parts, count * own, lanes))
+    scratch = (shape(BF16, count, rows, model), shape(F32, parts, count, 2, own, lanes))
     operands = (*units, grads, gain, bias, weight)
     return kernel(body, outs, (place,), operands, scratch, micros=4.0, name="grad_qkv")
 
@@ -931,7 +933,7 @@
     return kernel(body, outs, (place,), tuple(pieces), (shape(F32, chips, own, lanes),), micros=0.7, name="share")
 
 
-def finish_qkv_call(place, pieces, model, live, width):
+def finish_qkv_call(place, pieces, model, live):
     count, own = len(pieces), pieces[0].shape[0]
 
     def body(place_ref, *refs):
@@ -940,9 +942,9 @@
             in_ref[place_ref[0] ^ k] = refs[k][...].astype(F32)
         for at, ref in enumerate((q_ref, k_ref, v_ref)):
             ref[...] = jnp.concatenate(
-                [in_ref[k, :, at * width : at * width + live] for k in range(count)], axis=1
+                [in_ref[k, :, at * live : (at + 1) * live] for k in range(count)], axis=1
             )
-        total = jnp.sum(in_ref[:, :, live : live + 2], axis=0).T
+        total = jnp.sum(in_ref[:, :, 3 * live : 3 * live + 2], axis=0).T
         gain_ref[...] = total[0:1].reshape(own)
         bias_ref[...] = total[1:2].reshape(own)
 
@@ -1113,7 +1115,7 @@
     gwo, g2, b2, g3, b3, *up_rows = finish_up_call(place, up_keep, up_last, parts, own, part)
     with scope("plane_rows"):
         up_rows = trade(up_rows, "rows")
-    gwq, gwk, gwv, g1, b1 = finish_qkv_call(place, qkv_all, model, live, width)
+    gwq, gwk, gwv, g1, b1 = finish_qkv_call(place, qkv_all, model, live)
     gwu = place_up_call(place, up_rows)
     return (
         output[None], grad_inputs[None], g1, b1, gwq, gwk, gwv, g2, b2, gwo, g3, b3, gwu, gwd,

time: 134 us -> 133 us (level)
  waiting for transfers between devices: 43.1 us -> 41.6 us
    ppermute x34, waiting for transfers between devices: 39.5 us -> 38.1 us  [swap(): lax.ppermute(value, axis, [(k, k ^ bit) for k in range(lax.axis_size(axis...]
  transfers between devices with their start and end apart: 41 -> 41, of which waited for: 19 -> 19; matrix products, arithmetic and copies ran while one was open for 2% -> 2% of each run, Pallas kernels for 23% -> 24%
where the time goes in v9:
time: 133 us
  starting transfers between devices  48.3 us (36%)
  waiting for transfers between devices  41.6 us (31%)
  Pallas kernels  38.1 us (29%)
  local copies, waits for them, and re-layouts  3.65 us (3%)
    ppermute x34, starting transfers between devices, swap(): lax.ppermute(value, axis, [(k, k ^ bit) for k in range(lax.axis_size(axis...  46.9 us
    pallas_call x24, Pallas kernels, kernel(): pl.pallas_call(body, out_shape=outs if single else listed, in_specs=[smem...  38.1 us
    ppermute x34, waiting for transfers between devices, swap(): lax.ppermute(value, axis, [(k, k ^ bit) for k in range(lax.axis_size(axis...  38.1 us
    ppermute x7, waiting for transfers between devices, swap_core(): return lax.ppermute(value, 'core', [(0, 1), (1, 0)])  3.5 us
    dynamic_slice x2, local copies, waits for them, and re-layouts, columns(): mine = lax.dynamic_slice_in_dim(weight, z_index * live, live, 1)  2.82 us
  transfers between devices with their start and end apart: 41, of which 19 were waited for; matrix products, arithmetic and copies ran while one was open for 2% of the time, Pallas kernels for 24%

profile of v9, /device:TPU:0, one launch (start us, length us, event | category | flops | bytes accessed | tf_op | source)
XLA Modules:
  0.0 133.0 jit_solution(15686875525873493687)
XLA Ops:
  0.7 4.1 %collective-permute-start.1 = (bf16[128,768]{1,0:T(8,128)(2,1)}, bf16[128,768]{1,0:T(8,128)(2,1)S(1)}, u32[]{:S(2)}, u32[]{:S(2)}) collective-permute-start(bf16[128,768]{1,0:T(8,128)(2,1)} %bitcast.7), channel_id=1, source_target_pairs={{0,4},{2,6},{4,0},{6,2},{1,5},{3,7},{5,1},{7,3},{8,12},{10,14},{12... | collective-permute-start | bytes 589832 | tf_op jit(solution)/shard_map/gather_in/ppermute | solution.py:982
  4.8 1.6 %collective-permute-start = (bf16[128,768]{1,0:T(8,128)(2,1)}, bf16[128,768]{1,0:T(8,128)(2,1)S(1)}, u32[]{:S(2)}, u32[]{:S(2)}) collective-permute-start(bf16[128,768]{1,0:T(8,128)(2,1)} %bitcast.8), channel_id=1, source_target_pairs={{0,2},{2,0},{4,6},{6,4},{1,3},{3,1},{5,7},{7,5},{8,10},{10,8},{12,... | collective-permute-start | bytes 589832 | tf_op jit(solution)/shard_map/gather_in/ppermute | solution.py:982
  7.6 1.6 %constant_dynamic-slice_fusion = (bf16[768,192]{1,0:T(8,128)(2,1)S(1)}, bf16[768,192]{1,0:T(8,128)(2,1)S(1)}) fusion(bf16[768,768]{1,0:T(8,128)(2,1)} %refs_9_.3, s32[]{:T(128)S(6)} %select_n.2, bf16[768,768]{1,0:T(8,128)(2,1)} %refs_8_.3), kind=kLoop, calls=%fused_computation.10 | loop fusion | bytes 1179652 | tf_op jit(solution)/shard_map/dynamic_slice | solution.py:1029
  9.2 5.0 %collective-permute-done.1.refs_1_ = bf16[128,768]{1,0:T(8,128)(2,1)S(1)} collective-permute-done((bf16[128,768]{1,0:T(8,128)(2,1)}, bf16[128,768]{1,0:T(8,128)(2,1)S(1)}, u32[]{:S(2)}, u32[]{:S(2)}) %collective-permute-start.1) | collective-permute-done | bytes 196640 | tf_op jit(solution)/shard_map/gather_in/ppermute | solution.py:982
  18.4 2.5 %collective-permute-start.11 = (bf16[128,768]{1,0:T(8,128)(2,1)S(1)}, bf16[128,768]{1,0:T(8,128)(2,1)S(1)}, u32[]{:S(2)}, u32[]{:S(2)}) collective-permute-start(bf16[128,768]{1,0:T(8,128)(2,1)S(1)} %mask_grad.1.go_ref.refs_4_), channel_id=1, source_target_pairs={{0,24},{8,16},{16,8},{24,0},{1,25},{9,17},{17,9},{25,1},{2,26},{10... | collective-permute-start | bytes 589832 | tf_op jit(solution)/shard_map/plane_out/ppermute | solution.py:982
  22.6 1.3 collective-permute-done.5.refs_8_
  23.9 4.3 %attend.1 = (f32[4,128,256]{2,1,0:T(8,128)S(1)}, bf16[4,2,384,512]{3,2,1,0:T(8,128)(2,1)S(1)}, bf16[4,128,256]{2,1,0:T(8,128)(2,1)S(1)}, bf16[4,128,512]{2,1,0:T...) custom-call(s32[3]{0:T(128)S(1)} %pad_add_fusion.place_ref, ...), custom_call_target="tpu_custom_call" | custom-call | flops 6000000 | bytes 6000 | tf_op jit(solution)/shard_map/attend/pallas_call | solution.py:350
  28.2 1.4 %collective-permute-start.6 = (bf16[192,128]{1,0:T(8,128)(2,1)S(1)}, bf16[192,128]{1,0:T(8,128)(2,1)S(1)}, u32[]{:S(2)}, u32[]{:S(2)}) collective-permute-start(bf16[192,128]{1,0:T(8,128)(2,1)S(1)} %get-tuple-element.139), channel_id=1, source_target_pairs={{0,2},{2,0},{4,6},{6,4},{1,3},{3,1},{5,7},{7,5},{8,10},{10,8},{12,... | collective-permute-start | bytes 147464 | tf_op jit(solution)/shard_map/chip_attn/ppermute | solution.py:982
  29.5 3.3 %collective-permute-start.7 = (bf16[192,128]{1,0:T(8,128)(2,1)S(1)}, bf16[192,128]{1,0:T(8,128)(2,1)S(1)}, u32[]{:S(2)}, u32[]{:S(2)}) collective-permute-start(bf16[192,128]{1,0:T(8,128)(2,1)S(1)} %get-tuple-element.140), channel_id=1, source_target_pairs={{0,4},{2,6},{4,0},{6,2},{1,5},{3,7},{5,1},{7,3},{8,12},{10,14},{12... | collective-permute-start | bytes 147464 | tf_op jit(solution)/shard_map/chip_attn/ppermute | solution.py:982
  33.0 2.9 %collective-permute-done.7.refs_2_ = bf16[192,128]{1,0:T(8,128)(2,1)S(1)} collective-permute-done((bf16[192,128]{1,0:T(8,128)(2,1)S(1)}, bf16[192,128]{1,0:T(8,128)(2,1)S(1)}, u32[]{:S(2)}, u32[]{:S(2)}) %collective-permute-start.7) | collective-permute-done | bytes 49184 | tf_op jit(solution)/shard_map/chip_attn/ppermute | solution.py:982
  35.9 2.8 %collective-permute-done.8.refs_3_ = bf16[192,128]{1,0:T(8,128)(2,1)S(1)} collective-permute-done((bf16[192,128]{1,0:T(8,128)(2,1)S(1)}, bf16[192,128]{1,0:T(8,128)(2,1)S(1)}, u32[]{:S(2)}, u32[]{:S(2)}) %collective-permute-start.8) | collective-permute-done | bytes 49184 | tf_op jit(solution)/shard_map/chip_attn/ppermute | solution.py:982
  38.7 1.4 %norms.1 = (f32[128,768]{1,0:T(8,128)S(1)}, bf16[128,768]{1,0:T(8,128)(2,1)S(1)}, bf16[128,768]{1,0:T(8,128)(2,1)S(1)}) custom-call(s32[3]{0:T(128)S(1)} %pad_add_fusion.place_ref, bf16[192,128]{1,0:T(8,128)(2,1)S(1)} %get-tuple-element.143.refs_0_, bf16[192,128]{1,0:T(8,128)(2,1)S(1)} %collective-permute-done.6.refs_1_, ...), custom_call_target="tpu_custom_call" | custom-call | flops 1500000 | bytes 1500 | tf_op jit(solution)/shard_map/norms/pallas_call | solution.py:350
  40.1 1.9 %up_gelu.1 = (bf16[4,128,768]{2,1,0:T(8,128)(2,1)S(1)}, bf16[4,128,768]{2,1,0:T(8,128)(2,1)S(1)}, bf16[128,768]{1,0:T(8,128)(2,1)S(1)}, bf16[128,768]{1,0:T(8,12...) custom-call(s32[3]{0:T(128)S(1)} %pad_add_fusion.place_ref, ...), custom_call_target="tpu_custom_call" | custom-call | flops 2000000 | bytes 2000 | tf_op jit(solution)/shard_map/up_gelu/pallas_call | solution.py:350
  42.7 1.5 %collective-permute-start.17 = (bf16[128,768]{1,0:T(8,128)(2,1)S(1)}, bf16[128,768]{1,0:T(8,128)(2,1)S(1)}, u32[]{:S(2)}, u32[]{:S(2)}) collective-permute-start(bf16[128,768]{1,0:T(8,128)(2,1)S(1)} %get-tuple-element.167), channel_id=1, source_target_pairs={{0,16},{8,24},{16,0},{24,8},{1,17},{9,25},{17,1},{25,9},{2,18},{10... | collective-permute-start | bytes 589832 | tf_op jit(solution)/shard_map/plane_act/ppermute | solution.py:982
  44.2 1.4 %collective-permute-start.18 = (bf16[128,768]{1,0:T(8,128)(2,1)S(1)}, bf16[128,768]{1,0:T(8,128)(2,1)S(1)}, u32[]{:S(2)}, u32[]{:S(2)}) collective-permute-start(bf16[128,768]{1,0:T(8,128)(2,1)S(1)} %get-tuple-element.168), channel_id=1, source_target_pairs={{0,24},{8,16},{16,8},{24,0},{1,25},{9,17},{17,9},{25,1},{2,26},{10... | collective-permute-start | bytes 589832 | tf_op jit(solution)/shard_map/plane_act/ppermute | solution.py:982
  45.6 6.0 %token_backward.1 = (bf16[128,768]{1,0:T(8,128)(2,1)}, f32[128,768]{1,0:T(8,128)S(1)}, bf16[128,2560]{1,0:T(8,128)(2,1)S(1)}, bf16[128,2560]{1,0:T(8,128)(2,1)S(...) custom-call(s32[3]{0:T(128)S(1)} %pad_add_fusion.place_ref, ...), custom_call_target="tpu_custom_call" | custom-call | flops 9000000 | bytes 9000 | tf_op jit(solution)/shard_map/token_backward/pallas_call | solution.py:350
  52.6 1.8 %collective-permute-start.19 = (bf16[128,2560]{1,0:T(8,128)(2,1)S(1)}, bf16[128,2560]{1,0:T(8,128)(2,1)S(1)}, u32[]{:S(2)}, u32[]{:S(2)}) collective-permute-start(bf16[128,2560]{1,0:T(8,128)(2,1)S(1)} %get-tuple-element.178), channel_id=1, source_target_pairs={{0,24},{8,16},{16,8},{24,0},{1,25},{9,17},{17,9},{25,1},{2,26},{10... | collective-permute-start | bytes 1966088 | tf_op jit(solution)/shard_map/plane_back/ppermute | solution.py:982
  54.6 1.4 %collective-permute-start.13 = (bf16[192,128]{1,0:T(8,128)(2,1)S(1)}, bf16[192,128]{1,0:T(8,128)(2,1)S(1)}, u32[]{:S(2)}, u32[]{:S(2)}) collective-permute-start(bf16[192,128]{1,0:T(8,128)(2,1)S(1)} %get-tuple-element.160), channel_id=1, source_target_pairs={{0,4},{2,6},{4,0},{6,2},{1,5},{3,7},{5,1},{7,3},{8,12},{10,14},{12... | collective-permute-start | bytes 147464 | tf_op jit(solution)/shard_map/chip_grad/ppermute | solution.py:982
  56.0 2.8 %collective-permute-start.14 = (bf16[192,128]{1,0:T(8,128)(2,1)S(1)}, bf16[192,128]{1,0:T(8,128)(2,1)S(1)}, u32[]{:S(2)}, u32[]{:S(2)}) collective-permute-start(bf16[192,128]{1,0:T(8,128)(2,1)S(1)} %get-tuple-element.161), channel_id=1, source_target_pairs={{0,6},{2,4},{4,2},{6,0},{1,7},{3,5},{5,3},{7,1},{8,14},{10,12},{12... | collective-permute-start | bytes 147464 | tf_op jit(solution)/shard_map/chip_grad/ppermute | solution.py:982
  59.6 2.3 %collective-permute-done.14.refs_3_ = bf16[192,128]{1,0:T(8,128)(2,1)S(1)} collective-permute-done((bf16[192,128]{1,0:T(8,128)(2,1)S(1)}, bf16[192,128]{1,0:T(8,128)(2,1)S(1)}, u32[]{:S(2)}, u32[]{:S(2)}) %collective-permute-start.14) | collective-permute-done | bytes 49184 | tf_op jit(solution)/shard_map/chip_grad/ppermute | solution.py:982
  61.9 3.8 %attend_back.1 = (bf16[4,128,256]{2,1,0:T(8,128)(2,1)S(1)}, f32[4,128,512]{2,1,0:T(8,128)S(1)}, bf16[4,128,512]{2,1,0:T(8,128)(2,1)S(1)}) custom-call(s32[3]{0:T(128)S(1)} %pad_add_fusion.place_ref, bf16[4,128,256]{2,1,0:T(8,128)(2,1)S(1)} %get-tuple-element.153.q_ref, bf16[4,128,512]{2,1,0:T(8,128)(2,1)S(1)} %get-tuple-element.154.own_ref, ...), custom_call_target="tpu_custom_call" | custom-call | flops 6000000 | bytes 6000 | tf_op jit(solution)/shard_map/attend_back/pallas_call | solution.py:350
  65.8 1.5 %grad_down.1 = (f32[4,96,768]{2,1,0:T(8,128)S(1)}, bf16[4,96,768]{2,1,0:T(8,128)(2,1)S(1)}) custom-call(s32[3]{0:T(128)S(1)} %pad_add_fusion.place_ref, bf16[128,768]{1,0:T(8,128)(2,1)S(1)} %get-tuple-element.169.refs_0_, bf16[128,768]{1,0:T(8,128)(2,1)S(1)} %collective-permute-done.16.refs_1_, bf16[128,768]{1,0:T(8,128)(2,1)S(1)} %collective-permute-done.17.refs_2_, ...), custom_call_target="tpu_custom_call" | custom-call | flops 3000000 | bytes 3000 | tf_op jit(solution)/shard_map/grad_down/pallas_call | solution.py:350
  67.9 1.4 %collective-permute-start.28 = (bf16[128,2560]{1,0:T(8,128)(2,1)S(1)}, bf16[128,2560]{1,0:T(8,128)(2,1)S(1)}, u32[]{:S(2)}, u32[]{:S(2)}) collective-permute-start(bf16[128,2560]{1,0:T(8,128)(2,1)S(1)} %get-tuple-element.204), channel_id=1, source_target_pairs={{0,8},{8,0},{16,24},{24,16},{1,9},{9,1},{17,25},{25,17},{2,10},{10... | collective-permute-start | bytes 1966088 | tf_op jit(solution)/shard_map/plane_back/ppermute | solution.py:982
  71.4 1.6 %collective-permute-start.30 = (bf16[2,96,768]{2,1,0:T(8,128)(2,1)S(1)}, bf16[2,96,768]{2,1,0:T(8,128)(2,1)S(1)}, u32[]{:S(2)}, u32[]{:S(2)}) collective-permute-start(bf16[2,96,768]{2,1,0:T(8,128)(2,1)S(1)} %get-tuple-element.207), channel_id=1, source_target_pairs={{0,2},{2,0},{4,6},{6,4},{1,3},{3,1},{5,7},{7,5},{8,10},{10,8},{12,... | collective-permute-start | bytes 884744 | tf_op jit(solution)/shard_map/down_sum/ppermute | solution.py:982
  73.0 1.4 %collective-permute-start.21 = (bf16[576,128]{1,0:T(8,128)(2,1)S(1)}, bf16[576,128]{1,0:T(8,128)(2,1)S(1)}, u32[]{:S(2)}, u32[]{:S(2)}) collective-permute-start(bf16[576,128]{1,0:T(8,128)(2,1)S(1)} %get-tuple-element.182), channel_id=1, source_target_pairs={{0,4},{2,6},{4,0},{6,2},{1,5},{3,7},{5,1},{7,3},{8,12},{10,14},{12... | collective-permute-start | bytes 442376 | tf_op jit(solution)/shard_map/chip_qkv/ppermute | solution.py:982
  74.4 1.4 %collective-permute-start.22 = (bf16[576,128]{1,0:T(8,128)(2,1)S(1)}, bf16[576,128]{1,0:T(8,128)(2,1)S(1)}, u32[]{:S(2)}, u32[]{:S(2)}) collective-permute-start(bf16[576,128]{1,0:T(8,128)(2,1)S(1)} %get-tuple-element.183), channel_id=1, source_target_pairs={{0,6},{2,4},{4,2},{6,0},{1,7},{3,5},{5,3},{7,1},{8,14},{10,12},{12... | collective-permute-start | bytes 442376 | tf_op jit(solution)/shard_map/chip_qkv/ppermute | solution.py:982
  75.8 3.3 %grad_qkv.1 = (f32[4,96,640]{2,1,0:T(8,128)S(1)}, bf16[4,96,640]{2,1,0:T(8,128)(2,1)S(1)}) custom-call(s32[3]{0:T(128)S(1)} %pad_add_fusion.place_ref, bf16[1,128,768]{2,1,0:T(8,128)(2,1)S(1)} %get-tuple-element.185.refs_0_, bf16[2,128,768]{2,1,0:T(8,128)(2,1)S(1)} %get-tuple-element.186.refs_1_, bf16[1,128,768]{2,1,0:T(8,128)(2,1)S(1)} %get-tuple-element.187.refs_2_, ...), custom_call_target="tpu_custom_call" | custom-call | flops 4000000 | bytes 4000 | tf_op jit(solution)/shard_map/grad_qkv/pallas_call | solution.py:350
  79.1 4.2 %collective-permute-done.30.in_ref = bf16[2,96,768]{2,1,0:T(8,128)(2,1)S(1)} collective-permute-done((bf16[2,96,768]{2,1,0:T(8,128)(2,1)S(1)}, bf16[2,96,768]{2,1,0:T(8,128)(2,1)S(1)}, u32[]{:S(2)}, u32[]{:S(2)}) %collective-permute-start.30) | collective-permute-done | bytes 294944 | tf_op jit(solution)/shard_map/down_sum/ppermute | solution.py:982
  83.9 3.1 %collective-permute-start.31 = (bf16[1,96,768]{2,1,0:T(8,128)(2,1)S(1)}, bf16[1,96,768]{2,1,0:T(8,128)(2,1)S(1)}, u32[]{:S(2)}, u32[]{:S(2)}) collective-permute-start(bf16[1,96,768]{2,1,0:T(8,128)(2,1)S(1)} %get-tuple-element.216), channel_id=1, source_target_pairs={{0,4},{2,6},{4,0},{6,2},{1,5},{3,7},{5,1},{7,3},{8,12},{10,14},{12... | collective-permute-start | bytes 442376 | tf_op jit(solution)/shard_map/down_sum/ppermute | solution.py:982
  87.0 2.0 %collective-permute-done.22.refs_3_ = bf16[576,128]{1,0:T(8,128)(2,1)S(1)} collective-permute-done((bf16[576,128]{1,0:T(8,128)(2,1)S(1)}, bf16[576,128]{1,0:T(8,128)(2,1)S(1)}, u32[]{:S(2)}, u32[]{:S(2)}) %collective-permute-start.22) | collective-permute-done | bytes 147488 | tf_op jit(solution)/shard_map/chip_qkv/ppermute | solution.py:982
  89.0 1.7 %grad_up_out.1 = (f32[4,128,768]{2,1,0:T(8,128)S(1)}, bf16[4,128,768]{2,1,0:T(8,128)(2,1)S(1)}) custom-call(s32[3]{0:T(128)S(1)} %pad_add_fusion.place_ref, bf16[128,2560]{1,0:T(8,128)(2,1)S(1)} %get-tuple-element.210.refs_0_, bf16[128,2560]{1,0:T(8,128)(2,1)S(1)} %collective-permute-done.28.refs_1_, bf16[128,2560]{1,0:T(8,128)(2,1)S(1)} %collective-permute-done.29.refs_2_, ...), custom_call_target="tpu_custom_call" | custom-call | flops 4000000 | bytes 4000 | tf_op jit(solution)/shard_map/grad_up_out/pallas_call | solution.py:350
  90.7 2.3 %collective-permute-done.20.refs_1_ = bf16[576,128]{1,0:T(8,128)(2,1)S(1)} collective-permute-done((bf16[576,128]{1,0:T(8,128)(2,1)S(1)}, bf16[576,128]{1,0:T(8,128)(2,1)S(1)}, u32[]{:S(2)}, u32[]{:S(2)}) %collective-permute-start.20) | collective-permute-done | bytes 147488 | tf_op jit(solution)/shard_map/chip_qkv/ppermute | solution.py:982
  93.0 2.2 %collective-permute-done.31.in_ref = bf16[1,96,768]{2,1,0:T(8,128)(2,1)S(1)} collective-permute-done((bf16[1,96,768]{2,1,0:T(8,128)(2,1)S(1)}, bf16[1,96,768]{2,1,0:T(8,128)(2,1)S(1)}, u32[]{:S(2)}, u32[]{:S(2)}) %collective-permute-start.31) | collective-permute-done | bytes 147488 | tf_op jit(solution)/shard_map/down_sum/ppermute | solution.py:982
  95.7 1.8 %collective-permute-done.32.in_ref = bf16[4,128,768]{2,1,0:T(8,128)(2,1)S(1)} collective-permute-done((bf16[4,128,768]{2,1,0:T(8,128)(2,1)S(1)}, bf16[4,128,768]{2,1,0:T(8,128)(2,1)S(1)}, u32[]{:S(2)}, u32[]{:S(2)}) %collective-permute-start.32) | collective-permute-done | bytes 786464 | tf_op jit(solution)/shard_map/core_up/ppermute | solution.py:978
  98.9 1.7 %collective-permute-start.25 = (bf16[96,640]{1,0:T(8,128)(2,1)S(1)}, bf16[96,640]{1,0:T(8,128)(2,1)S(1)}, u32[]{:S(2)}, u32[]{:S(2)}) collective-permute-start(bf16[96,640]{1,0:T(8,128)(2,1)S(1)} %get-tuple-element.197), channel_id=1, source_target_pairs={{0,8},{8,0},{16,24},{24,16},{1,9},{9,1},{17,25},{25,17},{2,10},{10... | collective-permute-start | bytes 368648 | tf_op jit(solution)/shard_map/plane_w/ppermute | solution.py:982
  101.0 1.5 %collective-permute-start.27 = (bf16[96,640]{1,0:T(8,128)(2,1)S(1)}, bf16[96,640]{1,0:T(8,128)(2,1)S(1)}, u32[]{:S(2)}, u32[]{:S(2)}) collective-permute-start(bf16[96,640]{1,0:T(8,128)(2,1)S(1)} %get-tuple-element.199), channel_id=1, source_target_pairs={{0,24},{8,16},{16,8},{24,0},{1,25},{9,17},{17,9},{25,1},{2,26},{10... | collective-permute-start | bytes 368648 | tf_op jit(solution)/shard_map/plane_w/ppermute | solution.py:982
  102.5 2.0 %collective-permute-done.25.refs_1_ = bf16[96,640]{1,0:T(8,128)(2,1)S(1)} collective-permute-done((bf16[96,640]{1,0:T(8,128)(2,1)S(1)}, bf16[96,640]{1,0:T(8,128)(2,1)S(1)}, u32[]{:S(2)}, u32[]{:S(2)}) %collective-permute-start.25) | collective-permute-done | bytes 122912 | tf_op jit(solution)/shard_map/plane_w/ppermute | solution.py:982
  104.5 3.9 %collective-permute-done.26.refs_2_ = bf16[96,640]{1,0:T(8,128)(2,1)S(1)} collective-permute-done((bf16[96,640]{1,0:T(8,128)(2,1)S(1)}, bf16[96,640]{1,0:T(8,128)(2,1)S(1)}, u32[]{:S(2)}, u32[]{:S(2)}) %collective-permute-start.26) | collective-permute-done | bytes 122912 | tf_op jit(solution)/shard_map/plane_w/ppermute | solution.py:982
  110.1 1.4 %collective-permute-start.37 = (bf16[1,128,768]{2,1,0:T(8,128)(2,1)S(1)}, bf16[1,128,768]{2,1,0:T(8,128)(2,1)S(1)}, u32[]{:S(2)}, u32[]{:S(2)}) collective-permute-start(bf16[1,128,768]{2,1,0:T(8,128)(2,1)S(1)} %get-tuple-element.235), channel_id=1, source_target_pairs={{0,4},{2,6},{4,0},{6,2},{1,5},{3,7},{5,1},{7,3},{8,12},{10,14},{12... | collective-permute-start | bytes 589832 | tf_op jit(solution)/shard_map/up_sum/ppermute | solution.py:982
  112.5 1.9 %collective-permute-start.34 = (bf16[24,640]{1,0:T(8,128)(2,1)S(1)}, bf16[24,640]{1,0:T(8,128)(2,1)S(1)}, u32[]{:S(2)}, u32[]{:S(2)}) collective-permute-start(bf16[24,640]{1,0:T(8,128)(2,1)S(1)} %get-tuple-element.225), channel_id=1, source_target_pairs={{0,4},{2,6},{4,0},{6,2},{1,5},{3,7},{5,1},{7,3},{8,12},{10,14},{12... | collective-permute-start | bytes 92168 | tf_op jit(solution)/shard_map/chip_w/ppermute | solution.py:982
  114.4 1.4 %collective-permute-start.35 = (bf16[24,640]{1,0:T(8,128)(2,1)S(1)}, bf16[24,640]{1,0:T(8,128)(2,1)S(1)}, u32[]{:S(2)}, u32[]{:S(2)}) collective-permute-start(bf16[24,640]{1,0:T(8,128)(2,1)S(1)} %get-tuple-element.226), channel_id=1, source_target_pairs={{0,6},{2,4},{4,2},{6,0},{1,7},{3,5},{5,3},{7,1},{8,14},{10,12},{12... | collective-permute-start | bytes 92168 | tf_op jit(solution)/shard_map/chip_w/ppermute | solution.py:982
  115.8 2.7 %grad_inputs.1 = bf16[128,768]{1,0:T(8,128)(2,1)} custom-call(s32[3]{0:T(128)S(1)} %pad_add_fusion.place_ref, bf16[576,128]{1,0:T(8,128)(2,1)S(1)} %get-tuple-element.180.refs_0_, bf16[576,128]{1,0:T(8,128)(2,1)S(1)} %collective-permute-done.20.refs_1_, bf16[576,128]{1,0:T(8,128)(2,1)S(1)} %collective-permute-done.21.refs_2_, ...), custom_call_target="tpu_custom_call" | custom-call | flops 3000000 | bytes 3000 | tf_op jit(solution)/shard_map/grad_inputs/pallas_call | solution.py:350
  119.3 4.1 %collective-permute-done.34.refs_2_ = bf16[24,640]{1,0:T(8,128)(2,1)S(1)} collective-permute-done((bf16[24,640]{1,0:T(8,128)(2,1)S(1)}, bf16[24,640]{1,0:T(8,128)(2,1)S(1)}, u32[]{:S(2)}, u32[]{:S(2)}) %collective-permute-start.34) | collective-permute-done | bytes 30752 | tf_op jit(solution)/shard_map/chip_w/ppermute | solution.py:982
  124.7 1.6 %collective-permute-start.38 = (bf16[24,768]{1,0:T(8,128)(2,1)S(1)}, bf16[24,768]{1,0:T(8,128)(2,1)S(1)}, u32[]{:S(2)}, u32[]{:S(2)}) collective-permute-start(bf16[24,768]{1,0:T(8,128)(2,1)S(1)} %get-tuple-element.243), channel_id=1, source_target_pairs={{0,8},{8,0},{16,24},{24,16},{1,9},{9,1},{17,25},{25,17},{2,10},{10... | collective-permute-start | bytes 110600 | tf_op jit(solution)/shard_map/plane_rows/ppermute | solution.py:982
  126.8 1.3 %collective-permute-start.40 = (bf16[24,768]{1,0:T(8,128)(2,1)S(1)}, bf16[24,768]{1,0:T(8,128)(2,1)S(1)}, u32[]{:S(2)}, u32[]{:S(2)}) collective-permute-start(bf16[24,768]{1,0:T(8,128)(2,1)S(1)} %get-tuple-element.245), channel_id=1, source_target_pairs={{0,24},{8,16},{16,8},{24,0},{1,25},{9,17},{17,9},{25,1},{2,26},{10... | collective-permute-start | bytes 110600 | tf_op jit(solution)/shard_map/plane_rows/ppermute | solution.py:982
  128.2 1.3 %finish_qkv.1 = (f32[24,768]{1,0:T(8,128)}, f32[24,768]{1,0:T(8,128)}, f32[24,768]{1,0:T(8,128)}, f32[24]{0:T(128)}, f32[24]{0:T(128)}) custom-call(s32[3]{0:T(128)S(1)} %pad_add_fusion.place_ref, bf16[24,640]{1,0:T(8,128)(2,1)S(1)} %get-tuple-element.223.refs_0_, bf16[24,640]{1,0:T(8,128)(2,1)S(1)} %collective-permute-done.33.refs_1_, ...), custom_call_target="tpu_custom_call" | custom-call | flops 800000 | bytes 800 | tf_op jit(solution)/shard_map/finish_qkv/pallas_call | solution.py:350
  130.3 1.4 %collective-permute-done.40.refs_3_ = bf16[24,768]{1,0:T(8,128)(2,1)S(1)} collective-permute-done((bf16[24,768]{1,0:T(8,128)(2,1)S(1)}, bf16[24,768]{1,0:T(8,128)(2,1)S(1)}, u32[]{:S(2)}, u32[]{:S(2)}) %collective-permute-start.40) | collective-permute-done | bytes 36896 | tf_op jit(solution)/shard_map/plane_rows/ppermute | solution.py:982
  131.7 1.3 place_up.1
  (92 shorter events, 21.5 us)
Async XLA Ops:
  0.7 13.5 %collective-permute-start.1 = (bf16[128,768]{1,0:T(8,128)(2,1)}, bf16[128,768]{1,0:T(8,128)(2,1)S(1)}, u32[]{:S(2)}, u32[]{:S(2)}) collective-permute-start(bf16[128,768]{1,0:T(8,128)(2,1)} %bitcast.7), channel_id=1, source_target_pairs={{0,4},{2,6},{4,0},{6,2},{1,5},{3,7},{5,1},{7,3},{8,12},{10,14},{12... | collective-permute-start | bytes 589832 | tf_op jit(solution)/shard_map/gather_in/ppermute | solution.py:982
  4.8 11.7 %collective-permute-start = (bf16[128,768]{1,0:T(8,128)(2,1)}, bf16[128,768]{1,0:T(8,128)(2,1)S(1)}, u32[]{:S(2)}, u32[]{:S(2)}) collective-permute-start(bf16[128,768]{1,0:T(8,128)(2,1)} %bitcast.8), channel_id=1, source_target_pairs={{0,2},{2,0},{4,6},{6,4},{1,3},{3,1},{5,7},{7,5},{8,10},{10,8},{12,... | collective-permute-start | bytes 589832 | tf_op jit(solution)/shard_map/gather_in/ppermute | solution.py:982
  14.2 7.2 %collective-permute-start.2 = (bf16[128,768]{1,0:T(8,128)(2,1)S(1)}, bf16[128,768]{1,0:T(8,128)(2,1)S(1)}, u32[]{:S(2)}, u32[]{:S(2)}) collective-permute-start(bf16[128,768]{1,0:T(8,128)(2,1)S(1)} %collective-permute-done.1.refs_1_), channel_id=1, source_target_pairs={{0,2},{2,0},{4,6},{6,4},{1,3},{3,1},{5,7},{7,5},{8,10},{10,8},{12,... | collective-permute-start | bytes 589832 | tf_op jit(solution)/shard_map/gather_in/ppermute | solution.py:982
  16.4 6.1 %collective-permute-start.3 = (bf16[1,128,512]{2,1,0:T(8,128)(2,1)S(1)}, bf16[1,128,512]{2,1,0:T(8,128)(2,1)S(1)}, u32[]{:S(2)}, u32[]{:S(2)}) collective-permute-start(bf16[1,128,512]{2,1,0:T(8,128)(2,1)S(1)} %get-tuple-element.135.refs_3_), channel_id=1, source_target_pairs={{0,1},{1,0},{2,3},{3,2},{4,5},{5,4},{6,7},{7,6},{8,9},{9,8},{10,11... | collective-permute-start | bytes 393224 | tf_op jit(solution)/shard_map/core_kv/ppermute | solution.py:978
  16.5 22.2 %copy-start.1 = (bf16[768,768]{1,0:T(8,128)(2,1)S(1)}, bf16[768,768]{1,0:T(8,128)(2,1)}, u32[]{:S(2)}) copy-start(bf16[768,768]{1,0:T(8,128)(2,1)} %wo_ref.1) | copy-start | bytes 3538948
  16.5 22.2 %copy-start.10 = (f32[768]{0:T(1024)S(1)}, f32[768]{0:T(1024)}, u32[]{:S(2)}) copy-start(f32[768]{0:T(1024)} %g2.1) | copy-start | bytes 9220
  16.5 22.2 %copy-start.11 = (f32[768]{0:T(1024)S(1)}, f32[768]{0:T(1024)}, u32[]{:S(2)}) copy-start(f32[768]{0:T(1024)} %b2.1) | copy-start | bytes 9220
  16.5 22.2 %copy-start.12 = (f32[768]{0:T(1024)S(1)}, f32[768]{0:T(1024)}, u32[]{:S(2)}) copy-start(f32[768]{0:T(1024)} %g3.1) | copy-start | bytes 9220
  16.5 22.2 %copy-start.13 = (f32[768]{0:T(1024)S(1)}, f32[768]{0:T(1024)}, u32[]{:S(2)}) copy-start(f32[768]{0:T(1024)} %b3.1) | copy-start | bytes 9220
  16.5 23.6 %copy-start = (bf16[768,3072]{1,0:T(8,128)(2,1)S(1)}, bf16[768,3072]{1,0:T(8,128)(2,1)}, u32[]{:S(2)}) copy-start(bf16[768,3072]{1,0:T(8,128)(2,1)} %wu_ref.3) | copy-start | bytes 14155780
  17.3 5.3 %collective-permute-start.4 = (bf16[2,128,512]{2,1,0:T(8,128)(2,1)S(1)}, bf16[2,128,512]{2,1,0:T(8,128)(2,1)S(1)}, u32[]{:S(2)}, u32[]{:S(2)}) collective-permute-start(bf16[2,128,512]{2,1,0:T(8,128)(2,1)S(1)} %get-tuple-element.136.refs_4_), channel_id=1, source_target_pairs={{0,1},{1,0},{2,3},{3,2},{4,5},{5,4},{6,7},{7,6},{8,9},{9,8},{10,11... | collective-permute-start | bytes 786440 | tf_op jit(solution)/shard_map/core_kv/ppermute | solution.py:978
  18.4 14.4 %collective-permute-start.11 = (bf16[128,768]{1,0:T(8,128)(2,1)S(1)}, bf16[128,768]{1,0:T(8,128)(2,1)S(1)}, u32[]{:S(2)}, u32[]{:S(2)}) collective-permute-start(bf16[128,768]{1,0:T(8,128)(2,1)S(1)} %mask_grad.1.go_ref.refs_4_), channel_id=1, source_target_pairs={{0,24},{8,16},{16,8},{24,0},{1,25},{9,17},{17,9},{25,1},{2,26},{10... | collective-permute-start | bytes 589832 | tf_op jit(solution)/shard_map/plane_out/ppermute | solution.py:982
  20.9 12.1 %collective-permute-start.10 = (bf16[128,768]{1,0:T(8,128)(2,1)S(1)}, bf16[128,768]{1,0:T(8,128)(2,1)S(1)}, u32[]{:S(2)}, u32[]{:S(2)}) collective-permute-start(bf16[128,768]{1,0:T(8,128)(2,1)S(1)} %mask_grad.1.go_ref.refs_4_), channel_id=1, source_target_pairs={{0,16},{8,24},{16,0},{24,8},{1,17},{9,25},{17,1},{25,9},{2,18},{10... | collective-permute-start | bytes 589832 | tf_op jit(solution)/shard_map/plane_out/ppermute | solution.py:982
  21.4 11.5 %collective-permute-start.9 = (bf16[128,768]{1,0:T(8,128)(2,1)S(1)}, bf16[128,768]{1,0:T(8,128)(2,1)S(1)}, u32[]{:S(2)}, u32[]{:S(2)}) collective-permute-start(bf16[128,768]{1,0:T(8,128)(2,1)S(1)} %mask_grad.1.go_ref.refs_4_), channel_id=1, source_target_pairs={{0,8},{8,0},{16,24},{24,16},{1,9},{9,1},{17,25},{25,17},{2,10},{10... | collective-permute-start | bytes 589832 | tf_op jit(solution)/shard_map/plane_out/ppermute | solution.py:982
  22.5 1.4 %collective-permute-start.5 = (bf16[1,128,512]{2,1,0:T(8,128)(2,1)S(1)}, bf16[1,128,512]{2,1,0:T(8,128)(2,1)S(1)}, u32[]{:S(2)}, u32[]{:S(2)}) collective-permute-start(bf16[1,128,512]{2,1,0:T(8,128)(2,1)S(1)} %get-tuple-element.137.refs_5_), channel_id=1, source_target_pairs={{0,1},{1,0},{2,3},{3,2},{4,5},{5,4},{6,7},{7,6},{8,9},{9,8},{10,11... | collective-permute-start | bytes 393224 | tf_op jit(solution)/shard_map/core_kv/ppermute | solution.py:978
  28.2 4.8 %collective-permute-start.6 = (bf16[192,128]{1,0:T(8,128)(2,1)S(1)}, bf16[192,128]{1,0:T(8,128)(2,1)S(1)}, u32[]{:S(2)}, u32[]{:S(2)}) collective-permute-start(bf16[192,128]{1,0:T(8,128)(2,1)S(1)} %get-tuple-element.139), channel_id=1, source_target_pairs={{0,2},{2,0},{4,6},{6,4},{1,3},{3,1},{5,7},{7,5},{8,10},{10,8},{12,... | collective-permute-start | bytes 147464 | tf_op jit(solution)/shard_map/chip_attn/ppermute | solution.py:982
  29.5 6.4 %collective-permute-start.7 = (bf16[192,128]{1,0:T(8,128)(2,1)S(1)}, bf16[192,128]{1,0:T(8,128)(2,1)S(1)}, u32[]{:S(2)}, u32[]{:S(2)}) collective-permute-start(bf16[192,128]{1,0:T(8,128)(2,1)S(1)} %get-tuple-element.140), channel_id=1, source_target_pairs={{0,4},{2,6},{4,0},{6,2},{1,5},{3,7},{5,1},{7,3},{8,12},{10,14},{12... | collective-permute-start | bytes 147464 | tf_op jit(solution)/shard_map/chip_attn/ppermute | solution.py:982
  32.8 5.9 %collective-permute-start.8 = (bf16[192,128]{1,0:T(8,128)(2,1)S(1)}, bf16[192,128]{1,0:T(8,128)(2,1)S(1)}, u32[]{:S(2)}, u32[]{:S(2)}) collective-permute-start(bf16[192,128]{1,0:T(8,128)(2,1)S(1)} %get-tuple-element.141), channel_id=1, source_target_pairs={{0,6},{2,4},{4,2},{6,0},{1,7},{3,5},{5,3},{7,1},{8,14},{10,12},{12... | collective-permute-start | bytes 147464 | tf_op jit(solution)/shard_map/chip_attn/ppermute | solution.py:982
  42.0 9.6 %collective-permute-start.16 = (bf16[128,768]{1,0:T(8,128)(2,1)S(1)}, bf16[128,768]{1,0:T(8,128)(2,1)S(1)}, u32[]{:S(2)}, u32[]{:S(2)}) collective-permute-start(bf16[128,768]{1,0:T(8,128)(2,1)S(1)} %get-tuple-element.166), channel_id=1, source_target_pairs={{0,8},{8,0},{16,24},{24,16},{1,9},{9,1},{17,25},{25,17},{2,10},{10... | collective-permute-start | bytes 589832 | tf_op jit(solution)/shard_map/plane_act/ppermute | solution.py:982
  42.7 9.0 %collective-permute-start.17 = (bf16[128,768]{1,0:T(8,128)(2,1)S(1)}, bf16[128,768]{1,0:T(8,128)(2,1)S(1)}, u32[]{:S(2)}, u32[]{:S(2)}) collective-permute-start(bf16[128,768]{1,0:T(8,128)(2,1)S(1)} %get-tuple-element.167), channel_id=1, source_target_pairs={{0,16},{8,24},{16,0},{24,8},{1,17},{9,25},{17,1},{25,9},{2,18},{10... | collective-permute-start | bytes 589832 | tf_op jit(solution)/shard_map/plane_act/ppermute | solution.py:982
  44.2 8.4 %collective-permute-start.18 = (bf16[128,768]{1,0:T(8,128)(2,1)S(1)}, bf16[128,768]{1,0:T(8,128)(2,1)S(1)}, u32[]{:S(2)}, u32[]{:S(2)}) collective-permute-start(bf16[128,768]{1,0:T(8,128)(2,1)S(1)} %get-tuple-element.168), channel_id=1, source_target_pairs={{0,24},{8,16},{16,8},{24,0},{1,25},{9,17},{17,9},{25,1},{2,26},{10... | collective-permute-start | bytes 589832 | tf_op jit(solution)/shard_map/plane_act/ppermute | solution.py:982
  52.6 15.1 %collective-permute-start.19 = (bf16[128,2560]{1,0:T(8,128)(2,1)S(1)}, bf16[128,2560]{1,0:T(8,128)(2,1)S(1)}, u32[]{:S(2)}, u32[]{:S(2)}) collective-permute-start(bf16[128,2560]{1,0:T(8,128)(2,1)S(1)} %get-tuple-element.178), channel_id=1, source_target_pairs={{0,24},{8,16},{16,8},{24,0},{1,25},{9,17},{17,9},{25,1},{2,26},{10... | collective-permute-start | bytes 1966088 | tf_op jit(solution)/shard_map/plane_back/ppermute | solution.py:982
  54.4 4.4 %collective-permute-start.12 = (bf16[192,128]{1,0:T(8,128)(2,1)S(1)}, bf16[192,128]{1,0:T(8,128)(2,1)S(1)}, u32[]{:S(2)}, u32[]{:S(2)}) collective-permute-start(bf16[192,128]{1,0:T(8,128)(2,1)S(1)} %get-tuple-element.159), channel_id=1, source_target_pairs={{0,2},{2,0},{4,6},{6,4},{1,3},{3,1},{5,7},{7,5},{8,10},{10,8},{12,... | collective-permute-start | bytes 147464 | tf_op jit(solution)/shard_map/chip_grad/ppermute | solution.py:982
  54.6 5.0 %collective-permute-start.13 = (bf16[192,128]{1,0:T(8,128)(2,1)S(1)}, bf16[192,128]{1,0:T(8,128)(2,1)S(1)}, u32[]{:S(2)}, u32[]{:S(2)}) collective-permute-start(bf16[192,128]{1,0:T(8,128)(2,1)S(1)} %get-tuple-element.160), channel_id=1, source_target_pairs={{0,4},{2,6},{4,0},{6,2},{1,5},{3,7},{5,1},{7,3},{8,12},{10,14},{12... | collective-permute-start | bytes 147464 | tf_op jit(solution)/shard_map/chip_grad/ppermute | solution.py:982
  56.0 5.9 %collective-permute-start.14 = (bf16[192,128]{1,0:T(8,128)(2,1)S(1)}, bf16[192,128]{1,0:T(8,128)(2,1)S(1)}, u32[]{:S(2)}, u32[]{:S(2)}) collective-permute-start(bf16[192,128]{1,0:T(8,128)(2,1)S(1)} %get-tuple-element.161), channel_id=1, source_target_pairs={{0,6},{2,4},{4,2},{6,0},{1,7},{3,5},{5,3},{7,1},{8,14},{10,12},{12... | collective-permute-start | bytes 147464 | tf_op jit(solution)/shard_map/chip_grad/ppermute | solution.py:982
  65.7 2.0 %collective-permute-start.15 = (bf16[4,128,512]{2,1,0:T(8,128)(2,1)S(1)}, bf16[4,128,512]{2,1,0:T(8,128)(2,1)S(1)}, u32[]{:S(2)}, u32[]{:S(2)}) collective-permute-start(bf16[4,128,512]{2,1,0:T(8,128)(2,1)S(1)} %get-tuple-element.164), channel_id=1, source_target_pairs={{0,1},{1,0},{2,3},{3,2},{4,5},{5,4},{6,7},{7,6},{8,9},{9,8},{10,11... | collective-permute-start | bytes 1572872 | tf_op jit(solution)/shard_map/core_grad/ppermute | solution.py:978
  67.7 3.0 %collective-permute-start.23 = (bf16[4,96,768]{2,1,0:T(8,128)(2,1)S(1)}, bf16[4,96,768]{2,1,0:T(8,128)(2,1)S(1)}, u32[]{:S(2)}, u32[]{:S(2)}) collective-permute-start(bf16[4,96,768]{2,1,0:T(8,128)(2,1)S(1)} %get-tuple-element.190), channel_id=1, source_target_pairs={{0,1},{1,0},{2,3},{3,2},{4,5},{5,4},{6,7},{7,6},{8,9},{9,8},{10,11... | collective-permute-start | bytes 1769480 | tf_op jit(solution)/shard_map/core_down/ppermute | solution.py:978
  67.9 21.2 %collective-permute-start.28 = (bf16[128,2560]{1,0:T(8,128)(2,1)S(1)}, bf16[128,2560]{1,0:T(8,128)(2,1)S(1)}, u32[]{:S(2)}, u32[]{:S(2)}) collective-permute-start(bf16[128,2560]{1,0:T(8,128)(2,1)S(1)} %get-tuple-element.204), channel_id=1, source_target_pairs={{0,8},{8,0},{16,24},{24,16},{1,9},{9,1},{17,25},{25,17},{2,10},{10... | collective-permute-start | bytes 1966088 | tf_op jit(solution)/shard_map/plane_back/ppermute | solution.py:982
  69.3 19.7 %collective-permute-start.29 = (bf16[128,2560]{1,0:T(8,128)(2,1)S(1)}, bf16[128,2560]{1,0:T(8,128)(2,1)S(1)}, u32[]{:S(2)}, u32[]{:S(2)}) collective-permute-start(bf16[128,2560]{1,0:T(8,128)(2,1)S(1)} %get-tuple-element.205), channel_id=1, source_target_pairs={{0,16},{8,24},{16,0},{24,8},{1,17},{9,25},{17,1},{25,9},{2,18},{10... | collective-permute-start | bytes 1966088 | tf_op jit(solution)/shard_map/plane_back/ppermute | solution.py:982
  71.4 11.9 %collective-permute-start.30 = (bf16[2,96,768]{2,1,0:T(8,128)(2,1)S(1)}, bf16[2,96,768]{2,1,0:T(8,128)(2,1)S(1)}, u32[]{:S(2)}, u32[]{:S(2)}) collective-permute-start(bf16[2,96,768]{2,1,0:T(8,128)(2,1)S(1)} %get-tuple-element.207), channel_id=1, source_target_pairs={{0,2},{2,0},{4,6},{6,4},{1,3},{3,1},{5,7},{7,5},{8,10},{10,8},{12,... | collective-permute-start | bytes 884744 | tf_op jit(solution)/shard_map/down_sum/ppermute | solution.py:982
  73.0 10.9 %collective-permute-start.21 = (bf16[576,128]{1,0:T(8,128)(2,1)S(1)}, bf16[576,128]{1,0:T(8,128)(2,1)S(1)}, u32[]{:S(2)}, u32[]{:S(2)}) collective-permute-start(bf16[576,128]{1,0:T(8,128)(2,1)S(1)} %get-tuple-element.182), channel_id=1, source_target_pairs={{0,4},{2,6},{4,0},{6,2},{1,5},{3,7},{5,1},{7,3},{8,12},{10,14},{12... | collective-permute-start | bytes 442376 | tf_op jit(solution)/shard_map/chip_qkv/ppermute | solution.py:982
  74.4 14.6 %collective-permute-start.22 = (bf16[576,128]{1,0:T(8,128)(2,1)S(1)}, bf16[576,128]{1,0:T(8,128)(2,1)S(1)}, u32[]{:S(2)}, u32[]{:S(2)}) collective-permute-start(bf16[576,128]{1,0:T(8,128)(2,1)S(1)} %get-tuple-element.183), channel_id=1, source_target_pairs={{0,6},{2,4},{4,2},{6,0},{1,7},{3,5},{5,3},{7,1},{8,14},{10,12},{12... | collective-permute-start | bytes 442376 | tf_op jit(solution)/shard_map/chip_qkv/ppermute | solution.py:982
  83.3 9.7 %collective-permute-start.20 = (bf16[576,128]{1,0:T(8,128)(2,1)S(1)}, bf16[576,128]{1,0:T(8,128)(2,1)S(1)}, u32[]{:S(2)}, u32[]{:S(2)}) collective-permute-start(bf16[576,128]{1,0:T(8,128)(2,1)S(1)} %get-tuple-element.181), channel_id=1, source_target_pairs={{0,2},{2,0},{4,6},{6,4},{1,3},{3,1},{5,7},{7,5},{8,10},{10,8},{12,... | collective-permute-start | bytes 442376 | tf_op jit(solution)/shard_map/chip_qkv/ppermute | solution.py:982
  83.9 11.3 %collective-permute-start.31 = (bf16[1,96,768]{2,1,0:T(8,128)(2,1)S(1)}, bf16[1,96,768]{2,1,0:T(8,128)(2,1)S(1)}, u32[]{:S(2)}, u32[]{:S(2)}) collective-permute-start(bf16[1,96,768]{2,1,0:T(8,128)(2,1)S(1)} %get-tuple-element.216), channel_id=1, source_target_pairs={{0,4},{2,6},{4,0},{6,2},{1,5},{3,7},{5,1},{7,3},{8,12},{10,14},{12... | collective-permute-start | bytes 442376 | tf_op jit(solution)/shard_map/down_sum/ppermute | solution.py:982
  95.2 2.3 %collective-permute-start.32 = (bf16[4,128,768]{2,1,0:T(8,128)(2,1)S(1)}, bf16[4,128,768]{2,1,0:T(8,128)(2,1)S(1)}, u32[]{:S(2)}, u32[]{:S(2)}) collective-permute-start(bf16[4,128,768]{2,1,0:T(8,128)(2,1)S(1)} %get-tuple-element.217), channel_id=1, source_target_pairs={{0,1},{1,0},{2,3},{3,2},{4,5},{5,4},{6,7},{7,6},{8,9},{9,8},{10,11... | collective-permute-start | bytes 2359304 | tf_op jit(solution)/shard_map/core_up/ppermute | solution.py:978
  95.2 3.0 %collective-permute-start.24 = (bf16[4,96,640]{2,1,0:T(8,128)(2,1)S(1)}, bf16[4,96,640]{2,1,0:T(8,128)(2,1)S(1)}, u32[]{:S(2)}, u32[]{:S(2)}) collective-permute-start(bf16[4,96,640]{2,1,0:T(8,128)(2,1)S(1)} %get-tuple-element.195), channel_id=1, source_target_pairs={{0,1},{1,0},{2,3},{3,2},{4,5},{5,4},{6,7},{7,6},{8,9},{9,8},{10,11... | collective-permute-start | bytes 1474568 | tf_op jit(solution)/shard_map/core_w/ppermute | solution.py:978
  97.5 18.3 %copy-start.5 = (bf16[768,768]{1,0:T(8,128)(2,1)S(1)}, bf16[768,768]{1,0:T(8,128)(2,1)}, u32[]{:S(2)}) copy-start(bf16[768,768]{1,0:T(8,128)(2,1)} %refs_7_.3) | copy-start | bytes 3538948
  98.2 11.2 %collective-permute-start.36 = (bf16[2,128,768]{2,1,0:T(8,128)(2,1)S(1)}, bf16[2,128,768]{2,1,0:T(8,128)(2,1)S(1)}, u32[]{:S(2)}, u32[]{:S(2)}) collective-permute-start(bf16[2,128,768]{2,1,0:T(8,128)(2,1)S(1)} %get-tuple-element.218), channel_id=1, source_target_pairs={{0,2},{2,0},{4,6},{6,4},{1,3},{3,1},{5,7},{7,5},{8,10},{10,8},{12,... | collective-permute-start | bytes 1179656 | tf_op jit(solution)/shard_map/up_sum/ppermute | solution.py:982
  98.9 5.5 %collective-permute-start.25 = (bf16[96,640]{1,0:T(8,128)(2,1)S(1)}, bf16[96,640]{1,0:T(8,128)(2,1)S(1)}, u32[]{:S(2)}, u32[]{:S(2)}) collective-permute-start(bf16[96,640]{1,0:T(8,128)(2,1)S(1)} %get-tuple-element.197), channel_id=1, source_target_pairs={{0,8},{8,0},{16,24},{24,16},{1,9},{9,1},{17,25},{25,17},{2,10},{10... | collective-permute-start | bytes 368648 | tf_op jit(solution)/shard_map/plane_w/ppermute | solution.py:982
  100.6 7.7 %collective-permute-start.26 = (bf16[96,640]{1,0:T(8,128)(2,1)S(1)}, bf16[96,640]{1,0:T(8,128)(2,1)S(1)}, u32[]{:S(2)}, u32[]{:S(2)}) collective-permute-start(bf16[96,640]{1,0:T(8,128)(2,1)S(1)} %get-tuple-element.198), channel_id=1, source_target_pairs={{0,16},{8,24},{16,0},{24,8},{1,17},{9,25},{17,1},{25,9},{2,18},{10... | collective-permute-start | bytes 368648 | tf_op jit(solution)/shard_map/plane_w/ppermute | solution.py:982
  101.0 7.4 %collective-permute-start.27 = (bf16[96,640]{1,0:T(8,128)(2,1)S(1)}, bf16[96,640]{1,0:T(8,128)(2,1)S(1)}, u32[]{:S(2)}, u32[]{:S(2)}) collective-permute-start(bf16[96,640]{1,0:T(8,128)(2,1)S(1)} %get-tuple-element.199), channel_id=1, source_target_pairs={{0,24},{8,16},{16,8},{24,0},{1,25},{9,17},{17,9},{25,1},{2,26},{10... | collective-permute-start | bytes 368648 | tf_op jit(solution)/shard_map/plane_w/ppermute | solution.py:982
  110.1 13.4 %collective-permute-start.37 = (bf16[1,128,768]{2,1,0:T(8,128)(2,1)S(1)}, bf16[1,128,768]{2,1,0:T(8,128)(2,1)S(1)}, u32[]{:S(2)}, u32[]{:S(2)}) collective-permute-start(bf16[1,128,768]{2,1,0:T(8,128)(2,1)S(1)} %get-tuple-element.235), channel_id=1, source_target_pairs={{0,4},{2,6},{4,0},{6,2},{1,5},{3,7},{5,1},{7,3},{8,12},{10,14},{12... | collective-permute-start | bytes 589832 | tf_op jit(solution)/shard_map/up_sum/ppermute | solution.py:982
  111.4 7.9 %collective-permute-start.33 = (bf16[24,640]{1,0:T(8,128)(2,1)S(1)}, bf16[24,640]{1,0:T(8,128)(2,1)S(1)}, u32[]{:S(2)}, u32[]{:S(2)}) collective-permute-start(bf16[24,640]{1,0:T(8,128)(2,1)S(1)} %get-tuple-element.224), channel_id=1, source_target_pairs={{0,2},{2,0},{4,6},{6,4},{1,3},{3,1},{5,7},{7,5},{8,10},{10,8},{12,... | collective-permute-start | bytes 92168 | tf_op jit(solution)/shard_map/chip_w/ppermute | solution.py:982
  112.5 11.0 %collective-permute-start.34 = (bf16[24,640]{1,0:T(8,128)(2,1)S(1)}, bf16[24,640]{1,0:T(8,128)(2,1)S(1)}, u32[]{:S(2)}, u32[]{:S(2)}) collective-permute-start(bf16[24,640]{1,0:T(8,128)(2,1)S(1)} %get-tuple-element.225), channel_id=1, source_target_pairs={{0,4},{2,6},{4,0},{6,2},{1,5},{3,7},{5,1},{7,3},{8,12},{10,14},{12... | collective-permute-start | bytes 92168 | tf_op jit(solution)/shard_map/chip_w/ppermute | solution.py:982
  114.4 9.1 %collective-permute-start.35 = (bf16[24,640]{1,0:T(8,128)(2,1)S(1)}, bf16[24,640]{1,0:T(8,128)(2,1)S(1)}, u32[]{:S(2)}, u32[]{:S(2)}) collective-permute-start(bf16[24,640]{1,0:T(8,128)(2,1)S(1)} %get-tuple-element.226), channel_id=1, source_target_pairs={{0,6},{2,4},{4,2},{6,0},{1,7},{3,5},{5,3},{7,1},{8,14},{10,12},{12... | collective-permute-start | bytes 92168 | tf_op jit(solution)/shard_map/chip_w/ppermute | solution.py:982
  124.7 4.8 %collective-permute-start.38 = (bf16[24,768]{1,0:T(8,128)(2,1)S(1)}, bf16[24,768]{1,0:T(8,128)(2,1)S(1)}, u32[]{:S(2)}, u32[]{:S(2)}) collective-permute-start(bf16[24,768]{1,0:T(8,128)(2,1)S(1)} %get-tuple-element.243), channel_id=1, source_target_pairs={{0,8},{8,0},{16,24},{24,16},{1,9},{9,1},{17,25},{25,17},{2,10},{10... | collective-permute-start | bytes 110600 | tf_op jit(solution)/shard_map/plane_rows/ppermute | solution.py:982
  126.3 4.0 %collective-permute-start.39 = (bf16[24,768]{1,0:T(8,128)(2,1)S(1)}, bf16[24,768]{1,0:T(8,128)(2,1)S(1)}, u32[]{:S(2)}, u32[]{:S(2)}) collective-permute-start(bf16[24,768]{1,0:T(8,128)(2,1)S(1)} %get-tuple-element.244), channel_id=1, source_target_pairs={{0,16},{8,24},{16,0},{24,8},{1,17},{9,25},{17,1},{25,9},{2,18},{10... | collective-permute-start | bytes 110600 | tf_op jit(solution)/shard_map/plane_rows/ppermute | solution.py:982
  126.8 4.9 %collective-permute-start.40 = (bf16[24,768]{1,0:T(8,128)(2,1)S(1)}, bf16[24,768]{1,0:T(8,128)(2,1)S(1)}, u32[]{:S(2)}, u32[]{:S(2)}) collective-permute-start(bf16[24,768]{1,0:T(8,128)(2,1)S(1)} %get-tuple-element.245), channel_id=1, source_target_pairs={{0,24},{8,16},{16,8},{24,0},{1,25},{9,17},{17,9},{25,1},{2,26},{10... | collective-permute-start | bytes 110600 | tf_op jit(solution)/shard_map/plane_rows/ppermute | solution.py:982
  (8 other events, 46.5 us)
